TPU v7x, 256 devices: a whole 4x4x8 slice. The times are simulated.
256 devices in a mesh: seq: 32 (over x, z), head: 8 (over y, core).
Axes of the slice: x: 4, y: 4, z: 8, core: 2. Of those that a mesh axis runs over, the one named last changes fastest.
Arguments:
- query_in: bfloat16 [8192, 8192], P('seq', 'head'), may hold values from -1.796875 to 1.796875
- key_in: bfloat16 [8192, 8192], P('seq', 'head'), may hold values from -1.796875 to 1.796875
- value_in: bfloat16 [8192, 8192], P('seq', 'head'), may hold values from -11 to 11
- log_decay: float32 [8192, 64], P('seq', 'head'), may hold values from -1 to 0, as said below
- norm_gain: float32 [8192], P('head'), may hold values from 0.5 to 1.5
- prompt_lengths: int32 [4], replicated, may hold values from 1 to 6144, 8192 in all
- step_query: bfloat16 [4, 512, 8192], P(None, 'seq', 'head'), may hold values from -1.796875 to 1.796875
- step_key: bfloat16 [4, 512, 8192], P(None, 'seq', 'head'), may hold values from -1.796875 to 1.796875
- step_value: bfloat16 [4, 512, 8192], P(None, 'seq', 'head'), may hold values from -6 to 6
- step_decay: float32 [4, 512, 64], P(None, 'seq', 'head'), may hold values from -0.3 to -0.01
- row_prompt: int32 [512], P('seq'), may hold values from 0 to 3
Outputs:
- attn_out: bfloat16 [8192, 8192], P('seq', 'head')
- decode_out: bfloat16 [4, 512, 8192], P(None, 'seq', 'head')
Inputs may be any that keep to these rules, and one draw needn't show every extreme that they name: `log_decay`: Negative; per head and token.
All inputs are finite; a program needn't handle non-finite values.
Results may differ from a plain program's by a relative error of at most 0.0056.
Values sent between devices are 32-bit elements; how exact they have to be, the bound alone decides.
No kernel may reach another device: no remote copies, remote signals or barrier semaphores. Data moves between devices by JAX's collectives and lax.ppermute only.
A program may use at most 64 MiB of HBM per device.

v0:
```python
import jax
import jax.numpy as jnp
from jax import lax
from jax.sharding import Mesh
from jax.sharding import PartitionSpec as P

HEAD_COUNT = 64
HDIM = 128
BLOCK = 256
PROMPTS = 4
SEQ = ("seq_0", "seq_1")


EPSILON = 1e-06


def neutral_like(x, identity):
    return jax.tree.map(
        lambda a, e: jnp.broadcast_to(jnp.asarray(e, a.dtype), a.shape), x, identity
    )


def entering(x, axes, combine, identity):
    before = start = neutral_like(x, identity)
    so_far = x
    for axis in reversed(axes):
        size, here = (lax.axis_size(axis), lax.axis_index(axis))
        pieces = jax.tree.map(lambda part: lax.all_gather(part, axis), so_far)
        inside, so_far = (start, start)
        for k in range(size):
            passed = k < here
            so_far = combine(so_far, jax.tree.map(lambda part: part[k], pieces))
            inside = jax.tree.map(lambda new, old: jnp.where(passed, new, old), so_far, inside)
        before = combine(inside, before)
    return before


def sent_to_all(x, axis):
    copies = jnp.broadcast_to(x, (lax.axis_size(axis), *x.shape))
    return lax.all_to_all(copies, axis, split_axis=0, concat_axis=0, tiled=True)


def over_copies(x, axis):
    everything = sent_to_all(x, axis)
    return jnp.sum(everything, axis=0)


def segment_ids(prompt_lengths, positions):
    boundary = jnp.cumsum(prompt_lengths)
    return jnp.sum((positions[:, None] >= boundary[None, :]).astype(jnp.int32), axis=1)


def combine_pairs(earlier, later):
    return (earlier[0] * later[0], later[0][:, None, None] * earlier[1] + later[1])


def local(
    query_in,
    key_in,
    value_in,
    log_decay,
    norm_gain,
    prompt_lengths,
    step_query,
    step_key,
    step_value,
    step_decay,
    row_prompt,
):
    tok_count = query_in.shape[0]
    heads_here = log_decay.shape[1]
    nblocks = tok_count // BLOCK
    first = lax.axis_index(SEQ) * tok_count
    positions = first + jnp.arange(tok_count, dtype=jnp.int32)
    segs = segment_ids(prompt_lengths, positions)
    seg_entry = jnp.where(first > 0, segment_ids(prompt_lengths, (first - 1)[None])[0], -1)
    shape4 = (nblocks, BLOCK, heads_here, HDIM)
    queries = query_in.reshape(shape4)
    keys_blk = key_in.reshape(shape4)
    values_blk = value_in.reshape(shape4)
    cumul = jnp.cumsum(log_decay.reshape(nblocks, BLOCK, heads_here), axis=1)
    seg_blocks = segs.reshape(nblocks, BLOCK)
    seg_front = jnp.concatenate([seg_entry[None], seg_blocks[:-1, -1]])
    causal = jnp.arange(BLOCK)[:, None] >= jnp.arange(BLOCK)[None, :]
    linked = (causal[None] & (seg_blocks[:, :, None] == seg_blocks[:, None, :]))[:, None]
    cum_heads = jnp.transpose(cumul, (0, 2, 1))
    spread = cum_heads[:, :, :, None] - cum_heads[:, :, None, :]
    factor = jnp.where(linked, jnp.exp(jnp.where(linked, spread, 0.0)), 0.0)
    scores = jnp.einsum("nthd,nshd->nhts", queries, keys_blk, preferred_element_type=jnp.float32)
    weights = (scores * factor).astype(jnp.bfloat16)
    inner = jnp.einsum("nhts,nshd->nthd", weights, values_blk, preferred_element_type=jnp.float32)
    keep = (
        jnp.exp(cumul[:, -1:, :] - cumul)
        * (seg_blocks == seg_blocks[:, -1:]).astype(jnp.float32)[:, :, None]
    )
    keyed = (keys_blk.astype(jnp.float32) * keep[..., None]).astype(jnp.bfloat16)
    updates = jnp.einsum("nshd,nshe->nhde", keyed, values_blk, preferred_element_type=jnp.float32)
    onward = (
        jnp.exp(cumul[:, -1, :]) * (seg_blocks[:, -1] == seg_front).astype(jnp.float32)[:, None]
    )
    local_states = [jnp.zeros((heads_here, HDIM, HDIM), jnp.float32)]
    growth = [jnp.ones((heads_here,), jnp.float32)]
    blk_index = 0
    local_states.append(onward[blk_index][:, None, None] * local_states[-1] + updates[blk_index])
    growth.append(onward[blk_index] * growth[-1])
    summary = (growth[-1], local_states[-1])
    identity = (
        jnp.ones((heads_here,), jnp.float32),
        jnp.zeros((heads_here, HDIM, HDIM), jnp.float32),
    )
    entry = entering(summary, SEQ, combine_pairs, identity)
    entry_state = entry[1]
    start_states = jnp.stack([local_states[0] + growth[0][:, None, None] * entry_state])
    state_half = start_states.astype(jnp.bfloat16)
    carried = jnp.exp(cumul) * (seg_blocks == seg_front[:, None]).astype(jnp.float32)[:, :, None]
    outer = (
        jnp.einsum("nthd,nhde->nthe", queries, state_half, preferred_element_type=jnp.float32)
        * carried[..., None]
    )
    mixed = (inner + outer).reshape(tok_count, heads_here * HDIM)
    squares = over_copies(jnp.sum(mixed * mixed, axis=1), "head")
    scale = lax.rsqrt(squares / (HEAD_COUNT * HDIM) + EPSILON)
    attn_out = (mixed * scale[:, None] * norm_gain[None, :]).astype(jnp.bfloat16)
    boundary = jnp.cumsum(prompt_lengths)

    def prompt_end(prompt):
        last_tok = boundary[prompt] - 1
        local_tok = last_tok - first
        owned = (local_tok >= 0) & (local_tok < tok_count)
        safe_tok = jnp.clip(local_tok, 0, tok_count - 1)
        blk_index = safe_tok // BLOCK
        offset = safe_tok - blk_index * BLOCK
        cum_blk = cumul[blk_index]
        reached = cum_blk[offset]
        taken = (jnp.arange(BLOCK) <= offset) & (seg_blocks[blk_index] == prompt)
        keep_end = (
            jnp.exp(jnp.where(taken[:, None], reached[None, :] - cum_blk, 0.0))
            * taken.astype(jnp.float32)[:, None]
        )
        tailed = (keys_blk[blk_index].astype(jnp.float32) * keep_end[:, :, None]).astype(
            jnp.bfloat16
        )
        part = jnp.einsum(
            "shd,she->hde", tailed, values_blk[blk_index], preferred_element_type=jnp.float32
        )
        lead = jnp.exp(reached) * (seg_front[blk_index] == prompt).astype(jnp.float32)
        total = lead[:, None, None] * start_states[blk_index] + part
        return total * owned.astype(jnp.float32)

    candidates = lax.map(prompt_end, jnp.arange(PROMPTS, dtype=jnp.int32))
    prompt_state = lax.psum(candidates, SEQ)
    rows_here = row_prompt.shape[0]
    row_states = jnp.take(prompt_state, row_prompt, axis=0)
    results = []
    for section in range(step_query.shape[0]):
        query_now = step_query[section].astype(jnp.float32).reshape(rows_here, heads_here, HDIM)
        key_now = step_key[section].astype(jnp.float32).reshape(rows_here, heads_here, HDIM)
        value_now = step_value[section].astype(jnp.float32).reshape(rows_here, heads_here, HDIM)
        row_states = (
            jnp.exp(step_decay[section])[:, :, None, None] * row_states
            + key_now[:, :, :, None] * value_now[:, :, None, :]
        )
        results.append(
            jnp.einsum(
                "rhd,rhde->rhe", query_now, row_states, precision=lax.Precision.HIGHEST
            ).reshape(rows_here, heads_here * HDIM)
        )
    decoded = jnp.stack(results)
    step_squares = over_copies(jnp.sum(decoded * decoded, axis=2), "head")
    step_scale = lax.rsqrt(step_squares / (HEAD_COUNT * HDIM) + EPSILON)
    decode_out = (decoded * step_scale[:, :, None] * norm_gain[None, None, :]).astype(jnp.bfloat16)
    return (attn_out, decode_out)


def solution(mesh):
    split = Mesh(mesh.devices.reshape(4, 8, mesh.shape["head"]), ("seq_0", "seq_1", "head"))
    placed = (
        P(SEQ, "head"),
        P(SEQ, "head"),
        P(SEQ, "head"),
        P(SEQ, "head"),
        P("head"),
        P(),
        P(None, SEQ, "head"),
        P(None, SEQ, "head"),
        P(None, SEQ, "head"),
        P(None, SEQ, "head"),
        P(SEQ),
    )
    return jax.shard_map(
        local,
        mesh=split,
        in_specs=placed,
        out_specs=(P(SEQ, "head"), P(None, SEQ, "head")),
        check_vma=False,
    )
```

profile of v0, /device:TPU:1, one launch (start us, length us, event | category | flops | bytes accessed | tf_op | source)
XLA Modules:
  0.0 363.0 jit_solution(15198924258557551946)
XLA Ops:
  7.3 1.3 copy.163
  8.6 1.3 reduce-window.11
  10.0 0.8 reduce-window.10
  10.9 0.6 slice.202
  11.5 0.6 fusion.69
  12.8 0.7 compare_convert_fusion.1
  14.5 2.1 convolution_add_fusion.1
  16.8 16.1 %all-gather = f32[8,1,8]{2,1,0:T(1,128)S(1)} all-gather(f32[1,1,8]{2,1,0:T(1,128)S(1)} %copy.137), channel_id=2, replica_groups=mesh['seq_0'=4,'seq_1'=8,'head'=8] {'seq_1'}, dimensions={0}, use_global_device_ids=true | all-gather | bytes 288 | tf_op jit(solution)/shard_map/all_gather | solution.py:28
  32.9 42.5 %all-gather.8.cloned.1.call-done = f32[64,128,128]{2,1,0:T(8,128)} async-done(((f32[8,128,128]{2,1,0:T(8,128)}), f32[64,128,128]{2,1,0:T(8,128)}) %all-gather.8.cloned.1.call-update) | async-done | bytes 4194320 | tf_op jit(solution)/shard_map/all_gather | solution.py:28
  75.4 3.3 fusion.51
  78.8 7.6 %all-gather.2 = f32[4,1,8]{2,1,0:T(1,128)S(1)} all-gather(f32[1,1,8]{2,1,0:T(1,128)S(1)} %get-tuple-element.296), channel_id=1, replica_groups=mesh['seq_0'=4,'seq_1'=8,'head'=8] {'seq_0'}, dimensions={0}, use_global_device_ids=true | all-gather | bytes 160 | tf_op jit(solution)/shard_map/all_gather | solution.py:28
  86.9 0.5 compare_select_fusion
  87.4 0.7 bitcast_add_fusion.1
  88.1 22.8 %all-gather.6.cloned.1.call-done = f32[4,8,128,128]{3,2,1,0:T(8,128)} async-done(((f32[1,8,128,128]{3,2,1,0:T(8,128)}), f32[4,8,128,128]{3,2,1,0:T(8,128)}) %all-gather.6.cloned.1.call-update) | async-done | bytes 2097168 | tf_op jit(solution)/shard_map/all_gather | solution.py:28
  110.9 3.6 fusion.50
  114.6 25.8 %while.13 = (s32[]{:T(128)}, f32[4,8,128,128]{3,2,1,0:T(8,128)}, s32[4]{0:T(128)S(1)}, s32[4]{0:T(128)S(1)}, s32[]{:T(128)}, /*index=5*/f32[1,256,8]{1,2,0:T(8,1...) while((s32[]{:T(128)}, f32[4,8,128,128]{3,2,1,0:T(8,128)}, ...), condition=%wide.region_8.9_spmd, body=%wide.region_7.8_spmd.sunk | while | flops 68295712 | bytes 2126503 | solution.py:150
  114.6 0.6 dynamic_slice.29
  115.2 0.7 compare_reduce_fusion.2
  117.8 0.6 dynamic_slice.30
  119.9 1.1 fusion.95
  121.0 0.6 dynamic_slice.29
  121.6 0.7 compare_reduce_fusion.2
  124.2 0.6 dynamic_slice.30
  126.4 1.1 fusion.95
  127.5 0.6 dynamic_slice.29
  128.1 0.7 compare_reduce_fusion.2
  130.7 0.6 dynamic_slice.30
  132.8 1.1 fusion.95
  133.9 0.6 dynamic_slice.29
  134.5 0.7 compare_reduce_fusion.2
  137.1 0.6 dynamic_slice.30
  139.3 1.1 fusion.95
  140.4 0.6 compare_and_fusion.1
  141.0 0.6 exponential_bitcast_fusion
  141.7 0.7 fusion.76
  142.4 0.6 convert_bitcast_fusion
  143.0 0.6 convert_bitcast_fusion.1
  143.7 2.0 fusion.36
  145.7 1.6 multiply_reduce_fusion
  147.3 0.6 broadcast_in_dim.90
  147.9 5.0 %all-to-all-start = ((f32[8,1,256]{2,1,0:T(1,128)}), f32[8,1,256]{2,1,0:T(1,128)S(1)}, u32[]{:S(2)}, u32[]{:S(2)}) async-start(f32[8,1,256]{2,1,0:T(1,128)} %broadcast_in_dim.90), calls=%async_computation | async-start | bytes 16384 | tf_op jit(solution)/shard_map/all_to_all | solution.py:40
  152.9 0.6 pad_clamp_fusion
  153.5 0.8 reshape.654
  154.3 0.9 copy.167
  155.1 0.9 copy.166
  156.0 1.3 copy.144
  157.3 0.8 reshape.656
  158.2 0.7 copy.148
  158.9 0.8 reshape.658
  159.8 0.8 copy.149
  160.5 0.8 reshape.660
  161.3 0.7 copy.150
  162.1 0.3 copy.143
  162.5 127.9 %all-reduce.2.cloned.1.call-done = f32[4,8,128,128]{3,2,1,0:T(8,128)} async-done(((f32[4,8,128,128]{3,2,1,0:T(8,128)}), f32[4,8,128,128]{3,2,1,0:T(8,128)}) %all-reduce.2.cloned.1.call-update) | async-done | bytes 2097168 | tf_op jit(solution)/shard_map/psum | solution.py:151
  290.4 6.0 %gather_fusion = f32[16,8,128,128]{3,2,1,0:T(8,128)} fusion(f32[4,8,128,128]{3,2,1,0:T(8,128)} %all-reduce.2.cloned.1.call-done, s32[1024]{0:T(1024)} %pad_clamp_fusion), kind=kCustom, calls=%fused_computation | custom fusion | bytes 16777280 | tf_op jit(solution)/shard_map/jit(_take)/gather | solution.py:153
  296.4 7.4 %fusion.72 = f32[16,8,1,128]{3,2,1,0:T(1,128)S(1)} fusion(bf16[16,8,128,1]{2,3,1,0:T(2,128)(2,1)S(1)} %reshape.654, f32[16,8,128,128]{3,2,1,0:T(8,128)} %gather_fusion, f32[16,8,128]{2,1,0:T(8,128)S(1)} %bitcast.300, f32[16,8,128]{2,1,0:T(8,128)S(1)} %bitcast.304, f32[16,8]{1,0:T(8,128)S(1)} %copy-done.7, pred[16]{0:T(512)(128)(4,1)S(1)} %copy-done.11), kind=kOutput, calls=%fused_computation.159 | convolution fusion | flops 33554432 | bytes 8618512 | tf_op jit(solution)/shard_map/rhd,rhde->rhe/dot_general | solution.py:164
  303.9 9.2 %fusion.15 = f32[16,8,1,128]{3,2,1,0:T(1,128)S(1)} fusion(bf16[16,8,128,1]{2,3,1,0:T(2,128)(2,1)S(1)} %reshape.656, f32[16,8,128]{2,1,0:T(8,128)S(1)} %bitcast.308, f32[16,8,128]{2,1,0:T(8,128)S(1)} %bitcast.311, f32[16,8]{1,0:T(8,128)S(1)} %copy.148, f32[16,8,128,128]{3,2,1,0:T(8,128)} %gather_fusion, f32[16,8,128]{2,1,0:T(8,128)S(1)} %bitcast.301, ...), kind=kOutput, calls=%fused_computation.26 | convolution fusion | flops 39845888 | bytes 8750096 | tf_op jit(solution)/shard_map/rhd,rhde->rhe/dot_general | solution.py:164
  313.1 11.8 %fusion.16 = f32[16,8,1,128]{3,2,1,0:T(1,128)S(1)} fusion(bf16[16,8,128,1]{2,3,1,0:T(2,128)(2,1)S(1)} %reshape.658, f32[16,8,128]{2,1,0:T(8,128)S(1)} %bitcast.314, f32[16,8,128]{2,1,0:T(8,128)S(1)} %bitcast.316, f32[16,8]{1,0:T(8,128)S(1)} %copy.149, f32[16,8,128]{2,1,0:T(8,128)S(1)} %bitcast.309, f32[16,8,128]{2,1,0:T(8,128)S(1)} %bitcast.312, ...), kind=kOutput, calls=%fused_computation.27 | convolution fusion | flops 46137344 | bytes 8881680 | tf_op jit(solution)/shard_map/rhd,rhde->rhe/dot_general | solution.py:164
  325.0 15.7 %fusion.11 = f32[16,8,1,128]{3,2,1,0:T(1,128)S(1)} fusion(bf16[16,8,128,1]{2,3,1,0:T(2,128)(2,1)S(1)} %reshape.660, f32[16,8,128]{2,1,0:T(8,128)S(1)} %bitcast.318, f32[16,8,128]{2,1,0:T(8,128)S(1)} %bitcast.319, f32[16,8]{1,0:T(8,128)S(1)} %copy.150, f32[16,8,128]{2,1,0:T(8,128)S(1)} %bitcast.315, f32[16,8,128]{2,1,0:T(8,128)S(1)} %bitcast.317, ...), kind=kOutput, calls=%fused_computation.19 | convolution fusion | flops 52428800 | bytes 9013264 | tf_op jit(solution)/shard_map/rhd,rhde->rhe/dot_general | solution.py:164
  340.8 0.6 broadcast_in_dim.95
  341.4 9.6 %all-to-all-start.1 = ((f32[8,4,16]{2,1,0:T(4,128)}), f32[8,4,16]{2,1,0:T(4,128)S(1)}, u32[]{:S(2)}, u32[]{:S(2)}) async-start(f32[8,4,16]{2,1,0:T(4,128)} %broadcast_in_dim.95), calls=%async_computation.1 | async-start | bytes 32768 | tf_op jit(solution)/shard_map/all_to_all | solution.py:40
  351.1 0.9 multiply_convert_fusion.1
  352.0 3.7 %all-to-all-done.1 = f32[8,4,16]{2,1,0:T(4,128)S(1)} async-done(((f32[8,4,16]{2,1,0:T(4,128)}), f32[8,4,16]{2,1,0:T(4,128)S(1)}, u32[]{:S(2)}, u32[]{:S(2)}) %all-to-all-start.1) | async-done | bytes 2080 | tf_op jit(solution)/shard_map/all_to_all | solution.py:40
  355.8 0.8 multiply_convert_fusion.4
  (84 shorter events, 3.0 us)
Async XLA Ops:
  7.2 136.5 %copy-start = (bf16[256,1024]{1,0:T(8,128)(2,1)S(1)}, bf16[256,1024]{1,0:T(8,128)(2,1)}, u32[]{:S(2)}) copy-start(bf16[256,1024]{1,0:T(8,128)(2,1)} %param.13) | copy-start | bytes 1572868
  7.2 79.2 %copy-start.1 = (bf16[256,1024]{1,0:T(8,128)(2,1)S(1)}, bf16[256,1024]{1,0:T(8,128)(2,1)}, u32[]{:S(2)}) copy-start(bf16[256,1024]{1,0:T(8,128)(2,1)} %param.15) | copy-start | bytes 1572868
  7.2 79.7 %copy-start.10 = (s32[16]{0:T(128)S(1)}, s32[16]{0:T(128)}, u32[]{:S(2)}) copy-start(s32[16]{0:T(128)} %param.23) | copy-start | bytes 196
  7.2 68.2 %all-gather.8.cloned.1.call-start = ((), (), s32[]{:S(2)}) async-start(), calls=%async_computation.4 | async-start | bytes 4718592 | tf_op jit(solution)/shard_map/all_gather | solution.py:28
  16.6 94.3 %all-gather.6.cloned.1.call-start = ((), (), s32[]{:S(2)}) async-start(), calls=%async_computation.2 | async-start | bytes 2621440 | tf_op jit(solution)/shard_map/all_gather | solution.py:28
  78.8 211.6 %all-reduce.2.cloned.1.call-start = ((), (), s32[]{:S(2)}) async-start(), calls=%async_computation.3 | async-start | bytes 4194304 | tf_op jit(solution)/shard_map/psum | solution.py:151
  114.5 26.5 %copy-start.6 = (f32[4,16,8]{1,2,0:T(8,128)S(1)}, f32[4,16,8]{1,2,0:T(8,128)}, u32[]{:S(2)}) copy-start(f32[4,16,8]{1,2,0:T(8,128)} %param.22) | copy-start | bytes 6148
  114.5 27.2 %copy-start.4 = (bf16[4,16,1024]{2,1,0:T(8,128)(2,1)S(1)}, bf16[4,16,1024]{2,1,0:T(8,128)(2,1)}, u32[]{:S(2)}) copy-start(bf16[4,16,1024]{2,1,0:T(8,128)(2,1)} %param.19) | copy-start | bytes 393220
  114.5 27.9 %copy-start.2 = (bf16[4,16,1024]{2,1,0:T(8,128)(2,1)S(1)}, bf16[4,16,1024]{2,1,0:T(8,128)(2,1)}, u32[]{:S(2)}) copy-start(bf16[4,16,1024]{2,1,0:T(8,128)(2,1)} %param.21) | copy-start | bytes 393220
  114.5 28.5 %copy-start.3 = (bf16[4,16,1024]{2,1,0:T(8,128)(2,1)S(1)}, bf16[4,16,1024]{2,1,0:T(8,128)(2,1)}, u32[]{:S(2)}) copy-start(bf16[4,16,1024]{2,1,0:T(8,128)(2,1)} %param.20) | copy-start | bytes 393220
  114.5 29.1 %copy-start.8 = (f32[8,256]{1,0:T(8,128)S(1)}, f32[8,256]{1,0:T(8,128)}, u32[]{:S(2)}) copy-start(f32[8,256]{1,0:T(8,128)} %bitcast_add_fusion.1) | copy-start | bytes 24580
  140.4 12.5 %copy-start.9 = (s32[16]{0:T(128)S(1)}, s32[16]{0:T(128)}, u32[]{:S(2)}) copy-start(s32[16]{0:T(128)} %compare_select_fusion) | copy-start | bytes 196
  147.9 14.5 %all-to-all-start = ((f32[8,1,256]{2,1,0:T(1,128)}), f32[8,1,256]{2,1,0:T(1,128)S(1)}, u32[]{:S(2)}, u32[]{:S(2)}) async-start(f32[8,1,256]{2,1,0:T(1,128)} %broadcast_in_dim.90), calls=%async_computation | async-start | bytes 16384 | tf_op jit(solution)/shard_map/all_to_all | solution.py:40
  162.5 134.0 %copy-start.7 = (f32[16,8]{1,0:T(8,128)S(1)}, f32[16,8]{1,0:T(8,128)}, u32[]{:S(2)}) copy-start(f32[16,8]{1,0:T(8,128)} %copy.144) | copy-start | bytes 1540
  162.5 134.0 %copy-start.11 = (pred[16]{0:T(512)(128)(4,1)S(1)}, pred[16]{0:T(512)(128)(4,1)}, u32[]{:S(2)}) copy-start(pred[16]{0:T(512)(128)(4,1)} %compare_and_fusion.1) | copy-start | bytes 52
  325.0 26.1 %copy-start.5 = (f32[1024]{0:T(1024)S(1)}, f32[1024]{0:T(1024)}, u32[]{:S(2)}) copy-start(f32[1024]{0:T(1024)} %param.17) | copy-start | bytes 12292
  341.4 14.3 %all-to-all-start.1 = ((f32[8,4,16]{2,1,0:T(4,128)}), f32[8,4,16]{2,1,0:T(4,128)S(1)}, u32[]{:S(2)}, u32[]{:S(2)}) async-start(f32[8,4,16]{2,1,0:T(4,128)} %broadcast_in_dim.95), calls=%async_computation.1 | async-start | bytes 32768 | tf_op jit(solution)/shard_map/all_to_all | solution.py:40
Sparse Core Ops, SparseCore 0:
  16.8 58.6 all-gather.7
  78.9 31.9 all-gather.5
  140.5 149.8 all-reduce.1
where the time goes:
time: 364 us; the launch traced here: 363 us
  waiting for transfers between devices  197 us (54%)
  matrix products  54.3 us (15%)
  local copies, waits for them, and re-layouts  25.6 us (7%)
  blocking collectives  23.7 us (7%)
  other arithmetic  19.4 us (5%)
  between operations  15.4 us (4%)
  starting transfers between devices  14.7 us (4%)
  loops' own time  12.9 us (4%)
    psum x1, waiting for transfers between devices, local(): prompt_state = lax.psum(candidates, SEQ)  128 us
    all_gather x2, waiting for transfers between devices, entering(): pieces = jax.tree.map(lambda part: lax.all_gather(part, axis), so_far)  65.4 us
    dot_general x4, matrix products, local(): jnp.einsum('rhd,rhde->rhe', query_now, row_states, precision=lax.Precisio...  44.1 us
    all_gather x2, blocking collectives, entering(): pieces = jax.tree.map(lambda part: lax.all_gather(part, axis), so_far)  23.7 us
    all_to_all x2, starting transfers between devices, sent_to_all(): return lax.all_to_all(copies, axis, split_axis=0, concat_axis=0, tiled=True)  14.6 us
    another operation x1, loops' own time, local(): candidates = lax.map(prompt_end, jnp.arange(PROMPTS, dtype=jnp.int32))  12.9 us
  transfers between devices with their start and end apart: 5, of which 4 were waited for; matrix products, arithmetic and copies ran while one was open for 5% of the time, Pallas kernels for 0%

commit v1 on v0

v1 whole, which is shorter than its diff:
```python
import functools

import jax
import jax.numpy as jnp
from jax import lax
from jax.experimental import pallas as pl
from jax.experimental.pallas import tpu as pltpu
from jax.sharding import Mesh
from jax.sharding import PartitionSpec as P

HEAD_COUNT = 64
HDIM = 128
BLOCK = 256
PROMPTS = 4
STEPS = 4
SEQ = ("seq_0", "seq_1")
EPSILON = 1e-06

NX = 4
HEADS = 8
NDEV = NX * HEADS
QUART = HDIM // NX
ROWS_DEV = 16

U0, T0, Q0, S0, MSG = 0, 32, 64, 80, 88

BF = jnp.bfloat16
F32 = jnp.float32
HI = lax.Precision.HIGHEST

SMEM = pl.BlockSpec(memory_space=pltpu.SMEM)
VMEM = pl.BlockSpec(memory_space=pltpu.VMEM)


def params(mib=48):
    return pltpu.CompilerParams(vmem_limit_bytes=mib << 20)


def cost(us):
    return pl.CostEstimate(flops=int(us * 1e9), bytes_accessed=int(us * 3e6), transcendentals=0)


def bounds(lens):
    ends = []
    total = lens[0]
    for p in range(PROMPTS):
        if p:
            total = total + lens[p]
        ends.append(total)
    return ends


def seg_of(pos, ends):
    out = (pos >= ends[0]).astype(jnp.int32)
    for p in range(1, PROMPTS):
        out = out + (pos >= ends[p]).astype(jnp.int32)
    return out


def entry_seg(first, ends):
    return jnp.where(first > 0, seg_of(first - 1, ends), -1)


def cum_columns(logd):
    t = lax.broadcasted_iota(jnp.int32, (BLOCK, BLOCK), 0)
    s = lax.broadcasted_iota(jnp.int32, (BLOCK, BLOCK), 1)
    tri = (s <= t).astype(F32)
    return jnp.dot(tri, logd, precision=HI, preferred_element_type=F32)


def contract_rows(a, b):
    return lax.dot_general(a, b, (((0,), (0,)), ((), ())), preferred_element_type=F32)


def contract_cols(a, b):
    return lax.dot_general(a, b, (((1,), (1,)), ((), ())), preferred_element_type=F32)


def send_kernel(lens, here, rows, key_ref, value_ref, logd_ref, query_ref, out_ref, cum_ref):
    first = here[0] * BLOCK
    ends = bounds(lens)
    front = entry_seg(first, ends)
    seg_last = seg_of(first + (BLOCK - 1), ends)
    cum = cum_columns(logd_ref[...])
    cum_ref[...] = cum
    tok = lax.broadcasted_iota(jnp.int32, (BLOCK, HEADS), 0)
    seg = seg_of(tok + first, ends)
    last = cum[BLOCK - 1 : BLOCK, :]
    keep = jnp.where(seg == seg_last, jnp.exp(last - cum), 0.0)
    growth = jnp.exp(last) * (seg_last == front).astype(F32)
    leads = []
    found = jnp.int32(-1)
    spot = jnp.int32(0)
    for p in range(PROMPTS):
        local = ends[p] - 1 - first
        inside = (local >= 0) & (local < BLOCK)
        safe = jnp.clip(local, 0, BLOCK - 1)
        reached = cum_ref[pl.ds(safe, 1), :]
        leads.append(jnp.exp(reached) * (inside & (front == p)).astype(F32))
        interior = (local >= 0) & (local < BLOCK - 1)
        take = interior & (found < 0)
        found = jnp.where(take, p, found)
        spot = jnp.where(take, local, spot)
    lane = lax.broadcasted_iota(jnp.int32, (1, HDIM), 1)
    ids = jnp.zeros((1, HDIM), F32)
    for r in range(ROWS_DEV):
        ids = jnp.where(lane == r, rows[r].astype(F32), ids)

    for h in range(HEADS):
        cols = slice(h * HDIM, (h + 1) * HDIM)
        keyed = (key_ref[:, cols].astype(F32) * keep[:, h : h + 1]).astype(BF)
        update = contract_rows(keyed, value_ref[:, cols])
        scal = jnp.concatenate(
            [jnp.broadcast_to(growth[:, h : h + 1], (1, HDIM))]
            + [jnp.broadcast_to(leads[p][:, h : h + 1], (1, HDIM)) for p in range(PROMPTS)]
            + [ids, ids, ids],
            axis=0,
        )
        for x in range(NX):
            out_ref[x * HEADS + h, U0:T0, :] = update[x * QUART : (x + 1) * QUART, :]
            out_ref[x * HEADS + h, Q0:S0, :] = query_ref[x, :, cols].astype(F32)
            out_ref[x * HEADS + h, S0:MSG, :] = scal

    @pl.when(found < 0)
    def _():
        out_ref[:, T0:Q0, :] = jnp.zeros((NDEV, QUART, HDIM), F32)

    @pl.when(found >= 0)
    def _():
        reached = cum_ref[pl.ds(spot, 1), :]
        taken = (tok <= spot) & (seg == found)
        tail = jnp.where(taken, jnp.exp(jnp.where(taken, reached - cum, 0.0)), 0.0)
        for h in range(HEADS):
            cols = slice(h * HDIM, (h + 1) * HDIM)
            tailed = (key_ref[:, cols].astype(F32) * tail[:, h : h + 1]).astype(BF)
            part = contract_rows(tailed, value_ref[:, cols])
            for x in range(NX):
                out_ref[x * HEADS + h, T0:Q0, :] = part[x * QUART : (x + 1) * QUART, :]


def intra_kernel(
    lens, here, query_ref, key_ref, value_ref, logd_ref, sq_ref, sk_ref, sv_ref, sd_ref,
    intra_ref, carried_ref, local_ref, scarried_ref,
):
    first = here[0] * BLOCK
    ends = bounds(lens)
    front = entry_seg(first, ends)
    logd = logd_ref[...]
    t = lax.broadcasted_iota(jnp.int32, (BLOCK, BLOCK), 0)
    s = lax.broadcasted_iota(jnp.int32, (BLOCK, BLOCK), 1)
    cum = jnp.dot((s <= t).astype(F32), logd, precision=HI, preferred_element_type=F32)
    cum_rows = lax.dot_general(
        logd, (t <= s).astype(F32), (((0,), (0,)), ((), ())), precision=HI, preferred_element_type=F32
    )
    linked = (s <= t) & (seg_of(t + first, ends) == seg_of(s + first, ends))
    tok = lax.broadcasted_iota(jnp.int32, (BLOCK, HEADS), 0)
    carried_ref[...] = jnp.where(seg_of(tok + first, ends) == front, jnp.exp(cum), 0.0)
    for h in range(HEADS):
        cols = slice(h * HDIM, (h + 1) * HDIM)
        scores = contract_cols(query_ref[:, cols], key_ref[:, cols])
        spread = cum[:, h : h + 1] - cum_rows[h : h + 1, :]
        factor = jnp.exp(jnp.where(linked, spread, -1e30))
        weights = (scores * factor).astype(BF)
        intra_ref[:, cols] = jnp.dot(weights, value_ref[:, cols], preferred_element_type=F32)

    n = STEPS * ROWS_DEV
    a = lax.broadcasted_iota(jnp.int32, (n, n), 0)
    b = lax.broadcasted_iota(jnp.int32, (n, n), 1)
    same = (b <= a) & ((a - b) % ROWS_DEV == 0)
    sd = sd_ref[...].reshape(n, HEADS)
    scum = jnp.dot(same.astype(F32), sd, precision=HI, preferred_element_type=F32)
    scum_rows = lax.dot_general(
        sd, ((a <= b) & ((b - a) % ROWS_DEV == 0)).astype(F32), (((0,), (0,)), ((), ())),
        precision=HI, preferred_element_type=F32,
    )
    scarried_ref[...] = jnp.exp(scum)
    for h in range(HEADS):
        cols = slice(h * HDIM, (h + 1) * HDIM)
        q = sq_ref[:, :, cols].reshape(n, HDIM)
        k = sk_ref[:, :, cols].reshape(n, HDIM)
        v = sv_ref[:, :, cols].reshape(n, HDIM)
        spread = scum[:, h : h + 1] - scum_rows[h : h + 1, :]
        weights = contract_cols(q, k) * jnp.exp(jnp.where(same, spread, -1e30))
        high = weights.astype(BF)
        low = (weights - high.astype(F32)).astype(BF)
        local_ref[:, cols] = jnp.dot(high, v, preferred_element_type=F32) + jnp.dot(
            low, v, preferred_element_type=F32
        )


def scan_kernel(lens, got_ref, extra_ref, entry_ref, slice_ref):
    ends = bounds(lens)
    state = jnp.zeros((QUART, HDIM), F32)
    for k in range(NDEV):
        entry_ref[k] = state
        state = got_ref[k, S0 : S0 + 1, :] * state + got_ref[k, U0:T0, :]
    earlier = []
    for p in range(PROMPTS):
        e = ends[p] - 1
        b = e // BLOCK
        slot = jnp.int32(0)
        for other in earlier:
            slot = slot + (other == b).astype(jnp.int32)
        earlier.append(b)
        whole = e % BLOCK == BLOCK - 1
        lead = got_ref[b, S0 + 1 + p : S0 + 2 + p, :]
        tail = jnp.where(slot == 0, got_ref[b, T0:Q0, :], extra_ref[p])
        tail = jnp.where(whole, got_ref[b, U0:T0, :], tail)
        slice_ref[p] = lead * entry_ref[b] + tail


def project_kernel(here, got_ref, own_ref, s1_ref, s2_ref, s3_ref, out_ref, st_ref):
    x = here[0] // HEADS
    for shift, ref in enumerate((own_ref, s1_ref, s2_ref, s3_ref)):
        origin = lax.rem(x - shift + NX, NX)
        for p in range(PROMPTS):
            at = pl.multiple_of(p * HDIM + origin * QUART, QUART)
            st_ref[pl.ds(at, QUART), :] = ref[p]
    n = NDEV * ROWS_DEV
    q = got_ref[:, Q0:S0, :].reshape(n, HDIM).astype(BF)
    ids = jnp.broadcast_to(got_ref[:, S0 + 5 : S0 + 6, :], (NDEV, ROWS_DEV, HDIM))
    r = lax.broadcasted_iota(jnp.int32, (NDEV, ROWS_DEV, HDIM), 1)
    c = lax.broadcasted_iota(jnp.int32, (NDEV, ROWS_DEV, HDIM), 2)
    prompt = jnp.sum(jnp.where(r == c, ids, 0.0), axis=2, keepdims=True).reshape(n, 1)
    parts = [jnp.where(prompt == float(p), q, jnp.zeros_like(q)) for p in range(PROMPTS)]
    wide = jnp.concatenate(parts, axis=1)
    st = st_ref[...]
    high = st.astype(BF)
    low = (st - high.astype(F32)).astype(BF)
    res = jnp.dot(wide, high, preferred_element_type=F32) + jnp.dot(
        wide, low, preferred_element_type=F32
    )
    out_ref[...] = res.reshape(NDEV, ROWS_DEV, HDIM)


def mixed_kernel(query_ref, back_ref, intra_ref, carried_ref, mixed_ref, sums_ref):
    acc = jnp.zeros((BLOCK, HDIM), F32)
    for h in range(HEADS):
        cols = slice(h * HDIM, (h + 1) * HDIM)
        state = jnp.concatenate([back_ref[x * HEADS + h] for x in range(NX)], axis=0).astype(BF)
        outer = jnp.dot(query_ref[:, cols], state, preferred_element_type=F32)
        mixed = intra_ref[:, cols] + outer * carried_ref[:, h : h + 1]
        mixed_ref[:, cols] = mixed
        acc = acc + mixed * mixed
    flat = jnp.sum(acc.T, axis=0, keepdims=True)
    sums_ref[...] = jnp.concatenate(
        [flat[:, :HDIM], flat[:, HDIM:], jnp.zeros((6, HDIM), F32)], axis=0
    )


def decode_kernel(back_ref, local_ref, scarried_ref, sums_ref, dec_ref, send_ref):
    n = STEPS * ROWS_DEV
    acc = jnp.zeros((n, HDIM), F32)
    for h in range(HEADS):
        cols = slice(h * HDIM, (h + 1) * HDIM)
        carry = jnp.concatenate([back_ref[x * HEADS + h] for x in range(STEPS)], axis=0)
        dec = local_ref[:, cols] + carry * scarried_ref[:, h : h + 1]
        dec_ref[:, cols] = dec
        acc = acc + dec * dec
    full = jnp.concatenate([acc, jnp.zeros((HDIM - n, HDIM), F32)], axis=0)
    flat = jnp.sum(full.T, axis=0, keepdims=True)
    both = jnp.concatenate([sums_ref[0:2, :], flat, jnp.zeros((5, HDIM), F32)], axis=0)
    for k in range(HEADS):
        send_ref[k] = both


def final_kernel(sums_ref, mixed_ref, dec_ref, gain_ref, attn_ref, out_ref):
    total = sums_ref[0]
    for k in range(1, HEADS):
        total = total + sums_ref[k]
    scale = lax.rsqrt(total / (HEAD_COUNT * HDIM) + EPSILON)
    gain = gain_ref[...]

    def column(row):
        return jnp.broadcast_to(scale[row : row + 1, :], (HDIM, HDIM)).T

    for half in range(2):
        part = slice(half * HDIM, (half + 1) * HDIM)
        col = column(half)
        for h in range(HEADS):
            cols = slice(h * HDIM, (h + 1) * HDIM)
            attn_ref[part, cols] = (mixed_ref[part, cols] * col * gain[:, cols]).astype(BF)
    col = column(2)
    for h in range(HEADS):
        cols = slice(h * HDIM, (h + 1) * HDIM)
        res = (dec_ref[:, cols] * col[: STEPS * ROWS_DEV, :] * gain[:, cols]).astype(BF)
        for step in range(STEPS):
            out_ref[step, :, cols] = res[step * ROWS_DEV : (step + 1) * ROWS_DEV, :]


def shape(*dims, dtype=F32):
    return jax.ShapeDtypeStruct(dims, dtype)


def exchange(x, axis):
    return lax.all_to_all(x, axis, split_axis=0, concat_axis=0, tiled=True)


def more_tails(key_in, value_in, log_decay, prompt_lengths, first):
    ends = jnp.cumsum(prompt_lengths)
    positions = first + jnp.arange(BLOCK, dtype=jnp.int32)
    segs = jnp.sum((positions[:, None] >= ends[None, :]).astype(jnp.int32), axis=1)
    cum = jnp.cumsum(log_decay, axis=0)
    keys = key_in.reshape(BLOCK, HEADS, HDIM)
    values = value_in.reshape(BLOCK, HEADS, HDIM)
    parts = []
    for p in (1, 2):
        local = ends[p] - 1 - first
        owned = (local >= 0) & (local < BLOCK) & (ends[p - 1] - 1 >= first)
        safe = jnp.clip(local, 0, BLOCK - 1)
        taken = (jnp.arange(BLOCK) <= safe) & (segs == p) & owned
        spread = jnp.where(taken[:, None], cum[safe][None, :] - cum, 0.0)
        keep = jnp.where(taken[:, None], jnp.exp(spread), 0.0)
        tailed = (keys.astype(F32) * keep[:, :, None]).astype(BF)
        part = jnp.einsum("shd,she->hde", tailed, values, preferred_element_type=F32)
        part = part.reshape(HEADS, NX, QUART, HDIM).transpose(1, 0, 2, 3)
        parts.append(part.reshape(NDEV, QUART, HDIM))
    got = exchange(jnp.concatenate(parts, axis=1), SEQ)
    both = jnp.sum(got, axis=0)
    blank = jnp.zeros((QUART, HDIM), F32)
    return jnp.stack([blank, both[:QUART], both[QUART:], blank])


def local(
    query_in,
    key_in,
    value_in,
    log_decay,
    norm_gain,
    prompt_lengths,
    step_query,
    step_key,
    step_value,
    step_decay,
    row_prompt,
):
    me = lax.axis_index(SEQ).astype(jnp.int32)
    here = me[None]
    width = HEADS * HDIM
    n = STEPS * ROWS_DEV

    send = pl.pallas_call(
        send_kernel,
        out_shape=shape(NDEV, MSG, HDIM),
        in_specs=[SMEM] * 3 + [VMEM] * 4,
        out_specs=VMEM,
        scratch_shapes=[pltpu.VMEM((BLOCK, HEADS), F32)],
        compiler_params=params(),
        cost_estimate=cost(5),
        name="send",
    )(prompt_lengths, here, row_prompt, key_in, value_in, log_decay, step_query)
    got = exchange(send, SEQ)

    intra, carried, local_dec, scarried = pl.pallas_call(
        intra_kernel,
        out_shape=(shape(BLOCK, width), shape(BLOCK, HEADS), shape(n, width), shape(n, HEADS)),
        in_specs=[SMEM] * 2 + [VMEM] * 8,
        out_specs=(VMEM,) * 4,
        compiler_params=params(),
        cost_estimate=cost(6),
        name="intra",
    )(
        prompt_lengths, here, query_in, key_in, value_in, log_decay,
        step_query, step_key, step_value, step_decay,
    )

    ends = jnp.cumsum(prompt_lengths)
    blocks = (ends - 1) // BLOCK
    inner = (ends % BLOCK) != 0
    crowded = jnp.any((blocks[1:] == blocks[:-1]) & inner[1:])
    extra = lax.cond(
        crowded,
        lambda: more_tails(key_in, value_in, log_decay, prompt_lengths, me * BLOCK),
        lambda: jnp.zeros((PROMPTS, QUART, HDIM), F32),
    )

    entry, own = pl.pallas_call(
        scan_kernel,
        out_shape=(shape(NDEV, QUART, HDIM), shape(PROMPTS, QUART, HDIM)),
        in_specs=[SMEM] + [VMEM] * 2,
        out_specs=(VMEM,) * 2,
        compiler_params=params(),
        cost_estimate=cost(2),
        name="scan",
    )(prompt_lengths, got, extra)
    back = exchange(entry, SEQ)

    shifted = [
        lax.ppermute(own, "seq_0", [(i, (i + d) % NX) for i in range(NX)]) for d in range(1, NX)
    ]
    proj = pl.pallas_call(
        project_kernel,
        out_shape=shape(NDEV, ROWS_DEV, HDIM),
        in_specs=[SMEM] + [VMEM] * 5,
        out_specs=VMEM,
        scratch_shapes=[pltpu.VMEM((PROMPTS * HDIM, HDIM), F32)],
        compiler_params=params(),
        cost_estimate=cost(2),
        name="project",
    )(here, got, own, *shifted)
    proj_back = exchange(proj, SEQ)

    mixed, sums = pl.pallas_call(
        mixed_kernel,
        out_shape=(shape(BLOCK, width), shape(8, HDIM)),
        in_specs=[VMEM] * 4,
        out_specs=(VMEM,) * 2,
        compiler_params=params(),
        cost_estimate=cost(4),
        name="mixed",
    )(query_in, back, intra, carried)

    dec, sums_send = pl.pallas_call(
        decode_kernel,
        out_shape=(shape(n, width), shape(HEADS, 8, HDIM)),
        in_specs=[VMEM] * 4,
        out_specs=(VMEM,) * 2,
        compiler_params=params(),
        cost_estimate=cost(1),
        name="decode",
    )(proj_back, local_dec, scarried, sums)
    sums_all = exchange(sums_send, "head")

    return pl.pallas_call(
        final_kernel,
        out_shape=(shape(BLOCK, width, dtype=BF), shape(STEPS, ROWS_DEV, width, dtype=BF)),
        in_specs=[VMEM] * 4,
        out_specs=(VMEM,) * 2,
        compiler_params=params(),
        cost_estimate=cost(2),
        name="final",
    )(sums_all, mixed, dec, norm_gain.reshape(1, width))


def solution(mesh):
    split = Mesh(mesh.devices.reshape(NX, HEADS, mesh.shape["head"]), ("seq_0", "seq_1", "head"))
    placed = (
        P(SEQ, "head"),
        P(SEQ, "head"),
        P(SEQ, "head"),
        P(SEQ, "head"),
        P("head"),
        P(),
        P(None, SEQ, "head"),
        P(None, SEQ, "head"),
        P(None, SEQ, "head"),
        P(None, SEQ, "head"),
        P(SEQ),
    )
    return jax.shard_map(
        local,
        mesh=split,
        in_specs=placed,
        out_specs=(P(SEQ, "head"), P(None, SEQ, "head")),
        check_vma=False,
    )
```

time: 364 us -> 108 us (0.30)
  waiting for transfers between devices: 197 us -> 15.1 us
  matrix products: 54.3 us -> 0 us
  blocking collectives: 23.7 us -> 59.2 us
  local copies, waits for them, and re-layouts: 25.6 us -> 1.78 us
  other arithmetic: 19.4 us -> 1.56 us
  between operations: 15.4 us -> 1.42 us
  loops' own time: 12.9 us -> 0.02 us
  Pallas kernels: 0 us -> 9.92 us
  starting transfers between devices: 14.7 us -> 19.3 us
    psum x1 -> x0, waiting for transfers between devices: 128 us -> none  [local(): prompt_state = lax.psum(candidates, SEQ)]
    all_gather x2 -> x0, waiting for transfers between devices: 65.4 us -> none  [entering(): pieces = jax.tree.map(lambda part: lax.all_gather(part, axis), so_far)]
    all_to_all x0 -> x2, blocking collectives: none -> 59.2 us  [exchange(): return lax.all_to_all(x, axis, split_axis=0, concat_axis=0, tiled=True)]
    dot_general x11 -> x0, matrix products: 54.3 us -> none  [the longest x4 44.1 us: local(): jnp.einsum('rhd,rhde->rhe', query_now, row_states, precision=lax.Precisio...]
    all_gather x2 -> x0, blocking collectives: 23.7 us -> none  [entering(): pieces = jax.tree.map(lambda part: lax.all_gather(part, axis), so_far)]
    another operation x1, loops' own time: 12.9 us -> 0.02 us  [local(): lax.cond(crowded, lambda: more_tails(key_in, value_in, log_decay, prompt_...]
    pallas_call x0 -> x7, Pallas kernels: none -> 9.92 us  [the longest x1 3.03 us: local(): pl.pallas_call(intra_kernel, out_shape=(shape(BLOCK, width), shape(BLOCK,...]
    add x3 -> x0, other arithmetic: 6.93 us -> none  [the longest x2 6.93 us: combine_pairs(): later[0][:, None, None] * earlier[1] + later[1]]
  transfers between devices with their start and end apart: 5 -> 5, of which waited for: 4 -> 5; matrix products, arithmetic and copies ran while one was open for 5% -> 0% of each run, Pallas kernels for 0% -> 4%
where the time goes in v1:
time: 108 us
  blocking collectives  59.2 us (55%)
  starting transfers between devices  19.3 us (18%)
  waiting for transfers between devices  15.1 us (14%)
  Pallas kernels  9.92 us (9%)
  local copies, waits for them, and re-layouts  1.78 us (2%)
  other arithmetic  1.56 us (1%)
  between operations  1.42 us (1%)
    all_to_all x2, blocking collectives, exchange(): return lax.all_to_all(x, axis, split_axis=0, concat_axis=0, tiled=True)  59.2 us
    all_to_all x2, starting transfers between devices, exchange(): return lax.all_to_all(x, axis, split_axis=0, concat_axis=0, tiled=True)  15.6 us
    all_to_all x2, waiting for transfers between devices, exchange(): return lax.all_to_all(x, axis, split_axis=0, concat_axis=0, tiled=True)  10.2 us
    ppermute x3, waiting for transfers between devices, local(): lax.ppermute(own, 'seq_0', [(i, (i + d) % NX) for i in range(NX)])  4.94 us
    ppermute x3, starting transfers between devices, local(): lax.ppermute(own, 'seq_0', [(i, (i + d) % NX) for i in range(NX)])  3.68 us
    pallas_call x1, Pallas kernels, local(): pl.pallas_call(intra_kernel, out_shape=(shape(BLOCK, width), shape(BLOCK,...  3.03 us
    pallas_call x1, Pallas kernels, local(): pl.pallas_call(send_kernel, out_shape=shape(NDEV, MSG, HDIM), in_specs=[S...  2.48 us
  transfers between devices with their start and end apart: 5, of which 5 were waited for; matrix products, arithmetic and copies ran while one was open for 0% of the time, Pallas kernels for 4%

profile of v1, /device:TPU:1, one launch (start us, length us, event | category | flops | bytes accessed | tf_op | source)
XLA Modules:
  0.0 108.3 jit_solution(124783289816938768)
XLA Ops:
  0.6 0.8 reduce-window.24
  1.5 0.7 and_reduce_fusion
  2.9 0.8 copy.41.logd_ref
  3.7 0.0 copy-start.1
  3.7 0.0 copy-start.5
  3.8 0.8 copy-done.1
  4.6 0.0 copy-done.5
  4.6 2.5 %send.1 = f32[32,88,128]{2,1,0:T(8,128)S(1)} custom-call(s32[4]{0:T(128)} %lens.5, s32[1]{0:T(128)} %bitcast.20.here, s32[16]{0:T(128)S(1)} %copy-done.5, bf16[256,1024]{1,0:T(8,128)(2,1)} %key_ref.3, bf16[256,1024]{1,0:T(8,128)(2,1)} %value_ref.3, f32[256,8]{1,0:T(8,128)S(1)} %copy.41.logd_ref, bf16[4,16,1024]{2,1,0:T(8,128)(2,1)S(1)} %copy-done.1), custom_call_target="tpu_custom_call" | custom-call | flops 5000000000 | bytes 15000000 | tf_op jit(solution)/shard_map/send/pallas_call | solution.py:342
  7.1 0.0 copy-start.8
  7.1 46.5 %all_to_all.25.got_ref = f32[32,88,128]{2,1,0:T(8,128)S(1)} all-to-all(f32[32,88,128]{2,1,0:T(8,128)S(1)} %send.1), channel_id=1, replica_groups=mesh['seq_0'=4,'seq_1'=8,'head'=8] {'seq_0','seq_1'}, dimensions={0} | all-to-all | bytes 2883584 | tf_op jit(solution)/shard_map/all_to_all | solution.py:296
  53.6 0.0 copy-done.8
  53.6 0.0 copy-start.7
  53.6 1.4 %scan.1 = (f32[32,32,128]{2,1,0:T(8,128)}, f32[4,32,128]{2,1,0:T(8,128)S(1)}) custom-call(s32[4]{0:T(128)S(1)} %copy-done.8, f32[32,88,128]{2,1,0:T(8,128)S(1)} %all_to_all.25.got_ref, f32[4,32,128]{2,1,0:T(8,128)S(1)} %get-tuple-element.71.extra_ref), custom_call_target="tpu_custom_call" | custom-call | flops 2000000000 | bytes 6000000 | tf_op jit(solution)/shard_map/scan/pallas_call | solution.py:377
  55.0 7.8 %all-to-all-start.3 = ((f32[32,32,128]{2,1,0:T(8,128)}), f32[32,32,128]{2,1,0:T(8,128)S(1)}, u32[]{:S(2)}, u32[]{:S(2)}) async-start(f32[32,32,128]{2,1,0:T(8,128)} %get-tuple-element.33), calls=%async_computation.3 | async-start | bytes 1048576 | tf_op jit(solution)/shard_map/all_to_all | solution.py:296
  62.9 2.6 %collective-permute-start.2 = (f32[4,32,128]{2,1,0:T(8,128)S(1)}, f32[4,32,128]{2,1,0:T(8,128)S(1)}, u32[]{:S(2)}, u32[]{:S(2)}) collective-permute-start(f32[4,32,128]{2,1,0:T(8,128)S(1)} %get-tuple-element.30.own_ref), channel_id=1, source_target_pairs={{0,192},{64,0},{128,64},{192,128},{1,193},{65,1},{129,65},{193,129... | collective-permute-start | bytes 196616 | tf_op jit(solution)/shard_map/ppermute | solution.py:389
  65.4 0.5 collective-permute-start.1
  65.9 0.6 collective-permute-start
  66.5 0.0 copy-done.7
  66.5 0.1 copy.44.sd_ref
  66.6 0.0 copy-start
  66.6 0.0 copy-start.2
  66.6 0.0 copy-start.3
  66.6 0.8 collective-permute-done.2.s3_ref
  67.4 3.0 %collective-permute-done.1.s2_ref = f32[4,32,128]{2,1,0:T(8,128)S(1)} collective-permute-done((f32[4,32,128]{2,1,0:T(8,128)S(1)}, f32[4,32,128]{2,1,0:T(8,128)S(1)}, u32[]{:S(2)}, u32[]{:S(2)}) %collective-permute-start.1) | collective-permute-done | bytes 65568 | tf_op jit(solution)/shard_map/ppermute | solution.py:389
  70.4 1.1 %collective-permute-done.s1_ref = f32[4,32,128]{2,1,0:T(8,128)S(1)} collective-permute-done((f32[4,32,128]{2,1,0:T(8,128)S(1)}, f32[4,32,128]{2,1,0:T(8,128)S(1)}, u32[]{:S(2)}, u32[]{:S(2)}) %collective-permute-start) | collective-permute-done | bytes 65568 | tf_op jit(solution)/shard_map/ppermute | solution.py:389
  71.6 1.2 %project.1 = f32[32,16,128]{2,1,0:T(8,128)} custom-call(s32[1]{0:T(128)} %bitcast.20.here, f32[32,88,128]{2,1,0:T(8,128)S(1)} %all_to_all.25.got_ref, f32[4,32,128]{2,1,0:T(8,128)S(1)} %get-tuple-element.30.own_ref, f32[4,32,128]{2,1,0:T(8,128)S(1)} %collective-permute-done.s1_ref, f32[4,32,128]{2,1,0:T(8,128)S(1)} %collective-permute-done.1.s2_ref, ...), custom_call_target="tpu_custom_call" | custom-call | flops 2000000000 | bytes 6000000 | tf_op jit(solution)/shard_map/project/pallas_call | solution.py:391
  72.8 4.1 %all-to-all-done.3.back_ref = f32[32,32,128]{2,1,0:T(8,128)S(1)} async-done(((f32[32,32,128]{2,1,0:T(8,128)}), f32[32,32,128]{2,1,0:T(8,128)S(1)}, u32[]{:S(2)}, u32[]{:S(2)}) %all-to-all-start.3) | async-done | bytes 524320 | tf_op jit(solution)/shard_map/all_to_all | solution.py:296
  76.9 7.7 %all-to-all-start.2 = ((f32[32,16,128]{2,1,0:T(8,128)}), f32[32,16,128]{2,1,0:T(8,128)S(1)}, u32[]{:S(2)}, u32[]{:S(2)}) async-start(f32[32,16,128]{2,1,0:T(8,128)} %project.1), calls=%async_computation.2 | async-start | bytes 524288 | tf_op jit(solution)/shard_map/all_to_all | solution.py:296
  84.6 0.0 copy-done
  84.6 0.0 copy-done.2
  84.6 0.0 copy-done.3
  84.7 3.0 %intra.1 = (f32[256,1024]{1,0:T(8,128)S(1)}, f32[256,8]{1,0:T(8,128)S(1)}, f32[64,1024]{1,0:T(8,128)S(1)}, f32[64,8]{1,0:T(8,128)S(1)}) custom-call(s32[4]{0:T(128)S(1)} %copy-done.8, s32[1]{0:T(128)} %bitcast.20.here, bf16[256,1024]{1,0:T(8,128)(2,1)S(1)} %copy-done, bf16[256,1024]{1,0:T(8,128)(2,1)} %key_ref.3, bf16[256,1024]{1,0:T(8,128)(2,1)} %value_ref.3, ...), custom_call_target="tpu_custom_call" | custom-call | flops 6000000000 | bytes 18000000 | tf_op jit(solution)/shard_map/intra/pallas_call | solution.py:354
  87.7 0.5 mixed.1
  88.2 6.1 %all-to-all-done.2.back_ref = f32[32,16,128]{2,1,0:T(8,128)S(1)} async-done(((f32[32,16,128]{2,1,0:T(8,128)}), f32[32,16,128]{2,1,0:T(8,128)S(1)}, u32[]{:S(2)}, u32[]{:S(2)}) %all-to-all-start.2) | async-done | bytes 262176 | tf_op jit(solution)/shard_map/all_to_all | solution.py:296
  94.3 0.0 copy-start.4
  94.3 0.3 decode.1
  94.5 12.7 %all_to_all.26.sums_ref = f32[8,8,128]{2,1,0:T(8,128)S(1)} all-to-all(f32[8,8,128]{2,1,0:T(8,128)S(1)} %get-tuple-element.37), channel_id=1, replica_groups=mesh['seq_0'=4,'seq_1'=8,'head'=8] {'head'}, dimensions={0} | all-to-all | bytes 65536 | tf_op jit(solution)/shard_map/all_to_all | solution.py:296
  107.2 0.0 copy-done.4
  107.2 1.1 final.1
  (4 shorter events, 0.1 us)
Async XLA Ops:
  3.7 0.9 copy-start.1
  3.7 0.9 copy-start.5
  7.1 46.5 %copy-start.8 = (s32[4]{0:T(128)S(1)}, s32[4]{0:T(128)}, u32[]{:S(2)}) copy-start(s32[4]{0:T(128)} %lens.5) | copy-start | bytes 52
  53.6 12.9 %copy-start.7 = (f32[4,16,8]{1,2,0:T(8,128)S(1)}, f32[4,16,8]{1,2,0:T(8,128)}, u32[]{:S(2)}) copy-start(f32[4,16,8]{1,2,0:T(8,128)} %param.22) | copy-start | bytes 6148
  55.0 21.9 %all-to-all-start.3 = ((f32[32,32,128]{2,1,0:T(8,128)}), f32[32,32,128]{2,1,0:T(8,128)S(1)}, u32[]{:S(2)}, u32[]{:S(2)}) async-start(f32[32,32,128]{2,1,0:T(8,128)} %get-tuple-element.33), calls=%async_computation.3 | async-start | bytes 1048576 | tf_op jit(solution)/shard_map/all_to_all | solution.py:296
  62.9 4.6 %collective-permute-start.2 = (f32[4,32,128]{2,1,0:T(8,128)S(1)}, f32[4,32,128]{2,1,0:T(8,128)S(1)}, u32[]{:S(2)}, u32[]{:S(2)}) collective-permute-start(f32[4,32,128]{2,1,0:T(8,128)S(1)} %get-tuple-element.30.own_ref), channel_id=1, source_target_pairs={{0,192},{64,0},{128,64},{192,128},{1,193},{65,1},{129,65},{193,129... | collective-permute-start | bytes 196616 | tf_op jit(solution)/shard_map/ppermute | solution.py:389
  65.4 5.0 %collective-permute-start.1 = (f32[4,32,128]{2,1,0:T(8,128)S(1)}, f32[4,32,128]{2,1,0:T(8,128)S(1)}, u32[]{:S(2)}, u32[]{:S(2)}) collective-permute-start(f32[4,32,128]{2,1,0:T(8,128)S(1)} %get-tuple-element.30.own_ref), channel_id=1, source_target_pairs={{0,128},{64,192},{128,0},{192,64},{1,129},{65,193},{129,1},{193,65... | collective-permute-start | bytes 196616 | tf_op jit(solution)/shard_map/ppermute | solution.py:389
  65.9 5.6 %collective-permute-start = (f32[4,32,128]{2,1,0:T(8,128)S(1)}, f32[4,32,128]{2,1,0:T(8,128)S(1)}, u32[]{:S(2)}, u32[]{:S(2)}) collective-permute-start(f32[4,32,128]{2,1,0:T(8,128)S(1)} %get-tuple-element.30.own_ref), channel_id=1, source_target_pairs={{0,64},{64,128},{128,192},{192,0},{1,65},{65,129},{129,193},{193,1... | collective-permute-start | bytes 196616 | tf_op jit(solution)/shard_map/ppermute | solution.py:389
  66.6 18.0 %copy-start = (bf16[256,1024]{1,0:T(8,128)(2,1)S(1)}, bf16[256,1024]{1,0:T(8,128)(2,1)}, u32[]{:S(2)}) copy-start(bf16[256,1024]{1,0:T(8,128)(2,1)} %query_ref.5) | copy-start | bytes 1572868
  66.6 18.0 %copy-start.2 = (bf16[4,16,1024]{2,1,0:T(8,128)(2,1)S(1)}, bf16[4,16,1024]{2,1,0:T(8,128)(2,1)}, u32[]{:S(2)}) copy-start(bf16[4,16,1024]{2,1,0:T(8,128)(2,1)} %sk_ref.1) | copy-start | bytes 393220
  66.6 18.0 %copy-start.3 = (bf16[4,16,1024]{2,1,0:T(8,128)(2,1)S(1)}, bf16[4,16,1024]{2,1,0:T(8,128)(2,1)}, u32[]{:S(2)}) copy-start(bf16[4,16,1024]{2,1,0:T(8,128)(2,1)} %sv_ref.1) | copy-start | bytes 393220
  76.9 17.4 %all-to-all-start.2 = ((f32[32,16,128]{2,1,0:T(8,128)}), f32[32,16,128]{2,1,0:T(8,128)S(1)}, u32[]{:S(2)}, u32[]{:S(2)}) async-start(f32[32,16,128]{2,1,0:T(8,128)} %project.1), calls=%async_computation.2 | async-start | bytes 524288 | tf_op jit(solution)/shard_map/all_to_all | solution.py:296
  94.3 12.9 %copy-start.4 = (f32[1024]{0:T(1024)S(1)}, f32[1024]{0:T(1024)}, u32[]{:S(2)}) copy-start(f32[1024]{0:T(1024)} %param.17) | copy-start | bytes 12292

commit v2 on v1

--- a/solution.py
+++ b/solution.py
@@ -22,7 +22,8 @@
 QUART = HDIM // NX
 ROWS_DEV = 16
 
-U0, T0, Q0, S0, MSG = 0, 32, 64, 80, 88
+U0, Q0, S0, MSG = 0, 32, 48, 56
+TAILS = PROMPTS - 1
 
 BF = jnp.bfloat16
 F32 = jnp.float32
@@ -64,8 +65,9 @@
 def cum_columns(logd):
     t = lax.broadcasted_iota(jnp.int32, (BLOCK, BLOCK), 0)
     s = lax.broadcasted_iota(jnp.int32, (BLOCK, BLOCK), 1)
-    tri = (s <= t).astype(F32)
-    return jnp.dot(tri, logd, precision=HI, preferred_element_type=F32)
+    return lax.dot_general(
+        (s <= t).astype(F32), logd, (((1,), (1,)), ((), ())), precision=HI, preferred_element_type=F32
+    )
 
 
 def contract_rows(a, b):
@@ -76,7 +78,9 @@
     return lax.dot_general(a, b, (((1,), (1,)), ((), ())), preferred_element_type=F32)
 
 
-def send_kernel(lens, here, rows, key_ref, value_ref, logd_ref, query_ref, out_ref, cum_ref):
+def send_kernel(
+    lens, here, rows, key_ref, value_ref, logd_ref, query_ref, out_ref, tail_ref, cum_ref
+):
     first = here[0] * BLOCK
     ends = bounds(lens)
     front = entry_seg(first, ends)
@@ -85,57 +89,51 @@
     cum_ref[...] = cum
     tok = lax.broadcasted_iota(jnp.int32, (BLOCK, HEADS), 0)
     seg = seg_of(tok + first, ends)
+
+    leads = []
+    for p in range(TAILS):
+        at = ends[p] - 1 - first
+        inside = (at >= 0) & (at < BLOCK)
+        reached = cum_ref[pl.ds(jnp.clip(at, 0, BLOCK - 1), 1), :]
+        leads.append(jnp.exp(reached) * (inside & (front == p)).astype(F32))
+        rows_p = slice(p * QUART, (p + 1) * QUART)
+
+        @pl.when(jnp.logical_not(inside))
+        def _(rows_p=rows_p):
+            tail_ref[:, rows_p, :] = jnp.zeros((NDEV, QUART, HDIM), F32)
+
+        @pl.when(inside)
+        def _(p=p, at=at, reached=reached, rows_p=rows_p):
+            taken = (tok <= at) & (seg == p)
+            tail = jnp.where(taken, jnp.exp(jnp.where(taken, reached - cum, 0.0)), 0.0)
+            for h in range(HEADS):
+                cols = slice(h * HDIM, (h + 1) * HDIM)
+                tailed = (key_ref[:, cols].astype(F32) * tail[:, h : h + 1]).astype(BF)
+                part = contract_rows(tailed, value_ref[:, cols])
+                for x in range(NX):
+                    tail_ref[x * HEADS + h, rows_p, :] = part[x * QUART : (x + 1) * QUART, :]
+
     last = cum[BLOCK - 1 : BLOCK, :]
     keep = jnp.where(seg == seg_last, jnp.exp(last - cum), 0.0)
     growth = jnp.exp(last) * (seg_last == front).astype(F32)
-    leads = []
-    found = jnp.int32(-1)
-    spot = jnp.int32(0)
-    for p in range(PROMPTS):
-        local = ends[p] - 1 - first
-        inside = (local >= 0) & (local < BLOCK)
-        safe = jnp.clip(local, 0, BLOCK - 1)
-        reached = cum_ref[pl.ds(safe, 1), :]
-        leads.append(jnp.exp(reached) * (inside & (front == p)).astype(F32))
-        interior = (local >= 0) & (local < BLOCK - 1)
-        take = interior & (found < 0)
-        found = jnp.where(take, p, found)
-        spot = jnp.where(take, local, spot)
     lane = lax.broadcasted_iota(jnp.int32, (1, HDIM), 1)
     ids = jnp.zeros((1, HDIM), F32)
     for r in range(ROWS_DEV):
         ids = jnp.where(lane == r, rows[r].astype(F32), ids)
-
     for h in range(HEADS):
         cols = slice(h * HDIM, (h + 1) * HDIM)
         keyed = (key_ref[:, cols].astype(F32) * keep[:, h : h + 1]).astype(BF)
         update = contract_rows(keyed, value_ref[:, cols])
         scal = jnp.concatenate(
             [jnp.broadcast_to(growth[:, h : h + 1], (1, HDIM))]
-            + [jnp.broadcast_to(leads[p][:, h : h + 1], (1, HDIM)) for p in range(PROMPTS)]
-            + [ids, ids, ids],
+            + [jnp.broadcast_to(leads[p][:, h : h + 1], (1, HDIM)) for p in range(TAILS)]
+            + [ids, ids, ids, ids],
             axis=0,
         )
         for x in range(NX):
-            out_ref[x * HEADS + h, U0:T0, :] = update[x * QUART : (x + 1) * QUART, :]
+            out_ref[x * HEADS + h, U0:Q0, :] = update[x * QUART : (x + 1) * QUART, :]
             out_ref[x * HEADS + h, Q0:S0, :] = query_ref[x, :, cols].astype(F32)
             out_ref[x * HEADS + h, S0:MSG, :] = scal
-
-    @pl.when(found < 0)
-    def _():
-        out_ref[:, T0:Q0, :] = jnp.zeros((NDEV, QUART, HDIM), F32)
-
-    @pl.when(found >= 0)
-    def _():
-        reached = cum_ref[pl.ds(spot, 1), :]
-        taken = (tok <= spot) & (seg == found)
-        tail = jnp.where(taken, jnp.exp(jnp.where(taken, reached - cum, 0.0)), 0.0)
-        for h in range(HEADS):
-            cols = slice(h * HDIM, (h + 1) * HDIM)
-            tailed = (key_ref[:, cols].astype(F32) * tail[:, h : h + 1]).astype(BF)
-            part = contract_rows(tailed, value_ref[:, cols])
-            for x in range(NX):
-                out_ref[x * HEADS + h, T0:Q0, :] = part[x * QUART : (x + 1) * QUART, :]
 
 
 def intra_kernel(
@@ -148,10 +146,8 @@
     logd = logd_ref[...]
     t = lax.broadcasted_iota(jnp.int32, (BLOCK, BLOCK), 0)
     s = lax.broadcasted_iota(jnp.int32, (BLOCK, BLOCK), 1)
-    cum = jnp.dot((s <= t).astype(F32), logd, precision=HI, preferred_element_type=F32)
-    cum_rows = lax.dot_general(
-        logd, (t <= s).astype(F32), (((0,), (0,)), ((), ())), precision=HI, preferred_element_type=F32
-    )
+    cum = cum_columns(logd)
+    cum_rows = jnp.dot(logd, (t <= s).astype(F32), precision=HI, preferred_element_type=F32)
     linked = (s <= t) & (seg_of(t + first, ends) == seg_of(s + first, ends))
     tok = lax.broadcasted_iota(jnp.int32, (BLOCK, HEADS), 0)
     carried_ref[...] = jnp.where(seg_of(tok + first, ends) == front, jnp.exp(cum), 0.0)
@@ -167,11 +163,15 @@
     a = lax.broadcasted_iota(jnp.int32, (n, n), 0)
     b = lax.broadcasted_iota(jnp.int32, (n, n), 1)
     same = (b <= a) & ((a - b) % ROWS_DEV == 0)
-    sd = sd_ref[...].reshape(n, HEADS)
-    scum = jnp.dot(same.astype(F32), sd, precision=HI, preferred_element_type=F32)
-    scum_rows = lax.dot_general(
-        sd, ((a <= b) & ((b - a) % ROWS_DEV == 0)).astype(F32), (((0,), (0,)), ((), ())),
-        precision=HI, preferred_element_type=F32,
+    total = sd_ref[0]
+    pieces = [total]
+    for step in range(1, STEPS):
+        total = total + sd_ref[step]
+        pieces.append(total)
+    scum_rows = jnp.concatenate(pieces, axis=1)
+    scum = lax.dot_general(
+        (a == b).astype(F32), scum_rows, (((1,), (1,)), ((), ())), precision=HI,
+        preferred_element_type=F32,
     )
     scarried_ref[...] = jnp.exp(scum)
     for h in range(HEADS):
@@ -188,25 +188,22 @@
         )
 
 
-def scan_kernel(lens, got_ref, extra_ref, entry_ref, slice_ref):
+def scan_kernel(lens, got_ref, entry_ref, slice_ref):
     ends = bounds(lens)
     state = jnp.zeros((QUART, HDIM), F32)
     for k in range(NDEV):
         entry_ref[k] = state
-        state = got_ref[k, S0 : S0 + 1, :] * state + got_ref[k, U0:T0, :]
-    earlier = []
-    for p in range(PROMPTS):
-        e = ends[p] - 1
-        b = e // BLOCK
-        slot = jnp.int32(0)
-        for other in earlier:
-            slot = slot + (other == b).astype(jnp.int32)
-        earlier.append(b)
-        whole = e % BLOCK == BLOCK - 1
-        lead = got_ref[b, S0 + 1 + p : S0 + 2 + p, :]
-        tail = jnp.where(slot == 0, got_ref[b, T0:Q0, :], extra_ref[p])
-        tail = jnp.where(whole, got_ref[b, U0:T0, :], tail)
-        slice_ref[p] = lead * entry_ref[b] + tail
+        state = got_ref[k, S0 : S0 + 1, :] * state + got_ref[k, U0:Q0, :]
+    slice_ref[TAILS] = state
+    for p in range(TAILS):
+        b = (ends[p] - 1) // BLOCK
+        slice_ref[p] = got_ref[b, S0 + 1 + p : S0 + 2 + p, :] * entry_ref[b]
+
+
+def join_kernel(slice_ref, tail_ref, out_ref):
+    for p in range(TAILS):
+        out_ref[p] = slice_ref[p] + tail_ref[0, p * QUART : (p + 1) * QUART, :]
+    out_ref[TAILS] = slice_ref[TAILS]
 
 
 def project_kernel(here, got_ref, own_ref, s1_ref, s2_ref, s3_ref, out_ref, st_ref):
@@ -218,7 +215,7 @@
             st_ref[pl.ds(at, QUART), :] = ref[p]
     n = NDEV * ROWS_DEV
     q = got_ref[:, Q0:S0, :].reshape(n, HDIM).astype(BF)
-    ids = jnp.broadcast_to(got_ref[:, S0 + 5 : S0 + 6, :], (NDEV, ROWS_DEV, HDIM))
+    ids = jnp.broadcast_to(got_ref[:, S0 + 4 : S0 + 5, :], (NDEV, ROWS_DEV, HDIM))
     r = lax.broadcasted_iota(jnp.int32, (NDEV, ROWS_DEV, HDIM), 1)
     c = lax.broadcasted_iota(jnp.int32, (NDEV, ROWS_DEV, HDIM), 2)
     prompt = jnp.sum(jnp.where(r == c, ids, 0.0), axis=2, keepdims=True).reshape(n, 1)
@@ -294,31 +291,6 @@
 
 def exchange(x, axis):
     return lax.all_to_all(x, axis, split_axis=0, concat_axis=0, tiled=True)
-
-
-def more_tails(key_in, value_in, log_decay, prompt_lengths, first):
-    ends = jnp.cumsum(prompt_lengths)
-    positions = first + jnp.arange(BLOCK, dtype=jnp.int32)
-    segs = jnp.sum((positions[:, None] >= ends[None, :]).astype(jnp.int32), axis=1)
-    cum = jnp.cumsum(log_decay, axis=0)
-    keys = key_in.reshape(BLOCK, HEADS, HDIM)
-    values = value_in.reshape(BLOCK, HEADS, HDIM)
-    parts = []
-    for p in (1, 2):
-        local = ends[p] - 1 - first
-        owned = (local >= 0) & (local < BLOCK) & (ends[p - 1] - 1 >= first)
-        safe = jnp.clip(local, 0, BLOCK - 1)
-        taken = (jnp.arange(BLOCK) <= safe) & (segs == p) & owned
-        spread = jnp.where(taken[:, None], cum[safe][None, :] - cum, 0.0)
-        keep = jnp.where(taken[:, None], jnp.exp(spread), 0.0)
-        tailed = (keys.astype(F32) * keep[:, :, None]).astype(BF)
-        part = jnp.einsum("shd,she->hde", tailed, values, preferred_element_type=F32)
-        part = part.reshape(HEADS, NX, QUART, HDIM).transpose(1, 0, 2, 3)
-        parts.append(part.reshape(NDEV, QUART, HDIM))
-    got = exchange(jnp.concatenate(parts, axis=1), SEQ)
-    both = jnp.sum(got, axis=0)
-    blank = jnp.zeros((QUART, HDIM), F32)
-    return jnp.stack([blank, both[:QUART], both[QUART:], blank])
 
 
 def local(
@@ -339,16 +311,19 @@
     width = HEADS * HDIM
     n = STEPS * ROWS_DEV
 
-    send = pl.pallas_call(
+    logd = log_decay.T
+    send, tails = pl.pallas_call(
         send_kernel,
-        out_shape=shape(NDEV, MSG, HDIM),
+        out_shape=(shape(NDEV, MSG, HDIM), shape(NDEV, TAILS * QUART, HDIM)),
         in_specs=[SMEM] * 3 + [VMEM] * 4,
-        out_specs=VMEM,
+        out_specs=(VMEM,) * 2,
         scratch_shapes=[pltpu.VMEM((BLOCK, HEADS), F32)],
         compiler_params=params(),
         cost_estimate=cost(5),
         name="send",
-    )(prompt_lengths, here, row_prompt, key_in, value_in, log_decay, step_query)
+    )(prompt_lengths, here, row_prompt, key_in, value_in, logd, step_query)
+    tails = lax.psum_scatter(tails, "seq_0", scatter_dimension=0, tiled=True)
+    tails = lax.psum_scatter(tails, "seq_1", scatter_dimension=0, tiled=True)
     got = exchange(send, SEQ)
 
     intra, carried, local_dec, scarried = pl.pallas_call(
@@ -360,29 +335,31 @@
         cost_estimate=cost(6),
         name="intra",
     )(
-        prompt_lengths, here, query_in, key_in, value_in, log_decay,
-        step_query, step_key, step_value, step_decay,
-    )
-
-    ends = jnp.cumsum(prompt_lengths)
-    blocks = (ends - 1) // BLOCK
-    inner = (ends % BLOCK) != 0
-    crowded = jnp.any((blocks[1:] == blocks[:-1]) & inner[1:])
-    extra = lax.cond(
-        crowded,
-        lambda: more_tails(key_in, value_in, log_decay, prompt_lengths, me * BLOCK),
-        lambda: jnp.zeros((PROMPTS, QUART, HDIM), F32),
-    )
-
+        prompt_lengths, here, query_in, key_in, value_in, logd,
+        step_query, step_key, step_value, step_decay.transpose(0, 2, 1),
+    )
+
+    got, intra, carried, local_dec, scarried = lax.optimization_barrier(
+        (got, intra, carried, local_dec, scarried)
+    )
     entry, own = pl.pallas_call(
         scan_kernel,
         out_shape=(shape(NDEV, QUART, HDIM), shape(PROMPTS, QUART, HDIM)),
-        in_specs=[SMEM] + [VMEM] * 2,
+        in_specs=[SMEM, VMEM],
         out_specs=(VMEM,) * 2,
         compiler_params=params(),
         cost_estimate=cost(2),
         name="scan",
-    )(prompt_lengths, got, extra)
+    )(prompt_lengths, got)
+    own = pl.pallas_call(
+        join_kernel,
+        out_shape=shape(PROMPTS, QUART, HDIM),
+        in_specs=[VMEM] * 2,
+        out_specs=VMEM,
+        compiler_params=params(),
+        cost_estimate=cost(1),
+        name="join",
+    )(own, tails)
     back = exchange(entry, SEQ)
 
     shifted = [

time: 108 us -> 142 us (1.31)
  waiting for transfers between devices: 15.1 us -> 62.2 us
  blocking collectives: 59.2 us -> 15.9 us
  between operations: 1.42 us -> 14.3 us
  starting transfers between devices: 19.3 us -> 29.4 us
  local copies, waits for them, and re-layouts: 1.78 us -> 10 us
  other arithmetic: 1.56 us -> 0 us
    all_to_all x2 -> x1, blocking collectives: 59.2 us -> 15.9 us  [exchange(): return lax.all_to_all(x, axis, split_axis=0, concat_axis=0, tiled=True)]
    reduce_scatter x0 -> x2, waiting for transfers between devices: none -> 33.6 us  [the longest x1 27 us: local(): tails = lax.psum_scatter(tails, 'seq_1', scatter_dimension=0, tiled=True)]
    all_to_all x2 -> x3, waiting for transfers between devices: 10.2 us -> 24.5 us  [exchange(): return lax.all_to_all(x, axis, split_axis=0, concat_axis=0, tiled=True)]
    all_to_all x2 -> x3, starting transfers between devices: 15.6 us -> 25.5 us  [exchange(): return lax.all_to_all(x, axis, split_axis=0, concat_axis=0, tiled=True)]
    unnamed x18 -> x50, local copies, waits for them, and re-layouts: 1.77 us -> 10 us
    pallas_call x1 -> x2, Pallas kernels: 2.48 us -> 3 us  [the longest x1 2.99 us: local(): pl.pallas_call(send_kernel, out_shape=(shape(NDEV, MSG, HDIM), shape(NDEV...]
  transfers between devices with their start and end apart: 5 -> 8, of which waited for: 5 -> 7; matrix products, arithmetic and copies ran while one was open for 0% -> 0% of each run, Pallas kernels for 4% -> 4%
where the time goes in v2:
time: 142 us; the launch traced here: 141 us
  waiting for transfers between devices  62.2 us (44%)
  starting transfers between devices  29.4 us (21%)
  blocking collectives  15.9 us (11%)
  between operations  14.3 us (10%)
  local copies, waits for them, and re-layouts  10 us (7%)
  Pallas kernels  9.66 us (7%)
    reduce_scatter x1, waiting for transfers between devices, local(): tails = lax.psum_scatter(tails, 'seq_1', scatter_dimension=0, tiled=True)  27 us
    all_to_all x3, starting transfers between devices, exchange(): return lax.all_to_all(x, axis, split_axis=0, concat_axis=0, tiled=True)  25.5 us
    all_to_all x3, waiting for transfers between devices, exchange(): return lax.all_to_all(x, axis, split_axis=0, concat_axis=0, tiled=True)  24.5 us
    all_to_all x1, blocking collectives, exchange(): return lax.all_to_all(x, axis, split_axis=0, concat_axis=0, tiled=True)  15.9 us
    unnamed x50, local copies, waits for them, and re-layouts  10 us
    reduce_scatter x1, waiting for transfers between devices, local(): tails = lax.psum_scatter(tails, 'seq_0', scatter_dimension=0, tiled=True)  6.52 us
    ppermute x3, waiting for transfers between devices, local(): lax.ppermute(own, 'seq_0', [(i, (i + d) % NX) for i in range(NX)])  4.05 us
    ppermute x3, starting transfers between devices, local(): lax.ppermute(own, 'seq_0', [(i, (i + d) % NX) for i in range(NX)])  3.75 us
  transfers between devices with their start and end apart: 8, of which 7 were waited for; matrix products, arithmetic and copies ran while one was open for 0% of the time, Pallas kernels for 4%

profile of v2, /device:TPU:1, one launch (start us, length us, event | category | flops | bytes accessed | tf_op | source)
XLA Modules:
  0.0 141.4 jit_solution(15569937296866760679)
XLA Ops:
  7.2 0.0 reduce-scatter.3.cloned.1.call-start
  7.2 0.0 copy-start
  7.2 1.0 copy-done
  8.3 0.0 copy-start.2
  8.3 1.0 copy-done.2
  9.3 0.0 copy-start.5
  9.3 0.9 copy-done.5
  10.2 0.0 copy-start.11
  10.2 0.7 copy-done.11
  10.9 0.7 copy-done.14
  11.6 0.7 copy-done.15
  12.2 3.0 %send.1 = (f32[32,56,128]{2,1,0:T(8,128)}, f32[32,96,128]{2,1,0:T(8,128)}) custom-call(s32[4]{0:T(128)S(1)} %copy-done.15, s32[1]{0:T(128)} %bitcast.here, s32[16]{0:T(128)S(1)} %copy-done.14, bf16[256,1024]{1,0:T(8,128)(2,1)S(1)} %copy-done, bf16[256,1024]{1,0:T(8,128)(2,1)S(1)} %copy-done.2, f32[8,256]{1,0:T(8,128)S(1)} %bitcast.5, ...), custom_call_target="tpu_custom_call" | custom-call | flops 5000000000 | bytes 15000000 | tf_op jit(solution)/shard_map/send/pallas_call | solution.py:315
  15.2 0.0 copy-start.6
  15.2 0.0 copy-start.7
  15.2 0.0 copy-start.8
  15.3 0.0 copy-start.10
  15.3 0.0 copy-start.12
  15.3 0.0 copy-start.16
  15.3 0.0 reduce-scatter.3.cloned.1.call-update
  15.3 12.0 %all-to-all-start = ((f32[32,56,128]{2,1,0:T(8,128)}), f32[32,56,128]{2,1,0:T(8,128)S(1)}, u32[]{:S(2)}, u32[]{:S(2)}) async-start(f32[32,56,128]{2,1,0:T(8,128)} %get-tuple-element.19), calls=%async_computation | async-start | bytes 1835008 | tf_op jit(solution)/shard_map/all_to_all | solution.py:293
  27.3 0.0 reduce-scatter.5.cloned.1.call-start
  27.4 0.0 copy-done.1
  27.4 0.0 copy-done.3
  27.4 0.0 copy-done.4
  27.4 0.0 copy-done.6
  27.4 0.0 copy-done.7
  27.4 0.0 copy-done.8
  27.4 0.0 copy-done.10
  27.5 0.0 copy-done.12
  27.5 0.0 copy-done.16
  27.5 2.3 %intra.1 = (f32[256,1024]{1,0:T(8,128)S(1)}, f32[256,8]{1,0:T(8,128)S(1)}, f32[64,1024]{1,0:T(8,128)S(1)}, f32[64,8]{1,0:T(8,128)S(1)}) custom-call(s32[4]{0:T(128)S(1)} %copy-done.16, s32[1]{0:T(128)} %bitcast.here, bf16[256,1024]{1,0:T(8,128)(2,1)S(1)} %copy-done.4, bf16[256,1024]{1,0:T(8,128)(2,1)S(1)} %copy-done.1, bf16[256,1024]{1,0:T(8,128)(2,1)S(1)} %copy-done.3, ...), custom_call_target="tpu_custom_call" | custom-call | flops 6000000000 | bytes 18000000 | tf_op jit(solution)/shard_map/intra/pallas_call | solution.py:329
  29.7 0.0 copy-start.17
  29.7 0.7 copy-done.17
  30.5 1.0 copy-done.19
  31.4 0.6 copy-done.21
  32.0 0.7 copy-done.23
  32.7 16.6 %all-to-all-done.got_ref = f32[32,56,128]{2,1,0:T(8,128)S(1)} async-done(((f32[32,56,128]{2,1,0:T(8,128)}), f32[32,56,128]{2,1,0:T(8,128)S(1)}, u32[]{:S(2)}, u32[]{:S(2)}) %all-to-all-start) | async-done | bytes 917536 | tf_op jit(solution)/shard_map/all_to_all | solution.py:293
  49.3 6.5 %reduce-scatter.3.cloned.1.call-done = f32[8,96,128]{2,1,0:T(8,128)} async-done(((f32[32,96,128]{2,1,0:T(8,128)}), f32[8,96,128]{2,1,0:T(8,128)}) %reduce-scatter.3.cloned.1.call-update) | async-done | bytes 393232 | tf_op jit(solution)/shard_map/reduce_scatter | solution.py:325
  55.8 0.0 reduce-scatter.5.cloned.1.call-update
  55.8 1.4 scan.1
  57.2 7.4 %all-to-all-start.2 = ((f32[32,32,128]{2,1,0:T(8,128)}), f32[32,32,128]{2,1,0:T(8,128)S(1)}, u32[]{:S(2)}, u32[]{:S(2)}) async-start(f32[32,32,128]{2,1,0:T(8,128)} %get-tuple-element.29), calls=%async_computation.4 | async-start | bytes 1048576 | tf_op jit(solution)/shard_map/all_to_all | solution.py:293
  64.6 27.0 %reduce-scatter.5.cloned.1.call-done.tail_ref = f32[1,96,128]{2,1,0:T(8,128)} async-done(((f32[8,96,128]{2,1,0:T(8,128)}), f32[1,96,128]{2,1,0:T(8,128)}) %reduce-scatter.5.cloned.1.call-update) | async-done | bytes 49168 | tf_op jit(solution)/shard_map/reduce_scatter | solution.py:326
  91.6 0.8 copy-done.9
  92.4 0.0 copy-start.24
  92.5 2.5 %collective-permute-start.2 = (f32[4,32,128]{2,1,0:T(8,128)S(1)}, f32[4,32,128]{2,1,0:T(8,128)S(1)}, u32[]{:S(2)}, u32[]{:S(2)}) collective-permute-start(f32[4,32,128]{2,1,0:T(8,128)S(1)} %join.1.own_ref), channel_id=1, source_target_pairs={{0,192},{64,0},{128,64},{192,128},{1,193},{65,1},{129,65},{193,129... | collective-permute-start | bytes 196616 | tf_op jit(solution)/shard_map/ppermute | solution.py:366
  94.9 0.7 collective-permute-start.1
  95.7 0.5 collective-permute-start
  96.2 0.1 collective-permute-done.2.s3_ref
  96.3 3.3 %collective-permute-done.1.s2_ref = f32[4,32,128]{2,1,0:T(8,128)S(1)} collective-permute-done((f32[4,32,128]{2,1,0:T(8,128)S(1)}, f32[4,32,128]{2,1,0:T(8,128)S(1)}, u32[]{:S(2)}, u32[]{:S(2)}) %collective-permute-start.1) | collective-permute-done | bytes 65568 | tf_op jit(solution)/shard_map/ppermute | solution.py:366
  99.6 0.7 collective-permute-done.s1_ref
  100.3 1.2 project.1
  101.5 0.0 all-to-all-done.2.back_ref
  101.5 6.2 %all-to-all-start.1 = ((f32[32,16,128]{2,1,0:T(8,128)}), f32[32,16,128]{2,1,0:T(8,128)S(1)}, u32[]{:S(2)}, u32[]{:S(2)}) async-start(f32[32,16,128]{2,1,0:T(8,128)} %project.1), calls=%async_computation.3 | async-start | bytes 524288 | tf_op jit(solution)/shard_map/all_to_all | solution.py:293
  107.6 0.0 copy-done.24
  107.7 0.0 copy-start.20
  107.7 1.2 copy-done.20
  108.9 0.5 mixed.1
  109.4 7.9 %all-to-all-done.1.back_ref = f32[32,16,128]{2,1,0:T(8,128)S(1)} async-done(((f32[32,16,128]{2,1,0:T(8,128)}), f32[32,16,128]{2,1,0:T(8,128)S(1)}, u32[]{:S(2)}, u32[]{:S(2)}) %all-to-all-start.1) | async-done | bytes 262176 | tf_op jit(solution)/shard_map/all_to_all | solution.py:293
  117.3 0.0 copy-done.18
  117.3 0.0 copy-done.22
  117.3 0.3 decode.1
  117.6 15.9 %all_to_all.20.sums_ref = f32[8,8,128]{2,1,0:T(8,128)S(1)} all-to-all(f32[8,8,128]{2,1,0:T(8,128)S(1)} %get-tuple-element.33), channel_id=1, replica_groups=mesh['seq_0'=4,'seq_1'=8,'head'=8] {'head'}, dimensions={0} | all-to-all | bytes 65536 | tf_op jit(solution)/shard_map/all_to_all | solution.py:293
  133.5 0.0 copy-done.13
  133.5 1.1 final.1
  (13 shorter events, 0.0 us)
Async XLA Ops:
  7.2 48.6 %reduce-scatter.3.cloned.1.call-start = ((), (), s32[]{:S(2)}) async-start(), calls=%async_computation.6 | async-start | bytes 1966080 | tf_op jit(solution)/shard_map/reduce_scatter | solution.py:325
  7.2 1.0 copy-start
  8.3 1.0 copy-start.2
  9.3 0.9 copy-start.5
  10.2 0.7 copy-start.11
  10.9 0.7 copy-start.14
  11.6 0.7 copy-start.15
  15.2 12.2 %copy-start.1 = (bf16[256,1024]{1,0:T(8,128)(2,1)S(1)}, bf16[256,1024]{1,0:T(8,128)(2,1)}, u32[]{:S(2)}) copy-start(bf16[256,1024]{1,0:T(8,128)(2,1)} %key_ref.3) | copy-start | bytes 1572868
  15.2 12.2 %copy-start.3 = (bf16[256,1024]{1,0:T(8,128)(2,1)S(1)}, bf16[256,1024]{1,0:T(8,128)(2,1)}, u32[]{:S(2)}) copy-start(bf16[256,1024]{1,0:T(8,128)(2,1)} %value_ref.3) | copy-start | bytes 1572868
  15.2 12.2 %copy-start.4 = (bf16[256,1024]{1,0:T(8,128)(2,1)S(1)}, bf16[256,1024]{1,0:T(8,128)(2,1)}, u32[]{:S(2)}) copy-start(bf16[256,1024]{1,0:T(8,128)(2,1)} %query_ref.5) | copy-start | bytes 1572868
  15.2 12.2 %copy-start.6 = (bf16[4,16,1024]{2,1,0:T(8,128)(2,1)S(1)}, bf16[4,16,1024]{2,1,0:T(8,128)(2,1)}, u32[]{:S(2)}) copy-start(bf16[4,16,1024]{2,1,0:T(8,128)(2,1)} %sq_ref.1) | copy-start | bytes 393220
  15.2 12.2 %copy-start.7 = (bf16[4,16,1024]{2,1,0:T(8,128)(2,1)S(1)}, bf16[4,16,1024]{2,1,0:T(8,128)(2,1)}, u32[]{:S(2)}) copy-start(bf16[4,16,1024]{2,1,0:T(8,128)(2,1)} %sk_ref.1) | copy-start | bytes 393220
  15.2 12.2 %copy-start.8 = (bf16[4,16,1024]{2,1,0:T(8,128)(2,1)S(1)}, bf16[4,16,1024]{2,1,0:T(8,128)(2,1)}, u32[]{:S(2)}) copy-start(bf16[4,16,1024]{2,1,0:T(8,128)(2,1)} %sv_ref.1) | copy-start | bytes 393220
  15.3 12.2 %copy-start.10 = (f32[4,16,8]{1,2,0:T(8,128)S(1)}, f32[4,16,8]{1,2,0:T(8,128)}, u32[]{:S(2)}) copy-start(f32[4,16,8]{1,2,0:T(8,128)} %param.20) | copy-start | bytes 6148
  15.3 12.2 %copy-start.12 = (f32[256,8]{0,1:T(8,128)S(1)}, f32[256,8]{0,1:T(8,128)}, u32[]{:S(2)}) copy-start(f32[256,8]{0,1:T(8,128)} %param.14) | copy-start | bytes 24580
  15.3 12.2 %copy-start.16 = (s32[4]{0:T(128)S(1)}, s32[4]{0:T(128)}, u32[]{:S(2)}) copy-start(s32[4]{0:T(128)} %lens.5) | copy-start | bytes 52
  15.3 34.0 %all-to-all-start = ((f32[32,56,128]{2,1,0:T(8,128)}), f32[32,56,128]{2,1,0:T(8,128)S(1)}, u32[]{:S(2)}, u32[]{:S(2)}) async-start(f32[32,56,128]{2,1,0:T(8,128)} %get-tuple-element.19), calls=%async_computation | async-start | bytes 1835008 | tf_op jit(solution)/shard_map/all_to_all | solution.py:293
  27.3 64.3 %reduce-scatter.5.cloned.1.call-start = ((), (), s32[]{:S(2)}) async-start(), calls=%async_computation.7 | async-start | bytes 442368 | tf_op jit(solution)/shard_map/reduce_scatter | solution.py:326
  29.7 0.7 copy-start.17
  30.5 1.0 copy-start.19
  31.4 0.6 copy-start.21
  32.0 0.7 copy-start.23
  57.2 44.3 %all-to-all-start.2 = ((f32[32,32,128]{2,1,0:T(8,128)}), f32[32,32,128]{2,1,0:T(8,128)S(1)}, u32[]{:S(2)}, u32[]{:S(2)}) async-start(f32[32,32,128]{2,1,0:T(8,128)} %get-tuple-element.29), calls=%async_computation.4 | async-start | bytes 1048576 | tf_op jit(solution)/shard_map/all_to_all | solution.py:293
  91.6 0.8 copy-start.9
  92.4 15.2 %copy-start.24 = (f32[256,8]{1,0:T(8,128)S(1)}, f32[256,8]{1,0:T(8,128)}, u32[]{:S(2)}) copy-start(f32[256,8]{1,0:T(8,128)} %copy-done.23) | copy-start | bytes 24580
  92.5 3.8 %collective-permute-start.2 = (f32[4,32,128]{2,1,0:T(8,128)S(1)}, f32[4,32,128]{2,1,0:T(8,128)S(1)}, u32[]{:S(2)}, u32[]{:S(2)}) collective-permute-start(f32[4,32,128]{2,1,0:T(8,128)S(1)} %join.1.own_ref), channel_id=1, source_target_pairs={{0,192},{64,0},{128,64},{192,128},{1,193},{65,1},{129,65},{193,129... | collective-permute-start | bytes 196616 | tf_op jit(solution)/shard_map/ppermute | solution.py:366
  94.9 4.6 %collective-permute-start.1 = (f32[4,32,128]{2,1,0:T(8,128)S(1)}, f32[4,32,128]{2,1,0:T(8,128)S(1)}, u32[]{:S(2)}, u32[]{:S(2)}) collective-permute-start(f32[4,32,128]{2,1,0:T(8,128)S(1)} %join.1.own_ref), channel_id=1, source_target_pairs={{0,128},{64,192},{128,0},{192,64},{1,129},{65,193},{129,1},{193,65... | collective-permute-start | bytes 196616 | tf_op jit(solution)/shard_map/ppermute | solution.py:366
  95.7 4.6 %collective-permute-start = (f32[4,32,128]{2,1,0:T(8,128)S(1)}, f32[4,32,128]{2,1,0:T(8,128)S(1)}, u32[]{:S(2)}, u32[]{:S(2)}) collective-permute-start(f32[4,32,128]{2,1,0:T(8,128)S(1)} %join.1.own_ref), channel_id=1, source_target_pairs={{0,64},{64,128},{128,192},{192,0},{1,65},{65,129},{129,193},{193,1... | collective-permute-start | bytes 196616 | tf_op jit(solution)/shard_map/ppermute | solution.py:366
  101.5 15.8 %all-to-all-start.1 = ((f32[32,16,128]{2,1,0:T(8,128)}), f32[32,16,128]{2,1,0:T(8,128)S(1)}, u32[]{:S(2)}, u32[]{:S(2)}) async-start(f32[32,16,128]{2,1,0:T(8,128)} %project.1), calls=%async_computation.3 | async-start | bytes 524288 | tf_op jit(solution)/shard_map/all_to_all | solution.py:293
  107.7 1.2 copy-start.20
  108.9 8.4 %copy-start.18 = (f32[64,1024]{1,0:T(8,128)S(1)}, f32[64,1024]{1,0:T(8,128)}, u32[]{:S(2)}) copy-start(f32[64,1024]{1,0:T(8,128)} %copy-done.17) | copy-start | bytes 786436
  108.9 8.4 %copy-start.22 = (f32[64,8]{1,0:T(8,128)S(1)}, f32[64,8]{1,0:T(8,128)}, u32[]{:S(2)}) copy-start(f32[64,8]{1,0:T(8,128)} %copy-done.21) | copy-start | bytes 6148
  117.3 16.2 %copy-start.13 = (f32[1024]{0:T(1024)S(1)}, f32[1024]{0:T(1024)}, u32[]{:S(2)}) copy-start(f32[1024]{0:T(1024)} %param.15) | copy-start | bytes 12292
Sparse Core Ops, SparseCore 0:
  15.4 40.3 reduce-scatter.2
  58.3 33.2 reduce-scatter.4

commit v3 on v1

v3 whole, which is shorter than its diff:
```python
import functools

import jax
import jax.numpy as jnp
from jax import lax
from jax.experimental import pallas as pl
from jax.experimental.pallas import tpu as pltpu
from jax.sharding import Mesh
from jax.sharding import PartitionSpec as P

HEAD_COUNT = 64
HDIM = 128
BLOCK = 256
PROMPTS = 4
STEPS = 4
SEQ = ("seq_0", "seq_1")
EPSILON = 1e-06

NX = 4
HEADS = 8
NDEV = NX * HEADS
QUART = HDIM // NX
ROWS_DEV = 16

S0, ASK = 16, 24
IDS = S0 + 1 + PROMPTS
T0, GIVE = 32, 64
O0, BACK = 32, 48

BF = jnp.bfloat16
F32 = jnp.float32
HI = lax.Precision.HIGHEST

SMEM = pl.BlockSpec(memory_space=pltpu.SMEM)
VMEM = pl.BlockSpec(memory_space=pltpu.VMEM)


def params(mib=24):
    return pltpu.CompilerParams(vmem_limit_bytes=mib << 20)


def cost(us):
    return pl.CostEstimate(flops=int(us * 1e9), bytes_accessed=int(us * 3e6), transcendentals=0)


def bounds(lens):
    ends = []
    total = lens[0]
    for p in range(PROMPTS):
        if p:
            total = total + lens[p]
        ends.append(total)
    return ends


def seg_of(pos, ends):
    out = (pos >= ends[0]).astype(jnp.int32)
    for p in range(1, PROMPTS):
        out = out + (pos >= ends[p]).astype(jnp.int32)
    return out


def entry_seg(first, ends):
    return jnp.where(first > 0, seg_of(first - 1, ends), -1)


def cum_columns(logd):
    t = lax.broadcasted_iota(jnp.int32, (BLOCK, BLOCK), 0)
    s = lax.broadcasted_iota(jnp.int32, (BLOCK, BLOCK), 1)
    return lax.dot_general(
        (s <= t).astype(F32), logd, (((1,), (1,)), ((), ())), precision=HI, preferred_element_type=F32
    )


def contract_rows(a, b):
    return lax.dot_general(a, b, (((0,), (0,)), ((), ())), preferred_element_type=F32)


def contract_cols(a, b):
    return lax.dot_general(a, b, (((1,), (1,)), ((), ())), preferred_element_type=F32)


def ask_kernel(lens, here, rows, logd_ref, query_ref, out_ref, flag_ref, cum_ref):
    first = here[0] * BLOCK
    ends = bounds(lens)
    front = entry_seg(first, ends)
    seg_last = seg_of(first + (BLOCK - 1), ends)
    cum_ref[...] = cum_columns(logd_ref[...])
    growth = jnp.exp(cum_ref[BLOCK - 1 : BLOCK, :]) * (seg_last == front).astype(F32)
    leads = []
    crowded = jnp.int32(0)
    for p in range(PROMPTS):
        at = ends[p] - 1 - first
        inside = (at >= 0) & (at < BLOCK)
        reached = cum_ref[pl.ds(jnp.clip(at, 0, BLOCK - 1), 1), :]
        leads.append(jnp.exp(reached) * (inside & (front == p)).astype(F32))
        if p:
            same = (ends[p] - 1) // BLOCK == (ends[p - 1] - 1) // BLOCK
            crowded = crowded | (same & (ends[p] % BLOCK != 0)).astype(jnp.int32)
    flag_ref[0] = crowded
    lane = lax.broadcasted_iota(jnp.int32, (1, HDIM), 1)
    ids = jnp.zeros((1, HDIM), F32)
    for r in range(ROWS_DEV):
        ids = jnp.where(lane == r, rows[r].astype(F32), ids)
    for h in range(HEADS):
        cols = slice(h * HDIM, (h + 1) * HDIM)
        scal = jnp.concatenate(
            [jnp.broadcast_to(growth[:, h : h + 1], (1, HDIM))]
            + [jnp.broadcast_to(leads[p][:, h : h + 1], (1, HDIM)) for p in range(PROMPTS)]
            + [ids, ids, ids],
            axis=0,
        )
        for x in range(NX):
            out_ref[x * HEADS + h, 0:S0, :] = query_ref[x, :, cols].astype(F32)
            out_ref[x * HEADS + h, S0:ASK, :] = scal


def update_kernel(lens, here, key_ref, value_ref, logd_ref, out_ref, cum_ref):
    first = here[0] * BLOCK
    ends = bounds(lens)
    seg_last = seg_of(first + (BLOCK - 1), ends)
    cum = cum_columns(logd_ref[...])
    cum_ref[...] = cum
    tok = lax.broadcasted_iota(jnp.int32, (BLOCK, HEADS), 0)
    seg = seg_of(tok + first, ends)
    keep = jnp.where(seg == seg_last, jnp.exp(cum[BLOCK - 1 : BLOCK, :] - cum), 0.0)
    found = jnp.int32(-1)
    spot = jnp.int32(0)
    for p in range(PROMPTS):
        at = ends[p] - 1 - first
        take = (at >= 0) & (at < BLOCK - 1) & (found < 0)
        found = jnp.where(take, p, found)
        spot = jnp.where(take, at, spot)

    def emit(factor, row):
        for h in range(HEADS):
            cols = slice(h * HDIM, (h + 1) * HDIM)
            keyed = (key_ref[:, cols].astype(F32) * factor[:, h : h + 1]).astype(BF)
            total = contract_rows(value_ref[:, cols], keyed)
            for x in range(NX):
                out_ref[x * HEADS + h, row : row + QUART, :] = total[x * QUART : (x + 1) * QUART, :]

    emit(keep, 0)

    @pl.when(found < 0)
    def _():
        out_ref[:, T0:GIVE, :] = jnp.zeros((NDEV, QUART, HDIM), F32)

    @pl.when(found >= 0)
    def _():
        reached = cum_ref[pl.ds(spot, 1), :]
        taken = (tok <= spot) & (seg == found)
        emit(jnp.where(taken, jnp.exp(jnp.where(taken, reached - cum, 0.0)), 0.0), T0)


def intra_kernel(
    lens, here, query_ref, key_ref, value_ref, logd_ref, sq_ref, sk_ref, sv_ref, sd_ref,
    intra_ref, carried_ref, local_ref, scarried_ref,
):
    first = here[0] * BLOCK
    ends = bounds(lens)
    front = entry_seg(first, ends)
    logd = logd_ref[...]
    t = lax.broadcasted_iota(jnp.int32, (BLOCK, BLOCK), 0)
    s = lax.broadcasted_iota(jnp.int32, (BLOCK, BLOCK), 1)
    cum = cum_columns(logd)
    cum_rows = jnp.dot(logd, (t <= s).astype(F32), precision=HI, preferred_element_type=F32)
    linked = (s <= t) & (seg_of(t + first, ends) == seg_of(s + first, ends))
    tok = lax.broadcasted_iota(jnp.int32, (BLOCK, HEADS), 0)
    carried_ref[...] = jnp.where(seg_of(tok + first, ends) == front, jnp.exp(cum), 0.0)
    for h in range(HEADS):
        cols = slice(h * HDIM, (h + 1) * HDIM)
        scores = contract_cols(query_ref[:, cols], key_ref[:, cols])
        spread = cum[:, h : h + 1] - cum_rows[h : h + 1, :]
        factor = jnp.exp(jnp.where(linked, spread, -1e30))
        weights = (scores * factor).astype(BF)
        intra_ref[:, cols] = jnp.dot(weights, value_ref[:, cols], preferred_element_type=F32)

    n = STEPS * ROWS_DEV
    a = lax.broadcasted_iota(jnp.int32, (n, n), 0)
    b = lax.broadcasted_iota(jnp.int32, (n, n), 1)
    same = (b <= a) & ((a - b) % ROWS_DEV == 0)
    total = sd_ref[0]
    pieces = [total]
    for step in range(1, STEPS):
        total = total + sd_ref[step]
        pieces.append(total)
    scum_rows = jnp.concatenate(pieces, axis=1)
    scum = lax.dot_general(
        (a == b).astype(F32), scum_rows, (((1,), (1,)), ((), ())), precision=HI,
        preferred_element_type=F32,
    )
    scarried_ref[...] = jnp.exp(scum)
    for h in range(HEADS):
        cols = slice(h * HDIM, (h + 1) * HDIM)
        q = sq_ref[:, :, cols].reshape(n, HDIM)
        k = sk_ref[:, :, cols].reshape(n, HDIM)
        v = sv_ref[:, :, cols].reshape(n, HDIM)
        spread = scum[:, h : h + 1] - scum_rows[h : h + 1, :]
        weights = contract_cols(q, k) * jnp.exp(jnp.where(same, spread, -1e30))
        high = weights.astype(BF)
        low = (weights - high.astype(F32)).astype(BF)
        local_ref[:, cols] = jnp.dot(high, v, preferred_element_type=F32) + jnp.dot(
            low, v, preferred_element_type=F32
        )


def scan_kernel(lens, here, ask_ref, q1_ref, q2_ref, q3_ref, give_ref, extra_ref, out_ref, st_ref):
    ends = bounds(lens)
    state = jnp.zeros((QUART, HDIM), F32)
    for k in range(NDEV):
        out_ref[k, 0:O0, :] = state
        state = ask_ref[k, S0 : S0 + 1, :] * state + give_ref[k, 0:T0, :]
    finals = []
    earlier = []
    for p in range(PROMPTS):
        e = ends[p] - 1
        b = e // BLOCK
        slot = jnp.int32(0)
        for other in earlier:
            slot = slot + (other == b).astype(jnp.int32)
        earlier.append(b)
        whole = e % BLOCK == BLOCK - 1
        lead = ask_ref[b, S0 + 1 + p : S0 + 2 + p, :]
        tail = jnp.where(slot == 0, give_ref[b, T0:GIVE, :], extra_ref[p])
        tail = jnp.where(whole, give_ref[b, 0:T0, :], tail)
        finals.append(lead * out_ref[b, 0:O0, :] + tail)

    n = NDEV * ROWS_DEV
    x = here[0] // HEADS
    st_ref[...] = jnp.zeros_like(st_ref)
    ids = jnp.broadcast_to(ask_ref[:, IDS : IDS + 1, :], (NDEV, ROWS_DEV, HDIM))
    r = lax.broadcasted_iota(jnp.int32, (NDEV, ROWS_DEV, HDIM), 1)
    c = lax.broadcasted_iota(jnp.int32, (NDEV, ROWS_DEV, HDIM), 2)
    prompt = jnp.sum(jnp.where(r == c, ids, 0.0), axis=2, keepdims=True).reshape(n, 1)
    res = jnp.zeros((n, HDIM), F32)
    for shift in range(NX):
        step = lax.rem(x - shift + NX, NX)
        at = pl.multiple_of(step * QUART, QUART)
        if shift:
            q = (q1_ref, q2_ref, q3_ref)[shift - 1][...]
        else:
            q = ask_ref[:, 0:S0, :]
        q = q.reshape(n, HDIM)
        for p in range(PROMPTS):
            st_ref[shift, pl.ds(at, QUART), p * HDIM : (p + 1) * HDIM] = finals[p]
        wide = jnp.concatenate(
            [jnp.where(prompt == float(p), q, 0.0).astype(BF) for p in range(PROMPTS)], axis=1
        )
        st = st_ref[shift]
        high = st.astype(BF)
        low = (st - high.astype(F32)).astype(BF)
        res = res + contract_cols(wide, high) + contract_cols(wide, low)
    out_ref[:, O0:BACK, :] = res.reshape(NDEV, ROWS_DEV, HDIM)


def mixed_kernel(
    query_ref, back_ref, intra_ref, carried_ref, local_ref, scarried_ref,
    mixed_ref, dec_ref, send_ref,
):
    acc = jnp.zeros((BLOCK, HDIM), F32)
    for h in range(HEADS):
        cols = slice(h * HDIM, (h + 1) * HDIM)
        state = jnp.concatenate(
            [back_ref[x * HEADS + h, 0:O0, :] for x in range(NX)], axis=0
        ).astype(BF)
        outer = contract_cols(query_ref[:, cols], state)
        mixed = intra_ref[:, cols] + outer * carried_ref[:, h : h + 1]
        mixed_ref[:, cols] = mixed
        acc = acc + mixed * mixed
    flat = jnp.sum(acc.T, axis=0, keepdims=True)

    n = STEPS * ROWS_DEV
    acc = jnp.zeros((n, HDIM), F32)
    for h in range(HEADS):
        cols = slice(h * HDIM, (h + 1) * HDIM)
        got = [back_ref[x * HEADS + h, O0:BACK, :] for x in range(NX)]
        carry = jnp.concatenate(
            [
                jnp.concatenate([g[:, i * QUART : (i + 1) * QUART] for g in got], axis=1)
                for i in range(STEPS)
            ],
            axis=0,
        )
        dec = local_ref[:, cols] + carry * scarried_ref[:, h : h + 1]
        dec_ref[:, cols] = dec
        acc = acc + dec * dec
    full = jnp.concatenate([acc, jnp.zeros((HDIM - n, HDIM), F32)], axis=0)
    dflat = jnp.sum(full.T, axis=0, keepdims=True)
    both = jnp.concatenate(
        [flat[:, :HDIM], flat[:, HDIM:], dflat, jnp.zeros((5, HDIM), F32)], axis=0
    )
    for k in range(HEADS):
        send_ref[k] = both


def final_kernel(sums_ref, mixed_ref, dec_ref, gain_ref, attn_ref, out_ref):
    total = sums_ref[0]
    for k in range(1, HEADS):
        total = total + sums_ref[k]
    scale = lax.rsqrt(total / (HEAD_COUNT * HDIM) + EPSILON)
    gain = gain_ref[...]

    def column(row):
        return jnp.broadcast_to(scale[row : row + 1, :], (HDIM, HDIM)).T

    for half in range(2):
        part = slice(half * HDIM, (half + 1) * HDIM)
        col = column(half)
        for h in range(HEADS):
            cols = slice(h * HDIM, (h + 1) * HDIM)
            attn_ref[part, cols] = (mixed_ref[part, cols] * col * gain[:, cols]).astype(BF)
    col = column(2)
    for h in range(HEADS):
        cols = slice(h * HDIM, (h + 1) * HDIM)
        res = (dec_ref[:, cols] * col[: STEPS * ROWS_DEV, :] * gain[:, cols]).astype(BF)
        for step in range(STEPS):
            out_ref[step, :, cols] = res[step * ROWS_DEV : (step + 1) * ROWS_DEV, :]


def shape(*dims, dtype=F32):
    return jax.ShapeDtypeStruct(dims, dtype)


def exchange(x, axis):
    return lax.all_to_all(x, axis, split_axis=0, concat_axis=0, tiled=True)


def more_tails(key_in, value_in, log_decay, prompt_lengths, first):
    ends = jnp.cumsum(prompt_lengths)
    positions = first + jnp.arange(BLOCK, dtype=jnp.int32)
    segs = jnp.sum((positions[:, None] >= ends[None, :]).astype(jnp.int32), axis=1)
    cum = jnp.cumsum(log_decay, axis=0)
    keys = key_in.reshape(BLOCK, HEADS, HDIM)
    values = value_in.reshape(BLOCK, HEADS, HDIM)
    parts = []
    for p in (1, 2):
        local = ends[p] - 1 - first
        owned = (local >= 0) & (local < BLOCK) & (ends[p - 1] - 1 >= first)
        safe = jnp.clip(local, 0, BLOCK - 1)
        taken = (jnp.arange(BLOCK) <= safe) & (segs == p) & owned
        spread = jnp.where(taken[:, None], cum[safe][None, :] - cum, 0.0)
        keep = jnp.where(taken[:, None], jnp.exp(spread), 0.0)
        tailed = (keys.astype(F32) * keep[:, :, None]).astype(BF)
        part = jnp.einsum("shd,she->hed", tailed, values, preferred_element_type=F32)
        part = part.reshape(HEADS, NX, QUART, HDIM).transpose(1, 0, 2, 3)
        parts.append(part.reshape(NDEV, QUART, HDIM))
    got = exchange(jnp.concatenate(parts, axis=1), SEQ)
    both = jnp.sum(got, axis=0)
    blank = jnp.zeros((QUART, HDIM), F32)
    return jnp.stack([blank, both[:QUART], both[QUART:], blank])


def local(
    query_in,
    key_in,
    value_in,
    log_decay,
    norm_gain,
    prompt_lengths,
    step_query,
    step_key,
    step_value,
    step_decay,
    row_prompt,
):
    me = lax.axis_index(SEQ).astype(jnp.int32)
    here = me[None]
    width = HEADS * HDIM
    n = STEPS * ROWS_DEV

    logd = log_decay.T
    ask, crowded = pl.pallas_call(
        ask_kernel,
        out_shape=(shape(NDEV, ASK, HDIM), shape(1, dtype=jnp.int32)),
        in_specs=[SMEM] * 3 + [VMEM] * 2,
        out_specs=(VMEM, SMEM),
        scratch_shapes=[pltpu.VMEM((BLOCK, HEADS), F32)],
        compiler_params=params(),
        cost_estimate=cost(2),
        name="ask",
    )(prompt_lengths, here, row_prompt, logd, step_query)
    asked = exchange(ask, SEQ)

    give = pl.pallas_call(
        update_kernel,
        out_shape=shape(NDEV, GIVE, HDIM),
        in_specs=[SMEM] * 2 + [VMEM] * 3,
        out_specs=VMEM,
        scratch_shapes=[pltpu.VMEM((BLOCK, HEADS), F32)],
        compiler_params=params(),
        cost_estimate=cost(3),
        name="update",
    )(prompt_lengths, here, key_in, value_in, logd)
    asked, give = lax.optimization_barrier((asked, give))
    given = exchange(give, SEQ)
    queries = asked[:, :S0, :]
    shifted = [
        lax.ppermute(queries, "seq_0", [(i, (i + d) % NX) for i in range(NX)])
        for d in range(1, NX)
    ]

    intra, carried, local_dec, scarried = pl.pallas_call(
        intra_kernel,
        out_shape=(shape(BLOCK, width), shape(BLOCK, HEADS), shape(n, width), shape(n, HEADS)),
        in_specs=[SMEM] * 2 + [VMEM] * 8,
        out_specs=(VMEM,) * 4,
        compiler_params=params(),
        cost_estimate=cost(6),
        name="intra",
    )(
        prompt_lengths, here, query_in, key_in, value_in, logd,
        step_query, step_key, step_value, step_decay.transpose(0, 2, 1),
    )

    crowded, shifted = lax.optimization_barrier((crowded, shifted))
    extra = lax.cond(
        crowded[0] > 0,
        lambda: more_tails(key_in, value_in, log_decay, prompt_lengths, me * BLOCK),
        lambda: jnp.zeros((PROMPTS, QUART, HDIM), F32),
    )
    given, intra, carried, local_dec, scarried, extra, shifted = lax.optimization_barrier(
        (given, intra, carried, local_dec, scarried, extra, shifted)
    )
    out = pl.pallas_call(
        scan_kernel,
        out_shape=shape(NDEV, BACK, HDIM),
        in_specs=[SMEM] * 2 + [VMEM] * 6,
        out_specs=VMEM,
        scratch_shapes=[pltpu.VMEM((NX, HDIM, PROMPTS * HDIM), F32)],
        compiler_params=params(),
        cost_estimate=cost(3),
        name="scan",
    )(prompt_lengths, here, asked, *shifted, given, extra)
    back = exchange(out, SEQ)

    mixed, dec, sums_send = pl.pallas_call(
        mixed_kernel,
        out_shape=(shape(BLOCK, width), shape(n, width), shape(HEADS, 8, HDIM)),
        in_specs=[VMEM] * 6,
        out_specs=(VMEM,) * 3,
        compiler_params=params(),
        cost_estimate=cost(2),
        name="mixed",
    )(query_in, back, intra, carried, local_dec, scarried)
    sums_all = exchange(sums_send, "head")

    return pl.pallas_call(
        final_kernel,
        out_shape=(shape(BLOCK, width, dtype=BF), shape(STEPS, ROWS_DEV, width, dtype=BF)),
        in_specs=[VMEM] * 4,
        out_specs=(VMEM,) * 2,
        compiler_params=params(),
        cost_estimate=cost(2),
        name="final",
    )(sums_all, mixed, dec, norm_gain.reshape(1, width))


def solution(mesh):
    split = Mesh(mesh.devices.reshape(NX, HEADS, mesh.shape["head"]), ("seq_0", "seq_1", "head"))
    placed = (
        P(SEQ, "head"),
        P(SEQ, "head"),
        P(SEQ, "head"),
        P(SEQ, "head"),
        P("head"),
        P(),
        P(None, SEQ, "head"),
        P(None, SEQ, "head"),
        P(None, SEQ, "head"),
        P(None, SEQ, "head"),
        P(SEQ),
    )
    return jax.shard_map(
        local,
        mesh=split,
        in_specs=placed,
        out_specs=(P(SEQ, "head"), P(None, SEQ, "head")),
        check_vma=False,
    )
```

time: 108 us -> 125 us (1.16)
  waiting for transfers between devices: 15.1 us -> 41.4 us
  blocking collectives: 59.2 us -> 41.7 us
  local copies, waits for them, and re-layouts: 1.78 us -> 5.79 us
  starting transfers between devices: 19.3 us -> 22.5 us
  other arithmetic: 1.56 us -> 0 us
  Pallas kernels: 9.92 us -> 11.4 us
    all_to_all x2, waiting for transfers between devices: 10.2 us -> 28.6 us  [exchange(): return lax.all_to_all(x, axis, split_axis=0, concat_axis=0, tiled=True)]
    all_to_all x2, blocking collectives: 59.2 us -> 41.7 us  [exchange(): return lax.all_to_all(x, axis, split_axis=0, concat_axis=0, tiled=True)]
    ppermute x3, waiting for transfers between devices: 4.94 us -> 12.8 us  [local(): lax.ppermute(queries, 'seq_0', [(i, (i + d) % NX) for i in range(NX)])]
    all_to_all x2, starting transfers between devices: 15.6 us -> 19.9 us  [exchange(): return lax.all_to_all(x, axis, split_axis=0, concat_axis=0, tiled=True)]
    unnamed x18 -> x38, local copies, waits for them, and re-layouts: 1.77 us -> 5.76 us
    pallas_call x5 -> x4, Pallas kernels: 5.83 us -> 7.46 us  [the longest x1 2.48 us: local(): pl.pallas_call(update_kernel, out_shape=shape(NDEV, GIVE, HDIM), in_specs...]
where the time goes in v3:
time: 125 us; the launch traced here: 124 us
  blocking collectives  41.7 us (33%)
  waiting for transfers between devices  41.4 us (33%)
  starting transfers between devices  22.5 us (18%)
  Pallas kernels  11.4 us (9%)
  local copies, waits for them, and re-layouts  5.79 us (5%)
  between operations  1.52 us (1%)
    all_to_all x2, blocking collectives, exchange(): return lax.all_to_all(x, axis, split_axis=0, concat_axis=0, tiled=True)  41.7 us
    all_to_all x2, waiting for transfers between devices, exchange(): return lax.all_to_all(x, axis, split_axis=0, concat_axis=0, tiled=True)  28.6 us
    all_to_all x2, starting transfers between devices, exchange(): return lax.all_to_all(x, axis, split_axis=0, concat_axis=0, tiled=True)  19.9 us
    ppermute x3, waiting for transfers between devices, local(): lax.ppermute(queries, 'seq_0', [(i, (i + d) % NX) for i in range(NX)])  12.8 us
    unnamed x38, local copies, waits for them, and re-layouts  5.76 us
    pallas_call x1, Pallas kernels, local(): pl.pallas_call(intra_kernel, out_shape=(shape(BLOCK, width), shape(BLOCK,...  2.93 us
    ppermute x3, starting transfers between devices, local(): lax.ppermute(queries, 'seq_0', [(i, (i + d) % NX) for i in range(NX)])  2.53 us
  transfers between devices with their start and end apart: 5, of which 5 were waited for; matrix products, arithmetic and copies ran while one was open for 0% of the time, Pallas kernels for 4%

profile of v3, /device:TPU:1, one launch (start us, length us, event | category | flops | bytes accessed | tf_op | source)
XLA Modules:
  0.0 124.4 jit_solution(9759377222522562449)
XLA Ops:
  0.6 0.0 copy-start.15
  0.6 0.0 copy-start.7
  0.7 0.0 copy-start.16
  0.7 0.7 copy-done.15
  1.3 0.0 copy-done.7
  1.3 0.0 copy-done.16
  1.3 0.0 copy-start.1
  1.3 0.9 copy-done.1
  2.2 0.0 copy-start.13
  2.2 1.8 %ask.1 = (f32[32,24,128]{2,1,0:T(8,128)}, s32[1]{0:T(128)}) custom-call(s32[4]{0:T(128)S(1)} %copy-done.16, s32[1]{0:T(128)} %bitcast.21.here, s32[16]{0:T(128)S(1)} %copy-done.7, f32[8,256]{1,0:T(8,128)S(1)} %bitcast.63, bf16[4,16,1024]{2,1,0:T(8,128)(2,1)S(1)} %copy-done.1), custom_call_target="tpu_custom_call" | custom-call | flops 2000000000 | bytes 6000000 | tf_op jit(solution)/shard_map/ask/pallas_call | solution.py:373
  4.0 0.0 copy-start.12
  4.1 12.0 %all-to-all-start.1 = ((f32[32,24,128]{2,1,0:T(8,128)}), f32[32,24,128]{2,1,0:T(8,128)S(1)}, u32[]{:S(2)}, u32[]{:S(2)}) async-start(f32[32,24,128]{2,1,0:T(8,128)} %get-tuple-element.44), calls=%async_computation.1 | async-start | bytes 786432 | tf_op jit(solution)/shard_map/all_to_all | solution.py:326
  16.1 0.0 copy-done.13
  16.1 0.0 copy-done.12
  16.1 2.5 %update.1 = f32[32,64,128]{2,1,0:T(8,128)} custom-call(s32[4]{0:T(128)S(1)} %copy-done.16, s32[1]{0:T(128)} %bitcast.21.here, bf16[256,1024]{1,0:T(8,128)(2,1)S(1)} %copy-done.12, bf16[256,1024]{1,0:T(8,128)(2,1)S(1)} %copy-done.13, f32[8,256]{1,0:T(8,128)S(1)} %bitcast.64), custom_call_target="tpu_custom_call" | custom-call | flops 3000000000 | bytes 9000000 | tf_op jit(solution)/shard_map/update/pallas_call | solution.py:385
  18.6 9.1 %all-to-all-done.1.ask_ref = f32[32,24,128]{2,1,0:T(8,128)S(1)} async-done(((f32[32,24,128]{2,1,0:T(8,128)}), f32[32,24,128]{2,1,0:T(8,128)S(1)}, u32[]{:S(2)}, u32[]{:S(2)}) %all-to-all-start.1) | async-done | bytes 393248 | tf_op jit(solution)/shard_map/all_to_all | solution.py:326
  27.7 1.7 %collective-permute-start.2 = (f32[32,16,128]{2,1,0:T(8,128)S(1)}, f32[32,16,128]{2,1,0:T(8,128)S(1)}, u32[]{:S(2)}, u32[]{:S(2)}) collective-permute-start(f32[32,16,128]{2,1,0:T(8,128)S(1)} %slice.28), channel_id=1, source_target_pairs={{0,192},{64,0},{128,64},{192,128},{1,193},{65,1},{129,65},{193,129... | collective-permute-start | bytes 786440 | tf_op jit(solution)/shard_map/ppermute | solution.py:399
  29.4 0.8 collective-permute-start.1
  30.2 0.1 collective-permute-start
  30.3 4.5 %collective-permute-done.2.q3_ref = f32[32,16,128]{2,1,0:T(8,128)S(1)} collective-permute-done((f32[32,16,128]{2,1,0:T(8,128)S(1)}, f32[32,16,128]{2,1,0:T(8,128)S(1)}, u32[]{:S(2)}, u32[]{:S(2)}) %collective-permute-start.2) | collective-permute-done | bytes 262176 | tf_op jit(solution)/shard_map/ppermute | solution.py:399
  34.8 1.5 %collective-permute-done.1.q2_ref = f32[32,16,128]{2,1,0:T(8,128)S(1)} collective-permute-done((f32[32,16,128]{2,1,0:T(8,128)S(1)}, f32[32,16,128]{2,1,0:T(8,128)S(1)}, u32[]{:S(2)}, u32[]{:S(2)}) %collective-permute-start.1) | collective-permute-done | bytes 262176 | tf_op jit(solution)/shard_map/ppermute | solution.py:399
  36.3 6.8 %collective-permute-done.q1_ref = f32[32,16,128]{2,1,0:T(8,128)S(1)} collective-permute-done((f32[32,16,128]{2,1,0:T(8,128)S(1)}, f32[32,16,128]{2,1,0:T(8,128)S(1)}, u32[]{:S(2)}, u32[]{:S(2)}) %collective-permute-start) | collective-permute-done | bytes 262176 | tf_op jit(solution)/shard_map/ppermute | solution.py:399
  43.8 0.0 copy-start.14
  43.8 0.0 copy-start
  43.8 0.0 copy-start.2
  43.8 0.0 copy-start.3
  43.8 0.0 copy-start.4
  43.9 0.0 copy-start.5
  43.9 0.6 copy-done.14
  44.4 7.9 %all-to-all-start.2 = ((f32[32,64,128]{2,1,0:T(8,128)}), f32[32,64,128]{2,1,0:T(8,128)S(1)}, u32[]{:S(2)}, u32[]{:S(2)}) async-start(f32[32,64,128]{2,1,0:T(8,128)} %update.1), calls=%async_computation.2 | async-start | bytes 2097152 | tf_op jit(solution)/shard_map/all_to_all | solution.py:326
  52.4 0.0 copy-start.17
  52.4 0.0 copy-done
  52.4 0.0 copy-done.2
  52.4 0.0 copy-done.3
  52.4 0.0 copy-done.4
  52.4 0.0 copy-done.5
  52.4 0.6 copy-done.17
  53.0 2.9 %intra.1 = (f32[256,1024]{1,0:T(8,128)S(1)}, f32[256,8]{1,0:T(8,128)S(1)}, f32[64,1024]{1,0:T(8,128)S(1)}, f32[64,8]{1,0:T(8,128)S(1)}) custom-call(s32[4]{0:T(128)S(1)} %copy-done.17, s32[1]{0:T(128)} %bitcast.21.here, bf16[256,1024]{1,0:T(8,128)(2,1)S(1)} %copy-done, bf16[256,1024]{1,0:T(8,128)(2,1)} %key_ref.3, bf16[256,1024]{1,0:T(8,128)(2,1)} %value_ref.3, ...), custom_call_target="tpu_custom_call" | custom-call | flops 6000000000 | bytes 18000000 | tf_op jit(solution)/shard_map/intra/pallas_call | solution.py:403
  56.0 0.0 copy-start.8
  56.0 1.0 copy-done.8
  57.0 0.0 copy-start.10
  57.0 0.6 copy-done.10
  57.6 19.4 %all-to-all-done.2.give_ref = f32[32,64,128]{2,1,0:T(8,128)S(1)} async-done(((f32[32,64,128]{2,1,0:T(8,128)}), f32[32,64,128]{2,1,0:T(8,128)S(1)}, u32[]{:S(2)}, u32[]{:S(2)}) %all-to-all-start.2) | async-done | bytes 1048608 | tf_op jit(solution)/shard_map/all_to_all | solution.py:326
  77.0 0.0 copy-start.18
  77.0 0.7 copy-done.18
  77.7 2.3 %scan.1 = f32[32,48,128]{2,1,0:T(8,128)S(1)} custom-call(s32[4]{0:T(128)S(1)} %copy-done.18, s32[1]{0:T(128)} %bitcast.21.here, f32[32,24,128]{2,1,0:T(8,128)S(1)} %all-to-all-done.1.ask_ref, f32[32,16,128]{2,1,0:T(8,128)S(1)} %collective-permute-done.q1_ref, f32[32,16,128]{2,1,0:T(8,128)S(1)} %collective-permute-done.1.q2_ref, ...), custom_call_target="tpu_custom_call" | custom-call | flops 3000000000 | bytes 9000000 | tf_op jit(solution)/shard_map/scan/pallas_call | solution.py:425
  80.0 0.0 copy-start.9
  80.0 0.0 copy-start.11
  80.0 28.3 %all_to_all.25.back_ref = f32[32,48,128]{2,1,0:T(8,128)S(1)} all-to-all(f32[32,48,128]{2,1,0:T(8,128)S(1)} %scan.1), channel_id=1, replica_groups=mesh['seq_0'=4,'seq_1'=8,'head'=8] {'seq_0','seq_1'}, dimensions={0} | all-to-all | bytes 1572864 | tf_op jit(solution)/shard_map/all_to_all | solution.py:326
  108.3 0.0 copy-done.9
  108.3 0.0 copy-done.11
  108.3 0.9 mixed.1
  109.2 13.5 %all_to_all.26.sums_ref = f32[8,8,128]{2,1,0:T(8,128)S(1)} all-to-all(f32[8,8,128]{2,1,0:T(8,128)S(1)} %get-tuple-element.65), channel_id=1, replica_groups=mesh['seq_0'=4,'seq_1'=8,'head'=8] {'head'}, dimensions={0} | all-to-all | bytes 65536 | tf_op jit(solution)/shard_map/all_to_all | solution.py:326
  122.7 0.0 copy-start.6
  122.7 0.7 copy-done.6
  123.3 1.1 final.1
  (3 shorter events, 0.1 us)
Async XLA Ops:
  0.6 0.7 copy-start.15
  0.6 0.7 copy-start.7
  0.7 0.7 copy-start.16
  1.3 0.9 copy-start.1
  2.2 13.8 %copy-start.13 = (bf16[256,1024]{1,0:T(8,128)(2,1)S(1)}, bf16[256,1024]{1,0:T(8,128)(2,1)}, u32[]{:S(2)}) copy-start(bf16[256,1024]{1,0:T(8,128)(2,1)} %value_ref.3) | copy-start | bytes 1572868
  4.0 12.0 %copy-start.12 = (bf16[256,1024]{1,0:T(8,128)(2,1)S(1)}, bf16[256,1024]{1,0:T(8,128)(2,1)}, u32[]{:S(2)}) copy-start(bf16[256,1024]{1,0:T(8,128)(2,1)} %key_ref.3) | copy-start | bytes 1572868
  4.1 23.7 %all-to-all-start.1 = ((f32[32,24,128]{2,1,0:T(8,128)}), f32[32,24,128]{2,1,0:T(8,128)S(1)}, u32[]{:S(2)}, u32[]{:S(2)}) async-start(f32[32,24,128]{2,1,0:T(8,128)} %get-tuple-element.44), calls=%async_computation.1 | async-start | bytes 786432 | tf_op jit(solution)/shard_map/all_to_all | solution.py:326
  27.7 7.0 %collective-permute-start.2 = (f32[32,16,128]{2,1,0:T(8,128)S(1)}, f32[32,16,128]{2,1,0:T(8,128)S(1)}, u32[]{:S(2)}, u32[]{:S(2)}) collective-permute-start(f32[32,16,128]{2,1,0:T(8,128)S(1)} %slice.28), channel_id=1, source_target_pairs={{0,192},{64,0},{128,64},{192,128},{1,193},{65,1},{129,65},{193,129... | collective-permute-start | bytes 786440 | tf_op jit(solution)/shard_map/ppermute | solution.py:399
  29.4 6.8 %collective-permute-start.1 = (f32[32,16,128]{2,1,0:T(8,128)S(1)}, f32[32,16,128]{2,1,0:T(8,128)S(1)}, u32[]{:S(2)}, u32[]{:S(2)}) collective-permute-start(f32[32,16,128]{2,1,0:T(8,128)S(1)} %slice.28), channel_id=1, source_target_pairs={{0,128},{64,192},{128,0},{192,64},{1,129},{65,193},{129,1},{193,65... | collective-permute-start | bytes 786440 | tf_op jit(solution)/shard_map/ppermute | solution.py:399
  30.2 12.9 %collective-permute-start = (f32[32,16,128]{2,1,0:T(8,128)S(1)}, f32[32,16,128]{2,1,0:T(8,128)S(1)}, u32[]{:S(2)}, u32[]{:S(2)}) collective-permute-start(f32[32,16,128]{2,1,0:T(8,128)S(1)} %slice.28), channel_id=1, source_target_pairs={{0,64},{64,128},{128,192},{192,0},{1,65},{65,129},{129,193},{193,1... | collective-permute-start | bytes 786440 | tf_op jit(solution)/shard_map/ppermute | solution.py:399
  43.8 0.6 copy-start.14
  43.8 8.6 %copy-start = (bf16[256,1024]{1,0:T(8,128)(2,1)S(1)}, bf16[256,1024]{1,0:T(8,128)(2,1)}, u32[]{:S(2)}) copy-start(bf16[256,1024]{1,0:T(8,128)(2,1)} %query_ref.5) | copy-start | bytes 1572868
  43.8 8.6 %copy-start.2 = (bf16[4,16,1024]{2,1,0:T(8,128)(2,1)S(1)}, bf16[4,16,1024]{2,1,0:T(8,128)(2,1)}, u32[]{:S(2)}) copy-start(bf16[4,16,1024]{2,1,0:T(8,128)(2,1)} %sq_ref.1) | copy-start | bytes 393220
  43.8 8.6 %copy-start.3 = (bf16[4,16,1024]{2,1,0:T(8,128)(2,1)S(1)}, bf16[4,16,1024]{2,1,0:T(8,128)(2,1)}, u32[]{:S(2)}) copy-start(bf16[4,16,1024]{2,1,0:T(8,128)(2,1)} %sk_ref.1) | copy-start | bytes 393220
  43.8 8.6 %copy-start.4 = (bf16[4,16,1024]{2,1,0:T(8,128)(2,1)S(1)}, bf16[4,16,1024]{2,1,0:T(8,128)(2,1)}, u32[]{:S(2)}) copy-start(bf16[4,16,1024]{2,1,0:T(8,128)(2,1)} %sv_ref.1) | copy-start | bytes 393220
  43.9 8.6 %copy-start.5 = (f32[4,16,8]{1,2,0:T(8,128)S(1)}, f32[4,16,8]{1,2,0:T(8,128)}, u32[]{:S(2)}) copy-start(f32[4,16,8]{1,2,0:T(8,128)} %param.22) | copy-start | bytes 6148
  44.4 32.6 %all-to-all-start.2 = ((f32[32,64,128]{2,1,0:T(8,128)}), f32[32,64,128]{2,1,0:T(8,128)S(1)}, u32[]{:S(2)}, u32[]{:S(2)}) async-start(f32[32,64,128]{2,1,0:T(8,128)} %update.1), calls=%async_computation.2 | async-start | bytes 2097152 | tf_op jit(solution)/shard_map/all_to_all | solution.py:326
  52.4 0.7 copy-start.17
  56.0 1.0 copy-start.8
  57.0 0.6 copy-start.10
  77.0 0.7 copy-start.18
  80.0 28.3 %copy-start.9 = (f32[256,1024]{1,0:T(8,128)S(1)}, f32[256,1024]{1,0:T(8,128)}, u32[]{:S(2)}) copy-start(f32[256,1024]{1,0:T(8,128)} %copy-done.8) | copy-start | bytes 3145732
  80.0 28.3 %copy-start.11 = (f32[64,8]{1,0:T(8,128)S(1)}, f32[64,8]{1,0:T(8,128)}, u32[]{:S(2)}) copy-start(f32[64,8]{1,0:T(8,128)} %copy-done.10) | copy-start | bytes 6148
  122.7 0.7 copy-start.6

commit v4 on v1

v4 whole, which is shorter than its diff:
```python
import functools

import jax
import jax.numpy as jnp
from jax import lax
from jax.experimental import pallas as pl
from jax.experimental.pallas import tpu as pltpu
from jax.sharding import Mesh
from jax.sharding import PartitionSpec as P

HEAD_COUNT = 64
HDIM = 128
BLOCK = 256
PROMPTS = 4
STEPS = 4
SEQ = ("seq_0", "seq_1")
EPSILON = 1e-06

NX = 4
NZ = 8
PAIR = 2
HEADS = NX * PAIR
NDEV = NX * NZ
SLAB = HDIM // NZ
ROWS_DEV = 16
NROW = STEPS * ROWS_DEV
LAST = PROMPTS - 1

PART = PAIR * SLAB
S0 = 2 * PART
GIVE = S0 + PAIR * PROMPTS

BF = jnp.bfloat16
F32 = jnp.float32
HI = lax.Precision.HIGHEST

SMEM = pl.BlockSpec(memory_space=pltpu.SMEM)
VMEM = pl.BlockSpec(memory_space=pltpu.VMEM)


def params(mib=24):
    return pltpu.CompilerParams(vmem_limit_bytes=mib << 20)


def cost(us):
    return pl.CostEstimate(flops=int(us * 1e9), bytes_accessed=int(us * 3e6), transcendentals=0)


def bounds(lens):
    ends = []
    total = lens[0]
    for p in range(PROMPTS):
        if p:
            total = total + lens[p]
        ends.append(total)
    return ends


def seg_of(pos, ends):
    out = (pos >= ends[0]).astype(jnp.int32)
    for p in range(1, PROMPTS):
        out = out + (pos >= ends[p]).astype(jnp.int32)
    return out


def entry_seg(first, ends):
    return jnp.where(first > 0, seg_of(first - 1, ends), -1)


def cum_columns(logd):
    t = lax.broadcasted_iota(jnp.int32, (BLOCK, BLOCK), 0)
    s = lax.broadcasted_iota(jnp.int32, (BLOCK, BLOCK), 1)
    return lax.dot_general(
        (s <= t).astype(F32), logd, (((1,), (1,)), ((), ())), precision=HI, preferred_element_type=F32
    )


def contract_rows(a, b):
    return lax.dot_general(a, b, (((0,), (0,)), ((), ())), preferred_element_type=F32)


def contract_cols(a, b):
    return lax.dot_general(a, b, (((1,), (1,)), ((), ())), preferred_element_type=F32)


def send_kernel(lens, here, key_ref, value_ref, logd_ref, out_ref, flag_ref, cum_ref):
    first = here[0] * BLOCK
    ends = bounds(lens)
    front = entry_seg(first, ends)
    seg_last = seg_of(first + (BLOCK - 1), ends)
    cum = cum_columns(logd_ref[...])
    cum_ref[...] = cum
    tok = lax.broadcasted_iota(jnp.int32, (BLOCK, HEADS), 0)
    seg = seg_of(tok + first, ends)
    last = cum[BLOCK - 1 : BLOCK, :]
    keep = jnp.where(seg == seg_last, jnp.exp(last - cum), 0.0)
    factors = [jnp.exp(last) * (seg_last == front).astype(F32)]
    found = jnp.int32(-1)
    spot = jnp.int32(0)
    crowded = jnp.int32(0)
    for p in range(LAST):
        at = ends[p] - 1 - first
        inside = (at >= 0) & (at < BLOCK)
        reached = cum_ref[pl.ds(jnp.clip(at, 0, BLOCK - 1), 1), :]
        factors.append(jnp.exp(reached) * (inside & (front == p)).astype(F32))
        take = (at >= 0) & (at < BLOCK - 1) & (found < 0)
        found = jnp.where(take, p, found)
        spot = jnp.where(take, at, spot)
        if p:
            same = (ends[p] - 1) // BLOCK == (ends[p - 1] - 1) // BLOCK
            crowded = crowded | (same & (ends[p] % BLOCK != 0)).astype(jnp.int32)
    flag_ref[0] = crowded

    def emit(factor, row):
        for h in range(HEADS):
            x, j = h // PAIR, h % PAIR
            cols = slice(h * HDIM, (h + 1) * HDIM)
            keyed = (key_ref[:, cols].astype(F32) * factor[:, h : h + 1]).astype(BF)
            total = contract_rows(keyed, value_ref[:, cols])
            at = row + j * SLAB
            for z in range(NZ):
                out_ref[x * NZ + z, at : at + SLAB, :] = total[z * SLAB : (z + 1) * SLAB, :]

    emit(keep, 0)
    for x in range(NX):
        scal = jnp.concatenate(
            [
                jnp.broadcast_to(f[:, x * PAIR + j : x * PAIR + j + 1], (1, HDIM))
                for f in factors
                for j in range(PAIR)
            ],
            axis=0,
        )
        for z in range(NZ):
            out_ref[x * NZ + z, S0:GIVE, :] = scal

    @pl.when(found < 0)
    def _():
        out_ref[:, PART:S0, :] = jnp.zeros((NDEV, PART, HDIM), F32)

    @pl.when(found >= 0)
    def _():
        reached = cum_ref[pl.ds(spot, 1), :]
        taken = (tok <= spot) & (seg == found)
        emit(jnp.where(taken, jnp.exp(jnp.where(taken, reached - cum, 0.0)), 0.0), PART)


def query_kernel(here, rows, query_ref, *out_refs):
    x = here[0] // NZ
    r = lax.broadcasted_iota(jnp.int32, (NROW, HDIM), 0) % ROWS_DEV
    ids = jnp.zeros((NROW, HDIM), F32)
    for k in range(ROWS_DEV):
        ids = jnp.where(r == k, rows[k].astype(F32), ids)
    for d, out_ref in enumerate(out_refs):
        pair = lax.rem(x + d, NX)
        cols = pl.ds(pl.multiple_of(pair * (PAIR * HDIM), PAIR * HDIM), PAIR * HDIM)
        q = query_ref[:, :, cols].astype(F32).reshape(NROW, PAIR * HDIM)
        out_ref[:, : PAIR * HDIM] = q
        out_ref[:, PAIR * HDIM :] = ids


def intra_kernel(
    lens, here, query_ref, key_ref, value_ref, logd_ref, sq_ref, sk_ref, sv_ref, sd_ref,
    intra_ref, carried_ref, local_ref, scarried_ref,
):
    first = here[0] * BLOCK
    ends = bounds(lens)
    front = entry_seg(first, ends)
    logd = logd_ref[...]
    t = lax.broadcasted_iota(jnp.int32, (BLOCK, BLOCK), 0)
    s = lax.broadcasted_iota(jnp.int32, (BLOCK, BLOCK), 1)
    cum = cum_columns(logd)
    cum_rows = jnp.dot(logd, (t <= s).astype(F32), precision=HI, preferred_element_type=F32)
    linked = (s <= t) & (seg_of(t + first, ends) == seg_of(s + first, ends))
    tok = lax.broadcasted_iota(jnp.int32, (BLOCK, HEADS), 0)
    carried_ref[...] = jnp.where(seg_of(tok + first, ends) == front, jnp.exp(cum), 0.0)
    for h in range(HEADS):
        cols = slice(h * HDIM, (h + 1) * HDIM)
        scores = contract_cols(query_ref[:, cols], key_ref[:, cols])
        spread = cum[:, h : h + 1] - cum_rows[h : h + 1, :]
        factor = jnp.exp(jnp.where(linked, spread, -1e30))
        weights = (scores * factor).astype(BF)
        intra_ref[:, cols] = jnp.dot(weights, value_ref[:, cols], preferred_element_type=F32)

    n = STEPS * ROWS_DEV
    a = lax.broadcasted_iota(jnp.int32, (n, n), 0)
    b = lax.broadcasted_iota(jnp.int32, (n, n), 1)
    same = (b <= a) & ((a - b) % ROWS_DEV == 0)
    total = sd_ref[0]
    pieces = [total]
    for step in range(1, STEPS):
        total = total + sd_ref[step]
        pieces.append(total)
    scum_rows = jnp.concatenate(pieces, axis=1)
    scum = lax.dot_general(
        (a == b).astype(F32), scum_rows, (((1,), (1,)), ((), ())), precision=HI,
        preferred_element_type=F32,
    )
    scarried_ref[...] = jnp.exp(scum)
    for h in range(HEADS):
        cols = slice(h * HDIM, (h + 1) * HDIM)
        q = sq_ref[:, :, cols].reshape(n, HDIM)
        k = sk_ref[:, :, cols].reshape(n, HDIM)
        v = sv_ref[:, :, cols].reshape(n, HDIM)
        spread = scum[:, h : h + 1] - scum_rows[h : h + 1, :]
        weights = contract_cols(q, k) * jnp.exp(jnp.where(same, spread, -1e30))
        high = weights.astype(BF)
        low = (weights - high.astype(F32)).astype(BF)
        local_ref[:, cols] = jnp.dot(high, v, preferred_element_type=F32) + jnp.dot(
            low, v, preferred_element_type=F32
        )


def scan_kernel(lens, give_ref, extra_ref, entry_ref, slice_ref):
    ends = bounds(lens)
    states = [jnp.zeros((SLAB, HDIM), F32) for _ in range(PAIR)]
    for k in range(NDEV):
        for j in range(PAIR):
            rows = slice(j * SLAB, (j + 1) * SLAB)
            entry_ref[k, rows, :] = states[j]
            states[j] = give_ref[k, S0 + j : S0 + j + 1, :] * states[j] + give_ref[k, rows, :]
    for j in range(PAIR):
        slice_ref[LAST, j] = states[j]
    earlier = []
    for p in range(LAST):
        e = ends[p] - 1
        b = e // BLOCK
        slot = jnp.int32(0)
        for other in earlier:
            slot = slot + (other == b).astype(jnp.int32)
        earlier.append(b)
        whole = e % BLOCK == BLOCK - 1
        for j in range(PAIR):
            rows = slice(j * SLAB, (j + 1) * SLAB)
            at = S0 + (p + 1) * PAIR + j
            lead = give_ref[b, at : at + 1, :]
            tail = give_ref[b, PART + j * SLAB : PART + (j + 1) * SLAB, :]
            tail = jnp.where(slot == 0, tail, extra_ref[p, rows, :])
            tail = jnp.where(whole, give_ref[b, rows, :], tail)
            slice_ref[p, j] = lead * entry_ref[b, rows, :] + tail


def project_kernel(here, *refs):
    queries = refs[:NX]
    slabs = refs[NX : NX + NZ]
    outs = refs[NX + NZ : NX + NZ + NX]
    st_ref = refs[-1]
    z = lax.rem(here[0], NZ)
    for d, ref in enumerate(slabs):
        origin = lax.rem(z - d + NZ, NZ)
        for p in range(PROMPTS):
            at = pl.multiple_of(p * HDIM + origin * SLAB, SLAB)
            for j in range(PAIR):
                st_ref[j, pl.ds(at, SLAB), :] = ref[p, j]
    for j in range(PAIR):
        st = st_ref[j]
        high = st.astype(BF)
        low = (st - high.astype(F32)).astype(BF)
        cols = slice(j * HDIM, (j + 1) * HDIM)
        rows = []
        for ref in queries:
            q = ref[:, cols]
            ids = ref[:, PAIR * HDIM :]
            rows.append(
                jnp.concatenate(
                    [jnp.where(ids == float(p), q, 0.0).astype(BF) for p in range(PROMPTS)], axis=1
                )
            )
        wide = jnp.concatenate(rows, axis=0)
        res = jnp.dot(wide, high, preferred_element_type=F32) + jnp.dot(
            wide, low, preferred_element_type=F32
        )
        for d, ref in enumerate(outs):
            ref[:, cols] = res[d * NROW : (d + 1) * NROW, :]


def mixed_kernel(query_ref, back_ref, intra_ref, carried_ref, mixed_ref, sums_ref):
    acc = jnp.zeros((BLOCK, HDIM), F32)
    for h in range(HEADS):
        x, j = h // PAIR, h % PAIR
        cols = slice(h * HDIM, (h + 1) * HDIM)
        state = jnp.concatenate(
            [back_ref[x * NZ + z, j * SLAB : (j + 1) * SLAB, :] for z in range(NZ)], axis=0
        ).astype(BF)
        outer = jnp.dot(query_ref[:, cols], state, preferred_element_type=F32)
        mixed = intra_ref[:, cols] + outer * carried_ref[:, h : h + 1]
        mixed_ref[:, cols] = mixed
        acc = acc + mixed * mixed
    flat = jnp.sum(acc.T, axis=0, keepdims=True)
    sums_ref[...] = jnp.concatenate(
        [flat[:, :HDIM], flat[:, HDIM:], jnp.zeros((6, HDIM), F32)], axis=0
    )


def decode_kernel(here, o0, o1, o2, o3, local_ref, scarried_ref, sums_ref, dec_ref, send_ref, carry_ref):
    x = here[0] // NZ
    for d, ref in enumerate((o0, o1, o2, o3)):
        carry_ref[lax.rem(x + d, NX)] = ref[...]
    acc = jnp.zeros((NROW, HDIM), F32)
    for h in range(HEADS):
        cols = slice(h * HDIM, (h + 1) * HDIM)
        part = slice((h % PAIR) * HDIM, (h % PAIR + 1) * HDIM)
        dec = local_ref[:, cols] + carry_ref[h // PAIR, :, part] * scarried_ref[:, h : h + 1]
        dec_ref[:, cols] = dec
        acc = acc + dec * dec
    full = jnp.concatenate([acc, jnp.zeros((HDIM - NROW, HDIM), F32)], axis=0)
    flat = jnp.sum(full.T, axis=0, keepdims=True)
    both = jnp.concatenate([sums_ref[0:2, :], flat, jnp.zeros((5, HDIM), F32)], axis=0)
    for k in range(HEADS):
        send_ref[k] = both


def final_kernel(sums_ref, mixed_ref, dec_ref, gain_ref, attn_ref, out_ref):
    total = sums_ref[0]
    for k in range(1, HEADS):
        total = total + sums_ref[k]
    scale = lax.rsqrt(total / (HEAD_COUNT * HDIM) + EPSILON)
    gain = gain_ref[...]

    def column(row):
        return jnp.broadcast_to(scale[row : row + 1, :], (HDIM, HDIM)).T

    for half in range(2):
        part = slice(half * HDIM, (half + 1) * HDIM)
        col = column(half)
        for h in range(HEADS):
            cols = slice(h * HDIM, (h + 1) * HDIM)
            attn_ref[part, cols] = (mixed_ref[part, cols] * col * gain[:, cols]).astype(BF)
    col = column(2)
    for h in range(HEADS):
        cols = slice(h * HDIM, (h + 1) * HDIM)
        res = (dec_ref[:, cols] * col[: STEPS * ROWS_DEV, :] * gain[:, cols]).astype(BF)
        for step in range(STEPS):
            out_ref[step, :, cols] = res[step * ROWS_DEV : (step + 1) * ROWS_DEV, :]


def shape(*dims, dtype=F32):
    return jax.ShapeDtypeStruct(dims, dtype)


def shift(x, axis, size, d):
    return lax.ppermute(x, axis, [(i, (i + d) % size) for i in range(size)])


def exchange(x, axis):
    return lax.all_to_all(x, axis, split_axis=0, concat_axis=0, tiled=True)


def more_tails(key_in, value_in, log_decay, prompt_lengths, first):
    ends = jnp.cumsum(prompt_lengths)
    positions = first + jnp.arange(BLOCK, dtype=jnp.int32)
    segs = jnp.sum((positions[:, None] >= ends[None, :]).astype(jnp.int32), axis=1)
    cum = jnp.cumsum(log_decay, axis=0)
    keys = key_in.reshape(BLOCK, HEADS, HDIM)
    values = value_in.reshape(BLOCK, HEADS, HDIM)
    parts = []
    for p in (1, 2):
        local = ends[p] - 1 - first
        owned = (local >= 0) & (local < BLOCK) & (ends[p - 1] - 1 >= first)
        safe = jnp.clip(local, 0, BLOCK - 1)
        taken = (jnp.arange(BLOCK) <= safe) & (segs == p) & owned
        spread = jnp.where(taken[:, None], cum[safe][None, :] - cum, 0.0)
        keep = jnp.where(taken[:, None], jnp.exp(spread), 0.0)
        tailed = (keys.astype(F32) * keep[:, :, None]).astype(BF)
        part = jnp.einsum("shd,she->hde", tailed, values, preferred_element_type=F32)
        part = part.reshape(NX, PAIR, NZ, SLAB, HDIM).transpose(0, 2, 1, 3, 4)
        parts.append(part.reshape(NDEV, PART, HDIM))
    got = exchange(jnp.concatenate(parts, axis=1), SEQ)
    both = jnp.sum(got, axis=0)
    return jnp.stack([jnp.zeros((PART, HDIM), F32), both[:PART], both[PART:]])


def local(
    query_in,
    key_in,
    value_in,
    log_decay,
    norm_gain,
    prompt_lengths,
    step_query,
    step_key,
    step_value,
    step_decay,
    row_prompt,
):
    me = lax.axis_index(SEQ).astype(jnp.int32)
    here = me[None]
    width = HEADS * HDIM
    n = STEPS * ROWS_DEV

    logd = log_decay.T
    give, crowded = pl.pallas_call(
        send_kernel,
        out_shape=(shape(NDEV, GIVE, HDIM), shape(1, dtype=jnp.int32)),
        in_specs=[SMEM] * 2 + [VMEM] * 3,
        out_specs=(VMEM, SMEM),
        scratch_shapes=[pltpu.VMEM((BLOCK, HEADS), F32)],
        compiler_params=params(),
        cost_estimate=cost(3),
        name="send",
    )(prompt_lengths, here, key_in, value_in, logd)
    given = exchange(give, SEQ)

    queries = pl.pallas_call(
        query_kernel,
        out_shape=(shape(NROW, (PAIR + 1) * HDIM),) * NX,
        in_specs=[SMEM] * 2 + [VMEM],
        out_specs=(VMEM,) * NX,
        compiler_params=params(),
        cost_estimate=cost(1),
        name="query",
    )(here, row_prompt, step_query)
    queries = [queries[0]] + [shift(queries[d], "seq_0", NX, d) for d in range(1, NX)]

    intra, carried, local_dec, scarried = pl.pallas_call(
        intra_kernel,
        out_shape=(shape(BLOCK, width), shape(BLOCK, HEADS), shape(n, width), shape(n, HEADS)),
        in_specs=[SMEM] * 2 + [VMEM] * 8,
        out_specs=(VMEM,) * 4,
        compiler_params=params(),
        cost_estimate=cost(6),
        name="intra",
    )(
        prompt_lengths, here, query_in, key_in, value_in, logd,
        step_query, step_key, step_value, step_decay.transpose(0, 2, 1),
    )

    given, intra, carried, local_dec, scarried, queries, crowded = lax.optimization_barrier(
        (given, intra, carried, local_dec, scarried, queries, crowded)
    )
    extra = lax.cond(
        crowded[0] > 0,
        lambda: more_tails(key_in, value_in, log_decay, prompt_lengths, me * BLOCK),
        lambda: jnp.zeros((LAST, PART, HDIM), F32),
    )
    entry, own = pl.pallas_call(
        scan_kernel,
        out_shape=(shape(NDEV, PART, HDIM), shape(PROMPTS, PAIR, SLAB, HDIM)),
        in_specs=[SMEM] + [VMEM] * 2,
        out_specs=(VMEM,) * 2,
        compiler_params=params(),
        cost_estimate=cost(2),
        name="scan",
    )(prompt_lengths, given, extra)
    back = exchange(entry, SEQ)

    slabs = [own] * NZ
    for d in range(1, NZ // 2 + 1):
        slabs[d] = shift(slabs[d - 1], "seq_1", NZ, 1)
        if d < NZ // 2:
            slabs[NZ - d] = shift(slabs[(NZ - d + 1) % NZ], "seq_1", NZ, -1)
    products = pl.pallas_call(
        project_kernel,
        out_shape=(shape(NROW, PAIR * HDIM),) * NX,
        in_specs=[SMEM] + [VMEM] * (NX + NZ),
        out_specs=(VMEM,) * NX,
        scratch_shapes=[pltpu.VMEM((PAIR, PROMPTS * HDIM, HDIM), F32)],
        compiler_params=params(),
        cost_estimate=cost(2),
        name="project",
    )(here, *queries, *slabs)
    products = [products[0]] + [shift(products[d], "seq_0", NX, -d) for d in range(1, NX)]

    mixed, sums = pl.pallas_call(
        mixed_kernel,
        out_shape=(shape(BLOCK, width), shape(8, HDIM)),
        in_specs=[VMEM] * 4,
        out_specs=(VMEM,) * 2,
        compiler_params=params(),
        cost_estimate=cost(2),
        name="mixed",
    )(query_in, back, intra, carried)
    dec, sums_send = pl.pallas_call(
        decode_kernel,
        out_shape=(shape(n, width), shape(HEADS, 8, HDIM)),
        in_specs=[SMEM] + [VMEM] * 7,
        out_specs=(VMEM,) * 2,
        scratch_shapes=[pltpu.VMEM((NX, NROW, PAIR * HDIM), F32)],
        compiler_params=params(),
        cost_estimate=cost(1),
        name="decode",
    )(here, *products, local_dec, scarried, sums)
    sums_all = exchange(sums_send, "head")

    return pl.pallas_call(
        final_kernel,
        out_shape=(shape(BLOCK, width, dtype=BF), shape(STEPS, ROWS_DEV, width, dtype=BF)),
        in_specs=[VMEM] * 4,
        out_specs=(VMEM,) * 2,
        compiler_params=params(),
        cost_estimate=cost(2),
        name="final",
    )(sums_all, mixed, dec, norm_gain.reshape(1, width))


def solution(mesh):
    split = Mesh(mesh.devices.reshape(NX, NZ, mesh.shape["head"]), ("seq_0", "seq_1", "head"))
    placed = (
        P(SEQ, "head"),
        P(SEQ, "head"),
        P(SEQ, "head"),
        P(SEQ, "head"),
        P("head"),
        P(),
        P(None, SEQ, "head"),
        P(None, SEQ, "head"),
        P(None, SEQ, "head"),
        P(None, SEQ, "head"),
        P(SEQ),
    )
    return jax.shard_map(
        local,
        mesh=split,
        in_specs=placed,
        out_specs=(P(SEQ, "head"), P(None, SEQ, "head")),
        check_vma=False,
    )
```

time: 108 us -> 108 us (level)
  blocking collectives: 59.2 us -> 17.3 us
  waiting for transfers between devices: 15.1 us -> 41.3 us
  starting transfers between devices: 19.3 us -> 36.1 us
  other arithmetic: 1.56 us -> 0 us
    all_to_all x2 -> x1, blocking collectives: 59.2 us -> 17.3 us  [exchange(): return lax.all_to_all(x, axis, split_axis=0, concat_axis=0, tiled=True)]
    ppermute x3 -> x13, waiting for transfers between devices: 4.94 us -> 26.6 us  [shift(): return lax.ppermute(x, axis, [(i, (i + d) % size) for i in range(size)])]
    ppermute x3 -> x13, starting transfers between devices: 3.68 us -> 15.6 us  [shift(): return lax.ppermute(x, axis, [(i, (i + d) % size) for i in range(size)])]
    all_to_all x2, starting transfers between devices: 15.6 us -> 20.5 us  [exchange(): return lax.all_to_all(x, axis, split_axis=0, concat_axis=0, tiled=True)]
    all_to_all x2, waiting for transfers between devices: 10.2 us -> 14.7 us  [exchange(): return lax.all_to_all(x, axis, split_axis=0, concat_axis=0, tiled=True)]
    pallas_call x3 -> x4, Pallas kernels: 5.1 us -> 5.95 us  [the longest x1 3.48 us: local(): pl.pallas_call(send_kernel, out_shape=(shape(NDEV, GIVE, HDIM), shape(1,...]
  transfers between devices with their start and end apart: 5 -> 15, of which waited for: 5 -> 9; matrix products, arithmetic and copies ran while one was open for 0% -> 0% of each run, Pallas kernels for 4% -> 4%
where the time goes in v4:
time: 108 us
  waiting for transfers between devices  41.3 us (38%)
  starting transfers between devices  36.1 us (33%)
  blocking collectives  17.3 us (16%)
  Pallas kernels  9.99 us (9%)
  between operations  1.52 us (1%)
  local copies, waits for them, and re-layouts  1.36 us (1%)
    ppermute x13, waiting for transfers between devices, shift(): return lax.ppermute(x, axis, [(i, (i + d) % size) for i in range(size)])  26.6 us
    all_to_all x2, starting transfers between devices, exchange(): return lax.all_to_all(x, axis, split_axis=0, concat_axis=0, tiled=True)  20.5 us
    all_to_all x1, blocking collectives, exchange(): return lax.all_to_all(x, axis, split_axis=0, concat_axis=0, tiled=True)  17.3 us
    ppermute x13, starting transfers between devices, shift(): return lax.ppermute(x, axis, [(i, (i + d) % size) for i in range(size)])  15.6 us
    all_to_all x2, waiting for transfers between devices, exchange(): return lax.all_to_all(x, axis, split_axis=0, concat_axis=0, tiled=True)  14.7 us
    pallas_call x1, Pallas kernels, local(): pl.pallas_call(send_kernel, out_shape=(shape(NDEV, GIVE, HDIM), shape(1,...  3.48 us
    pallas_call x1, Pallas kernels, local(): pl.pallas_call(intra_kernel, out_shape=(shape(BLOCK, width), shape(BLOCK,...  2.26 us
  transfers between devices with their start and end apart: 15, of which 9 were waited for; matrix products, arithmetic and copies ran while one was open for 0% of the time, Pallas kernels for 4%

profile of v4, /device:TPU:1, one launch (start us, length us, event | category | flops | bytes accessed | tf_op | source)
XLA Modules:
  0.0 107.5 jit_solution(15000386428189510631)
XLA Ops:
  0.6 3.5 %send.1 = (f32[32,72,128]{2,1,0:T(8,128)}, s32[1]{0:T(128)}) custom-call(s32[4]{0:T(128)} %lens.5, s32[1]{0:T(128)} %bitcast.20.here, bf16[256,1024]{1,0:T(8,128)(2,1)} %key_ref.3, bf16[256,1024]{1,0:T(8,128)(2,1)} %value_ref.3, f32[8,256]{1,0:T(8,128)} %bitcast.55), custom_call_target="tpu_custom_call" | custom-call | flops 3000000000 | bytes 9000000 | tf_op jit(solution)/shard_map/send/pallas_call | solution.py:392
  4.1 0.0 copy-start.1
  4.1 0.0 copy-start.6
  4.1 12.0 %all-to-all-start.1 = ((f32[32,72,128]{2,1,0:T(8,128)}), f32[32,72,128]{2,1,0:T(8,128)S(1)}, u32[]{:S(2)}, u32[]{:S(2)}) async-start(f32[32,72,128]{2,1,0:T(8,128)} %get-tuple-element.50), calls=%async_computation.1 | async-start | bytes 2359296 | tf_op jit(solution)/shard_map/all_to_all | solution.py:346
  16.2 0.0 copy-done.1
  16.2 0.0 copy-done.6
  16.2 0.0 copy-start
  16.2 0.0 copy-start.2
  16.2 0.0 copy-start.3
  16.2 0.0 copy-start.4
  16.2 0.0 copy-start.12
  16.2 0.0 copy-start.14
  16.3 0.0 copy-start.15
  16.3 0.0 copy-start.16
  16.3 0.6 query.1
  16.9 1.3 %collective-permute-start = (f32[64,384]{1,0:T(8,128)S(1)}, f32[64,384]{1,0:T(8,128)S(1)}, u32[]{:S(2)}, u32[]{:S(2)}) collective-permute-start(f32[64,384]{1,0:T(8,128)S(1)} %get-tuple-element.56), channel_id=1, source_target_pairs={{0,64},{64,128},{128,192},{192,0},{1,65},{65,129},{129,193},{193,1... | collective-permute-start | bytes 294920 | tf_op jit(solution)/shard_map/ppermute | solution.py:342
  18.2 2.4 %collective-permute-start.1 = (f32[64,384]{1,0:T(8,128)S(1)}, f32[64,384]{1,0:T(8,128)S(1)}, u32[]{:S(2)}, u32[]{:S(2)}) collective-permute-start(f32[64,384]{1,0:T(8,128)S(1)} %get-tuple-element.57), channel_id=1, source_target_pairs={{0,128},{64,192},{128,0},{192,64},{1,129},{65,193},{129,1},{193,65... | collective-permute-start | bytes 294920 | tf_op jit(solution)/shard_map/ppermute | solution.py:342
  20.6 1.1 %collective-permute-start.2 = (f32[64,384]{1,0:T(8,128)S(1)}, f32[64,384]{1,0:T(8,128)S(1)}, u32[]{:S(2)}, u32[]{:S(2)}) collective-permute-start(f32[64,384]{1,0:T(8,128)S(1)} %get-tuple-element.58), channel_id=1, source_target_pairs={{0,192},{64,0},{128,64},{192,128},{1,193},{65,1},{129,65},{193,129... | collective-permute-start | bytes 294920 | tf_op jit(solution)/shard_map/ppermute | solution.py:342
  21.8 0.0 copy-done
  21.8 0.0 copy-done.2
  21.8 0.0 copy-done.3
  21.8 0.0 copy-done.4
  21.8 0.0 copy-done.12
  21.8 0.0 copy-done.14
  21.8 0.0 copy-done.15
  21.8 0.0 copy-done.16
  21.8 2.3 %intra.1 = (f32[256,1024]{1,0:T(8,128)S(1)}, f32[256,8]{1,0:T(8,128)S(1)}, f32[64,1024]{1,0:T(8,128)S(1)}, f32[64,8]{1,0:T(8,128)S(1)}) custom-call(s32[4]{0:T(128)S(1)} %copy-done.16, s32[1]{0:T(128)} %bitcast.20.here, bf16[256,1024]{1,0:T(8,128)(2,1)S(1)} %copy-done, bf16[256,1024]{1,0:T(8,128)(2,1)S(1)} %copy-done.14, bf16[256,1024]{1,0:T(8,128)(2,1)S(1)} %copy-done.12, ...), custom_call_target="tpu_custom_call" | custom-call | flops 6000000000 | bytes 18000000 | tf_op jit(solution)/shard_map/intra/pallas_call | solution.py:415
  24.1 0.0 copy-start.7
  24.1 0.7 copy-done.7
  24.8 0.6 copy-done.9
  25.4 0.0 collective-permute-done.refs_1_
  25.4 3.6 %collective-permute-done.1.refs_2_ = f32[64,384]{1,0:T(8,128)S(1)} collective-permute-done((f32[64,384]{1,0:T(8,128)S(1)}, f32[64,384]{1,0:T(8,128)S(1)}, u32[]{:S(2)}, u32[]{:S(2)}) %collective-permute-start.1) | collective-permute-done | bytes 98336 | tf_op jit(solution)/shard_map/ppermute | solution.py:342
  29.0 0.0 collective-permute-done.2.refs_3_
  29.0 14.7 %all-to-all-done.1.give_ref = f32[32,72,128]{2,1,0:T(8,128)S(1)} async-done(((f32[32,72,128]{2,1,0:T(8,128)}), f32[32,72,128]{2,1,0:T(8,128)S(1)}, u32[]{:S(2)}, u32[]{:S(2)}) %all-to-all-start.1) | async-done | bytes 1179680 | tf_op jit(solution)/shard_map/all_to_all | solution.py:346
  44.4 1.4 %scan.1 = (f32[32,32,128]{2,1,0:T(8,128)}, f32[4,2,16,128]{3,2,1,0:T(8,128)S(1)}) custom-call(s32[4]{0:T(128)S(1)} %copy-done.16, f32[32,72,128]{2,1,0:T(8,128)S(1)} %all-to-all-done.1.give_ref, f32[3,32,128]{2,1,0:T(8,128)S(1)} %get-tuple-element.111.extra_ref), custom_call_target="tpu_custom_call" | custom-call | flops 2000000000 | bytes 6000000 | tf_op jit(solution)/shard_map/scan/pallas_call | solution.py:436
  45.8 8.5 %all-to-all-start.2 = ((f32[32,32,128]{2,1,0:T(8,128)}), f32[32,32,128]{2,1,0:T(8,128)S(1)}, u32[]{:S(2)}, u32[]{:S(2)}) async-start(f32[32,32,128]{2,1,0:T(8,128)} %get-tuple-element.73), calls=%async_computation.2 | async-start | bytes 1048576 | tf_op jit(solution)/shard_map/all_to_all | solution.py:346
  54.3 0.0 copy-start.8
  54.3 1.3 %collective-permute-start.3 = (f32[4,2,16,128]{3,2,1,0:T(8,128)S(1)}, f32[4,2,16,128]{3,2,1,0:T(8,128)S(1)}, u32[]{:S(2)}, u32[]{:S(2)}) collective-permute-start(f32[4,2,16,128]{3,2,1,0:T(8,128)S(1)} %get-tuple-element.66.refs_4_), channel_id=1, source_target_pairs={{0,8},{8,16},{16,24},{24,32},{32,40},{40,48},{48,56},{56,0},{1,9},... | collective-permute-start | bytes 196616 | tf_op jit(solution)/shard_map/ppermute | solution.py:342
  55.6 1.4 %collective-permute-start.7 = (f32[4,2,16,128]{3,2,1,0:T(8,128)S(1)}, f32[4,2,16,128]{3,2,1,0:T(8,128)S(1)}, u32[]{:S(2)}, u32[]{:S(2)}) collective-permute-start(f32[4,2,16,128]{3,2,1,0:T(8,128)S(1)} %get-tuple-element.66.refs_4_), channel_id=1, source_target_pairs={{0,56},{8,0},{16,8},{24,16},{32,24},{40,32},{48,40},{56,48},{1,57}... | collective-permute-start | bytes 196616 | tf_op jit(solution)/shard_map/ppermute | solution.py:342
  57.0 10.3 %collective-permute-done.3.refs_5_ = f32[4,2,16,128]{3,2,1,0:T(8,128)S(1)} collective-permute-done((f32[4,2,16,128]{3,2,1,0:T(8,128)S(1)}, f32[4,2,16,128]{3,2,1,0:T(8,128)S(1)}, u32[]{:S(2)}, u32[]{:S(2)}) %collective-permute-start.3) | collective-permute-done | bytes 65568 | tf_op jit(solution)/shard_map/ppermute | solution.py:342
  67.3 0.0 collective-permute-start.4
  67.3 0.3 collective-permute-done.7.refs_11_
  67.7 2.3 %collective-permute-start.8 = (f32[4,2,16,128]{3,2,1,0:T(8,128)S(1)}, f32[4,2,16,128]{3,2,1,0:T(8,128)S(1)}, u32[]{:S(2)}, u32[]{:S(2)}) collective-permute-start(f32[4,2,16,128]{3,2,1,0:T(8,128)S(1)} %collective-permute-done.7.refs_11_), channel_id=1, source_target_pairs={{0,56},{8,0},{16,8},{24,16},{32,24},{40,32},{48,40},{56,48},{1,57}... | collective-permute-start | bytes 196616 | tf_op jit(solution)/shard_map/ppermute | solution.py:342
  70.0 1.9 %collective-permute-done.4.refs_6_ = f32[4,2,16,128]{3,2,1,0:T(8,128)S(1)} collective-permute-done((f32[4,2,16,128]{3,2,1,0:T(8,128)S(1)}, f32[4,2,16,128]{3,2,1,0:T(8,128)S(1)}, u32[]{:S(2)}, u32[]{:S(2)}) %collective-permute-start.4) | collective-permute-done | bytes 65568 | tf_op jit(solution)/shard_map/ppermute | solution.py:342
  72.0 0.0 collective-permute-start.5
  72.0 0.0 collective-permute-done.8.refs_10_
  72.0 2.7 %collective-permute-start.9 = (f32[4,2,16,128]{3,2,1,0:T(8,128)S(1)}, f32[4,2,16,128]{3,2,1,0:T(8,128)S(1)}, u32[]{:S(2)}, u32[]{:S(2)}) collective-permute-start(f32[4,2,16,128]{3,2,1,0:T(8,128)S(1)} %collective-permute-done.8.refs_10_), channel_id=1, source_target_pairs={{0,56},{8,0},{16,8},{24,16},{32,24},{40,32},{48,40},{56,48},{1,57}... | collective-permute-start | bytes 196616 | tf_op jit(solution)/shard_map/ppermute | solution.py:342
  74.6 1.6 %collective-permute-done.5.refs_7_ = f32[4,2,16,128]{3,2,1,0:T(8,128)S(1)} collective-permute-done((f32[4,2,16,128]{3,2,1,0:T(8,128)S(1)}, f32[4,2,16,128]{3,2,1,0:T(8,128)S(1)}, u32[]{:S(2)}, u32[]{:S(2)}) %collective-permute-start.5) | collective-permute-done | bytes 65568 | tf_op jit(solution)/shard_map/ppermute | solution.py:342
  76.3 0.0 collective-permute-start.6
  76.3 0.0 collective-permute-done.9.refs_9_
  76.3 5.0 %collective-permute-done.6.refs_8_ = f32[4,2,16,128]{3,2,1,0:T(8,128)S(1)} collective-permute-done((f32[4,2,16,128]{3,2,1,0:T(8,128)S(1)}, f32[4,2,16,128]{3,2,1,0:T(8,128)S(1)}, u32[]{:S(2)}, u32[]{:S(2)}) %collective-permute-start.6) | collective-permute-done | bytes 65568 | tf_op jit(solution)/shard_map/ppermute | solution.py:342
  81.3 0.5 project.1
  81.8 1.8 %collective-permute-start.10 = (f32[64,256]{1,0:T(8,128)S(1)}, f32[64,256]{1,0:T(8,128)S(1)}, u32[]{:S(2)}, u32[]{:S(2)}) collective-permute-start(f32[64,256]{1,0:T(8,128)S(1)} %get-tuple-element.68), channel_id=1, source_target_pairs={{0,192},{64,0},{128,64},{192,128},{1,193},{65,1},{129,65},{193,129... | collective-permute-start | bytes 196616 | tf_op jit(solution)/shard_map/ppermute | solution.py:342
  83.6 0.5 collective-permute-start.11
  84.1 0.6 collective-permute-start.12
  84.7 0.0 all-to-all-done.2.back_ref
  84.7 0.0 copy-done.8
  84.7 0.5 mixed.1
  85.2 0.0 collective-permute-done.10.o1
  85.2 3.1 %collective-permute-done.11.o2 = f32[64,256]{1,0:T(8,128)S(1)} collective-permute-done((f32[64,256]{1,0:T(8,128)S(1)}, f32[64,256]{1,0:T(8,128)S(1)}, u32[]{:S(2)}, u32[]{:S(2)}) %collective-permute-start.11) | collective-permute-done | bytes 65568 | tf_op jit(solution)/shard_map/ppermute | solution.py:342
  88.3 0.6 collective-permute-done.12.o3
  88.9 0.3 decode.1
  89.2 17.3 %all_to_all.19.sums_ref = f32[8,8,128]{2,1,0:T(8,128)S(1)} all-to-all(f32[8,8,128]{2,1,0:T(8,128)S(1)} %get-tuple-element.77), channel_id=1, replica_groups=mesh['seq_0'=4,'seq_1'=8,'head'=8] {'head'}, dimensions={0} | all-to-all | bytes 65536 | tf_op jit(solution)/shard_map/all_to_all | solution.py:346
  106.5 1.1 final.1
  (7 shorter events, 0.0 us)
Async XLA Ops:
  4.1 12.0 %copy-start.1 = (bf16[4,16,1024]{2,1,0:T(8,128)(2,1)S(1)}, bf16[4,16,1024]{2,1,0:T(8,128)(2,1)}, u32[]{:S(2)}) copy-start(bf16[4,16,1024]{2,1,0:T(8,128)(2,1)} %query_ref.4) | copy-start | bytes 393220
  4.1 12.0 %copy-start.6 = (s32[16]{0:T(128)S(1)}, s32[16]{0:T(128)}, u32[]{:S(2)}) copy-start(s32[16]{0:T(128)} %rows.1) | copy-start | bytes 196
  4.1 39.5 %all-to-all-start.1 = ((f32[32,72,128]{2,1,0:T(8,128)}), f32[32,72,128]{2,1,0:T(8,128)S(1)}, u32[]{:S(2)}, u32[]{:S(2)}) async-start(f32[32,72,128]{2,1,0:T(8,128)} %get-tuple-element.50), calls=%async_computation.1 | async-start | bytes 2359296 | tf_op jit(solution)/shard_map/all_to_all | solution.py:346
  16.2 5.6 %copy-start = (bf16[256,1024]{1,0:T(8,128)(2,1)S(1)}, bf16[256,1024]{1,0:T(8,128)(2,1)}, u32[]{:S(2)}) copy-start(bf16[256,1024]{1,0:T(8,128)(2,1)} %query_ref.5) | copy-start | bytes 1572868
  16.2 5.6 %copy-start.2 = (bf16[4,16,1024]{2,1,0:T(8,128)(2,1)S(1)}, bf16[4,16,1024]{2,1,0:T(8,128)(2,1)}, u32[]{:S(2)}) copy-start(bf16[4,16,1024]{2,1,0:T(8,128)(2,1)} %sk_ref.1) | copy-start | bytes 393220
  16.2 5.6 %copy-start.3 = (bf16[4,16,1024]{2,1,0:T(8,128)(2,1)S(1)}, bf16[4,16,1024]{2,1,0:T(8,128)(2,1)}, u32[]{:S(2)}) copy-start(bf16[4,16,1024]{2,1,0:T(8,128)(2,1)} %sv_ref.1) | copy-start | bytes 393220
  16.2 5.6 %copy-start.4 = (f32[4,16,8]{1,2,0:T(8,128)S(1)}, f32[4,16,8]{1,2,0:T(8,128)}, u32[]{:S(2)}) copy-start(f32[4,16,8]{1,2,0:T(8,128)} %param.22) | copy-start | bytes 6148
  16.2 5.5 %copy-start.12 = (bf16[256,1024]{1,0:T(8,128)(2,1)S(1)}, bf16[256,1024]{1,0:T(8,128)(2,1)}, u32[]{:S(2)}) copy-start(bf16[256,1024]{1,0:T(8,128)(2,1)} %value_ref.3) | copy-start | bytes 1572868
  16.2 5.5 %copy-start.14 = (bf16[256,1024]{1,0:T(8,128)(2,1)S(1)}, bf16[256,1024]{1,0:T(8,128)(2,1)}, u32[]{:S(2)}) copy-start(bf16[256,1024]{1,0:T(8,128)(2,1)} %key_ref.3) | copy-start | bytes 1572868
  16.3 5.5 %copy-start.15 = (f32[256,8]{0,1:T(8,128)S(1)}, f32[256,8]{0,1:T(8,128)}, u32[]{:S(2)}) copy-start(f32[256,8]{0,1:T(8,128)} %param.16) | copy-start | bytes 24580
  16.3 5.5 %copy-start.16 = (s32[4]{0:T(128)S(1)}, s32[4]{0:T(128)}, u32[]{:S(2)}) copy-start(s32[4]{0:T(128)} %lens.5) | copy-start | bytes 52
  16.9 8.5 %collective-permute-start = (f32[64,384]{1,0:T(8,128)S(1)}, f32[64,384]{1,0:T(8,128)S(1)}, u32[]{:S(2)}, u32[]{:S(2)}) collective-permute-start(f32[64,384]{1,0:T(8,128)S(1)} %get-tuple-element.56), channel_id=1, source_target_pairs={{0,64},{64,128},{128,192},{192,0},{1,65},{65,129},{129,193},{193,1... | collective-permute-start | bytes 294920 | tf_op jit(solution)/shard_map/ppermute | solution.py:342
  18.2 10.8 %collective-permute-start.1 = (f32[64,384]{1,0:T(8,128)S(1)}, f32[64,384]{1,0:T(8,128)S(1)}, u32[]{:S(2)}, u32[]{:S(2)}) collective-permute-start(f32[64,384]{1,0:T(8,128)S(1)} %get-tuple-element.57), channel_id=1, source_target_pairs={{0,128},{64,192},{128,0},{192,64},{1,129},{65,193},{129,1},{193,65... | collective-permute-start | bytes 294920 | tf_op jit(solution)/shard_map/ppermute | solution.py:342
  20.6 8.4 %collective-permute-start.2 = (f32[64,384]{1,0:T(8,128)S(1)}, f32[64,384]{1,0:T(8,128)S(1)}, u32[]{:S(2)}, u32[]{:S(2)}) collective-permute-start(f32[64,384]{1,0:T(8,128)S(1)} %get-tuple-element.58), channel_id=1, source_target_pairs={{0,192},{64,0},{128,64},{192,128},{1,193},{65,1},{129,65},{193,129... | collective-permute-start | bytes 294920 | tf_op jit(solution)/shard_map/ppermute | solution.py:342
  24.1 0.7 copy-start.7
  24.7 0.6 copy-start.9
  45.8 38.9 %all-to-all-start.2 = ((f32[32,32,128]{2,1,0:T(8,128)}), f32[32,32,128]{2,1,0:T(8,128)S(1)}, u32[]{:S(2)}, u32[]{:S(2)}) async-start(f32[32,32,128]{2,1,0:T(8,128)} %get-tuple-element.73), calls=%async_computation.2 | async-start | bytes 1048576 | tf_op jit(solution)/shard_map/all_to_all | solution.py:346
  54.3 30.4 %copy-start.8 = (f32[256,8]{1,0:T(8,128)S(1)}, f32[256,8]{1,0:T(8,128)}, u32[]{:S(2)}) copy-start(f32[256,8]{1,0:T(8,128)} %copy-done.7) | copy-start | bytes 24580
  54.3 13.1 %collective-permute-start.3 = (f32[4,2,16,128]{3,2,1,0:T(8,128)S(1)}, f32[4,2,16,128]{3,2,1,0:T(8,128)S(1)}, u32[]{:S(2)}, u32[]{:S(2)}) collective-permute-start(f32[4,2,16,128]{3,2,1,0:T(8,128)S(1)} %get-tuple-element.66.refs_4_), channel_id=1, source_target_pairs={{0,8},{8,16},{16,24},{24,32},{32,40},{40,48},{48,56},{56,0},{1,9},... | collective-permute-start | bytes 196616 | tf_op jit(solution)/shard_map/ppermute | solution.py:342
  55.6 12.1 %collective-permute-start.7 = (f32[4,2,16,128]{3,2,1,0:T(8,128)S(1)}, f32[4,2,16,128]{3,2,1,0:T(8,128)S(1)}, u32[]{:S(2)}, u32[]{:S(2)}) collective-permute-start(f32[4,2,16,128]{3,2,1,0:T(8,128)S(1)} %get-tuple-element.66.refs_4_), channel_id=1, source_target_pairs={{0,56},{8,0},{16,8},{24,16},{32,24},{40,32},{48,40},{56,48},{1,57}... | collective-permute-start | bytes 196616 | tf_op jit(solution)/shard_map/ppermute | solution.py:342
  67.3 4.6 %collective-permute-start.4 = (f32[4,2,16,128]{3,2,1,0:T(8,128)S(1)}, f32[4,2,16,128]{3,2,1,0:T(8,128)S(1)}, u32[]{:S(2)}, u32[]{:S(2)}) collective-permute-start(f32[4,2,16,128]{3,2,1,0:T(8,128)S(1)} %collective-permute-done.3.refs_5_), channel_id=1, source_target_pairs={{0,8},{8,16},{16,24},{24,32},{32,40},{40,48},{48,56},{56,0},{1,9},... | collective-permute-start | bytes 196616 | tf_op jit(solution)/shard_map/ppermute | solution.py:342
  67.7 4.3 %collective-permute-start.8 = (f32[4,2,16,128]{3,2,1,0:T(8,128)S(1)}, f32[4,2,16,128]{3,2,1,0:T(8,128)S(1)}, u32[]{:S(2)}, u32[]{:S(2)}) collective-permute-start(f32[4,2,16,128]{3,2,1,0:T(8,128)S(1)} %collective-permute-done.7.refs_11_), channel_id=1, source_target_pairs={{0,56},{8,0},{16,8},{24,16},{32,24},{40,32},{48,40},{56,48},{1,57}... | collective-permute-start | bytes 196616 | tf_op jit(solution)/shard_map/ppermute | solution.py:342
  72.0 4.3 %collective-permute-start.5 = (f32[4,2,16,128]{3,2,1,0:T(8,128)S(1)}, f32[4,2,16,128]{3,2,1,0:T(8,128)S(1)}, u32[]{:S(2)}, u32[]{:S(2)}) collective-permute-start(f32[4,2,16,128]{3,2,1,0:T(8,128)S(1)} %collective-permute-done.4.refs_6_), channel_id=1, source_target_pairs={{0,8},{8,16},{16,24},{24,32},{32,40},{40,48},{48,56},{56,0},{1,9},... | collective-permute-start | bytes 196616 | tf_op jit(solution)/shard_map/ppermute | solution.py:342
  72.0 4.3 %collective-permute-start.9 = (f32[4,2,16,128]{3,2,1,0:T(8,128)S(1)}, f32[4,2,16,128]{3,2,1,0:T(8,128)S(1)}, u32[]{:S(2)}, u32[]{:S(2)}) collective-permute-start(f32[4,2,16,128]{3,2,1,0:T(8,128)S(1)} %collective-permute-done.8.refs_10_), channel_id=1, source_target_pairs={{0,56},{8,0},{16,8},{24,16},{32,24},{40,32},{48,40},{56,48},{1,57}... | collective-permute-start | bytes 196616 | tf_op jit(solution)/shard_map/ppermute | solution.py:342
  76.3 5.0 %collective-permute-start.6 = (f32[4,2,16,128]{3,2,1,0:T(8,128)S(1)}, f32[4,2,16,128]{3,2,1,0:T(8,128)S(1)}, u32[]{:S(2)}, u32[]{:S(2)}) collective-permute-start(f32[4,2,16,128]{3,2,1,0:T(8,128)S(1)} %collective-permute-done.5.refs_7_), channel_id=1, source_target_pairs={{0,8},{8,16},{16,24},{24,32},{32,40},{40,48},{48,56},{56,0},{1,9},... | collective-permute-start | bytes 196616 | tf_op jit(solution)/shard_map/ppermute | solution.py:342
  81.8 3.4 %collective-permute-start.10 = (f32[64,256]{1,0:T(8,128)S(1)}, f32[64,256]{1,0:T(8,128)S(1)}, u32[]{:S(2)}, u32[]{:S(2)}) collective-permute-start(f32[64,256]{1,0:T(8,128)S(1)} %get-tuple-element.68), channel_id=1, source_target_pairs={{0,192},{64,0},{128,64},{192,128},{1,193},{65,1},{129,65},{193,129... | collective-permute-start | bytes 196616 | tf_op jit(solution)/shard_map/ppermute | solution.py:342
  83.6 4.7 %collective-permute-start.11 = (f32[64,256]{1,0:T(8,128)S(1)}, f32[64,256]{1,0:T(8,128)S(1)}, u32[]{:S(2)}, u32[]{:S(2)}) collective-permute-start(f32[64,256]{1,0:T(8,128)S(1)} %get-tuple-element.69), channel_id=1, source_target_pairs={{0,128},{64,192},{128,0},{192,64},{1,129},{65,193},{129,1},{193,65... | collective-permute-start | bytes 196616 | tf_op jit(solution)/shard_map/ppermute | solution.py:342
  84.1 4.8 %copy-start.10 = (f32[64,8]{1,0:T(8,128)S(1)}, f32[64,8]{1,0:T(8,128)}, u32[]{:S(2)}) copy-start(f32[64,8]{1,0:T(8,128)} %copy-done.9) | copy-start | bytes 6148
  84.1 4.8 %collective-permute-start.12 = (f32[64,256]{1,0:T(8,128)S(1)}, f32[64,256]{1,0:T(8,128)S(1)}, u32[]{:S(2)}, u32[]{:S(2)}) collective-permute-start(f32[64,256]{1,0:T(8,128)S(1)} %get-tuple-element.70), channel_id=1, source_target_pairs={{0,64},{64,128},{128,192},{192,0},{1,65},{65,129},{129,193},{193,1... | collective-permute-start | bytes 196616 | tf_op jit(solution)/shard_map/ppermute | solution.py:342
  88.9 17.6 %copy-start.5 = (f32[1024]{0:T(1024)S(1)}, f32[1024]{0:T(1024)}, u32[]{:S(2)}) copy-start(f32[1024]{0:T(1024)} %param.17) | copy-start | bytes 12292

commit v5 on v4

--- a/solution.py
+++ b/solution.py
@@ -83,66 +83,77 @@
     return lax.dot_general(a, b, (((1,), (1,)), ((), ())), preferred_element_type=F32)
 
 
-def send_kernel(lens, here, key_ref, value_ref, logd_ref, out_ref, flag_ref, cum_ref):
+def send_kernel(lens, here, key_ref, value_ref, logd_ref, out_ref, flag_ref, keep_ref, tail_ref, scal_ref):
+    x = pl.program_id(0)
     first = here[0] * BLOCK
     ends = bounds(lens)
     front = entry_seg(first, ends)
     seg_last = seg_of(first + (BLOCK - 1), ends)
-    cum = cum_columns(logd_ref[...])
-    cum_ref[...] = cum
-    tok = lax.broadcasted_iota(jnp.int32, (BLOCK, HEADS), 0)
-    seg = seg_of(tok + first, ends)
-    last = cum[BLOCK - 1 : BLOCK, :]
-    keep = jnp.where(seg == seg_last, jnp.exp(last - cum), 0.0)
-    factors = [jnp.exp(last) * (seg_last == front).astype(F32)]
     found = jnp.int32(-1)
     spot = jnp.int32(0)
     crowded = jnp.int32(0)
     for p in range(LAST):
         at = ends[p] - 1 - first
-        inside = (at >= 0) & (at < BLOCK)
-        reached = cum_ref[pl.ds(jnp.clip(at, 0, BLOCK - 1), 1), :]
-        factors.append(jnp.exp(reached) * (inside & (front == p)).astype(F32))
         take = (at >= 0) & (at < BLOCK - 1) & (found < 0)
         found = jnp.where(take, p, found)
         spot = jnp.where(take, at, spot)
         if p:
             same = (ends[p] - 1) // BLOCK == (ends[p - 1] - 1) // BLOCK
             crowded = crowded | (same & (ends[p] % BLOCK != 0)).astype(jnp.int32)
-    flag_ref[0] = crowded
+
+    @pl.when(x == 0)
+    def _():
+        flag_ref[0] = crowded
+        cum = cum_columns(logd_ref[...])
+        tok = lax.broadcasted_iota(jnp.int32, (BLOCK, HEADS), 0)
+        seg = seg_of(tok + first, ends)
+        last = cum[BLOCK - 1 : BLOCK, :]
+        keep = jnp.where(seg == seg_last, jnp.exp(last - cum), 0.0)
+        tail_ref[0] = cum
+        factors = [jnp.exp(last) * (seg_last == front).astype(F32)]
+        for p in range(LAST):
+            at = ends[p] - 1 - first
+            inside = (at >= 0) & (at < BLOCK)
+            reached = tail_ref[0, pl.ds(jnp.clip(at, 0, BLOCK - 1), 1), :]
+            factors.append(jnp.exp(reached) * (inside & (front == p)).astype(F32))
+        reached = tail_ref[0, pl.ds(spot, 1), :]
+        taken = (tok <= spot) & (seg == found)
+        tail = jnp.where(taken, jnp.exp(jnp.where(taken, reached - cum, 0.0)), 0.0)
+        for k in range(NX):
+            keep_ref[k] = keep[:, k * PAIR : (k + 1) * PAIR]
+            tail_ref[k] = jnp.concatenate(
+                [tail[:, k * PAIR : (k + 1) * PAIR]] * (HEADS // PAIR), axis=1
+            )
+            scal_ref[k] = jnp.concatenate(
+                [
+                    jnp.broadcast_to(f[:, k * PAIR + j : k * PAIR + j + 1], (1, HDIM))
+                    for f in factors
+                    for j in range(PAIR)
+                ],
+                axis=0,
+            )
 
     def emit(factor, row):
-        for h in range(HEADS):
-            x, j = h // PAIR, h % PAIR
-            cols = slice(h * HDIM, (h + 1) * HDIM)
-            keyed = (key_ref[:, cols].astype(F32) * factor[:, h : h + 1]).astype(BF)
+        for j in range(PAIR):
+            cols = slice(j * HDIM, (j + 1) * HDIM)
+            keyed = (key_ref[:, cols].astype(F32) * factor[:, j : j + 1]).astype(BF)
             total = contract_rows(keyed, value_ref[:, cols])
             at = row + j * SLAB
             for z in range(NZ):
-                out_ref[x * NZ + z, at : at + SLAB, :] = total[z * SLAB : (z + 1) * SLAB, :]
-
-    emit(keep, 0)
-    for x in range(NX):
-        scal = jnp.concatenate(
-            [
-                jnp.broadcast_to(f[:, x * PAIR + j : x * PAIR + j + 1], (1, HDIM))
-                for f in factors
-                for j in range(PAIR)
-            ],
-            axis=0,
-        )
-        for z in range(NZ):
-            out_ref[x * NZ + z, S0:GIVE, :] = scal
+                out_ref[z, at : at + SLAB, :] = total[z * SLAB : (z + 1) * SLAB, :]
+
+    emit(keep_ref[x], 0)
+    scal = scal_ref[x]
+    for z in range(NZ):
+        out_ref[z, S0:GIVE, :] = scal
 
     @pl.when(found < 0)
     def _():
-        out_ref[:, PART:S0, :] = jnp.zeros((NDEV, PART, HDIM), F32)
+        out_ref[:, PART:S0, :] = jnp.zeros((NZ, PART, HDIM), F32)
 
     @pl.when(found >= 0)
     def _():
-        reached = cum_ref[pl.ds(spot, 1), :]
-        taken = (tok <= spot) & (seg == found)
-        emit(jnp.where(taken, jnp.exp(jnp.where(taken, reached - cum, 0.0)), 0.0), PART)
+        emit(tail_ref[x], PART)
 
 
 def query_kernel(here, rows, query_ref, *out_refs):
@@ -274,7 +285,23 @@
             ref[:, cols] = res[d * NROW : (d + 1) * NROW, :]
 
 
-def mixed_kernel(query_ref, back_ref, intra_ref, carried_ref, mixed_ref, sums_ref):
+def mixed_kernel(
+    here, query_ref, back_ref, intra_ref, carried_ref, o0, o1, o2, o3, local_ref, scarried_ref,
+    mixed_ref, dec_ref, send_ref, carry_ref,
+):
+    x = here[0] // NZ
+    for d, ref in enumerate((o0, o1, o2, o3)):
+        carry_ref[lax.rem(x + d, NX)] = ref[...]
+    acc = jnp.zeros((NROW, HDIM), F32)
+    for h in range(HEADS):
+        cols = slice(h * HDIM, (h + 1) * HDIM)
+        part = slice((h % PAIR) * HDIM, (h % PAIR + 1) * HDIM)
+        dec = local_ref[:, cols] + carry_ref[h // PAIR, :, part] * scarried_ref[:, h : h + 1]
+        dec_ref[:, cols] = dec
+        acc = acc + dec * dec
+    full = jnp.concatenate([acc, jnp.zeros((HDIM - NROW, HDIM), F32)], axis=0)
+    dflat = jnp.sum(full.T, axis=0, keepdims=True)
+
     acc = jnp.zeros((BLOCK, HDIM), F32)
     for h in range(HEADS):
         x, j = h // PAIR, h % PAIR
@@ -287,25 +314,7 @@
         mixed_ref[:, cols] = mixed
         acc = acc + mixed * mixed
     flat = jnp.sum(acc.T, axis=0, keepdims=True)
-    sums_ref[...] = jnp.concatenate(
-        [flat[:, :HDIM], flat[:, HDIM:], jnp.zeros((6, HDIM), F32)], axis=0
-    )
-
-
-def decode_kernel(here, o0, o1, o2, o3, local_ref, scarried_ref, sums_ref, dec_ref, send_ref, carry_ref):
-    x = here[0] // NZ
-    for d, ref in enumerate((o0, o1, o2, o3)):
-        carry_ref[lax.rem(x + d, NX)] = ref[...]
-    acc = jnp.zeros((NROW, HDIM), F32)
-    for h in range(HEADS):
-        cols = slice(h * HDIM, (h + 1) * HDIM)
-        part = slice((h % PAIR) * HDIM, (h % PAIR + 1) * HDIM)
-        dec = local_ref[:, cols] + carry_ref[h // PAIR, :, part] * scarried_ref[:, h : h + 1]
-        dec_ref[:, cols] = dec
-        acc = acc + dec * dec
-    full = jnp.concatenate([acc, jnp.zeros((HDIM - NROW, HDIM), F32)], axis=0)
-    flat = jnp.sum(full.T, axis=0, keepdims=True)
-    both = jnp.concatenate([sums_ref[0:2, :], flat, jnp.zeros((5, HDIM), F32)], axis=0)
+    both = jnp.concatenate([flat[:, :HDIM], flat[:, HDIM:], dflat, dflat], axis=0)
     for k in range(HEADS):
         send_ref[k] = both
 
@@ -389,12 +398,24 @@
     n = STEPS * ROWS_DEV
 
     logd = log_decay.T
+    pair = PAIR * HDIM
     give, crowded = pl.pallas_call(
         send_kernel,
         out_shape=(shape(NDEV, GIVE, HDIM), shape(1, dtype=jnp.int32)),
-        in_specs=[SMEM] * 2 + [VMEM] * 3,
-        out_specs=(VMEM, SMEM),
-        scratch_shapes=[pltpu.VMEM((BLOCK, HEADS), F32)],
+        grid=(NX,),
+        in_specs=[
+            SMEM,
+            SMEM,
+            pl.BlockSpec((BLOCK, pair), lambda i: (0, i)),
+            pl.BlockSpec((BLOCK, pair), lambda i: (0, i)),
+            pl.BlockSpec((HEADS, BLOCK), lambda i: (0, 0)),
+        ],
+        out_specs=(pl.BlockSpec((NZ, GIVE, HDIM), lambda i: (i, 0, 0)), SMEM),
+        scratch_shapes=[
+            pltpu.VMEM((NX, BLOCK, PAIR), F32),
+            pltpu.VMEM((NX, BLOCK, HEADS), F32),
+            pltpu.VMEM((NX, PAIR * PROMPTS, HDIM), F32),
+        ],
         compiler_params=params(),
         cost_estimate=cost(3),
         name="send",
@@ -442,13 +463,13 @@
         cost_estimate=cost(2),
         name="scan",
     )(prompt_lengths, given, extra)
-    back = exchange(entry, SEQ)
-
     slabs = [own] * NZ
     for d in range(1, NZ // 2 + 1):
         slabs[d] = shift(slabs[d - 1], "seq_1", NZ, 1)
         if d < NZ // 2:
             slabs[NZ - d] = shift(slabs[(NZ - d + 1) % NZ], "seq_1", NZ, -1)
+    entry, slabs = lax.optimization_barrier((entry, slabs))
+    back = exchange(entry, SEQ)
     products = pl.pallas_call(
         project_kernel,
         out_shape=(shape(NROW, PAIR * HDIM),) * NX,
@@ -461,25 +482,16 @@
     )(here, *queries, *slabs)
     products = [products[0]] + [shift(products[d], "seq_0", NX, -d) for d in range(1, NX)]
 
-    mixed, sums = pl.pallas_call(
+    mixed, dec, sums_send = pl.pallas_call(
         mixed_kernel,
-        out_shape=(shape(BLOCK, width), shape(8, HDIM)),
-        in_specs=[VMEM] * 4,
-        out_specs=(VMEM,) * 2,
+        out_shape=(shape(BLOCK, width), shape(n, width), shape(HEADS, 4, HDIM)),
+        in_specs=[SMEM] + [VMEM] * 10,
+        out_specs=(VMEM,) * 3,
+        scratch_shapes=[pltpu.VMEM((NX, NROW, PAIR * HDIM), F32)],
         compiler_params=params(),
         cost_estimate=cost(2),
         name="mixed",
-    )(query_in, back, intra, carried)
-    dec, sums_send = pl.pallas_call(
-        decode_kernel,
-        out_shape=(shape(n, width), shape(HEADS, 8, HDIM)),
-        in_specs=[SMEM] + [VMEM] * 7,
-        out_specs=(VMEM,) * 2,
-        scratch_shapes=[pltpu.VMEM((NX, NROW, PAIR * HDIM), F32)],
-        compiler_params=params(),
-        cost_estimate=cost(1),
-        name="decode",
-    )(here, *products, local_dec, scarried, sums)
+    )(here, query_in, back, intra, carried, *products, local_dec, scarried)
     sums_all = exchange(sums_send, "head")
 
     return pl.pallas_call(

time: 108 us -> 104 us (0.963)
  waiting for transfers between devices: 41.3 us -> 34.5 us
  Pallas kernels: 9.99 us -> 11.5 us
  starting transfers between devices: 36.1 us -> 37.3 us
    ppermute x13, waiting for transfers between devices: 26.6 us -> 17.5 us  [shift(): return lax.ppermute(x, axis, [(i, (i + d) % size) for i in range(size)])]
    ppermute x13, starting transfers between devices: 15.6 us -> 18.1 us  [shift(): return lax.ppermute(x, axis, [(i, (i + d) % size) for i in range(size)])]
    all_to_all x2, waiting for transfers between devices: 14.7 us -> 17 us  [exchange(): return lax.all_to_all(x, axis, split_axis=0, concat_axis=0, tiled=True)]
    pallas_call x1, Pallas kernels: 3.48 us -> 5.08 us  [local(): pl.pallas_call(send_kernel, out_shape=(shape(NDEV, GIVE, HDIM), shape(1,...]
    all_to_all x2, starting transfers between devices: 20.5 us -> 19.1 us  [exchange(): return lax.all_to_all(x, axis, split_axis=0, concat_axis=0, tiled=True)]
  transfers between devices with their start and end apart: 15 -> 15, of which waited for: 9 -> 11; matrix products, arithmetic and copies ran while one was open for 0% -> 0% of each run, Pallas kernels for 4% -> 3%
where the time goes in v5:
time: 104 us; the launch traced here: 103 us
  starting transfers between devices  37.3 us (36%)
  waiting for transfers between devices  34.5 us (33%)
  blocking collectives  16.9 us (16%)
  Pallas kernels  11.5 us (11%)
  between operations  1.5 us (1%)
  local copies, waits for them, and re-layouts  1.34 us (1%)
    all_to_all x2, starting transfers between devices, exchange(): return lax.all_to_all(x, axis, split_axis=0, concat_axis=0, tiled=True)  19.1 us
    ppermute x13, starting transfers between devices, shift(): return lax.ppermute(x, axis, [(i, (i + d) % size) for i in range(size)])  18.1 us
    ppermute x13, waiting for transfers between devices, shift(): return lax.ppermute(x, axis, [(i, (i + d) % size) for i in range(size)])  17.5 us
    all_to_all x2, waiting for transfers between devices, exchange(): return lax.all_to_all(x, axis, split_axis=0, concat_axis=0, tiled=True)  17 us
    all_to_all x1, blocking collectives, exchange(): return lax.all_to_all(x, axis, split_axis=0, concat_axis=0, tiled=True)  16.9 us
    pallas_call x1, Pallas kernels, local(): pl.pallas_call(send_kernel, out_shape=(shape(NDEV, GIVE, HDIM), shape(1,...  5.08 us
    pallas_call x1, Pallas kernels, local(): pl.pallas_call(intra_kernel, out_shape=(shape(BLOCK, width), shape(BLOCK,...  2.26 us
  transfers between devices with their start and end apart: 15, of which 11 were waited for; matrix products, arithmetic and copies ran while one was open for 0% of the time, Pallas kernels for 3%

profile of v5, /device:TPU:1, one launch (start us, length us, event | category | flops | bytes accessed | tf_op | source)
XLA Modules:
  0.0 103.1 jit_solution(8837708596865962196)
XLA Ops:
  0.6 5.1 %send.1 = (f32[32,72,128]{2,1,0:T(8,128)}, s32[1]{0:T(128)}) custom-call(s32[4]{0:T(128)} %lens.5, s32[1]{0:T(128)} %bitcast.20.here, bf16[256,1024]{1,0:T(8,128)(2,1)} %key_ref.3, bf16[256,1024]{1,0:T(8,128)(2,1)} %value_ref.3, f32[8,256]{1,0:T(8,128)} %bitcast.55), custom_call_target="tpu_custom_call" | custom-call | flops 3000000000 | bytes 9000000 | tf_op jit(solution)/shard_map/send/pallas_call | solution.py:402
  5.7 12.0 %all-to-all-start.1 = ((f32[32,72,128]{2,1,0:T(8,128)}), f32[32,72,128]{2,1,0:T(8,128)S(1)}, u32[]{:S(2)}, u32[]{:S(2)}) async-start(f32[32,72,128]{2,1,0:T(8,128)} %get-tuple-element.58), calls=%async_computation.1 | async-start | bytes 2359296 | tf_op jit(solution)/shard_map/all_to_all | solution.py:355
  17.7 0.0 copy-done.1
  17.8 0.0 copy-done.6
  17.8 0.0 copy-start
  17.8 0.0 copy-start.2
  17.8 0.0 copy-start.3
  17.8 0.0 copy-start.4
  17.8 0.0 copy-start.12
  17.8 0.0 copy-start.14
  17.8 0.0 copy-start.15
  17.8 0.0 copy-start.16
  17.9 0.6 query.1
  18.5 1.3 %collective-permute-start = (f32[64,384]{1,0:T(8,128)S(1)}, f32[64,384]{1,0:T(8,128)S(1)}, u32[]{:S(2)}, u32[]{:S(2)}) collective-permute-start(f32[64,384]{1,0:T(8,128)S(1)} %get-tuple-element.64), channel_id=1, source_target_pairs={{0,64},{64,128},{128,192},{192,0},{1,65},{65,129},{129,193},{193,1... | collective-permute-start | bytes 294920 | tf_op jit(solution)/shard_map/ppermute | solution.py:351
  19.8 2.4 %collective-permute-start.1 = (f32[64,384]{1,0:T(8,128)S(1)}, f32[64,384]{1,0:T(8,128)S(1)}, u32[]{:S(2)}, u32[]{:S(2)}) collective-permute-start(f32[64,384]{1,0:T(8,128)S(1)} %get-tuple-element.65), channel_id=1, source_target_pairs={{0,128},{64,192},{128,0},{192,64},{1,129},{65,193},{129,1},{193,65... | collective-permute-start | bytes 294920 | tf_op jit(solution)/shard_map/ppermute | solution.py:351
  22.2 1.1 %collective-permute-start.2 = (f32[64,384]{1,0:T(8,128)S(1)}, f32[64,384]{1,0:T(8,128)S(1)}, u32[]{:S(2)}, u32[]{:S(2)}) collective-permute-start(f32[64,384]{1,0:T(8,128)S(1)} %get-tuple-element.66), channel_id=1, source_target_pairs={{0,192},{64,0},{128,64},{192,128},{1,193},{65,1},{129,65},{193,129... | collective-permute-start | bytes 294920 | tf_op jit(solution)/shard_map/ppermute | solution.py:351
  23.3 0.0 copy-done
  23.3 0.0 copy-done.2
  23.4 0.0 copy-done.3
  23.4 0.0 copy-done.4
  23.4 0.0 copy-done.12
  23.4 0.0 copy-done.14
  23.4 0.0 copy-done.15
  23.4 0.0 copy-done.16
  23.4 2.3 %intra.1 = (f32[256,1024]{1,0:T(8,128)S(1)}, f32[256,8]{1,0:T(8,128)S(1)}, f32[64,1024]{1,0:T(8,128)S(1)}, f32[64,8]{1,0:T(8,128)S(1)}) custom-call(s32[4]{0:T(128)S(1)} %copy-done.16, s32[1]{0:T(128)} %bitcast.20.here, bf16[256,1024]{1,0:T(8,128)(2,1)S(1)} %copy-done, bf16[256,1024]{1,0:T(8,128)(2,1)S(1)} %copy-done.14, bf16[256,1024]{1,0:T(8,128)(2,1)S(1)} %copy-done.12, ...), custom_call_target="tpu_custom_call" | custom-call | flops 6000000000 | bytes 18000000 | tf_op jit(solution)/shard_map/intra/pallas_call | solution.py:436
  25.7 0.0 copy-start.7
  25.7 0.7 copy-done.7
  26.3 0.6 copy-done.9
  26.9 0.0 collective-permute-done.refs_1_
  26.9 3.6 %collective-permute-done.1.refs_2_ = f32[64,384]{1,0:T(8,128)S(1)} collective-permute-done((f32[64,384]{1,0:T(8,128)S(1)}, f32[64,384]{1,0:T(8,128)S(1)}, u32[]{:S(2)}, u32[]{:S(2)}) %collective-permute-start.1) | collective-permute-done | bytes 98336 | tf_op jit(solution)/shard_map/ppermute | solution.py:351
  30.6 0.0 collective-permute-done.2.refs_3_
  30.6 14.7 %all-to-all-done.1.give_ref = f32[32,72,128]{2,1,0:T(8,128)S(1)} async-done(((f32[32,72,128]{2,1,0:T(8,128)}), f32[32,72,128]{2,1,0:T(8,128)S(1)}, u32[]{:S(2)}, u32[]{:S(2)}) %all-to-all-start.1) | async-done | bytes 1179680 | tf_op jit(solution)/shard_map/all_to_all | solution.py:355
  46.0 1.4 %scan.1 = (f32[32,32,128]{2,1,0:T(8,128)}, f32[4,2,16,128]{3,2,1,0:T(8,128)S(1)}) custom-call(s32[4]{0:T(128)S(1)} %copy-done.16, f32[32,72,128]{2,1,0:T(8,128)S(1)} %all-to-all-done.1.give_ref, f32[3,32,128]{2,1,0:T(8,128)S(1)} %get-tuple-element.127.extra_ref), custom_call_target="tpu_custom_call" | custom-call | flops 2000000000 | bytes 6000000 | tf_op jit(solution)/shard_map/scan/pallas_call | solution.py:457
  47.4 3.6 %collective-permute-start.3 = (f32[4,2,16,128]{3,2,1,0:T(8,128)S(1)}, f32[4,2,16,128]{3,2,1,0:T(8,128)S(1)}, u32[]{:S(2)}, u32[]{:S(2)}) collective-permute-start(f32[4,2,16,128]{3,2,1,0:T(8,128)S(1)} %get-tuple-element.79.refs_4_), channel_id=1, source_target_pairs={{0,8},{8,16},{16,24},{24,32},{32,40},{40,48},{48,56},{56,0},{1,9},... | collective-permute-start | bytes 196616 | tf_op jit(solution)/shard_map/ppermute | solution.py:351
  51.0 0.0 collective-permute-start.7
  51.0 1.3 %collective-permute-done.3.refs_5_ = f32[4,2,16,128]{3,2,1,0:T(8,128)S(1)} collective-permute-done((f32[4,2,16,128]{3,2,1,0:T(8,128)S(1)}, f32[4,2,16,128]{3,2,1,0:T(8,128)S(1)}, u32[]{:S(2)}, u32[]{:S(2)}) %collective-permute-start.3) | collective-permute-done | bytes 65568 | tf_op jit(solution)/shard_map/ppermute | solution.py:351
  52.3 1.8 %collective-permute-start.4 = (f32[4,2,16,128]{3,2,1,0:T(8,128)S(1)}, f32[4,2,16,128]{3,2,1,0:T(8,128)S(1)}, u32[]{:S(2)}, u32[]{:S(2)}) collective-permute-start(f32[4,2,16,128]{3,2,1,0:T(8,128)S(1)} %collective-permute-done.3.refs_5_), channel_id=1, source_target_pairs={{0,8},{8,16},{16,24},{24,32},{32,40},{40,48},{48,56},{56,0},{1,9},... | collective-permute-start | bytes 196616 | tf_op jit(solution)/shard_map/ppermute | solution.py:351
  54.1 0.0 collective-permute-done.7.refs_11_
  54.1 1.2 %collective-permute-start.8 = (f32[4,2,16,128]{3,2,1,0:T(8,128)S(1)}, f32[4,2,16,128]{3,2,1,0:T(8,128)S(1)}, u32[]{:S(2)}, u32[]{:S(2)}) collective-permute-start(f32[4,2,16,128]{3,2,1,0:T(8,128)S(1)} %collective-permute-done.7.refs_11_), channel_id=1, source_target_pairs={{0,56},{8,0},{16,8},{24,16},{32,24},{40,32},{48,40},{56,48},{1,57}... | collective-permute-start | bytes 196616 | tf_op jit(solution)/shard_map/ppermute | solution.py:351
  55.3 2.0 %collective-permute-done.4.refs_6_ = f32[4,2,16,128]{3,2,1,0:T(8,128)S(1)} collective-permute-done((f32[4,2,16,128]{3,2,1,0:T(8,128)S(1)}, f32[4,2,16,128]{3,2,1,0:T(8,128)S(1)}, u32[]{:S(2)}, u32[]{:S(2)}) %collective-permute-start.4) | collective-permute-done | bytes 65568 | tf_op jit(solution)/shard_map/ppermute | solution.py:351
  57.3 0.7 collective-permute-start.5
  58.0 0.1 collective-permute-done.8.refs_10_
  58.0 2.3 %collective-permute-start.9 = (f32[4,2,16,128]{3,2,1,0:T(8,128)S(1)}, f32[4,2,16,128]{3,2,1,0:T(8,128)S(1)}, u32[]{:S(2)}, u32[]{:S(2)}) collective-permute-start(f32[4,2,16,128]{3,2,1,0:T(8,128)S(1)} %collective-permute-done.8.refs_10_), channel_id=1, source_target_pairs={{0,56},{8,0},{16,8},{24,16},{32,24},{40,32},{48,40},{56,48},{1,57}... | collective-permute-start | bytes 196616 | tf_op jit(solution)/shard_map/ppermute | solution.py:351
  60.4 1.3 %collective-permute-done.5.refs_7_ = f32[4,2,16,128]{3,2,1,0:T(8,128)S(1)} collective-permute-done((f32[4,2,16,128]{3,2,1,0:T(8,128)S(1)}, f32[4,2,16,128]{3,2,1,0:T(8,128)S(1)}, u32[]{:S(2)}, u32[]{:S(2)}) %collective-permute-start.5) | collective-permute-done | bytes 65568 | tf_op jit(solution)/shard_map/ppermute | solution.py:351
  61.6 0.0 collective-permute-start.6
  61.6 0.0 collective-permute-done.9.refs_9_
  61.7 4.3 %collective-permute-done.6.refs_8_ = f32[4,2,16,128]{3,2,1,0:T(8,128)S(1)} collective-permute-done((f32[4,2,16,128]{3,2,1,0:T(8,128)S(1)}, f32[4,2,16,128]{3,2,1,0:T(8,128)S(1)}, u32[]{:S(2)}, u32[]{:S(2)}) %collective-permute-start.6) | collective-permute-done | bytes 65568 | tf_op jit(solution)/shard_map/ppermute | solution.py:351
  66.0 7.1 %all-to-all-start.2 = ((f32[32,32,128]{2,1,0:T(8,128)}), f32[32,32,128]{2,1,0:T(8,128)S(1)}, u32[]{:S(2)}, u32[]{:S(2)}) async-start(f32[32,32,128]{2,1,0:T(8,128)} %get-tuple-element.72), calls=%async_computation.2 | async-start | bytes 1048576 | tf_op jit(solution)/shard_map/all_to_all | solution.py:355
  73.1 0.0 copy-start.8
  73.1 0.0 copy-start.10
  73.1 0.5 project.1
  73.6 2.6 %collective-permute-start.10 = (f32[64,256]{1,0:T(8,128)S(1)}, f32[64,256]{1,0:T(8,128)S(1)}, u32[]{:S(2)}, u32[]{:S(2)}) collective-permute-start(f32[64,256]{1,0:T(8,128)S(1)} %get-tuple-element.88), channel_id=1, source_target_pairs={{0,192},{64,0},{128,64},{192,128},{1,193},{65,1},{129,65},{193,129... | collective-permute-start | bytes 196616 | tf_op jit(solution)/shard_map/ppermute | solution.py:351
  76.2 0.5 collective-permute-start.11
  76.7 0.6 collective-permute-start.12
  77.3 0.6 collective-permute-done.10.o1
  77.9 3.5 %collective-permute-done.11.o2 = f32[64,256]{1,0:T(8,128)S(1)} collective-permute-done((f32[64,256]{1,0:T(8,128)S(1)}, f32[64,256]{1,0:T(8,128)S(1)}, u32[]{:S(2)}, u32[]{:S(2)}) %collective-permute-start.11) | collective-permute-done | bytes 65568 | tf_op jit(solution)/shard_map/ppermute | solution.py:351
  81.5 0.7 collective-permute-done.12.o3
  82.2 2.3 %all-to-all-done.2.back_ref = f32[32,32,128]{2,1,0:T(8,128)S(1)} async-done(((f32[32,32,128]{2,1,0:T(8,128)}), f32[32,32,128]{2,1,0:T(8,128)S(1)}, u32[]{:S(2)}, u32[]{:S(2)}) %all-to-all-start.2) | async-done | bytes 524320 | tf_op jit(solution)/shard_map/all_to_all | solution.py:355
  84.5 0.0 copy-done.8
  84.5 0.0 copy-done.10
  84.5 0.6 mixed.1
  85.1 16.9 %all_to_all.19.sums_ref = f32[8,4,128]{2,1,0:T(4,128)S(1)} all-to-all(f32[8,4,128]{2,1,0:T(4,128)S(1)} %get-tuple-element.93), channel_id=1, replica_groups=mesh['seq_0'=4,'seq_1'=8,'head'=8] {'head'}, dimensions={0} | all-to-all | bytes 32768 | tf_op jit(solution)/shard_map/all_to_all | solution.py:355
  102.0 0.0 copy-done.5
  102.0 1.1 %final.1 = (bf16[256,1024]{1,0:T(8,128)(2,1)}, bf16[4,16,1024]{2,1,0:T(8,128)(2,1)}) custom-call(f32[8,4,128]{2,1,0:T(4,128)S(1)} %all_to_all.19.sums_ref, f32[256,1024]{1,0:T(8,128)S(1)} %get-tuple-element.94.mixed_ref, f32[64,1024]{1,0:T(8,128)S(1)} %get-tuple-element.95.dec_ref, f32[1,1024]{1,0:T(1,128)S(1)} %bitcast.47), custom_call_target="tpu_custom_call" | custom-call | flops 2000000000 | bytes 6000000 | tf_op jit(solution)/shard_map/final/pallas_call | solution.py:497
  (6 shorter events, 0.0 us)
Async XLA Ops:
  5.7 12.0 %copy-start.1 = (bf16[4,16,1024]{2,1,0:T(8,128)(2,1)S(1)}, bf16[4,16,1024]{2,1,0:T(8,128)(2,1)}, u32[]{:S(2)}) copy-start(bf16[4,16,1024]{2,1,0:T(8,128)(2,1)} %query_ref.4) | copy-start | bytes 393220
  5.7 12.0 %copy-start.6 = (s32[16]{0:T(128)S(1)}, s32[16]{0:T(128)}, u32[]{:S(2)}) copy-start(s32[16]{0:T(128)} %rows.1) | copy-start | bytes 196
  5.7 39.5 %all-to-all-start.1 = ((f32[32,72,128]{2,1,0:T(8,128)}), f32[32,72,128]{2,1,0:T(8,128)S(1)}, u32[]{:S(2)}, u32[]{:S(2)}) async-start(f32[32,72,128]{2,1,0:T(8,128)} %get-tuple-element.58), calls=%async_computation.1 | async-start | bytes 2359296 | tf_op jit(solution)/shard_map/all_to_all | solution.py:355
  17.8 5.6 %copy-start = (bf16[256,1024]{1,0:T(8,128)(2,1)S(1)}, bf16[256,1024]{1,0:T(8,128)(2,1)}, u32[]{:S(2)}) copy-start(bf16[256,1024]{1,0:T(8,128)(2,1)} %query_ref.5) | copy-start | bytes 1572868
  17.8 5.6 %copy-start.2 = (bf16[4,16,1024]{2,1,0:T(8,128)(2,1)S(1)}, bf16[4,16,1024]{2,1,0:T(8,128)(2,1)}, u32[]{:S(2)}) copy-start(bf16[4,16,1024]{2,1,0:T(8,128)(2,1)} %sk_ref.1) | copy-start | bytes 393220
  17.8 5.6 %copy-start.3 = (bf16[4,16,1024]{2,1,0:T(8,128)(2,1)S(1)}, bf16[4,16,1024]{2,1,0:T(8,128)(2,1)}, u32[]{:S(2)}) copy-start(bf16[4,16,1024]{2,1,0:T(8,128)(2,1)} %sv_ref.1) | copy-start | bytes 393220
  17.8 5.6 %copy-start.4 = (f32[4,16,8]{1,2,0:T(8,128)S(1)}, f32[4,16,8]{1,2,0:T(8,128)}, u32[]{:S(2)}) copy-start(f32[4,16,8]{1,2,0:T(8,128)} %param.22) | copy-start | bytes 6148
  17.8 5.5 %copy-start.12 = (bf16[256,1024]{1,0:T(8,128)(2,1)S(1)}, bf16[256,1024]{1,0:T(8,128)(2,1)}, u32[]{:S(2)}) copy-start(bf16[256,1024]{1,0:T(8,128)(2,1)} %value_ref.3) | copy-start | bytes 1572868
  17.8 5.5 %copy-start.14 = (bf16[256,1024]{1,0:T(8,128)(2,1)S(1)}, bf16[256,1024]{1,0:T(8,128)(2,1)}, u32[]{:S(2)}) copy-start(bf16[256,1024]{1,0:T(8,128)(2,1)} %key_ref.3) | copy-start | bytes 1572868
  17.8 5.5 %copy-start.15 = (f32[256,8]{0,1:T(8,128)S(1)}, f32[256,8]{0,1:T(8,128)}, u32[]{:S(2)}) copy-start(f32[256,8]{0,1:T(8,128)} %param.16) | copy-start | bytes 24580
  17.8 5.5 %copy-start.16 = (s32[4]{0:T(128)S(1)}, s32[4]{0:T(128)}, u32[]{:S(2)}) copy-start(s32[4]{0:T(128)} %lens.5) | copy-start | bytes 52
  18.5 8.5 %collective-permute-start = (f32[64,384]{1,0:T(8,128)S(1)}, f32[64,384]{1,0:T(8,128)S(1)}, u32[]{:S(2)}, u32[]{:S(2)}) collective-permute-start(f32[64,384]{1,0:T(8,128)S(1)} %get-tuple-element.64), channel_id=1, source_target_pairs={{0,64},{64,128},{128,192},{192,0},{1,65},{65,129},{129,193},{193,1... | collective-permute-start | bytes 294920 | tf_op jit(solution)/shard_map/ppermute | solution.py:351
  19.8 10.8 %collective-permute-start.1 = (f32[64,384]{1,0:T(8,128)S(1)}, f32[64,384]{1,0:T(8,128)S(1)}, u32[]{:S(2)}, u32[]{:S(2)}) collective-permute-start(f32[64,384]{1,0:T(8,128)S(1)} %get-tuple-element.65), channel_id=1, source_target_pairs={{0,128},{64,192},{128,0},{192,64},{1,129},{65,193},{129,1},{193,65... | collective-permute-start | bytes 294920 | tf_op jit(solution)/shard_map/ppermute | solution.py:351
  22.2 8.4 %collective-permute-start.2 = (f32[64,384]{1,0:T(8,128)S(1)}, f32[64,384]{1,0:T(8,128)S(1)}, u32[]{:S(2)}, u32[]{:S(2)}) collective-permute-start(f32[64,384]{1,0:T(8,128)S(1)} %get-tuple-element.66), channel_id=1, source_target_pairs={{0,192},{64,0},{128,64},{192,128},{1,193},{65,1},{129,65},{193,129... | collective-permute-start | bytes 294920 | tf_op jit(solution)/shard_map/ppermute | solution.py:351
  25.7 0.7 copy-start.7
  26.3 0.6 copy-start.9
  47.4 4.9 %collective-permute-start.3 = (f32[4,2,16,128]{3,2,1,0:T(8,128)S(1)}, f32[4,2,16,128]{3,2,1,0:T(8,128)S(1)}, u32[]{:S(2)}, u32[]{:S(2)}) collective-permute-start(f32[4,2,16,128]{3,2,1,0:T(8,128)S(1)} %get-tuple-element.79.refs_4_), channel_id=1, source_target_pairs={{0,8},{8,16},{16,24},{24,32},{32,40},{40,48},{48,56},{56,0},{1,9},... | collective-permute-start | bytes 196616 | tf_op jit(solution)/shard_map/ppermute | solution.py:351
  51.0 3.1 %collective-permute-start.7 = (f32[4,2,16,128]{3,2,1,0:T(8,128)S(1)}, f32[4,2,16,128]{3,2,1,0:T(8,128)S(1)}, u32[]{:S(2)}, u32[]{:S(2)}) collective-permute-start(f32[4,2,16,128]{3,2,1,0:T(8,128)S(1)} %get-tuple-element.79.refs_4_), channel_id=1, source_target_pairs={{0,56},{8,0},{16,8},{24,16},{32,24},{40,32},{48,40},{56,48},{1,57}... | collective-permute-start | bytes 196616 | tf_op jit(solution)/shard_map/ppermute | solution.py:351
  52.3 5.0 %collective-permute-start.4 = (f32[4,2,16,128]{3,2,1,0:T(8,128)S(1)}, f32[4,2,16,128]{3,2,1,0:T(8,128)S(1)}, u32[]{:S(2)}, u32[]{:S(2)}) collective-permute-start(f32[4,2,16,128]{3,2,1,0:T(8,128)S(1)} %collective-permute-done.3.refs_5_), channel_id=1, source_target_pairs={{0,8},{8,16},{16,24},{24,32},{32,40},{40,48},{48,56},{56,0},{1,9},... | collective-permute-start | bytes 196616 | tf_op jit(solution)/shard_map/ppermute | solution.py:351
  54.1 3.9 %collective-permute-start.8 = (f32[4,2,16,128]{3,2,1,0:T(8,128)S(1)}, f32[4,2,16,128]{3,2,1,0:T(8,128)S(1)}, u32[]{:S(2)}, u32[]{:S(2)}) collective-permute-start(f32[4,2,16,128]{3,2,1,0:T(8,128)S(1)} %collective-permute-done.7.refs_11_), channel_id=1, source_target_pairs={{0,56},{8,0},{16,8},{24,16},{32,24},{40,32},{48,40},{56,48},{1,57}... | collective-permute-start | bytes 196616 | tf_op jit(solution)/shard_map/ppermute | solution.py:351
  57.3 4.3 %collective-permute-start.5 = (f32[4,2,16,128]{3,2,1,0:T(8,128)S(1)}, f32[4,2,16,128]{3,2,1,0:T(8,128)S(1)}, u32[]{:S(2)}, u32[]{:S(2)}) collective-permute-start(f32[4,2,16,128]{3,2,1,0:T(8,128)S(1)} %collective-permute-done.4.refs_6_), channel_id=1, source_target_pairs={{0,8},{8,16},{16,24},{24,32},{32,40},{40,48},{48,56},{56,0},{1,9},... | collective-permute-start | bytes 196616 | tf_op jit(solution)/shard_map/ppermute | solution.py:351
  58.0 3.7 %collective-permute-start.9 = (f32[4,2,16,128]{3,2,1,0:T(8,128)S(1)}, f32[4,2,16,128]{3,2,1,0:T(8,128)S(1)}, u32[]{:S(2)}, u32[]{:S(2)}) collective-permute-start(f32[4,2,16,128]{3,2,1,0:T(8,128)S(1)} %collective-permute-done.8.refs_10_), channel_id=1, source_target_pairs={{0,56},{8,0},{16,8},{24,16},{32,24},{40,32},{48,40},{56,48},{1,57}... | collective-permute-start | bytes 196616 | tf_op jit(solution)/shard_map/ppermute | solution.py:351
  61.6 4.3 %collective-permute-start.6 = (f32[4,2,16,128]{3,2,1,0:T(8,128)S(1)}, f32[4,2,16,128]{3,2,1,0:T(8,128)S(1)}, u32[]{:S(2)}, u32[]{:S(2)}) collective-permute-start(f32[4,2,16,128]{3,2,1,0:T(8,128)S(1)} %collective-permute-done.5.refs_7_), channel_id=1, source_target_pairs={{0,8},{8,16},{16,24},{24,32},{32,40},{40,48},{48,56},{56,0},{1,9},... | collective-permute-start | bytes 196616 | tf_op jit(solution)/shard_map/ppermute | solution.py:351
  66.0 18.5 %all-to-all-start.2 = ((f32[32,32,128]{2,1,0:T(8,128)}), f32[32,32,128]{2,1,0:T(8,128)S(1)}, u32[]{:S(2)}, u32[]{:S(2)}) async-start(f32[32,32,128]{2,1,0:T(8,128)} %get-tuple-element.72), calls=%async_computation.2 | async-start | bytes 1048576 | tf_op jit(solution)/shard_map/all_to_all | solution.py:355
  73.1 11.4 %copy-start.8 = (f32[256,8]{1,0:T(8,128)S(1)}, f32[256,8]{1,0:T(8,128)}, u32[]{:S(2)}) copy-start(f32[256,8]{1,0:T(8,128)} %copy-done.7) | copy-start | bytes 24580
  73.1 11.4 %copy-start.10 = (f32[64,8]{1,0:T(8,128)S(1)}, f32[64,8]{1,0:T(8,128)}, u32[]{:S(2)}) copy-start(f32[64,8]{1,0:T(8,128)} %copy-done.9) | copy-start | bytes 6148
  73.6 4.3 %collective-permute-start.10 = (f32[64,256]{1,0:T(8,128)S(1)}, f32[64,256]{1,0:T(8,128)S(1)}, u32[]{:S(2)}, u32[]{:S(2)}) collective-permute-start(f32[64,256]{1,0:T(8,128)S(1)} %get-tuple-element.88), channel_id=1, source_target_pairs={{0,192},{64,0},{128,64},{192,128},{1,193},{65,1},{129,65},{193,129... | collective-permute-start | bytes 196616 | tf_op jit(solution)/shard_map/ppermute | solution.py:351
  76.2 5.3 %collective-permute-start.11 = (f32[64,256]{1,0:T(8,128)S(1)}, f32[64,256]{1,0:T(8,128)S(1)}, u32[]{:S(2)}, u32[]{:S(2)}) collective-permute-start(f32[64,256]{1,0:T(8,128)S(1)} %get-tuple-element.89), channel_id=1, source_target_pairs={{0,128},{64,192},{128,0},{192,64},{1,129},{65,193},{129,1},{193,65... | collective-permute-start | bytes 196616 | tf_op jit(solution)/shard_map/ppermute | solution.py:351
  76.7 5.4 %collective-permute-start.12 = (f32[64,256]{1,0:T(8,128)S(1)}, f32[64,256]{1,0:T(8,128)S(1)}, u32[]{:S(2)}, u32[]{:S(2)}) collective-permute-start(f32[64,256]{1,0:T(8,128)S(1)} %get-tuple-element.90), channel_id=1, source_target_pairs={{0,64},{64,128},{128,192},{192,0},{1,65},{65,129},{129,193},{193,1... | collective-permute-start | bytes 196616 | tf_op jit(solution)/shard_map/ppermute | solution.py:351
  84.5 17.5 %copy-start.5 = (f32[1024]{0:T(1024)S(1)}, f32[1024]{0:T(1024)}, u32[]{:S(2)}) copy-start(f32[1024]{0:T(1024)} %param.17) | copy-start | bytes 12292

commit v6 on v4

--- a/solution.py
+++ b/solution.py
@@ -18,17 +18,18 @@
 
 NX = 4
 NZ = 8
-PAIR = 2
-HEADS = NX * PAIR
+HEADS = 8
 NDEV = NX * NZ
-SLAB = HDIM // NZ
+NQ = NZ // 2
+QUART = HDIM // NQ
 ROWS_DEV = 16
 NROW = STEPS * ROWS_DEV
 LAST = PROMPTS - 1
-
-PART = PAIR * SLAB
-S0 = 2 * PART
-GIVE = S0 + PAIR * PROMPTS
+MATES = [(dx, db) for db in range(2) for dx in range(NX)]
+
+T0 = QUART
+S0 = 2 * QUART
+GIVE = S0 + 8
 
 BF = jnp.bfloat16
 F32 = jnp.float32
@@ -81,6 +82,10 @@
 
 def contract_cols(a, b):
     return lax.dot_general(a, b, (((1,), (1,)), ((), ())), preferred_element_type=F32)
+
+
+def owner(head, quarter):
+    return (head // 2) * NZ + 2 * quarter + head % 2
 
 
 def send_kernel(lens, here, key_ref, value_ref, logd_ref, out_ref, flag_ref, cum_ref):
@@ -113,50 +118,48 @@
 
     def emit(factor, row):
         for h in range(HEADS):
-            x, j = h // PAIR, h % PAIR
             cols = slice(h * HDIM, (h + 1) * HDIM)
             keyed = (key_ref[:, cols].astype(F32) * factor[:, h : h + 1]).astype(BF)
             total = contract_rows(keyed, value_ref[:, cols])
-            at = row + j * SLAB
-            for z in range(NZ):
-                out_ref[x * NZ + z, at : at + SLAB, :] = total[z * SLAB : (z + 1) * SLAB, :]
+            for g in range(NQ):
+                out_ref[owner(h, g), row : row + QUART, :] = total[g * QUART : (g + 1) * QUART, :]
 
     emit(keep, 0)
-    for x in range(NX):
+    for h in range(HEADS):
         scal = jnp.concatenate(
-            [
-                jnp.broadcast_to(f[:, x * PAIR + j : x * PAIR + j + 1], (1, HDIM))
-                for f in factors
-                for j in range(PAIR)
-            ],
+            [jnp.broadcast_to(f[:, h : h + 1], (1, HDIM)) for f in factors]
+            + [jnp.zeros((8 - len(factors), HDIM), F32)],
             axis=0,
         )
-        for z in range(NZ):
-            out_ref[x * NZ + z, S0:GIVE, :] = scal
+        for g in range(NQ):
+            out_ref[owner(h, g), S0:GIVE, :] = scal
 
     @pl.when(found < 0)
     def _():
-        out_ref[:, PART:S0, :] = jnp.zeros((NDEV, PART, HDIM), F32)
+        out_ref[:, T0:S0, :] = jnp.zeros((NDEV, QUART, HDIM), F32)
 
     @pl.when(found >= 0)
     def _():
         reached = cum_ref[pl.ds(spot, 1), :]
         taken = (tok <= spot) & (seg == found)
-        emit(jnp.where(taken, jnp.exp(jnp.where(taken, reached - cum, 0.0)), 0.0), PART)
+        emit(jnp.where(taken, jnp.exp(jnp.where(taken, reached - cum, 0.0)), 0.0), T0)
+
+
+def mate_head(here, dx, db):
+    x = here[0] // NZ
+    parity = lax.rem(here[0], 2)
+    return 2 * lax.rem(x + dx, NX) + (1 - parity if db else parity)
 
 
 def query_kernel(here, rows, query_ref, *out_refs):
-    x = here[0] // NZ
     r = lax.broadcasted_iota(jnp.int32, (NROW, HDIM), 0) % ROWS_DEV
     ids = jnp.zeros((NROW, HDIM), F32)
     for k in range(ROWS_DEV):
         ids = jnp.where(r == k, rows[k].astype(F32), ids)
-    for d, out_ref in enumerate(out_refs):
-        pair = lax.rem(x + d, NX)
-        cols = pl.ds(pl.multiple_of(pair * (PAIR * HDIM), PAIR * HDIM), PAIR * HDIM)
-        q = query_ref[:, :, cols].astype(F32).reshape(NROW, PAIR * HDIM)
-        out_ref[:, : PAIR * HDIM] = q
-        out_ref[:, PAIR * HDIM :] = ids
+    for (dx, db), out_ref in zip(MATES, out_refs):
+        cols = pl.ds(pl.multiple_of(mate_head(here, dx, db) * HDIM, HDIM), HDIM)
+        out_ref[:, :HDIM] = query_ref[:, :, cols].astype(F32).reshape(NROW, HDIM)
+        out_ref[:, HDIM:] = ids
 
 
 def intra_kernel(
@@ -213,14 +216,11 @@
 
 def scan_kernel(lens, give_ref, extra_ref, entry_ref, slice_ref):
     ends = bounds(lens)
-    states = [jnp.zeros((SLAB, HDIM), F32) for _ in range(PAIR)]
+    state = jnp.zeros((QUART, HDIM), F32)
     for k in range(NDEV):
-        for j in range(PAIR):
-            rows = slice(j * SLAB, (j + 1) * SLAB)
-            entry_ref[k, rows, :] = states[j]
-            states[j] = give_ref[k, S0 + j : S0 + j + 1, :] * states[j] + give_ref[k, rows, :]
-    for j in range(PAIR):
-        slice_ref[LAST, j] = states[j]
+        entry_ref[k] = state
+        state = give_ref[k, S0 : S0 + 1, :] * state + give_ref[k, 0:T0, :]
+    slice_ref[LAST] = state
     earlier = []
     for p in range(LAST):
         e = ends[p] - 1
@@ -230,82 +230,65 @@
             slot = slot + (other == b).astype(jnp.int32)
         earlier.append(b)
         whole = e % BLOCK == BLOCK - 1
-        for j in range(PAIR):
-            rows = slice(j * SLAB, (j + 1) * SLAB)
-            at = S0 + (p + 1) * PAIR + j
-            lead = give_ref[b, at : at + 1, :]
-            tail = give_ref[b, PART + j * SLAB : PART + (j + 1) * SLAB, :]
-            tail = jnp.where(slot == 0, tail, extra_ref[p, rows, :])
-            tail = jnp.where(whole, give_ref[b, rows, :], tail)
-            slice_ref[p, j] = lead * entry_ref[b, rows, :] + tail
+        lead = give_ref[b, S0 + 1 + p : S0 + 2 + p, :]
+        tail = jnp.where(slot == 0, give_ref[b, T0:S0, :], extra_ref[p])
+        tail = jnp.where(whole, give_ref[b, 0:T0, :], tail)
+        slice_ref[p] = lead * entry_ref[b] + tail
 
 
 def project_kernel(here, *refs):
-    queries = refs[:NX]
-    slabs = refs[NX : NX + NZ]
-    outs = refs[NX + NZ : NX + NZ + NX]
-    st_ref = refs[-1]
-    z = lax.rem(here[0], NZ)
+    n = len(MATES)
+    queries, slabs, outs, st_ref = refs[:n], refs[n : n + NQ], refs[n + NQ : 2 * n + NQ], refs[-1]
+    quarter = lax.rem(here[0], NZ) // 2
     for d, ref in enumerate(slabs):
-        origin = lax.rem(z - d + NZ, NZ)
+        origin = lax.rem(quarter - d + NQ, NQ)
         for p in range(PROMPTS):
-            at = pl.multiple_of(p * HDIM + origin * SLAB, SLAB)
-            for j in range(PAIR):
-                st_ref[j, pl.ds(at, SLAB), :] = ref[p, j]
-    for j in range(PAIR):
-        st = st_ref[j]
-        high = st.astype(BF)
-        low = (st - high.astype(F32)).astype(BF)
-        cols = slice(j * HDIM, (j + 1) * HDIM)
-        rows = []
-        for ref in queries:
-            q = ref[:, cols]
-            ids = ref[:, PAIR * HDIM :]
-            rows.append(
-                jnp.concatenate(
-                    [jnp.where(ids == float(p), q, 0.0).astype(BF) for p in range(PROMPTS)], axis=1
-                )
+            at = pl.multiple_of(p * HDIM + origin * QUART, QUART)
+            st_ref[pl.ds(at, QUART), :] = ref[p]
+    st = st_ref[...]
+    high = st.astype(BF)
+    low = (st - high.astype(F32)).astype(BF)
+    rows = []
+    for ref in queries:
+        q = ref[:, :HDIM]
+        ids = ref[:, HDIM:]
+        rows.append(
+            jnp.concatenate(
+                [jnp.where(ids == float(p), q, 0.0).astype(BF) for p in range(PROMPTS)], axis=1
             )
-        wide = jnp.concatenate(rows, axis=0)
-        res = jnp.dot(wide, high, preferred_element_type=F32) + jnp.dot(
-            wide, low, preferred_element_type=F32
         )
-        for d, ref in enumerate(outs):
-            ref[:, cols] = res[d * NROW : (d + 1) * NROW, :]
-
-
-def mixed_kernel(query_ref, back_ref, intra_ref, carried_ref, mixed_ref, sums_ref):
+    wide = jnp.concatenate(rows, axis=0)
+    res = jnp.dot(wide, high, preferred_element_type=F32) + jnp.dot(
+        wide, low, preferred_element_type=F32
+    )
+    for d, ref in enumerate(outs):
+        ref[...] = res[d * NROW : (d + 1) * NROW, :]
+
+
+def mixed_kernel(here, query_ref, back_ref, intra_ref, carried_ref, local_ref, scarried_ref, *refs):
+    products = refs[: len(MATES)]
+    mixed_ref, dec_ref, send_ref, carry_ref = refs[len(MATES) :]
+    for (dx, db), ref in zip(MATES, products):
+        carry_ref[mate_head(here, dx, db)] = ref[...]
+    acc = jnp.zeros((NROW, HDIM), F32)
+    for h in range(HEADS):
+        cols = slice(h * HDIM, (h + 1) * HDIM)
+        dec = local_ref[:, cols] + carry_ref[h] * scarried_ref[:, h : h + 1]
+        dec_ref[:, cols] = dec
+        acc = acc + dec * dec
+    full = jnp.concatenate([acc, jnp.zeros((HDIM - NROW, HDIM), F32)], axis=0)
+    dflat = jnp.sum(full.T, axis=0, keepdims=True)
+
     acc = jnp.zeros((BLOCK, HDIM), F32)
     for h in range(HEADS):
-        x, j = h // PAIR, h % PAIR
         cols = slice(h * HDIM, (h + 1) * HDIM)
-        state = jnp.concatenate(
-            [back_ref[x * NZ + z, j * SLAB : (j + 1) * SLAB, :] for z in range(NZ)], axis=0
-        ).astype(BF)
+        state = jnp.concatenate([back_ref[owner(h, g)] for g in range(NQ)], axis=0).astype(BF)
         outer = jnp.dot(query_ref[:, cols], state, preferred_element_type=F32)
         mixed = intra_ref[:, cols] + outer * carried_ref[:, h : h + 1]
         mixed_ref[:, cols] = mixed
         acc = acc + mixed * mixed
     flat = jnp.sum(acc.T, axis=0, keepdims=True)
-    sums_ref[...] = jnp.concatenate(
-        [flat[:, :HDIM], flat[:, HDIM:], jnp.zeros((6, HDIM), F32)], axis=0
-    )
-
-
-def decode_kernel(here, o0, o1, o2, o3, local_ref, scarried_ref, sums_ref, dec_ref, send_ref, carry_ref):
-    x = here[0] // NZ
-    for d, ref in enumerate((o0, o1, o2, o3)):
-        carry_ref[lax.rem(x + d, NX)] = ref[...]
-    acc = jnp.zeros((NROW, HDIM), F32)
-    for h in range(HEADS):
-        cols = slice(h * HDIM, (h + 1) * HDIM)
-        part = slice((h % PAIR) * HDIM, (h % PAIR + 1) * HDIM)
-        dec = local_ref[:, cols] + carry_ref[h // PAIR, :, part] * scarried_ref[:, h : h + 1]
-        dec_ref[:, cols] = dec
-        acc = acc + dec * dec
-    full = jnp.concatenate([acc, jnp.zeros((HDIM - NROW, HDIM), F32)], axis=0)
-    flat = jnp.sum(full.T, axis=0, keepdims=True)
-    both = jnp.concatenate([sums_ref[0:2, :], flat, jnp.zeros((5, HDIM), F32)], axis=0)
+    both = jnp.concatenate([flat[:, :HDIM], flat[:, HDIM:], dflat, dflat], axis=0)
     for k in range(HEADS):
         send_ref[k] = both
 
@@ -340,6 +323,14 @@
 
 def shift(x, axis, size, d):
     return lax.ppermute(x, axis, [(i, (i + d) % size) for i in range(size)])
+
+
+def to_mate(x, dx, db):
+    moves = []
+    for i in range(NDEV):
+        there = (i // NZ + dx) % NX * NZ + (i % NZ ^ db)
+        moves.append((i, there))
+    return lax.ppermute(x, SEQ, moves)
 
 
 def exchange(x, axis):
@@ -363,11 +354,11 @@
         keep = jnp.where(taken[:, None], jnp.exp(spread), 0.0)
         tailed = (keys.astype(F32) * keep[:, :, None]).astype(BF)
         part = jnp.einsum("shd,she->hde", tailed, values, preferred_element_type=F32)
-        part = part.reshape(NX, PAIR, NZ, SLAB, HDIM).transpose(0, 2, 1, 3, 4)
-        parts.append(part.reshape(NDEV, PART, HDIM))
+        part = part.reshape(NX, 2, NQ, QUART, HDIM).transpose(0, 2, 1, 3, 4)
+        parts.append(part.reshape(NDEV, QUART, HDIM))
     got = exchange(jnp.concatenate(parts, axis=1), SEQ)
     both = jnp.sum(got, axis=0)
-    return jnp.stack([jnp.zeros((PART, HDIM), F32), both[:PART], both[PART:]])
+    return jnp.stack([jnp.zeros((QUART, HDIM), F32), both[:QUART], both[QUART:]])
 
 
 def local(
@@ -403,14 +394,14 @@
 
     queries = pl.pallas_call(
         query_kernel,
-        out_shape=(shape(NROW, (PAIR + 1) * HDIM),) * NX,
+        out_shape=(shape(NROW, 2 * HDIM),) * len(MATES),
         in_specs=[SMEM] * 2 + [VMEM],
-        out_specs=(VMEM,) * NX,
+        out_specs=(VMEM,) * len(MATES),
         compiler_params=params(),
         cost_estimate=cost(1),
         name="query",
     )(here, row_prompt, step_query)
-    queries = [queries[0]] + [shift(queries[d], "seq_0", NX, d) for d in range(1, NX)]
+    queries = [queries[0]] + [to_mate(q, dx, db) for q, (dx, db) in zip(queries[1:], MATES[1:])]
 
     intra, carried, local_dec, scarried = pl.pallas_call(
         intra_kernel,
@@ -431,55 +422,43 @@
     extra = lax.cond(
         crowded[0] > 0,
         lambda: more_tails(key_in, value_in, log_decay, prompt_lengths, me * BLOCK),
-        lambda: jnp.zeros((LAST, PART, HDIM), F32),
+        lambda: jnp.zeros((LAST, QUART, HDIM), F32),
     )
     entry, own = pl.pallas_call(
         scan_kernel,
-        out_shape=(shape(NDEV, PART, HDIM), shape(PROMPTS, PAIR, SLAB, HDIM)),
+        out_shape=(shape(NDEV, QUART, HDIM), shape(PROMPTS, QUART, HDIM)),
         in_specs=[SMEM] + [VMEM] * 2,
         out_specs=(VMEM,) * 2,
         compiler_params=params(),
         cost_estimate=cost(2),
         name="scan",
     )(prompt_lengths, given, extra)
+    slabs = [own] + [shift(own, "seq_1", NZ, 2 * d) for d in range(1, NQ)]
+    entry, slabs = lax.optimization_barrier((entry, slabs))
     back = exchange(entry, SEQ)
 
-    slabs = [own] * NZ
-    for d in range(1, NZ // 2 + 1):
-        slabs[d] = shift(slabs[d - 1], "seq_1", NZ, 1)
-        if d < NZ // 2:
-            slabs[NZ - d] = shift(slabs[(NZ - d + 1) % NZ], "seq_1", NZ, -1)
     products = pl.pallas_call(
         project_kernel,
-        out_shape=(shape(NROW, PAIR * HDIM),) * NX,
-        in_specs=[SMEM] + [VMEM] * (NX + NZ),
-        out_specs=(VMEM,) * NX,
-        scratch_shapes=[pltpu.VMEM((PAIR, PROMPTS * HDIM, HDIM), F32)],
+        out_shape=(shape(NROW, HDIM),) * len(MATES),
+        in_specs=[SMEM] + [VMEM] * (len(MATES) + NQ),
+        out_specs=(VMEM,) * len(MATES),
+        scratch_shapes=[pltpu.VMEM((PROMPTS * HDIM, HDIM), F32)],
         compiler_params=params(),
         cost_estimate=cost(2),
         name="project",
     )(here, *queries, *slabs)
-    products = [products[0]] + [shift(products[d], "seq_0", NX, -d) for d in range(1, NX)]
-
-    mixed, sums = pl.pallas_call(
+    products = [products[0]] + [to_mate(q, -dx, db) for q, (dx, db) in zip(products[1:], MATES[1:])]
+
+    mixed, dec, sums_send = pl.pallas_call(
         mixed_kernel,
-        out_shape=(shape(BLOCK, width), shape(8, HDIM)),
-        in_specs=[VMEM] * 4,
-        out_specs=(VMEM,) * 2,
+        out_shape=(shape(BLOCK, width), shape(n, width), shape(HEADS, 4, HDIM)),
+        in_specs=[SMEM] + [VMEM] * (6 + len(MATES)),
+        out_specs=(VMEM,) * 3,
+        scratch_shapes=[pltpu.VMEM((HEADS, NROW, HDIM), F32)],
         compiler_params=params(),
         cost_estimate=cost(2),
         name="mixed",
-    )(query_in, back, intra, carried)
-    dec, sums_send = pl.pallas_call(
-        decode_kernel,
-        out_shape=(shape(n, width), shape(HEADS, 8, HDIM)),
-        in_specs=[SMEM] + [VMEM] * 7,
-        out_specs=(VMEM,) * 2,
-        scratch_shapes=[pltpu.VMEM((NX, NROW, PAIR * HDIM), F32)],
-        compiler_params=params(),
-        cost_estimate=cost(1),
-        name="decode",
-    )(here, *products, local_dec, scarried, sums)
+    )(here, query_in, back, intra, carried, local_dec, scarried, *products)
     sums_all = exchange(sums_send, "head")
 
     return pl.pallas_call(

time: 108 us -> 103 us (0.954)
  starting transfers between devices: 36.1 us -> 47.1 us
  waiting for transfers between devices: 41.3 us -> 31.5 us
  blocking collectives: 17.3 us -> 10.8 us
    ppermute x0 -> x14, waiting for transfers between devices: none -> 26 us  [to_mate(): return lax.ppermute(x, SEQ, moves)]
    ppermute x13 -> x3, waiting for transfers between devices: 26.6 us -> 5.42 us  [shift(): return lax.ppermute(x, axis, [(i, (i + d) % size) for i in range(size)])]
    ppermute x0 -> x14, starting transfers between devices: none -> 19.9 us  [to_mate(): return lax.ppermute(x, SEQ, moves)]
    all_to_all x2, waiting for transfers between devices: 14.7 us -> 0.01 us  [exchange(): return lax.all_to_all(x, axis, split_axis=0, concat_axis=0, tiled=True)]
    ppermute x13 -> x3, starting transfers between devices: 15.6 us -> 8.37 us  [shift(): return lax.ppermute(x, axis, [(i, (i + d) % size) for i in range(size)])]
    all_to_all x1, blocking collectives: 17.3 us -> 10.8 us  [exchange(): return lax.all_to_all(x, axis, split_axis=0, concat_axis=0, tiled=True)]
    all_to_all x2, starting transfers between devices: 20.5 us -> 18.8 us  [exchange(): return lax.all_to_all(x, axis, split_axis=0, concat_axis=0, tiled=True)]
    pallas_call x5 -> x4, Pallas kernels: 3.2 us -> 3.07 us  [the longest x1 1.41 us: local(): pl.pallas_call(scan_kernel, out_shape=(shape(NDEV, QUART, HDIM), shape(PR...]
  transfers between devices with their start and end apart: 15 -> 19, of which waited for: 9 -> 10; matrix products, arithmetic and copies ran while one was open for 0% -> 0% of each run, Pallas kernels for 4% -> 3%
where the time goes in v6:
time: 103 us; the launch traced here: 102 us
  starting transfers between devices  47.1 us (46%)
  waiting for transfers between devices  31.5 us (31%)
  blocking collectives  10.8 us (10%)
  Pallas kernels  9.85 us (10%)
  between operations  1.53 us (1%)
  local copies, waits for them, and re-layouts  1.4 us (1%)
    ppermute x14, waiting for transfers between devices, to_mate(): return lax.ppermute(x, SEQ, moves)  26 us
    ppermute x14, starting transfers between devices, to_mate(): return lax.ppermute(x, SEQ, moves)  19.9 us
    all_to_all x2, starting transfers between devices, exchange(): return lax.all_to_all(x, axis, split_axis=0, concat_axis=0, tiled=True)  18.8 us
    all_to_all x1, blocking collectives, exchange(): return lax.all_to_all(x, axis, split_axis=0, concat_axis=0, tiled=True)  10.8 us
    ppermute x3, starting transfers between devices, shift(): return lax.ppermute(x, axis, [(i, (i + d) % size) for i in range(size)])  8.37 us
    ppermute x3, waiting for transfers between devices, shift(): return lax.ppermute(x, axis, [(i, (i + d) % size) for i in range(size)])  5.42 us
    pallas_call x1, Pallas kernels, local(): pl.pallas_call(send_kernel, out_shape=(shape(NDEV, GIVE, HDIM), shape(1,...  3.45 us
    pallas_call x1, Pallas kernels, local(): pl.pallas_call(intra_kernel, out_shape=(shape(BLOCK, width), shape(BLOCK,...  2.28 us
  transfers between devices with their start and end apart: 19, of which 10 were waited for; matrix products, arithmetic and copies ran while one was open for 0% of the time, Pallas kernels for 3%

profile of v6, /device:TPU:1, one launch (start us, length us, event | category | flops | bytes accessed | tf_op | source)
XLA Modules:
  0.0 102.2 jit_solution(8536450730003211073)
XLA Ops:
  0.6 3.5 %send.1 = (f32[32,72,128]{2,1,0:T(8,128)}, s32[1]{0:T(128)}) custom-call(s32[4]{0:T(128)} %lens.5, s32[1]{0:T(128)} %bitcast.20.here, bf16[256,1024]{1,0:T(8,128)(2,1)} %key_ref.3, bf16[256,1024]{1,0:T(8,128)(2,1)} %value_ref.3, f32[8,256]{1,0:T(8,128)} %bitcast.55), custom_call_target="tpu_custom_call" | custom-call | flops 3000000000 | bytes 9000000 | tf_op jit(solution)/shard_map/send/pallas_call | solution.py:383
  4.1 0.0 copy-start.1
  4.1 0.0 copy-start.6
  4.1 12.0 %all-to-all-start.1 = ((f32[32,72,128]{2,1,0:T(8,128)}), f32[32,72,128]{2,1,0:T(8,128)S(1)}, u32[]{:S(2)}, u32[]{:S(2)}) async-start(f32[32,72,128]{2,1,0:T(8,128)} %get-tuple-element.66), calls=%async_computation.1 | async-start | bytes 2359296 | tf_op jit(solution)/shard_map/all_to_all | solution.py:337
  16.1 0.0 copy-done.1
  16.2 0.0 copy-start
  16.2 0.0 copy-start.2
  16.2 0.0 copy-start.3
  16.2 0.0 copy-start.4
  16.2 0.0 copy-start.12
  16.2 0.0 copy-start.14
  16.2 0.0 copy-start.15
  16.2 0.0 copy-start.16
  16.3 0.6 query.1
  16.9 1.3 %collective-permute-start = (f32[64,256]{1,0:T(8,128)S(1)}, f32[64,256]{1,0:T(8,128)S(1)}, u32[]{:S(2)}, u32[]{:S(2)}) collective-permute-start(f32[64,256]{1,0:T(8,128)S(1)} %get-tuple-element.72), channel_id=1, source_target_pairs={{0,64},{8,72},{16,80},{24,88},{32,96},{40,104},{48,112},{56,120},{... | collective-permute-start | bytes 196616 | tf_op jit(solution)/shard_map/ppermute | solution.py:333
  18.2 2.4 %collective-permute-start.1 = (f32[64,256]{1,0:T(8,128)S(1)}, f32[64,256]{1,0:T(8,128)S(1)}, u32[]{:S(2)}, u32[]{:S(2)}) collective-permute-start(f32[64,256]{1,0:T(8,128)S(1)} %get-tuple-element.73), channel_id=1, source_target_pairs={{0,128},{8,136},{16,144},{24,152},{32,160},{40,168},{48,176},{56,1... | collective-permute-start | bytes 196616 | tf_op jit(solution)/shard_map/ppermute | solution.py:333
  20.6 1.1 %collective-permute-start.2 = (f32[64,256]{1,0:T(8,128)S(1)}, f32[64,256]{1,0:T(8,128)S(1)}, u32[]{:S(2)}, u32[]{:S(2)}) collective-permute-start(f32[64,256]{1,0:T(8,128)S(1)} %get-tuple-element.74), channel_id=1, source_target_pairs={{0,192},{8,200},{16,208},{24,216},{32,224},{40,232},{48,240},{56,2... | collective-permute-start | bytes 196616 | tf_op jit(solution)/shard_map/ppermute | solution.py:333
  21.8 1.2 %collective-permute-start.3 = (f32[64,256]{1,0:T(8,128)S(1)}, f32[64,256]{1,0:T(8,128)S(1)}, u32[]{:S(2)}, u32[]{:S(2)}) collective-permute-start(f32[64,256]{1,0:T(8,128)S(1)} %get-tuple-element.75), channel_id=1, source_target_pairs={{0,8},{8,0},{16,24},{24,16},{32,40},{40,32},{48,56},{56,48},{64,72... | collective-permute-start | bytes 196616 | tf_op jit(solution)/shard_map/ppermute | solution.py:333
  22.9 0.3 collective-permute-start.4
  23.3 0.0 collective-permute-done.refs_1_
  23.3 4.0 %collective-permute-start.5 = (f32[64,256]{1,0:T(8,128)S(1)}, f32[64,256]{1,0:T(8,128)S(1)}, u32[]{:S(2)}, u32[]{:S(2)}) collective-permute-start(f32[64,256]{1,0:T(8,128)S(1)} %get-tuple-element.77), channel_id=1, source_target_pairs={{0,136},{8,128},{16,152},{24,144},{32,168},{40,160},{48,184},{56,1... | collective-permute-start | bytes 196616 | tf_op jit(solution)/shard_map/ppermute | solution.py:333
  27.2 0.0 collective-permute-done.1.refs_2_
  27.2 0.4 collective-permute-start.6
  27.7 0.0 copy-done.2
  27.7 0.0 copy-done.4
  27.7 2.3 %intra.1 = (f32[256,1024]{1,0:T(8,128)S(1)}, f32[256,8]{1,0:T(8,128)S(1)}, f32[64,1024]{1,0:T(8,128)S(1)}, f32[64,8]{1,0:T(8,128)S(1)}) custom-call(s32[4]{0:T(128)S(1)} %copy-done.16, s32[1]{0:T(128)} %bitcast.20.here, bf16[256,1024]{1,0:T(8,128)(2,1)S(1)} %copy-done, bf16[256,1024]{1,0:T(8,128)(2,1)S(1)} %copy-done.14, bf16[256,1024]{1,0:T(8,128)(2,1)S(1)} %copy-done.12, ...), custom_call_target="tpu_custom_call" | custom-call | flops 6000000000 | bytes 18000000 | tf_op jit(solution)/shard_map/intra/pallas_call | solution.py:406
  30.0 0.7 copy-done.7
  30.7 0.6 copy-done.9
  31.3 0.0 collective-permute-done.2.refs_3_
  31.3 12.5 %collective-permute-done.3.refs_4_ = f32[64,256]{1,0:T(8,128)S(1)} collective-permute-done((f32[64,256]{1,0:T(8,128)S(1)}, f32[64,256]{1,0:T(8,128)S(1)}, u32[]{:S(2)}, u32[]{:S(2)}) %collective-permute-start.3) | collective-permute-done | bytes 65568 | tf_op jit(solution)/shard_map/ppermute | solution.py:333
  43.9 4.0 %collective-permute-done.4.refs_5_ = f32[64,256]{1,0:T(8,128)S(1)} collective-permute-done((f32[64,256]{1,0:T(8,128)S(1)}, f32[64,256]{1,0:T(8,128)S(1)}, u32[]{:S(2)}, u32[]{:S(2)}) %collective-permute-start.4) | collective-permute-done | bytes 65568 | tf_op jit(solution)/shard_map/ppermute | solution.py:333
  47.8 1.5 %collective-permute-done.5.refs_6_ = f32[64,256]{1,0:T(8,128)S(1)} collective-permute-done((f32[64,256]{1,0:T(8,128)S(1)}, f32[64,256]{1,0:T(8,128)S(1)}, u32[]{:S(2)}, u32[]{:S(2)}) %collective-permute-start.5) | collective-permute-done | bytes 65568 | tf_op jit(solution)/shard_map/ppermute | solution.py:333
  49.3 0.2 collective-permute-done.6.refs_7_
  49.5 0.0 all-to-all-done.1.give_ref
  50.2 1.4 %scan.1 = (f32[32,32,128]{2,1,0:T(8,128)}, f32[4,32,128]{2,1,0:T(8,128)S(1)}) custom-call(s32[4]{0:T(128)S(1)} %copy-done.16, f32[32,72,128]{2,1,0:T(8,128)S(1)} %all-to-all-done.1.give_ref, f32[3,32,128]{2,1,0:T(8,128)S(1)} %get-tuple-element.143.extra_ref), custom_call_target="tpu_custom_call" | custom-call | flops 2000000000 | bytes 6000000 | tf_op jit(solution)/shard_map/scan/pallas_call | solution.py:427
  51.6 1.9 %collective-permute-start.7 = (f32[4,32,128]{2,1,0:T(8,128)S(1)}, f32[4,32,128]{2,1,0:T(8,128)S(1)}, u32[]{:S(2)}, u32[]{:S(2)}) collective-permute-start(f32[4,32,128]{2,1,0:T(8,128)S(1)} %get-tuple-element.97.refs_8_), channel_id=1, source_target_pairs={{0,16},{8,24},{16,32},{24,40},{32,48},{40,56},{48,0},{56,8},{1,17}... | collective-permute-start | bytes 196616 | tf_op jit(solution)/shard_map/ppermute | solution.py:325
  53.5 3.6 %collective-permute-start.8 = (f32[4,32,128]{2,1,0:T(8,128)S(1)}, f32[4,32,128]{2,1,0:T(8,128)S(1)}, u32[]{:S(2)}, u32[]{:S(2)}) collective-permute-start(f32[4,32,128]{2,1,0:T(8,128)S(1)} %get-tuple-element.97.refs_8_), channel_id=1, source_target_pairs={{0,32},{8,40},{16,48},{24,56},{32,0},{40,8},{48,16},{56,24},{1,33}... | collective-permute-start | bytes 196616 | tf_op jit(solution)/shard_map/ppermute | solution.py:325
  57.1 2.9 %collective-permute-start.9 = (f32[4,32,128]{2,1,0:T(8,128)S(1)}, f32[4,32,128]{2,1,0:T(8,128)S(1)}, u32[]{:S(2)}, u32[]{:S(2)}) collective-permute-start(f32[4,32,128]{2,1,0:T(8,128)S(1)} %get-tuple-element.97.refs_8_), channel_id=1, source_target_pairs={{0,48},{8,56},{16,0},{24,8},{32,16},{40,24},{48,32},{56,40},{1,49}... | collective-permute-start | bytes 196616 | tf_op jit(solution)/shard_map/ppermute | solution.py:325
  60.0 0.0 collective-permute-done.7.refs_9_
  60.0 0.6 collective-permute-done.8.refs_10_
  60.6 4.8 %collective-permute-done.9.refs_11_ = f32[4,32,128]{2,1,0:T(8,128)S(1)} collective-permute-done((f32[4,32,128]{2,1,0:T(8,128)S(1)}, f32[4,32,128]{2,1,0:T(8,128)S(1)}, u32[]{:S(2)}, u32[]{:S(2)}) %collective-permute-start.9) | collective-permute-done | bytes 65568 | tf_op jit(solution)/shard_map/ppermute | solution.py:325
  65.4 6.8 %all-to-all-start.2 = ((f32[32,32,128]{2,1,0:T(8,128)}), f32[32,32,128]{2,1,0:T(8,128)S(1)}, u32[]{:S(2)}, u32[]{:S(2)}) async-start(f32[32,32,128]{2,1,0:T(8,128)} %get-tuple-element.84), calls=%async_computation.2 | async-start | bytes 1048576 | tf_op jit(solution)/shard_map/all_to_all | solution.py:337
  72.2 0.0 copy-start.10
  72.2 0.5 project.1
  72.7 2.6 %collective-permute-start.10 = (f32[64,128]{1,0:T(8,128)S(1)}, f32[64,128]{1,0:T(8,128)S(1)}, u32[]{:S(2)}, u32[]{:S(2)}) collective-permute-start(f32[64,128]{1,0:T(8,128)S(1)} %get-tuple-element.102), channel_id=1, source_target_pairs={{0,192},{8,200},{16,208},{24,216},{32,224},{40,232},{48,240},{56,2... | collective-permute-start | bytes 98312 | tf_op jit(solution)/shard_map/ppermute | solution.py:333
  75.3 0.5 collective-permute-start.11
  75.8 0.6 collective-permute-start.12
  76.4 1.2 %collective-permute-start.13 = (f32[64,128]{1,0:T(8,128)S(1)}, f32[64,128]{1,0:T(8,128)S(1)}, u32[]{:S(2)}, u32[]{:S(2)}) collective-permute-start(f32[64,128]{1,0:T(8,128)S(1)} %get-tuple-element.105), channel_id=1, source_target_pairs={{0,8},{8,0},{16,24},{24,16},{32,40},{40,32},{48,56},{56,48},{64,72... | collective-permute-start | bytes 98312 | tf_op jit(solution)/shard_map/ppermute | solution.py:333
  77.6 2.1 %collective-permute-start.14 = (f32[64,128]{1,0:T(8,128)S(1)}, f32[64,128]{1,0:T(8,128)S(1)}, u32[]{:S(2)}, u32[]{:S(2)}) collective-permute-start(f32[64,128]{1,0:T(8,128)S(1)} %get-tuple-element.106), channel_id=1, source_target_pairs={{0,200},{8,192},{16,216},{24,208},{32,232},{40,224},{48,248},{56,2... | collective-permute-start | bytes 98312 | tf_op jit(solution)/shard_map/ppermute | solution.py:333
  79.6 0.0 collective-permute-done.10.refs_1_
  79.6 2.1 %collective-permute-start.15 = (f32[64,128]{1,0:T(8,128)S(1)}, f32[64,128]{1,0:T(8,128)S(1)}, u32[]{:S(2)}, u32[]{:S(2)}) collective-permute-start(f32[64,128]{1,0:T(8,128)S(1)} %get-tuple-element.107), channel_id=1, source_target_pairs={{0,136},{8,128},{16,152},{24,144},{32,168},{40,160},{48,184},{56,1... | collective-permute-start | bytes 98312 | tf_op jit(solution)/shard_map/ppermute | solution.py:333
  81.8 0.0 collective-permute-done.11.refs_2_
  81.8 0.0 collective-permute-start.16
  81.8 0.0 collective-permute-done.12.refs_3_
  81.8 3.3 %collective-permute-done.13.refs_4_ = f32[64,128]{1,0:T(8,128)S(1)} collective-permute-done((f32[64,128]{1,0:T(8,128)S(1)}, f32[64,128]{1,0:T(8,128)S(1)}, u32[]{:S(2)}, u32[]{:S(2)}) %collective-permute-start.13) | collective-permute-done | bytes 32800 | tf_op jit(solution)/shard_map/ppermute | solution.py:333
  85.1 1.7 %collective-permute-done.14.refs_5_ = f32[64,128]{1,0:T(8,128)S(1)} collective-permute-done((f32[64,128]{1,0:T(8,128)S(1)}, f32[64,128]{1,0:T(8,128)S(1)}, u32[]{:S(2)}, u32[]{:S(2)}) %collective-permute-start.14) | collective-permute-done | bytes 32800 | tf_op jit(solution)/shard_map/ppermute | solution.py:333
  86.8 2.3 %collective-permute-done.15.refs_6_ = f32[64,128]{1,0:T(8,128)S(1)} collective-permute-done((f32[64,128]{1,0:T(8,128)S(1)}, f32[64,128]{1,0:T(8,128)S(1)}, u32[]{:S(2)}, u32[]{:S(2)}) %collective-permute-start.15) | collective-permute-done | bytes 32800 | tf_op jit(solution)/shard_map/ppermute | solution.py:333
  89.1 0.5 collective-permute-done.16.refs_7_
  89.7 0.0 all-to-all-done.2.back_ref
  89.7 0.0 copy-done.10
  89.7 0.0 copy-start.5
  89.7 0.6 mixed.1
  90.3 10.8 %all_to_all.19.sums_ref = f32[8,4,128]{2,1,0:T(4,128)S(1)} all-to-all(f32[8,4,128]{2,1,0:T(4,128)S(1)} %get-tuple-element.109), channel_id=1, replica_groups=mesh['seq_0'=4,'seq_1'=8,'head'=8] {'head'}, dimensions={0} | all-to-all | bytes 32768 | tf_op jit(solution)/shard_map/all_to_all | solution.py:337
  101.1 1.1 %final.1 = (bf16[256,1024]{1,0:T(8,128)(2,1)}, bf16[4,16,1024]{2,1,0:T(8,128)(2,1)}) custom-call(f32[8,4,128]{2,1,0:T(4,128)S(1)} %all_to_all.19.sums_ref, f32[256,1024]{1,0:T(8,128)S(1)} %get-tuple-element.110.mixed_ref, f32[64,1024]{1,0:T(8,128)S(1)} %get-tuple-element.111.dec_ref, f32[1,1024]{1,0:T(1,128)S(1)} %bitcast.47), custom_call_target="tpu_custom_call" | custom-call | flops 2000000000 | bytes 6000000 | tf_op jit(solution)/shard_map/final/pallas_call | solution.py:464
  (14 shorter events, 0.1 us)
Async XLA Ops:
  4.1 12.0 %copy-start.1 = (bf16[4,16,1024]{2,1,0:T(8,128)(2,1)S(1)}, bf16[4,16,1024]{2,1,0:T(8,128)(2,1)}, u32[]{:S(2)}) copy-start(bf16[4,16,1024]{2,1,0:T(8,128)(2,1)} %query_ref.4) | copy-start | bytes 393220
  4.1 12.0 %copy-start.6 = (s32[16]{0:T(128)S(1)}, s32[16]{0:T(128)}, u32[]{:S(2)}) copy-start(s32[16]{0:T(128)} %rows.1) | copy-start | bytes 196
  4.1 45.4 %all-to-all-start.1 = ((f32[32,72,128]{2,1,0:T(8,128)}), f32[32,72,128]{2,1,0:T(8,128)S(1)}, u32[]{:S(2)}, u32[]{:S(2)}) async-start(f32[32,72,128]{2,1,0:T(8,128)} %get-tuple-element.66), calls=%async_computation.1 | async-start | bytes 2359296 | tf_op jit(solution)/shard_map/all_to_all | solution.py:337
  16.2 11.5 %copy-start = (bf16[256,1024]{1,0:T(8,128)(2,1)S(1)}, bf16[256,1024]{1,0:T(8,128)(2,1)}, u32[]{:S(2)}) copy-start(bf16[256,1024]{1,0:T(8,128)(2,1)} %query_ref.5) | copy-start | bytes 1572868
  16.2 11.5 %copy-start.2 = (bf16[4,16,1024]{2,1,0:T(8,128)(2,1)S(1)}, bf16[4,16,1024]{2,1,0:T(8,128)(2,1)}, u32[]{:S(2)}) copy-start(bf16[4,16,1024]{2,1,0:T(8,128)(2,1)} %sk_ref.1) | copy-start | bytes 393220
  16.2 11.5 %copy-start.3 = (bf16[4,16,1024]{2,1,0:T(8,128)(2,1)S(1)}, bf16[4,16,1024]{2,1,0:T(8,128)(2,1)}, u32[]{:S(2)}) copy-start(bf16[4,16,1024]{2,1,0:T(8,128)(2,1)} %sv_ref.1) | copy-start | bytes 393220
  16.2 11.5 %copy-start.4 = (f32[4,16,8]{1,2,0:T(8,128)S(1)}, f32[4,16,8]{1,2,0:T(8,128)}, u32[]{:S(2)}) copy-start(f32[4,16,8]{1,2,0:T(8,128)} %param.22) | copy-start | bytes 6148
  16.2 11.5 %copy-start.12 = (bf16[256,1024]{1,0:T(8,128)(2,1)S(1)}, bf16[256,1024]{1,0:T(8,128)(2,1)}, u32[]{:S(2)}) copy-start(bf16[256,1024]{1,0:T(8,128)(2,1)} %value_ref.3) | copy-start | bytes 1572868
  16.2 11.5 %copy-start.14 = (bf16[256,1024]{1,0:T(8,128)(2,1)S(1)}, bf16[256,1024]{1,0:T(8,128)(2,1)}, u32[]{:S(2)}) copy-start(bf16[256,1024]{1,0:T(8,128)(2,1)} %key_ref.3) | copy-start | bytes 1572868
  16.2 11.5 %copy-start.15 = (f32[256,8]{0,1:T(8,128)S(1)}, f32[256,8]{0,1:T(8,128)}, u32[]{:S(2)}) copy-start(f32[256,8]{0,1:T(8,128)} %param.16) | copy-start | bytes 24580
  16.2 11.5 %copy-start.16 = (s32[4]{0:T(128)S(1)}, s32[4]{0:T(128)}, u32[]{:S(2)}) copy-start(s32[4]{0:T(128)} %lens.5) | copy-start | bytes 52
  16.9 6.4 %collective-permute-start = (f32[64,256]{1,0:T(8,128)S(1)}, f32[64,256]{1,0:T(8,128)S(1)}, u32[]{:S(2)}, u32[]{:S(2)}) collective-permute-start(f32[64,256]{1,0:T(8,128)S(1)} %get-tuple-element.72), channel_id=1, source_target_pairs={{0,64},{8,72},{16,80},{24,88},{32,96},{40,104},{48,112},{56,120},{... | collective-permute-start | bytes 196616 | tf_op jit(solution)/shard_map/ppermute | solution.py:333
  18.2 9.1 %collective-permute-start.1 = (f32[64,256]{1,0:T(8,128)S(1)}, f32[64,256]{1,0:T(8,128)S(1)}, u32[]{:S(2)}, u32[]{:S(2)}) collective-permute-start(f32[64,256]{1,0:T(8,128)S(1)} %get-tuple-element.73), channel_id=1, source_target_pairs={{0,128},{8,136},{16,144},{24,152},{32,160},{40,168},{48,176},{56,1... | collective-permute-start | bytes 196616 | tf_op jit(solution)/shard_map/ppermute | solution.py:333
  20.6 10.7 %collective-permute-start.2 = (f32[64,256]{1,0:T(8,128)S(1)}, f32[64,256]{1,0:T(8,128)S(1)}, u32[]{:S(2)}, u32[]{:S(2)}) collective-permute-start(f32[64,256]{1,0:T(8,128)S(1)} %get-tuple-element.74), channel_id=1, source_target_pairs={{0,192},{8,200},{16,208},{24,216},{32,224},{40,232},{48,240},{56,2... | collective-permute-start | bytes 196616 | tf_op jit(solution)/shard_map/ppermute | solution.py:333
  21.8 22.1 %collective-permute-start.3 = (f32[64,256]{1,0:T(8,128)S(1)}, f32[64,256]{1,0:T(8,128)S(1)}, u32[]{:S(2)}, u32[]{:S(2)}) collective-permute-start(f32[64,256]{1,0:T(8,128)S(1)} %get-tuple-element.75), channel_id=1, source_target_pairs={{0,8},{8,0},{16,24},{24,16},{32,40},{40,32},{48,56},{56,48},{64,72... | collective-permute-start | bytes 196616 | tf_op jit(solution)/shard_map/ppermute | solution.py:333
  22.9 24.9 %collective-permute-start.4 = (f32[64,256]{1,0:T(8,128)S(1)}, f32[64,256]{1,0:T(8,128)S(1)}, u32[]{:S(2)}, u32[]{:S(2)}) collective-permute-start(f32[64,256]{1,0:T(8,128)S(1)} %get-tuple-element.76), channel_id=1, source_target_pairs={{0,72},{8,64},{16,88},{24,80},{32,104},{40,96},{48,120},{56,112},{... | collective-permute-start | bytes 196616 | tf_op jit(solution)/shard_map/ppermute | solution.py:333
  23.3 26.0 %collective-permute-start.5 = (f32[64,256]{1,0:T(8,128)S(1)}, f32[64,256]{1,0:T(8,128)S(1)}, u32[]{:S(2)}, u32[]{:S(2)}) collective-permute-start(f32[64,256]{1,0:T(8,128)S(1)} %get-tuple-element.77), channel_id=1, source_target_pairs={{0,136},{8,128},{16,152},{24,144},{32,168},{40,160},{48,184},{56,1... | collective-permute-start | bytes 196616 | tf_op jit(solution)/shard_map/ppermute | solution.py:333
  27.2 22.3 %collective-permute-start.6 = (f32[64,256]{1,0:T(8,128)S(1)}, f32[64,256]{1,0:T(8,128)S(1)}, u32[]{:S(2)}, u32[]{:S(2)}) collective-permute-start(f32[64,256]{1,0:T(8,128)S(1)} %get-tuple-element.78), channel_id=1, source_target_pairs={{0,200},{8,192},{16,216},{24,208},{32,232},{40,224},{48,248},{56,2... | collective-permute-start | bytes 196616 | tf_op jit(solution)/shard_map/ppermute | solution.py:333
  30.0 0.7 copy-start.7
  30.7 0.6 copy-start.9
  51.6 8.4 %collective-permute-start.7 = (f32[4,32,128]{2,1,0:T(8,128)S(1)}, f32[4,32,128]{2,1,0:T(8,128)S(1)}, u32[]{:S(2)}, u32[]{:S(2)}) collective-permute-start(f32[4,32,128]{2,1,0:T(8,128)S(1)} %get-tuple-element.97.refs_8_), channel_id=1, source_target_pairs={{0,16},{8,24},{16,32},{24,40},{32,48},{40,56},{48,0},{56,8},{1,17}... | collective-permute-start | bytes 196616 | tf_op jit(solution)/shard_map/ppermute | solution.py:325
  53.5 7.1 %collective-permute-start.8 = (f32[4,32,128]{2,1,0:T(8,128)S(1)}, f32[4,32,128]{2,1,0:T(8,128)S(1)}, u32[]{:S(2)}, u32[]{:S(2)}) collective-permute-start(f32[4,32,128]{2,1,0:T(8,128)S(1)} %get-tuple-element.97.refs_8_), channel_id=1, source_target_pairs={{0,32},{8,40},{16,48},{24,56},{32,0},{40,8},{48,16},{56,24},{1,33}... | collective-permute-start | bytes 196616 | tf_op jit(solution)/shard_map/ppermute | solution.py:325
  57.1 8.3 %collective-permute-start.9 = (f32[4,32,128]{2,1,0:T(8,128)S(1)}, f32[4,32,128]{2,1,0:T(8,128)S(1)}, u32[]{:S(2)}, u32[]{:S(2)}) collective-permute-start(f32[4,32,128]{2,1,0:T(8,128)S(1)} %get-tuple-element.97.refs_8_), channel_id=1, source_target_pairs={{0,48},{8,56},{16,0},{24,8},{32,16},{40,24},{48,32},{56,40},{1,49}... | collective-permute-start | bytes 196616 | tf_op jit(solution)/shard_map/ppermute | solution.py:325
  65.4 24.3 %all-to-all-start.2 = ((f32[32,32,128]{2,1,0:T(8,128)}), f32[32,32,128]{2,1,0:T(8,128)S(1)}, u32[]{:S(2)}, u32[]{:S(2)}) async-start(f32[32,32,128]{2,1,0:T(8,128)} %get-tuple-element.84), calls=%async_computation.2 | async-start | bytes 1048576 | tf_op jit(solution)/shard_map/all_to_all | solution.py:337
  72.2 17.5 %copy-start.8 = (f32[64,1024]{1,0:T(8,128)S(1)}, f32[64,1024]{1,0:T(8,128)}, u32[]{:S(2)}) copy-start(f32[64,1024]{1,0:T(8,128)} %copy-done.7) | copy-start | bytes 786436
  72.2 17.5 %copy-start.10 = (f32[64,8]{1,0:T(8,128)S(1)}, f32[64,8]{1,0:T(8,128)}, u32[]{:S(2)}) copy-start(f32[64,8]{1,0:T(8,128)} %copy-done.9) | copy-start | bytes 6148
  72.7 7.0 %collective-permute-start.10 = (f32[64,128]{1,0:T(8,128)S(1)}, f32[64,128]{1,0:T(8,128)S(1)}, u32[]{:S(2)}, u32[]{:S(2)}) collective-permute-start(f32[64,128]{1,0:T(8,128)S(1)} %get-tuple-element.102), channel_id=1, source_target_pairs={{0,192},{8,200},{16,208},{24,216},{32,224},{40,232},{48,240},{56,2... | collective-permute-start | bytes 98312 | tf_op jit(solution)/shard_map/ppermute | solution.py:333
  75.3 6.5 %collective-permute-start.11 = (f32[64,128]{1,0:T(8,128)S(1)}, f32[64,128]{1,0:T(8,128)S(1)}, u32[]{:S(2)}, u32[]{:S(2)}) collective-permute-start(f32[64,128]{1,0:T(8,128)S(1)} %get-tuple-element.103), channel_id=1, source_target_pairs={{0,128},{8,136},{16,144},{24,152},{32,160},{40,168},{48,176},{56,1... | collective-permute-start | bytes 98312 | tf_op jit(solution)/shard_map/ppermute | solution.py:333
  75.8 6.0 %collective-permute-start.12 = (f32[64,128]{1,0:T(8,128)S(1)}, f32[64,128]{1,0:T(8,128)S(1)}, u32[]{:S(2)}, u32[]{:S(2)}) collective-permute-start(f32[64,128]{1,0:T(8,128)S(1)} %get-tuple-element.104), channel_id=1, source_target_pairs={{0,64},{8,72},{16,80},{24,88},{32,96},{40,104},{48,112},{56,120},{... | collective-permute-start | bytes 98312 | tf_op jit(solution)/shard_map/ppermute | solution.py:333
  76.4 8.8 %collective-permute-start.13 = (f32[64,128]{1,0:T(8,128)S(1)}, f32[64,128]{1,0:T(8,128)S(1)}, u32[]{:S(2)}, u32[]{:S(2)}) collective-permute-start(f32[64,128]{1,0:T(8,128)S(1)} %get-tuple-element.105), channel_id=1, source_target_pairs={{0,8},{8,0},{16,24},{24,16},{32,40},{40,32},{48,56},{56,48},{64,72... | collective-permute-start | bytes 98312 | tf_op jit(solution)/shard_map/ppermute | solution.py:333
  77.6 9.3 %collective-permute-start.14 = (f32[64,128]{1,0:T(8,128)S(1)}, f32[64,128]{1,0:T(8,128)S(1)}, u32[]{:S(2)}, u32[]{:S(2)}) collective-permute-start(f32[64,128]{1,0:T(8,128)S(1)} %get-tuple-element.106), channel_id=1, source_target_pairs={{0,200},{8,192},{16,216},{24,208},{32,232},{40,224},{48,248},{56,2... | collective-permute-start | bytes 98312 | tf_op jit(solution)/shard_map/ppermute | solution.py:333
  79.6 9.5 %collective-permute-start.15 = (f32[64,128]{1,0:T(8,128)S(1)}, f32[64,128]{1,0:T(8,128)S(1)}, u32[]{:S(2)}, u32[]{:S(2)}) collective-permute-start(f32[64,128]{1,0:T(8,128)S(1)} %get-tuple-element.107), channel_id=1, source_target_pairs={{0,136},{8,128},{16,152},{24,144},{32,168},{40,160},{48,184},{56,1... | collective-permute-start | bytes 98312 | tf_op jit(solution)/shard_map/ppermute | solution.py:333
  81.8 7.9 %collective-permute-start.16 = (f32[64,128]{1,0:T(8,128)S(1)}, f32[64,128]{1,0:T(8,128)S(1)}, u32[]{:S(2)}, u32[]{:S(2)}) collective-permute-start(f32[64,128]{1,0:T(8,128)S(1)} %get-tuple-element.108), channel_id=1, source_target_pairs={{0,72},{8,64},{16,88},{24,80},{32,104},{40,96},{48,120},{56,112},{... | collective-permute-start | bytes 98312 | tf_op jit(solution)/shard_map/ppermute | solution.py:333
  89.7 11.4 %copy-start.5 = (f32[1024]{0:T(1024)S(1)}, f32[1024]{0:T(1024)}, u32[]{:S(2)}) copy-start(f32[1024]{0:T(1024)} %param.17) | copy-start | bytes 12292

commit v7 on v6

--- a/solution.py
+++ b/solution.py
@@ -25,7 +25,7 @@
 ROWS_DEV = 16
 NROW = STEPS * ROWS_DEV
 LAST = PROMPTS - 1
-MATES = [(dx, db) for db in range(2) for dx in range(NX)]
+ASK = NROW + 8
 
 T0 = QUART
 S0 = 2 * QUART
@@ -39,7 +39,7 @@
 VMEM = pl.BlockSpec(memory_space=pltpu.VMEM)
 
 
-def params(mib=24):
+def params(mib=12):
     return pltpu.CompilerParams(vmem_limit_bytes=mib << 20)
 
 
@@ -152,14 +152,15 @@
 
 
 def query_kernel(here, rows, query_ref, *out_refs):
-    r = lax.broadcasted_iota(jnp.int32, (NROW, HDIM), 0) % ROWS_DEV
-    ids = jnp.zeros((NROW, HDIM), F32)
+    lane = lax.broadcasted_iota(jnp.int32, (8, HDIM), 1)
+    ids = jnp.zeros((8, HDIM), F32)
     for k in range(ROWS_DEV):
-        ids = jnp.where(r == k, rows[k].astype(F32), ids)
-    for (dx, db), out_ref in zip(MATES, out_refs):
-        cols = pl.ds(pl.multiple_of(mate_head(here, dx, db) * HDIM, HDIM), HDIM)
-        out_ref[:, :HDIM] = query_ref[:, :, cols].astype(F32).reshape(NROW, HDIM)
-        out_ref[:, HDIM:] = ids
+        ids = jnp.where(lane == k, rows[k].astype(F32), ids)
+    for dx, out_ref in enumerate(out_refs):
+        for db in range(2):
+            cols = pl.ds(pl.multiple_of(mate_head(here, dx, db) * HDIM, HDIM), HDIM)
+            out_ref[db, :NROW, :] = query_ref[:, :, cols].astype(F32).reshape(NROW, HDIM)
+            out_ref[db, NROW:, :] = ids
 
 
 def intra_kernel(
@@ -237,8 +238,7 @@
 
 
 def project_kernel(here, *refs):
-    n = len(MATES)
-    queries, slabs, outs, st_ref = refs[:n], refs[n : n + NQ], refs[n + NQ : 2 * n + NQ], refs[-1]
+    near, far, slabs, outs, st_ref = refs[:NX], refs[NX], refs[NX + 1 : NX + 1 + NQ], refs[NX + 1 + NQ : -1], refs[-1]
     quarter = lax.rem(here[0], NZ) // 2
     for d, ref in enumerate(slabs):
         origin = lax.rem(quarter - d + NQ, NQ)
@@ -248,28 +248,34 @@
     st = st_ref[...]
     high = st.astype(BF)
     low = (st - high.astype(F32)).astype(BF)
+    r = lax.broadcasted_iota(jnp.int32, (NROW, HDIM), 0) % ROWS_DEV
+    c = lax.broadcasted_iota(jnp.int32, (NROW, HDIM), 1)
     rows = []
-    for ref in queries:
-        q = ref[:, :HDIM]
-        ids = ref[:, HDIM:]
+    for msg in [ref[0] for ref in near] + [far[dx] for dx in range(NX)]:
+        q = msg[:NROW, :]
+        ids = jnp.broadcast_to(msg[NROW : NROW + 1, :], (NROW, HDIM))
+        prompt = jnp.sum(jnp.where(r == c, ids, 0.0), axis=1, keepdims=True)
         rows.append(
             jnp.concatenate(
-                [jnp.where(ids == float(p), q, 0.0).astype(BF) for p in range(PROMPTS)], axis=1
+                [jnp.where(prompt == float(p), q, 0.0).astype(BF) for p in range(PROMPTS)], axis=1
             )
         )
     wide = jnp.concatenate(rows, axis=0)
     res = jnp.dot(wide, high, preferred_element_type=F32) + jnp.dot(
         wide, low, preferred_element_type=F32
     )
-    for d, ref in enumerate(outs):
-        ref[...] = res[d * NROW : (d + 1) * NROW, :]
+    for dx, ref in enumerate(outs):
+        for db in range(2):
+            at = (db * NX + dx) * NROW
+            ref[db] = res[at : at + NROW, :]
 
 
 def mixed_kernel(here, query_ref, back_ref, intra_ref, carried_ref, local_ref, scarried_ref, *refs):
-    products = refs[: len(MATES)]
-    mixed_ref, dec_ref, send_ref, carry_ref = refs[len(MATES) :]
-    for (dx, db), ref in zip(MATES, products):
-        carry_ref[mate_head(here, dx, db)] = ref[...]
+    near, far = refs[:NX], refs[NX]
+    mixed_ref, dec_ref, send_ref, carry_ref = refs[NX + 1 :]
+    for dx in range(NX):
+        carry_ref[mate_head(here, dx, 0)] = near[dx][0]
+        carry_ref[mate_head(here, dx, 1)] = far[dx]
     acc = jnp.zeros((NROW, HDIM), F32)
     for h in range(HEADS):
         cols = slice(h * HDIM, (h + 1) * HDIM)
@@ -325,12 +331,9 @@
     return lax.ppermute(x, axis, [(i, (i + d) % size) for i in range(size)])
 
 
-def to_mate(x, dx, db):
-    moves = []
-    for i in range(NDEV):
-        there = (i // NZ + dx) % NX * NZ + (i % NZ ^ db)
-        moves.append((i, there))
-    return lax.ppermute(x, SEQ, moves)
+def over_pair(pieces):
+    both = jnp.stack([piece[1] for piece in pieces])
+    return lax.ppermute(both, "seq_1", [(i, i ^ 1) for i in range(NZ)])
 
 
 def exchange(x, axis):
@@ -394,14 +397,15 @@
 
     queries = pl.pallas_call(
         query_kernel,
-        out_shape=(shape(NROW, 2 * HDIM),) * len(MATES),
+        out_shape=(shape(2, ASK, HDIM),) * NX,
         in_specs=[SMEM] * 2 + [VMEM],
-        out_specs=(VMEM,) * len(MATES),
+        out_specs=(VMEM,) * NX,
         compiler_params=params(),
         cost_estimate=cost(1),
         name="query",
     )(here, row_prompt, step_query)
-    queries = [queries[0]] + [to_mate(q, dx, db) for q, (dx, db) in zip(queries[1:], MATES[1:])]
+    queries = [queries[0]] + [shift(queries[d], "seq_0", NX, d) for d in range(1, NX)]
+    far_queries = over_pair(queries)
 
     intra, carried, local_dec, scarried = pl.pallas_call(
         intra_kernel,
@@ -416,8 +420,10 @@
         step_query, step_key, step_value, step_decay.transpose(0, 2, 1),
     )
 
-    given, intra, carried, local_dec, scarried, queries, crowded = lax.optimization_barrier(
-        (given, intra, carried, local_dec, scarried, queries, crowded)
+    given, intra, carried, local_dec, scarried, crowded, queries, far_queries = (
+        lax.optimization_barrier(
+            (given, intra, carried, local_dec, scarried, crowded, queries, far_queries)
+        )
     )
     extra = lax.cond(
         crowded[0] > 0,
@@ -439,26 +445,27 @@
 
     products = pl.pallas_call(
         project_kernel,
-        out_shape=(shape(NROW, HDIM),) * len(MATES),
-        in_specs=[SMEM] + [VMEM] * (len(MATES) + NQ),
-        out_specs=(VMEM,) * len(MATES),
+        out_shape=(shape(2, NROW, HDIM),) * NX,
+        in_specs=[SMEM] + [VMEM] * (NX + 1 + NQ),
+        out_specs=(VMEM,) * NX,
         scratch_shapes=[pltpu.VMEM((PROMPTS * HDIM, HDIM), F32)],
         compiler_params=params(),
         cost_estimate=cost(2),
         name="project",
-    )(here, *queries, *slabs)
-    products = [products[0]] + [to_mate(q, -dx, db) for q, (dx, db) in zip(products[1:], MATES[1:])]
+    )(here, *queries, far_queries, *slabs)
+    products = [products[0]] + [shift(products[d], "seq_0", NX, -d) for d in range(1, NX)]
+    far_products = over_pair(products)
 
     mixed, dec, sums_send = pl.pallas_call(
         mixed_kernel,
         out_shape=(shape(BLOCK, width), shape(n, width), shape(HEADS, 4, HDIM)),
-        in_specs=[SMEM] + [VMEM] * (6 + len(MATES)),
+        in_specs=[SMEM] + [VMEM] * (7 + NX),
         out_specs=(VMEM,) * 3,
         scratch_shapes=[pltpu.VMEM((HEADS, NROW, HDIM), F32)],
         compiler_params=params(),
         cost_estimate=cost(2),
         name="mixed",
-    )(here, query_in, back, intra, carried, local_dec, scarried, *products)
+    )(here, query_in, back, intra, carried, local_dec, scarried, *products, far_products)
     sums_all = exchange(sums_send, "head")
 
     return pl.pallas_call(

time: 103 us -> 98.2 us (0.953)
  starting transfers between devices: 47.1 us -> 41.4 us
  blocking collectives: 10.8 us -> 12.7 us
    ppermute x14 -> x2, starting transfers between devices: 19.9 us -> 3.7 us  [over_pair(): return lax.ppermute(both, 'seq_1', [(i, i ^ 1) for i in range(NZ)])]
    ppermute x3 -> x9, starting transfers between devices: 8.37 us -> 17.4 us  [shift(): return lax.ppermute(x, axis, [(i, (i + d) % size) for i in range(size)])]
    ppermute x14 -> x2, waiting for transfers between devices: 26 us -> 18 us  [over_pair(): return lax.ppermute(both, 'seq_1', [(i, i ^ 1) for i in range(NZ)])]
    ppermute x3 -> x9, waiting for transfers between devices: 5.42 us -> 12.5 us  [shift(): return lax.ppermute(x, axis, [(i, (i + d) % size) for i in range(size)])]
    all_to_all x1, blocking collectives: 10.8 us -> 12.7 us  [exchange(): return lax.all_to_all(x, axis, split_axis=0, concat_axis=0, tiled=True)]
    all_to_all x2, starting transfers between devices: 18.8 us -> 20.4 us  [exchange(): return lax.all_to_all(x, axis, split_axis=0, concat_axis=0, tiled=True)]
  transfers between devices with their start and end apart: 19 -> 13, of which waited for: 10 -> 9; matrix products, arithmetic and copies ran while one was open for 0% -> 0% of each run, Pallas kernels for 3% -> 3%
where the time goes in v7:
time: 98.2 us; the launch traced here: 97.8 us
  starting transfers between devices  41.4 us (42%)
  waiting for transfers between devices  30.5 us (31%)
  blocking collectives  12.7 us (13%)
  Pallas kernels  9.85 us (10%)
  local copies, waits for them, and re-layouts  1.76 us (2%)
  between operations  1.52 us (2%)
    all_to_all x2, starting transfers between devices, exchange(): return lax.all_to_all(x, axis, split_axis=0, concat_axis=0, tiled=True)  20.4 us
    ppermute x2, waiting for transfers between devices, over_pair(): return lax.ppermute(both, 'seq_1', [(i, i ^ 1) for i in range(NZ)])  18 us
    ppermute x9, starting transfers between devices, shift(): return lax.ppermute(x, axis, [(i, (i + d) % size) for i in range(size)])  17.4 us
    all_to_all x1, blocking collectives, exchange(): return lax.all_to_all(x, axis, split_axis=0, concat_axis=0, tiled=True)  12.7 us
    ppermute x9, waiting for transfers between devices, shift(): return lax.ppermute(x, axis, [(i, (i + d) % size) for i in range(size)])  12.5 us
    ppermute x2, starting transfers between devices, over_pair(): return lax.ppermute(both, 'seq_1', [(i, i ^ 1) for i in range(NZ)])  3.7 us
    pallas_call x1, Pallas kernels, local(): pl.pallas_call(send_kernel, out_shape=(shape(NDEV, GIVE, HDIM), shape(1,...  3.47 us
    pallas_call x1, Pallas kernels, local(): pl.pallas_call(intra_kernel, out_shape=(shape(BLOCK, width), shape(BLOCK,...  2.26 us
  transfers between devices with their start and end apart: 13, of which 9 were waited for; matrix products, arithmetic and copies ran while one was open for 0% of the time, Pallas kernels for 3%

profile of v7, /device:TPU:1, one launch (start us, length us, event | category | flops | bytes accessed | tf_op | source)
XLA Modules:
  0.0 97.8 jit_solution(6392270616664847123)
XLA Ops:
  0.6 3.5 %send.1 = (f32[32,72,128]{2,1,0:T(8,128)}, s32[1]{0:T(128)}) custom-call(s32[4]{0:T(128)} %lens.5, s32[1]{0:T(128)} %bitcast.20.here, bf16[256,1024]{1,0:T(8,128)(2,1)} %key_ref.3, bf16[256,1024]{1,0:T(8,128)(2,1)} %value_ref.3, f32[8,256]{1,0:T(8,128)} %bitcast.55), custom_call_target="tpu_custom_call" | custom-call | flops 3000000000 | bytes 9000000 | tf_op jit(solution)/shard_map/send/pallas_call | solution.py:386
  4.1 0.0 copy-start.1
  4.1 0.0 copy-start.6
  4.1 12.0 %all-to-all-start.1 = ((f32[32,72,128]{2,1,0:T(8,128)}), f32[32,72,128]{2,1,0:T(8,128)S(1)}, u32[]{:S(2)}, u32[]{:S(2)}) async-start(f32[32,72,128]{2,1,0:T(8,128)} %get-tuple-element.55), calls=%async_computation.1 | async-start | bytes 2359296 | tf_op jit(solution)/shard_map/all_to_all | solution.py:340
  16.2 0.0 copy-done.1
  16.2 0.0 copy-done.6
  16.2 0.0 copy-start
  16.2 0.0 copy-start.2
  16.2 0.0 copy-start.3
  16.2 0.0 copy-start.4
  16.2 0.0 copy-start.10
  16.2 0.0 copy-start.12
  16.2 0.0 copy-start.13
  16.3 0.0 copy-start.14
  16.3 0.6 query.1
  16.9 1.3 %collective-permute-start = (f32[2,72,128]{2,1,0:T(8,128)S(1)}, f32[2,72,128]{2,1,0:T(8,128)S(1)}, u32[]{:S(2)}, u32[]{:S(2)}) collective-permute-start(f32[2,72,128]{2,1,0:T(8,128)S(1)} %get-tuple-element.62), channel_id=1, source_target_pairs={{0,64},{64,128},{128,192},{192,0},{1,65},{65,129},{129,193},{193,1... | collective-permute-start | bytes 221192 | tf_op jit(solution)/shard_map/ppermute | solution.py:331
  18.2 2.4 %collective-permute-start.1 = (f32[2,72,128]{2,1,0:T(8,128)S(1)}, f32[2,72,128]{2,1,0:T(8,128)S(1)}, u32[]{:S(2)}, u32[]{:S(2)}) collective-permute-start(f32[2,72,128]{2,1,0:T(8,128)S(1)} %get-tuple-element.63), channel_id=1, source_target_pairs={{0,128},{64,192},{128,0},{192,64},{1,129},{65,193},{129,1},{193,65... | collective-permute-start | bytes 221192 | tf_op jit(solution)/shard_map/ppermute | solution.py:331
  20.6 1.1 %collective-permute-start.2 = (f32[2,72,128]{2,1,0:T(8,128)S(1)}, f32[2,72,128]{2,1,0:T(8,128)S(1)}, u32[]{:S(2)}, u32[]{:S(2)}) collective-permute-start(f32[2,72,128]{2,1,0:T(8,128)S(1)} %get-tuple-element.64), channel_id=1, source_target_pairs={{0,192},{64,0},{128,64},{192,128},{1,193},{65,1},{129,65},{193,129... | collective-permute-start | bytes 221192 | tf_op jit(solution)/shard_map/ppermute | solution.py:331
  21.8 0.5 collective-permute-done.refs_1_
  22.3 4.3 %collective-permute-done.1.refs_2_ = f32[2,72,128]{2,1,0:T(8,128)S(1)} collective-permute-done((f32[2,72,128]{2,1,0:T(8,128)S(1)}, f32[2,72,128]{2,1,0:T(8,128)S(1)}, u32[]{:S(2)}, u32[]{:S(2)}) %collective-permute-start.1) | collective-permute-done | bytes 73760 | tf_op jit(solution)/shard_map/ppermute | solution.py:331
  26.6 0.0 collective-permute-done.2.refs_3_
  26.6 2.3 %collective-permute-start.3 = (f32[4,72,128]{2,1,0:T(8,128)S(1)}, f32[4,72,128]{2,1,0:T(8,128)S(1)}, u32[]{:S(2)}, u32[]{:S(2)}) collective-permute-start(f32[4,72,128]{2,1,0:T(8,128)S(1)} %pad_maximum_fusion.2), channel_id=1, source_target_pairs={{0,8},{8,0},{16,24},{24,16},{32,40},{40,32},{48,56},{56,48},{1,9},... | collective-permute-start | bytes 442376 | tf_op jit(solution)/shard_map/ppermute | solution.py:336
  29.0 0.0 copy-done
  29.0 0.0 copy-done.2
  29.0 0.0 copy-done.3
  29.0 0.0 copy-done.4
  29.0 0.0 copy-done.10
  29.0 0.0 copy-done.12
  29.0 0.0 copy-done.13
  29.0 0.0 copy-done.14
  29.0 2.3 %intra.1 = (f32[256,1024]{1,0:T(8,128)S(1)}, f32[256,8]{1,0:T(8,128)S(1)}, f32[64,1024]{1,0:T(8,128)S(1)}, f32[64,8]{1,0:T(8,128)S(1)}) custom-call(s32[4]{0:T(128)S(1)} %copy-done.14, s32[1]{0:T(128)} %bitcast.20.here, bf16[256,1024]{1,0:T(8,128)(2,1)S(1)} %copy-done, bf16[256,1024]{1,0:T(8,128)(2,1)S(1)} %copy-done.12, bf16[256,1024]{1,0:T(8,128)(2,1)S(1)} %copy-done.10, ...), custom_call_target="tpu_custom_call" | custom-call | flops 6000000000 | bytes 18000000 | tf_op jit(solution)/shard_map/intra/pallas_call | solution.py:410
  31.3 0.0 copy-start.7
  31.3 0.7 copy-done.7
  32.0 14.1 %collective-permute-done.3.refs_4_ = f32[4,72,128]{2,1,0:T(8,128)S(1)} collective-permute-done((f32[4,72,128]{2,1,0:T(8,128)S(1)}, f32[4,72,128]{2,1,0:T(8,128)S(1)}, u32[]{:S(2)}, u32[]{:S(2)}) %collective-permute-start.3) | collective-permute-done | bytes 147488 | tf_op jit(solution)/shard_map/ppermute | solution.py:336
  46.1 0.0 all-to-all-done.1.give_ref
  46.8 1.4 %scan.1 = (f32[32,32,128]{2,1,0:T(8,128)}, f32[4,32,128]{2,1,0:T(8,128)S(1)}) custom-call(s32[4]{0:T(128)S(1)} %copy-done.14, f32[32,72,128]{2,1,0:T(8,128)S(1)} %all-to-all-done.1.give_ref, f32[3,32,128]{2,1,0:T(8,128)S(1)} %get-tuple-element.121.extra_ref), custom_call_target="tpu_custom_call" | custom-call | flops 2000000000 | bytes 6000000 | tf_op jit(solution)/shard_map/scan/pallas_call | solution.py:433
  48.2 1.7 %collective-permute-start.4 = (f32[4,32,128]{2,1,0:T(8,128)S(1)}, f32[4,32,128]{2,1,0:T(8,128)S(1)}, u32[]{:S(2)}, u32[]{:S(2)}) collective-permute-start(f32[4,32,128]{2,1,0:T(8,128)S(1)} %get-tuple-element.79.refs_5_), channel_id=1, source_target_pairs={{0,16},{8,24},{16,32},{24,40},{32,48},{40,56},{48,0},{56,8},{1,17}... | collective-permute-start | bytes 196616 | tf_op jit(solution)/shard_map/ppermute | solution.py:331
  49.9 3.5 %collective-permute-start.5 = (f32[4,32,128]{2,1,0:T(8,128)S(1)}, f32[4,32,128]{2,1,0:T(8,128)S(1)}, u32[]{:S(2)}, u32[]{:S(2)}) collective-permute-start(f32[4,32,128]{2,1,0:T(8,128)S(1)} %get-tuple-element.79.refs_5_), channel_id=1, source_target_pairs={{0,32},{8,40},{16,48},{24,56},{32,0},{40,8},{48,16},{56,24},{1,33}... | collective-permute-start | bytes 196616 | tf_op jit(solution)/shard_map/ppermute | solution.py:331
  53.5 3.3 %collective-permute-start.6 = (f32[4,32,128]{2,1,0:T(8,128)S(1)}, f32[4,32,128]{2,1,0:T(8,128)S(1)}, u32[]{:S(2)}, u32[]{:S(2)}) collective-permute-start(f32[4,32,128]{2,1,0:T(8,128)S(1)} %get-tuple-element.79.refs_5_), channel_id=1, source_target_pairs={{0,48},{8,56},{16,0},{24,8},{32,16},{40,24},{48,32},{56,40},{1,49}... | collective-permute-start | bytes 196616 | tf_op jit(solution)/shard_map/ppermute | solution.py:331
  56.8 0.0 collective-permute-done.4.refs_6_
  56.8 1.1 %collective-permute-done.5.refs_7_ = f32[4,32,128]{2,1,0:T(8,128)S(1)} collective-permute-done((f32[4,32,128]{2,1,0:T(8,128)S(1)}, f32[4,32,128]{2,1,0:T(8,128)S(1)}, u32[]{:S(2)}, u32[]{:S(2)}) %collective-permute-start.5) | collective-permute-done | bytes 65568 | tf_op jit(solution)/shard_map/ppermute | solution.py:331
  57.9 1.0 %collective-permute-done.6.refs_8_ = f32[4,32,128]{2,1,0:T(8,128)S(1)} collective-permute-done((f32[4,32,128]{2,1,0:T(8,128)S(1)}, f32[4,32,128]{2,1,0:T(8,128)S(1)}, u32[]{:S(2)}, u32[]{:S(2)}) %collective-permute-start.6) | collective-permute-done | bytes 65568 | tf_op jit(solution)/shard_map/ppermute | solution.py:331
  58.9 8.4 %all-to-all-start.2 = ((f32[32,32,128]{2,1,0:T(8,128)}), f32[32,32,128]{2,1,0:T(8,128)S(1)}, u32[]{:S(2)}, u32[]{:S(2)}) async-start(f32[32,32,128]{2,1,0:T(8,128)} %get-tuple-element.69), calls=%async_computation.2 | async-start | bytes 1048576 | tf_op jit(solution)/shard_map/all_to_all | solution.py:340
  67.3 0.5 project.1
  67.8 2.7 %collective-permute-start.7 = (f32[2,64,128]{2,1,0:T(8,128)S(1)}, f32[2,64,128]{2,1,0:T(8,128)S(1)}, u32[]{:S(2)}, u32[]{:S(2)}) collective-permute-start(f32[2,64,128]{2,1,0:T(8,128)S(1)} %get-tuple-element.84), channel_id=1, source_target_pairs={{0,192},{64,0},{128,64},{192,128},{1,193},{65,1},{129,65},{193,129... | collective-permute-start | bytes 196616 | tf_op jit(solution)/shard_map/ppermute | solution.py:331
  70.5 0.5 collective-permute-start.8
  71.0 0.6 collective-permute-start.9
  71.6 2.3 %collective-permute-done.7.refs_1_ = f32[2,64,128]{2,1,0:T(8,128)S(1)} collective-permute-done((f32[2,64,128]{2,1,0:T(8,128)S(1)}, f32[2,64,128]{2,1,0:T(8,128)S(1)}, u32[]{:S(2)}, u32[]{:S(2)}) %collective-permute-start.7) | collective-permute-done | bytes 65568 | tf_op jit(solution)/shard_map/ppermute | solution.py:331
  73.9 2.1 %collective-permute-done.8.refs_2_ = f32[2,64,128]{2,1,0:T(8,128)S(1)} collective-permute-done((f32[2,64,128]{2,1,0:T(8,128)S(1)}, f32[2,64,128]{2,1,0:T(8,128)S(1)}, u32[]{:S(2)}, u32[]{:S(2)}) %collective-permute-start.8) | collective-permute-done | bytes 65568 | tf_op jit(solution)/shard_map/ppermute | solution.py:331
  76.0 1.3 %collective-permute-done.9.refs_3_ = f32[2,64,128]{2,1,0:T(8,128)S(1)} collective-permute-done((f32[2,64,128]{2,1,0:T(8,128)S(1)}, f32[2,64,128]{2,1,0:T(8,128)S(1)}, u32[]{:S(2)}, u32[]{:S(2)}) %collective-permute-start.9) | collective-permute-done | bytes 65568 | tf_op jit(solution)/shard_map/ppermute | solution.py:331
  77.3 0.0 copy-start.5
  77.3 1.4 %collective-permute-start.10 = (f32[4,64,128]{2,1,0:T(8,128)S(1)}, f32[4,64,128]{2,1,0:T(8,128)S(1)}, u32[]{:S(2)}, u32[]{:S(2)}) collective-permute-start(f32[4,64,128]{2,1,0:T(8,128)S(1)} %pad_maximum_fusion.3), channel_id=1, source_target_pairs={{0,8},{8,0},{16,24},{24,16},{32,40},{40,32},{48,56},{56,48},{1,9},... | collective-permute-start | bytes 393224 | tf_op jit(solution)/shard_map/ppermute | solution.py:336
  78.6 3.9 %collective-permute-done.10.refs_4_ = f32[4,64,128]{2,1,0:T(8,128)S(1)} collective-permute-done((f32[4,64,128]{2,1,0:T(8,128)S(1)}, f32[4,64,128]{2,1,0:T(8,128)S(1)}, u32[]{:S(2)}, u32[]{:S(2)}) %collective-permute-start.10) | collective-permute-done | bytes 131104 | tf_op jit(solution)/shard_map/ppermute | solution.py:336
  82.5 0.0 all-to-all-done.2.back_ref
  82.5 0.0 copy-start.8
  82.5 0.9 copy-done.8
  83.5 0.6 mixed.1
  84.1 12.7 %all_to_all.19.sums_ref = f32[8,4,128]{2,1,0:T(4,128)S(1)} all-to-all(f32[8,4,128]{2,1,0:T(4,128)S(1)} %get-tuple-element.87), channel_id=1, replica_groups=mesh['seq_0'=4,'seq_1'=8,'head'=8] {'head'}, dimensions={0} | all-to-all | bytes 32768 | tf_op jit(solution)/shard_map/all_to_all | solution.py:340
  96.8 0.0 copy-done.5
  96.8 1.1 %final.1 = (bf16[256,1024]{1,0:T(8,128)(2,1)}, bf16[4,16,1024]{2,1,0:T(8,128)(2,1)}) custom-call(f32[8,4,128]{2,1,0:T(4,128)S(1)} %all_to_all.19.sums_ref, f32[256,1024]{1,0:T(8,128)S(1)} %get-tuple-element.88.mixed_ref, f32[64,1024]{1,0:T(8,128)S(1)} %get-tuple-element.89.dec_ref, f32[1,1024]{1,0:T(1,128)S(1)} %bitcast.47), custom_call_target="tpu_custom_call" | custom-call | flops 2000000000 | bytes 6000000 | tf_op jit(solution)/shard_map/final/pallas_call | solution.py:471
  (12 shorter events, 0.1 us)
Async XLA Ops:
  4.1 12.0 %copy-start.1 = (bf16[4,16,1024]{2,1,0:T(8,128)(2,1)S(1)}, bf16[4,16,1024]{2,1,0:T(8,128)(2,1)}, u32[]{:S(2)}) copy-start(bf16[4,16,1024]{2,1,0:T(8,128)(2,1)} %query_ref.4) | copy-start | bytes 393220
  4.1 12.0 %copy-start.6 = (s32[16]{0:T(128)S(1)}, s32[16]{0:T(128)}, u32[]{:S(2)}) copy-start(s32[16]{0:T(128)} %rows.1) | copy-start | bytes 196
  4.1 42.0 %all-to-all-start.1 = ((f32[32,72,128]{2,1,0:T(8,128)}), f32[32,72,128]{2,1,0:T(8,128)S(1)}, u32[]{:S(2)}, u32[]{:S(2)}) async-start(f32[32,72,128]{2,1,0:T(8,128)} %get-tuple-element.55), calls=%async_computation.1 | async-start | bytes 2359296 | tf_op jit(solution)/shard_map/all_to_all | solution.py:340
  16.2 12.8 %copy-start = (bf16[256,1024]{1,0:T(8,128)(2,1)S(1)}, bf16[256,1024]{1,0:T(8,128)(2,1)}, u32[]{:S(2)}) copy-start(bf16[256,1024]{1,0:T(8,128)(2,1)} %query_ref.5) | copy-start | bytes 1572868
  16.2 12.8 %copy-start.2 = (bf16[4,16,1024]{2,1,0:T(8,128)(2,1)S(1)}, bf16[4,16,1024]{2,1,0:T(8,128)(2,1)}, u32[]{:S(2)}) copy-start(bf16[4,16,1024]{2,1,0:T(8,128)(2,1)} %sk_ref.1) | copy-start | bytes 393220
  16.2 12.8 %copy-start.3 = (bf16[4,16,1024]{2,1,0:T(8,128)(2,1)S(1)}, bf16[4,16,1024]{2,1,0:T(8,128)(2,1)}, u32[]{:S(2)}) copy-start(bf16[4,16,1024]{2,1,0:T(8,128)(2,1)} %sv_ref.1) | copy-start | bytes 393220
  16.2 12.8 %copy-start.4 = (f32[4,16,8]{1,2,0:T(8,128)S(1)}, f32[4,16,8]{1,2,0:T(8,128)}, u32[]{:S(2)}) copy-start(f32[4,16,8]{1,2,0:T(8,128)} %param.22) | copy-start | bytes 6148
  16.2 12.8 %copy-start.10 = (bf16[256,1024]{1,0:T(8,128)(2,1)S(1)}, bf16[256,1024]{1,0:T(8,128)(2,1)}, u32[]{:S(2)}) copy-start(bf16[256,1024]{1,0:T(8,128)(2,1)} %value_ref.3) | copy-start | bytes 1572868
  16.2 12.8 %copy-start.12 = (bf16[256,1024]{1,0:T(8,128)(2,1)S(1)}, bf16[256,1024]{1,0:T(8,128)(2,1)}, u32[]{:S(2)}) copy-start(bf16[256,1024]{1,0:T(8,128)(2,1)} %key_ref.3) | copy-start | bytes 1572868
  16.2 12.8 %copy-start.13 = (f32[256,8]{0,1:T(8,128)S(1)}, f32[256,8]{0,1:T(8,128)}, u32[]{:S(2)}) copy-start(f32[256,8]{0,1:T(8,128)} %param.16) | copy-start | bytes 24580
  16.3 12.8 %copy-start.14 = (s32[4]{0:T(128)S(1)}, s32[4]{0:T(128)}, u32[]{:S(2)}) copy-start(s32[4]{0:T(128)} %lens.5) | copy-start | bytes 52
  16.9 5.4 %collective-permute-start = (f32[2,72,128]{2,1,0:T(8,128)S(1)}, f32[2,72,128]{2,1,0:T(8,128)S(1)}, u32[]{:S(2)}, u32[]{:S(2)}) collective-permute-start(f32[2,72,128]{2,1,0:T(8,128)S(1)} %get-tuple-element.62), channel_id=1, source_target_pairs={{0,64},{64,128},{128,192},{192,0},{1,65},{65,129},{129,193},{193,1... | collective-permute-start | bytes 221192 | tf_op jit(solution)/shard_map/ppermute | solution.py:331
  18.2 8.4 %collective-permute-start.1 = (f32[2,72,128]{2,1,0:T(8,128)S(1)}, f32[2,72,128]{2,1,0:T(8,128)S(1)}, u32[]{:S(2)}, u32[]{:S(2)}) collective-permute-start(f32[2,72,128]{2,1,0:T(8,128)S(1)} %get-tuple-element.63), channel_id=1, source_target_pairs={{0,128},{64,192},{128,0},{192,64},{1,129},{65,193},{129,1},{193,65... | collective-permute-start | bytes 221192 | tf_op jit(solution)/shard_map/ppermute | solution.py:331
  20.6 6.0 %collective-permute-start.2 = (f32[2,72,128]{2,1,0:T(8,128)S(1)}, f32[2,72,128]{2,1,0:T(8,128)S(1)}, u32[]{:S(2)}, u32[]{:S(2)}) collective-permute-start(f32[2,72,128]{2,1,0:T(8,128)S(1)} %get-tuple-element.64), channel_id=1, source_target_pairs={{0,192},{64,0},{128,64},{192,128},{1,193},{65,1},{129,65},{193,129... | collective-permute-start | bytes 221192 | tf_op jit(solution)/shard_map/ppermute | solution.py:331
  26.6 19.4 %collective-permute-start.3 = (f32[4,72,128]{2,1,0:T(8,128)S(1)}, f32[4,72,128]{2,1,0:T(8,128)S(1)}, u32[]{:S(2)}, u32[]{:S(2)}) collective-permute-start(f32[4,72,128]{2,1,0:T(8,128)S(1)} %pad_maximum_fusion.2), channel_id=1, source_target_pairs={{0,8},{8,0},{16,24},{24,16},{32,40},{40,32},{48,56},{56,48},{1,9},... | collective-permute-start | bytes 442376 | tf_op jit(solution)/shard_map/ppermute | solution.py:336
  31.3 0.7 copy-start.7
  48.2 8.6 %collective-permute-start.4 = (f32[4,32,128]{2,1,0:T(8,128)S(1)}, f32[4,32,128]{2,1,0:T(8,128)S(1)}, u32[]{:S(2)}, u32[]{:S(2)}) collective-permute-start(f32[4,32,128]{2,1,0:T(8,128)S(1)} %get-tuple-element.79.refs_5_), channel_id=1, source_target_pairs={{0,16},{8,24},{16,32},{24,40},{32,48},{40,56},{48,0},{56,8},{1,17}... | collective-permute-start | bytes 196616 | tf_op jit(solution)/shard_map/ppermute | solution.py:331
  49.9 8.0 %collective-permute-start.5 = (f32[4,32,128]{2,1,0:T(8,128)S(1)}, f32[4,32,128]{2,1,0:T(8,128)S(1)}, u32[]{:S(2)}, u32[]{:S(2)}) collective-permute-start(f32[4,32,128]{2,1,0:T(8,128)S(1)} %get-tuple-element.79.refs_5_), channel_id=1, source_target_pairs={{0,32},{8,40},{16,48},{24,56},{32,0},{40,8},{48,16},{56,24},{1,33}... | collective-permute-start | bytes 196616 | tf_op jit(solution)/shard_map/ppermute | solution.py:331
  53.5 5.4 %collective-permute-start.6 = (f32[4,32,128]{2,1,0:T(8,128)S(1)}, f32[4,32,128]{2,1,0:T(8,128)S(1)}, u32[]{:S(2)}, u32[]{:S(2)}) collective-permute-start(f32[4,32,128]{2,1,0:T(8,128)S(1)} %get-tuple-element.79.refs_5_), channel_id=1, source_target_pairs={{0,48},{8,56},{16,0},{24,8},{32,16},{40,24},{48,32},{56,40},{1,49}... | collective-permute-start | bytes 196616 | tf_op jit(solution)/shard_map/ppermute | solution.py:331
  58.9 23.6 %all-to-all-start.2 = ((f32[32,32,128]{2,1,0:T(8,128)}), f32[32,32,128]{2,1,0:T(8,128)S(1)}, u32[]{:S(2)}, u32[]{:S(2)}) async-start(f32[32,32,128]{2,1,0:T(8,128)} %get-tuple-element.69), calls=%async_computation.2 | async-start | bytes 1048576 | tf_op jit(solution)/shard_map/all_to_all | solution.py:340
  67.8 6.1 %collective-permute-start.7 = (f32[2,64,128]{2,1,0:T(8,128)S(1)}, f32[2,64,128]{2,1,0:T(8,128)S(1)}, u32[]{:S(2)}, u32[]{:S(2)}) collective-permute-start(f32[2,64,128]{2,1,0:T(8,128)S(1)} %get-tuple-element.84), channel_id=1, source_target_pairs={{0,192},{64,0},{128,64},{192,128},{1,193},{65,1},{129,65},{193,129... | collective-permute-start | bytes 196616 | tf_op jit(solution)/shard_map/ppermute | solution.py:331
  70.5 5.5 %collective-permute-start.8 = (f32[2,64,128]{2,1,0:T(8,128)S(1)}, f32[2,64,128]{2,1,0:T(8,128)S(1)}, u32[]{:S(2)}, u32[]{:S(2)}) collective-permute-start(f32[2,64,128]{2,1,0:T(8,128)S(1)} %get-tuple-element.85), channel_id=1, source_target_pairs={{0,128},{64,192},{128,0},{192,64},{1,129},{65,193},{129,1},{193,65... | collective-permute-start | bytes 196616 | tf_op jit(solution)/shard_map/ppermute | solution.py:331
  71.0 6.2 %collective-permute-start.9 = (f32[2,64,128]{2,1,0:T(8,128)S(1)}, f32[2,64,128]{2,1,0:T(8,128)S(1)}, u32[]{:S(2)}, u32[]{:S(2)}) collective-permute-start(f32[2,64,128]{2,1,0:T(8,128)S(1)} %get-tuple-element.86), channel_id=1, source_target_pairs={{0,64},{64,128},{128,192},{192,0},{1,65},{65,129},{129,193},{193,1... | collective-permute-start | bytes 196616 | tf_op jit(solution)/shard_map/ppermute | solution.py:331
  77.3 19.5 %copy-start.5 = (f32[1024]{0:T(1024)S(1)}, f32[1024]{0:T(1024)}, u32[]{:S(2)}) copy-start(f32[1024]{0:T(1024)} %param.17) | copy-start | bytes 12292
  77.3 5.2 %collective-permute-start.10 = (f32[4,64,128]{2,1,0:T(8,128)S(1)}, f32[4,64,128]{2,1,0:T(8,128)S(1)}, u32[]{:S(2)}, u32[]{:S(2)}) collective-permute-start(f32[4,64,128]{2,1,0:T(8,128)S(1)} %pad_maximum_fusion.3), channel_id=1, source_target_pairs={{0,8},{8,0},{16,24},{24,16},{32,40},{40,32},{48,56},{56,48},{1,9},... | collective-permute-start | bytes 393224 | tf_op jit(solution)/shard_map/ppermute | solution.py:336
  82.5 1.0 copy-start.8

commit v8 on v7

--- a/solution.py
+++ b/solution.py
@@ -37,6 +37,7 @@
 
 SMEM = pl.BlockSpec(memory_space=pltpu.SMEM)
 VMEM = pl.BlockSpec(memory_space=pltpu.VMEM)
+PLACE = pl.BlockSpec(memory_space=pl.ANY)
 
 
 def params(mib=12):
@@ -88,7 +89,21 @@
     return (head // 2) * NZ + 2 * quarter + head % 2
 
 
-def send_kernel(lens, here, key_ref, value_ref, logd_ref, out_ref, flag_ref, cum_ref):
+def send_kernel(
+    lens, here, key_in, value_in, logd_in, out, flag_ref,
+    key_ref, value_ref, logd_ref, out_ref, cum_ref, sems,
+):
+    moves = [pltpu.make_async_copy(logd_in, logd_ref, sems.at[0])]
+    half = HEADS * HDIM // 2
+    for k in range(2):
+        cols = slice(k * half, (k + 1) * half)
+        moves.append(pltpu.make_async_copy(key_in.at[:, cols], key_ref.at[:, cols], sems.at[1 + 2 * k]))
+        moves.append(
+            pltpu.make_async_copy(value_in.at[:, cols], value_ref.at[:, cols], sems.at[2 + 2 * k])
+        )
+    for move in moves:
+        move.start()
+    moves[0].wait()
     first = here[0] * BLOCK
     ends = bounds(lens)
     front = entry_seg(first, ends)
@@ -116,33 +131,46 @@
             crowded = crowded | (same & (ends[p] % BLOCK != 0)).astype(jnp.int32)
     flag_ref[0] = crowded
 
-    def emit(factor, row):
-        for h in range(HEADS):
-            cols = slice(h * HDIM, (h + 1) * HDIM)
-            keyed = (key_ref[:, cols].astype(F32) * factor[:, h : h + 1]).astype(BF)
-            total = contract_rows(keyed, value_ref[:, cols])
+    reached = cum_ref[pl.ds(spot, 1), :]
+    taken = (tok <= spot) & (seg == found)
+    tail = jnp.where(taken, jnp.exp(jnp.where(taken, reached - cum, 0.0)), 0.0)
+
+    def emit(h, factor, row):
+        cols = slice(h * HDIM, (h + 1) * HDIM)
+        keyed = (key_ref[:, cols].astype(F32) * factor[:, h : h + 1]).astype(BF)
+        total = contract_rows(keyed, value_ref[:, cols])
+        for g in range(NQ):
+            out_ref[owner(h, g), row : row + QUART, :] = total[g * QUART : (g + 1) * QUART, :]
+
+    leaving = []
+    for x in range(NX):
+        if x % 2 == 0:
+            moves[1 + x].wait()
+            moves[2 + x].wait()
+        for h in (2 * x, 2 * x + 1):
+            emit(h, keep, 0)
+            scal = jnp.concatenate(
+                [jnp.broadcast_to(f[:, h : h + 1], (1, HDIM)) for f in factors]
+                + [jnp.zeros((8 - len(factors), HDIM), F32)],
+                axis=0,
+            )
             for g in range(NQ):
-                out_ref[owner(h, g), row : row + QUART, :] = total[g * QUART : (g + 1) * QUART, :]
-
-    emit(keep, 0)
-    for h in range(HEADS):
-        scal = jnp.concatenate(
-            [jnp.broadcast_to(f[:, h : h + 1], (1, HDIM)) for f in factors]
-            + [jnp.zeros((8 - len(factors), HDIM), F32)],
-            axis=0,
-        )
-        for g in range(NQ):
-            out_ref[owner(h, g), S0:GIVE, :] = scal
-
-    @pl.when(found < 0)
-    def _():
-        out_ref[:, T0:S0, :] = jnp.zeros((NDEV, QUART, HDIM), F32)
-
-    @pl.when(found >= 0)
-    def _():
-        reached = cum_ref[pl.ds(spot, 1), :]
-        taken = (tok <= spot) & (seg == found)
-        emit(jnp.where(taken, jnp.exp(jnp.where(taken, reached - cum, 0.0)), 0.0), T0)
+                out_ref[owner(h, g), S0:GIVE, :] = scal
+
+        @pl.when(found < 0)
+        def _(x=x):
+            out_ref[x * NZ : (x + 1) * NZ, T0:S0, :] = jnp.zeros((NZ, QUART, HDIM), F32)
+
+        @pl.when(found >= 0)
+        def _(x=x):
+            for h in (2 * x, 2 * x + 1):
+                emit(h, tail, T0)
+
+        group = slice(x * NZ, (x + 1) * NZ)
+        leaving.append(pltpu.make_async_copy(out_ref.at[group], out.at[group], sems.at[5 + x]))
+        leaving[-1].start()
+    for move in leaving:
+        move.wait()
 
 
 def mate_head(here, dx, db):
@@ -164,8 +192,7 @@
 
 
 def intra_kernel(
-    lens, here, query_ref, key_ref, value_ref, logd_ref, sq_ref, sk_ref, sv_ref, sd_ref,
-    intra_ref, carried_ref, local_ref, scarried_ref,
+    lens, here, query_ref, key_ref, value_ref, logd_ref, intra_ref, carried_ref
 ):
     first = here[0] * BLOCK
     ends = bounds(lens)
@@ -186,7 +213,9 @@
         weights = (scores * factor).astype(BF)
         intra_ref[:, cols] = jnp.dot(weights, value_ref[:, cols], preferred_element_type=F32)
 
-    n = STEPS * ROWS_DEV
+
+def local_kernel(sq_ref, sk_ref, sv_ref, sd_ref, local_ref, scarried_ref):
+    n = NROW
     a = lax.broadcasted_iota(jnp.int32, (n, n), 0)
     b = lax.broadcasted_iota(jnp.int32, (n, n), 1)
     same = (b <= a) & ((a - b) % ROWS_DEV == 0)
@@ -386,9 +415,16 @@
     give, crowded = pl.pallas_call(
         send_kernel,
         out_shape=(shape(NDEV, GIVE, HDIM), shape(1, dtype=jnp.int32)),
-        in_specs=[SMEM] * 2 + [VMEM] * 3,
-        out_specs=(VMEM, SMEM),
-        scratch_shapes=[pltpu.VMEM((BLOCK, HEADS), F32)],
+        in_specs=[SMEM] * 2 + [PLACE] * 3,
+        out_specs=(PLACE, SMEM),
+        scratch_shapes=[
+            pltpu.VMEM((BLOCK, width), BF),
+            pltpu.VMEM((BLOCK, width), BF),
+            pltpu.VMEM((HEADS, BLOCK), F32),
+            pltpu.VMEM((NDEV, GIVE, HDIM), F32),
+            pltpu.VMEM((BLOCK, HEADS), F32),
+            pltpu.SemaphoreType.DMA((5 + NX,)),
+        ],
         compiler_params=params(),
         cost_estimate=cost(3),
         name="send",
@@ -407,23 +443,18 @@
     queries = [queries[0]] + [shift(queries[d], "seq_0", NX, d) for d in range(1, NX)]
     far_queries = over_pair(queries)
 
-    intra, carried, local_dec, scarried = pl.pallas_call(
+    intra, carried = pl.pallas_call(
         intra_kernel,
-        out_shape=(shape(BLOCK, width), shape(BLOCK, HEADS), shape(n, width), shape(n, HEADS)),
-        in_specs=[SMEM] * 2 + [VMEM] * 8,
-        out_specs=(VMEM,) * 4,
-        compiler_params=params(),
-        cost_estimate=cost(6),
+        out_shape=(shape(BLOCK, width), shape(BLOCK, HEADS)),
+        in_specs=[SMEM] * 2 + [VMEM] * 4,
+        out_specs=(VMEM,) * 2,
+        compiler_params=params(),
+        cost_estimate=cost(3),
         name="intra",
-    )(
-        prompt_lengths, here, query_in, key_in, value_in, logd,
-        step_query, step_key, step_value, step_decay.transpose(0, 2, 1),
-    )
-
-    given, intra, carried, local_dec, scarried, crowded, queries, far_queries = (
-        lax.optimization_barrier(
-            (given, intra, carried, local_dec, scarried, crowded, queries, far_queries)
-        )
+    )(prompt_lengths, here, query_in, key_in, value_in, logd)
+
+    given, intra, carried, crowded, queries, far_queries = lax.optimization_barrier(
+        (given, intra, carried, crowded, queries, far_queries)
     )
     extra = lax.cond(
         crowded[0] > 0,
@@ -440,8 +471,18 @@
         name="scan",
     )(prompt_lengths, given, extra)
     slabs = [own] + [shift(own, "seq_1", NZ, 2 * d) for d in range(1, NQ)]
-    entry, slabs = lax.optimization_barrier((entry, slabs))
+    entry, slabs, step_key = lax.optimization_barrier((entry, slabs, step_key))
     back = exchange(entry, SEQ)
+
+    local_dec, scarried = pl.pallas_call(
+        local_kernel,
+        out_shape=(shape(n, width), shape(n, HEADS)),
+        in_specs=[VMEM] * 4,
+        out_specs=(VMEM,) * 2,
+        compiler_params=params(),
+        cost_estimate=cost(1),
+        name="local",
+    )(step_query, step_key, step_value, step_decay.transpose(0, 2, 1))
 
     products = pl.pallas_call(
         project_kernel,

time: 98.2 us -> 99.4 us (1.012)
  Pallas kernels: 9.85 us -> 11.6 us
  local copies, waits for them, and re-layouts: 1.76 us -> 0.72 us
    unnamed x26 -> x22, local copies, waits for them, and re-layouts: 1.73 us -> 0.07 us
    pallas_call x1, Pallas kernels: 3.47 us -> 4.6 us  [local(): pl.pallas_call(send_kernel, out_shape=(shape(NDEV, GIVE, HDIM), shape(1,...]
  transfers between devices with their start and end apart: 13 -> 13, of which waited for: 9 -> 9; matrix products, arithmetic and copies ran while one was open for 0% -> 0% of each run, Pallas kernels for 3% -> 4%
where the time goes in v8:
time: 99.4 us; the launch traced here: 98.9 us
  starting transfers between devices  41.3 us (42%)
  waiting for transfers between devices  31 us (31%)
  blocking collectives  12.7 us (13%)
  Pallas kernels  11.6 us (12%)
  between operations  1.48 us (1%)
    all_to_all x2, starting transfers between devices, exchange(): return lax.all_to_all(x, axis, split_axis=0, concat_axis=0, tiled=True)  20.4 us
    ppermute x2, waiting for transfers between devices, over_pair(): return lax.ppermute(both, 'seq_1', [(i, i ^ 1) for i in range(NZ)])  18.5 us
    ppermute x9, starting transfers between devices, shift(): return lax.ppermute(x, axis, [(i, (i + d) % size) for i in range(size)])  17.4 us
    all_to_all x1, blocking collectives, exchange(): return lax.all_to_all(x, axis, split_axis=0, concat_axis=0, tiled=True)  12.7 us
    ppermute x9, waiting for transfers between devices, shift(): return lax.ppermute(x, axis, [(i, (i + d) % size) for i in range(size)])  12.5 us
    pallas_call x1, Pallas kernels, local(): pl.pallas_call(send_kernel, out_shape=(shape(NDEV, GIVE, HDIM), shape(1,...  4.6 us
    ppermute x2, starting transfers between devices, over_pair(): return lax.ppermute(both, 'seq_1', [(i, i ^ 1) for i in range(NZ)])  3.6 us
  transfers between devices with their start and end apart: 13, of which 9 were waited for; matrix products, arithmetic and copies ran while one was open for 0% of the time, Pallas kernels for 4%

profile of v8, /device:TPU:1, one launch (start us, length us, event | category | flops | bytes accessed | tf_op | source)
XLA Modules:
  0.0 98.9 jit_solution(3941669931732790312)
XLA Ops:
  0.6 4.6 %send.1 = (f32[32,72,128]{2,1,0:T(8,128)}, s32[1]{0:T(128)}) custom-call(s32[4]{0:T(128)} %lens.5, s32[1]{0:T(128)} %bitcast.20.here, bf16[256,1024]{1,0:T(8,128)(2,1)} %key_ref.1, bf16[256,1024]{1,0:T(8,128)(2,1)} %value_ref.1, f32[8,256]{1,0:T(8,128)} %bitcast.55), custom_call_target="tpu_custom_call" | custom-call | flops 3000000000 | bytes 9000000 | tf_op jit(solution)/shard_map/send/pallas_call | solution.py:415
  5.2 0.0 copy-start.1
  5.3 0.0 copy-start.6
  5.3 12.0 %all-to-all-start.1 = ((f32[32,72,128]{2,1,0:T(8,128)}), f32[32,72,128]{2,1,0:T(8,128)S(1)}, u32[]{:S(2)}, u32[]{:S(2)}) async-start(f32[32,72,128]{2,1,0:T(8,128)} %get-tuple-element.54), calls=%async_computation.1 | async-start | bytes 2359296 | tf_op jit(solution)/shard_map/all_to_all | solution.py:369
  17.3 0.0 copy-done.1
  17.3 0.0 copy-done.6
  17.3 0.0 copy-start
  17.3 0.0 copy-start.8
  17.3 0.0 copy-start.10
  17.3 0.0 copy-start.11
  17.4 0.0 copy-start.12
  17.4 0.6 query.1
  18.0 1.3 %collective-permute-start = (f32[2,72,128]{2,1,0:T(8,128)S(1)}, f32[2,72,128]{2,1,0:T(8,128)S(1)}, u32[]{:S(2)}, u32[]{:S(2)}) collective-permute-start(f32[2,72,128]{2,1,0:T(8,128)S(1)} %get-tuple-element.59), channel_id=1, source_target_pairs={{0,64},{64,128},{128,192},{192,0},{1,65},{65,129},{129,193},{193,1... | collective-permute-start | bytes 221192 | tf_op jit(solution)/shard_map/ppermute | solution.py:360
  19.3 2.4 %collective-permute-start.1 = (f32[2,72,128]{2,1,0:T(8,128)S(1)}, f32[2,72,128]{2,1,0:T(8,128)S(1)}, u32[]{:S(2)}, u32[]{:S(2)}) collective-permute-start(f32[2,72,128]{2,1,0:T(8,128)S(1)} %get-tuple-element.60), channel_id=1, source_target_pairs={{0,128},{64,192},{128,0},{192,64},{1,129},{65,193},{129,1},{193,65... | collective-permute-start | bytes 221192 | tf_op jit(solution)/shard_map/ppermute | solution.py:360
  21.7 1.1 %collective-permute-start.2 = (f32[2,72,128]{2,1,0:T(8,128)S(1)}, f32[2,72,128]{2,1,0:T(8,128)S(1)}, u32[]{:S(2)}, u32[]{:S(2)}) collective-permute-start(f32[2,72,128]{2,1,0:T(8,128)S(1)} %get-tuple-element.61), channel_id=1, source_target_pairs={{0,192},{64,0},{128,64},{192,128},{1,193},{65,1},{129,65},{193,129... | collective-permute-start | bytes 221192 | tf_op jit(solution)/shard_map/ppermute | solution.py:360
  22.9 0.6 collective-permute-done.refs_1_
  23.4 4.3 %collective-permute-done.1.refs_2_ = f32[2,72,128]{2,1,0:T(8,128)S(1)} collective-permute-done((f32[2,72,128]{2,1,0:T(8,128)S(1)}, f32[2,72,128]{2,1,0:T(8,128)S(1)}, u32[]{:S(2)}, u32[]{:S(2)}) %collective-permute-start.1) | collective-permute-done | bytes 73760 | tf_op jit(solution)/shard_map/ppermute | solution.py:360
  27.7 0.0 collective-permute-done.2.refs_3_
  27.7 2.3 %collective-permute-start.3 = (f32[4,72,128]{2,1,0:T(8,128)S(1)}, f32[4,72,128]{2,1,0:T(8,128)S(1)}, u32[]{:S(2)}, u32[]{:S(2)}) collective-permute-start(f32[4,72,128]{2,1,0:T(8,128)S(1)} %pad_maximum_fusion.2), channel_id=1, source_target_pairs={{0,8},{8,0},{16,24},{24,16},{32,40},{40,32},{48,56},{56,48},{1,9},... | collective-permute-start | bytes 442376 | tf_op jit(solution)/shard_map/ppermute | solution.py:365
  30.0 0.0 copy-done
  30.0 0.0 copy-done.8
  30.0 0.0 copy-done.10
  30.0 0.0 copy-done.11
  30.1 0.0 copy-done.12
  30.1 1.9 %intra.1 = (f32[256,1024]{1,0:T(8,128)S(1)}, f32[256,8]{1,0:T(8,128)S(1)}) custom-call(s32[4]{0:T(128)S(1)} %copy-done.12, s32[1]{0:T(128)} %bitcast.20.here, bf16[256,1024]{1,0:T(8,128)(2,1)S(1)} %copy-done, bf16[256,1024]{1,0:T(8,128)(2,1)S(1)} %copy-done.10, bf16[256,1024]{1,0:T(8,128)(2,1)S(1)} %copy-done.8, f32[8,256]{1,0:T(8,128)S(1)} %bitcast.56), custom_call_target="tpu_custom_call" | custom-call | flops 3000000000 | bytes 9000000 | tf_op jit(solution)/shard_map/intra/pallas_call | solution.py:446
  32.0 15.3 %collective-permute-done.3.refs_4_ = f32[4,72,128]{2,1,0:T(8,128)S(1)} collective-permute-done((f32[4,72,128]{2,1,0:T(8,128)S(1)}, f32[4,72,128]{2,1,0:T(8,128)S(1)}, u32[]{:S(2)}, u32[]{:S(2)}) %collective-permute-start.3) | collective-permute-done | bytes 147488 | tf_op jit(solution)/shard_map/ppermute | solution.py:365
  47.2 0.0 all-to-all-done.1.give_ref
  47.9 0.6 conditional.1
  47.9 0.6 broadcast.53
  48.5 1.7 %scan.1 = (f32[32,32,128]{2,1,0:T(8,128)}, f32[4,32,128]{2,1,0:T(8,128)S(1)}) custom-call(s32[4]{0:T(128)S(1)} %copy-done.12, f32[32,72,128]{2,1,0:T(8,128)S(1)} %all-to-all-done.1.give_ref, f32[3,32,128]{2,1,0:T(8,128)} %get-tuple-element.119.extra_ref), custom_call_target="tpu_custom_call" | custom-call | flops 2000000000 | bytes 6000000 | tf_op jit(solution)/shard_map/scan/pallas_call | solution.py:464
  50.2 1.7 %collective-permute-start.4 = (f32[4,32,128]{2,1,0:T(8,128)S(1)}, f32[4,32,128]{2,1,0:T(8,128)S(1)}, u32[]{:S(2)}, u32[]{:S(2)}) collective-permute-start(f32[4,32,128]{2,1,0:T(8,128)S(1)} %get-tuple-element.77.refs_5_), channel_id=1, source_target_pairs={{0,16},{8,24},{16,32},{24,40},{32,48},{40,56},{48,0},{56,8},{1,17}... | collective-permute-start | bytes 196616 | tf_op jit(solution)/shard_map/ppermute | solution.py:360
  51.9 3.5 %collective-permute-start.5 = (f32[4,32,128]{2,1,0:T(8,128)S(1)}, f32[4,32,128]{2,1,0:T(8,128)S(1)}, u32[]{:S(2)}, u32[]{:S(2)}) collective-permute-start(f32[4,32,128]{2,1,0:T(8,128)S(1)} %get-tuple-element.77.refs_5_), channel_id=1, source_target_pairs={{0,32},{8,40},{16,48},{24,56},{32,0},{40,8},{48,16},{56,24},{1,33}... | collective-permute-start | bytes 196616 | tf_op jit(solution)/shard_map/ppermute | solution.py:360
  55.5 3.3 %collective-permute-start.6 = (f32[4,32,128]{2,1,0:T(8,128)S(1)}, f32[4,32,128]{2,1,0:T(8,128)S(1)}, u32[]{:S(2)}, u32[]{:S(2)}) collective-permute-start(f32[4,32,128]{2,1,0:T(8,128)S(1)} %get-tuple-element.77.refs_5_), channel_id=1, source_target_pairs={{0,48},{8,56},{16,0},{24,8},{32,16},{40,24},{48,32},{56,40},{1,49}... | collective-permute-start | bytes 196616 | tf_op jit(solution)/shard_map/ppermute | solution.py:360
  58.8 0.0 collective-permute-done.4.refs_6_
  58.8 1.1 %collective-permute-done.5.refs_7_ = f32[4,32,128]{2,1,0:T(8,128)S(1)} collective-permute-done((f32[4,32,128]{2,1,0:T(8,128)S(1)}, f32[4,32,128]{2,1,0:T(8,128)S(1)}, u32[]{:S(2)}, u32[]{:S(2)}) %collective-permute-start.5) | collective-permute-done | bytes 65568 | tf_op jit(solution)/shard_map/ppermute | solution.py:360
  59.9 1.0 %collective-permute-done.6.refs_8_ = f32[4,32,128]{2,1,0:T(8,128)S(1)} collective-permute-done((f32[4,32,128]{2,1,0:T(8,128)S(1)}, f32[4,32,128]{2,1,0:T(8,128)S(1)}, u32[]{:S(2)}, u32[]{:S(2)}) %collective-permute-start.6) | collective-permute-done | bytes 65568 | tf_op jit(solution)/shard_map/ppermute | solution.py:360
  60.9 8.4 %all-to-all-start.2 = ((f32[32,32,128]{2,1,0:T(8,128)}), f32[32,32,128]{2,1,0:T(8,128)S(1)}, u32[]{:S(2)}, u32[]{:S(2)}) async-start(f32[32,32,128]{2,1,0:T(8,128)} %get-tuple-element.66), calls=%async_computation.2 | async-start | bytes 1048576 | tf_op jit(solution)/shard_map/all_to_all | solution.py:369
  69.3 0.0 copy-start.2
  69.3 0.0 copy-start.3
  69.3 0.0 copy-start.4
  69.3 0.5 project.1
  69.8 2.7 %collective-permute-start.7 = (f32[2,64,128]{2,1,0:T(8,128)S(1)}, f32[2,64,128]{2,1,0:T(8,128)S(1)}, u32[]{:S(2)}, u32[]{:S(2)}) collective-permute-start(f32[2,64,128]{2,1,0:T(8,128)S(1)} %get-tuple-element.82), channel_id=1, source_target_pairs={{0,192},{64,0},{128,64},{192,128},{1,193},{65,1},{129,65},{193,129... | collective-permute-start | bytes 196616 | tf_op jit(solution)/shard_map/ppermute | solution.py:360
  72.6 0.5 collective-permute-start.8
  73.1 0.6 collective-permute-start.9
  73.7 2.2 %collective-permute-done.7.refs_1_ = f32[2,64,128]{2,1,0:T(8,128)S(1)} collective-permute-done((f32[2,64,128]{2,1,0:T(8,128)S(1)}, f32[2,64,128]{2,1,0:T(8,128)S(1)}, u32[]{:S(2)}, u32[]{:S(2)}) %collective-permute-start.7) | collective-permute-done | bytes 65568 | tf_op jit(solution)/shard_map/ppermute | solution.py:360
  75.9 2.1 %collective-permute-done.8.refs_2_ = f32[2,64,128]{2,1,0:T(8,128)S(1)} collective-permute-done((f32[2,64,128]{2,1,0:T(8,128)S(1)}, f32[2,64,128]{2,1,0:T(8,128)S(1)}, u32[]{:S(2)}, u32[]{:S(2)}) %collective-permute-start.8) | collective-permute-done | bytes 65568 | tf_op jit(solution)/shard_map/ppermute | solution.py:360
  78.0 1.3 %collective-permute-done.9.refs_3_ = f32[2,64,128]{2,1,0:T(8,128)S(1)} collective-permute-done((f32[2,64,128]{2,1,0:T(8,128)S(1)}, f32[2,64,128]{2,1,0:T(8,128)S(1)}, u32[]{:S(2)}, u32[]{:S(2)}) %collective-permute-start.9) | collective-permute-done | bytes 65568 | tf_op jit(solution)/shard_map/ppermute | solution.py:360
  79.3 1.3 %collective-permute-start.10 = (f32[4,64,128]{2,1,0:T(8,128)S(1)}, f32[4,64,128]{2,1,0:T(8,128)S(1)}, u32[]{:S(2)}, u32[]{:S(2)}) collective-permute-start(f32[4,64,128]{2,1,0:T(8,128)S(1)} %pad_maximum_fusion.3), channel_id=1, source_target_pairs={{0,8},{8,0},{16,24},{24,16},{32,40},{40,32},{48,56},{56,48},{1,9},... | collective-permute-start | bytes 393224 | tf_op jit(solution)/shard_map/ppermute | solution.py:365
  80.6 0.0 copy-done.2
  80.6 0.0 copy-done.3
  80.6 0.0 copy-done.4
  80.6 0.7 local.1
  81.3 3.2 %collective-permute-done.10.refs_4_ = f32[4,64,128]{2,1,0:T(8,128)S(1)} collective-permute-done((f32[4,64,128]{2,1,0:T(8,128)S(1)}, f32[4,64,128]{2,1,0:T(8,128)S(1)}, u32[]{:S(2)}, u32[]{:S(2)}) %collective-permute-start.10) | collective-permute-done | bytes 131104 | tf_op jit(solution)/shard_map/ppermute | solution.py:365
  84.5 0.0 all-to-all-done.2.back_ref
  84.5 0.0 copy-start.5
  84.5 0.6 mixed.1
  85.1 12.7 %all_to_all.19.sums_ref = f32[8,4,128]{2,1,0:T(4,128)S(1)} all-to-all(f32[8,4,128]{2,1,0:T(4,128)S(1)} %get-tuple-element.85), channel_id=1, replica_groups=mesh['seq_0'=4,'seq_1'=8,'head'=8] {'head'}, dimensions={0} | all-to-all | bytes 32768 | tf_op jit(solution)/shard_map/all_to_all | solution.py:369
  97.8 0.0 copy-done.5
  97.8 1.1 %final.1 = (bf16[256,1024]{1,0:T(8,128)(2,1)}, bf16[4,16,1024]{2,1,0:T(8,128)(2,1)}) custom-call(f32[8,4,128]{2,1,0:T(4,128)S(1)} %all_to_all.19.sums_ref, f32[256,1024]{1,0:T(8,128)S(1)} %get-tuple-element.86.mixed_ref, f32[64,1024]{1,0:T(8,128)S(1)} %get-tuple-element.87.dec_ref, f32[1,1024]{1,0:T(1,128)S(1)} %bitcast.47), custom_call_target="tpu_custom_call" | custom-call | flops 2000000000 | bytes 6000000 | tf_op jit(solution)/shard_map/final/pallas_call | solution.py:512
  (10 shorter events, 0.1 us)
Async XLA Ops:
  5.2 12.0 %copy-start.1 = (bf16[4,16,1024]{2,1,0:T(8,128)(2,1)S(1)}, bf16[4,16,1024]{2,1,0:T(8,128)(2,1)}, u32[]{:S(2)}) copy-start(bf16[4,16,1024]{2,1,0:T(8,128)(2,1)} %sq_ref.1) | copy-start | bytes 393220
  5.3 12.0 %copy-start.6 = (s32[16]{0:T(128)S(1)}, s32[16]{0:T(128)}, u32[]{:S(2)}) copy-start(s32[16]{0:T(128)} %rows.1) | copy-start | bytes 196
  5.3 41.9 %all-to-all-start.1 = ((f32[32,72,128]{2,1,0:T(8,128)}), f32[32,72,128]{2,1,0:T(8,128)S(1)}, u32[]{:S(2)}, u32[]{:S(2)}) async-start(f32[32,72,128]{2,1,0:T(8,128)} %get-tuple-element.54), calls=%async_computation.1 | async-start | bytes 2359296 | tf_op jit(solution)/shard_map/all_to_all | solution.py:369
  17.3 12.7 %copy-start = (bf16[256,1024]{1,0:T(8,128)(2,1)S(1)}, bf16[256,1024]{1,0:T(8,128)(2,1)}, u32[]{:S(2)}) copy-start(bf16[256,1024]{1,0:T(8,128)(2,1)} %query_ref.5) | copy-start | bytes 1572868
  17.3 12.7 %copy-start.8 = (bf16[256,1024]{1,0:T(8,128)(2,1)S(1)}, bf16[256,1024]{1,0:T(8,128)(2,1)}, u32[]{:S(2)}) copy-start(bf16[256,1024]{1,0:T(8,128)(2,1)} %value_ref.1) | copy-start | bytes 1572868
  17.3 12.7 %copy-start.10 = (bf16[256,1024]{1,0:T(8,128)(2,1)S(1)}, bf16[256,1024]{1,0:T(8,128)(2,1)}, u32[]{:S(2)}) copy-start(bf16[256,1024]{1,0:T(8,128)(2,1)} %key_ref.1) | copy-start | bytes 1572868
  17.3 12.7 %copy-start.11 = (f32[256,8]{0,1:T(8,128)S(1)}, f32[256,8]{0,1:T(8,128)}, u32[]{:S(2)}) copy-start(f32[256,8]{0,1:T(8,128)} %param.16) | copy-start | bytes 24580
  17.4 12.7 %copy-start.12 = (s32[4]{0:T(128)S(1)}, s32[4]{0:T(128)}, u32[]{:S(2)}) copy-start(s32[4]{0:T(128)} %lens.5) | copy-start | bytes 52
  18.0 5.5 %collective-permute-start = (f32[2,72,128]{2,1,0:T(8,128)S(1)}, f32[2,72,128]{2,1,0:T(8,128)S(1)}, u32[]{:S(2)}, u32[]{:S(2)}) collective-permute-start(f32[2,72,128]{2,1,0:T(8,128)S(1)} %get-tuple-element.59), channel_id=1, source_target_pairs={{0,64},{64,128},{128,192},{192,0},{1,65},{65,129},{129,193},{193,1... | collective-permute-start | bytes 221192 | tf_op jit(solution)/shard_map/ppermute | solution.py:360
  19.3 8.4 %collective-permute-start.1 = (f32[2,72,128]{2,1,0:T(8,128)S(1)}, f32[2,72,128]{2,1,0:T(8,128)S(1)}, u32[]{:S(2)}, u32[]{:S(2)}) collective-permute-start(f32[2,72,128]{2,1,0:T(8,128)S(1)} %get-tuple-element.60), channel_id=1, source_target_pairs={{0,128},{64,192},{128,0},{192,64},{1,129},{65,193},{129,1},{193,65... | collective-permute-start | bytes 221192 | tf_op jit(solution)/shard_map/ppermute | solution.py:360
  21.7 6.0 %collective-permute-start.2 = (f32[2,72,128]{2,1,0:T(8,128)S(1)}, f32[2,72,128]{2,1,0:T(8,128)S(1)}, u32[]{:S(2)}, u32[]{:S(2)}) collective-permute-start(f32[2,72,128]{2,1,0:T(8,128)S(1)} %get-tuple-element.61), channel_id=1, source_target_pairs={{0,192},{64,0},{128,64},{192,128},{1,193},{65,1},{129,65},{193,129... | collective-permute-start | bytes 221192 | tf_op jit(solution)/shard_map/ppermute | solution.py:360
  27.7 19.5 %collective-permute-start.3 = (f32[4,72,128]{2,1,0:T(8,128)S(1)}, f32[4,72,128]{2,1,0:T(8,128)S(1)}, u32[]{:S(2)}, u32[]{:S(2)}) collective-permute-start(f32[4,72,128]{2,1,0:T(8,128)S(1)} %pad_maximum_fusion.2), channel_id=1, source_target_pairs={{0,8},{8,0},{16,24},{24,16},{32,40},{40,32},{48,56},{56,48},{1,9},... | collective-permute-start | bytes 442376 | tf_op jit(solution)/shard_map/ppermute | solution.py:365
  50.2 8.6 %collective-permute-start.4 = (f32[4,32,128]{2,1,0:T(8,128)S(1)}, f32[4,32,128]{2,1,0:T(8,128)S(1)}, u32[]{:S(2)}, u32[]{:S(2)}) collective-permute-start(f32[4,32,128]{2,1,0:T(8,128)S(1)} %get-tuple-element.77.refs_5_), channel_id=1, source_target_pairs={{0,16},{8,24},{16,32},{24,40},{32,48},{40,56},{48,0},{56,8},{1,17}... | collective-permute-start | bytes 196616 | tf_op jit(solution)/shard_map/ppermute | solution.py:360
  51.9 7.9 %collective-permute-start.5 = (f32[4,32,128]{2,1,0:T(8,128)S(1)}, f32[4,32,128]{2,1,0:T(8,128)S(1)}, u32[]{:S(2)}, u32[]{:S(2)}) collective-permute-start(f32[4,32,128]{2,1,0:T(8,128)S(1)} %get-tuple-element.77.refs_5_), channel_id=1, source_target_pairs={{0,32},{8,40},{16,48},{24,56},{32,0},{40,8},{48,16},{56,24},{1,33}... | collective-permute-start | bytes 196616 | tf_op jit(solution)/shard_map/ppermute | solution.py:360
  55.5 5.4 %collective-permute-start.6 = (f32[4,32,128]{2,1,0:T(8,128)S(1)}, f32[4,32,128]{2,1,0:T(8,128)S(1)}, u32[]{:S(2)}, u32[]{:S(2)}) collective-permute-start(f32[4,32,128]{2,1,0:T(8,128)S(1)} %get-tuple-element.77.refs_5_), channel_id=1, source_target_pairs={{0,48},{8,56},{16,0},{24,8},{32,16},{40,24},{48,32},{56,40},{1,49}... | collective-permute-start | bytes 196616 | tf_op jit(solution)/shard_map/ppermute | solution.py:360
  60.9 23.6 %all-to-all-start.2 = ((f32[32,32,128]{2,1,0:T(8,128)}), f32[32,32,128]{2,1,0:T(8,128)S(1)}, u32[]{:S(2)}, u32[]{:S(2)}) async-start(f32[32,32,128]{2,1,0:T(8,128)} %get-tuple-element.66), calls=%async_computation.2 | async-start | bytes 1048576 | tf_op jit(solution)/shard_map/all_to_all | solution.py:369
  69.3 11.3 %copy-start.2 = (bf16[4,16,1024]{2,1,0:T(8,128)(2,1)S(1)}, bf16[4,16,1024]{2,1,0:T(8,128)(2,1)}, u32[]{:S(2)}) copy-start(bf16[4,16,1024]{2,1,0:T(8,128)(2,1)} %sk_ref) | copy-start | bytes 393220
  69.3 11.3 %copy-start.3 = (bf16[4,16,1024]{2,1,0:T(8,128)(2,1)S(1)}, bf16[4,16,1024]{2,1,0:T(8,128)(2,1)}, u32[]{:S(2)}) copy-start(bf16[4,16,1024]{2,1,0:T(8,128)(2,1)} %sv_ref.1) | copy-start | bytes 393220
  69.3 11.3 %copy-start.4 = (f32[4,16,8]{1,2,0:T(8,128)S(1)}, f32[4,16,8]{1,2,0:T(8,128)}, u32[]{:S(2)}) copy-start(f32[4,16,8]{1,2,0:T(8,128)} %param.22) | copy-start | bytes 6148
  69.8 6.1 %collective-permute-start.7 = (f32[2,64,128]{2,1,0:T(8,128)S(1)}, f32[2,64,128]{2,1,0:T(8,128)S(1)}, u32[]{:S(2)}, u32[]{:S(2)}) collective-permute-start(f32[2,64,128]{2,1,0:T(8,128)S(1)} %get-tuple-element.82), channel_id=1, source_target_pairs={{0,192},{64,0},{128,64},{192,128},{1,193},{65,1},{129,65},{193,129... | collective-permute-start | bytes 196616 | tf_op jit(solution)/shard_map/ppermute | solution.py:360
  72.6 5.4 %collective-permute-start.8 = (f32[2,64,128]{2,1,0:T(8,128)S(1)}, f32[2,64,128]{2,1,0:T(8,128)S(1)}, u32[]{:S(2)}, u32[]{:S(2)}) collective-permute-start(f32[2,64,128]{2,1,0:T(8,128)S(1)} %get-tuple-element.83), channel_id=1, source_target_pairs={{0,128},{64,192},{128,0},{192,64},{1,129},{65,193},{129,1},{193,65... | collective-permute-start | bytes 196616 | tf_op jit(solution)/shard_map/ppermute | solution.py:360
  73.1 6.2 %collective-permute-start.9 = (f32[2,64,128]{2,1,0:T(8,128)S(1)}, f32[2,64,128]{2,1,0:T(8,128)S(1)}, u32[]{:S(2)}, u32[]{:S(2)}) collective-permute-start(f32[2,64,128]{2,1,0:T(8,128)S(1)} %get-tuple-element.84), channel_id=1, source_target_pairs={{0,64},{64,128},{128,192},{192,0},{1,65},{65,129},{129,193},{193,1... | collective-permute-start | bytes 196616 | tf_op jit(solution)/shard_map/ppermute | solution.py:360
  79.3 5.2 %collective-permute-start.10 = (f32[4,64,128]{2,1,0:T(8,128)S(1)}, f32[4,64,128]{2,1,0:T(8,128)S(1)}, u32[]{:S(2)}, u32[]{:S(2)}) collective-permute-start(f32[4,64,128]{2,1,0:T(8,128)S(1)} %pad_maximum_fusion.3), channel_id=1, source_target_pairs={{0,8},{8,0},{16,24},{24,16},{32,40},{40,32},{48,56},{56,48},{1,9},... | collective-permute-start | bytes 393224 | tf_op jit(solution)/shard_map/ppermute | solution.py:365
  84.5 13.3 %copy-start.5 = (f32[1024]{0:T(1024)S(1)}, f32[1024]{0:T(1024)}, u32[]{:S(2)}) copy-start(f32[1024]{0:T(1024)} %param.17) | copy-start | bytes 12292

commit v9 on v7

--- a/solution.py
+++ b/solution.py
@@ -37,6 +37,7 @@
 
 SMEM = pl.BlockSpec(memory_space=pltpu.SMEM)
 VMEM = pl.BlockSpec(memory_space=pltpu.VMEM)
+PLACE = pl.BlockSpec(memory_space=pl.ANY)
 
 
 def params(mib=12):
@@ -88,7 +89,15 @@
     return (head // 2) * NZ + 2 * quarter + head % 2
 
 
-def send_kernel(lens, here, key_ref, value_ref, logd_ref, out_ref, flag_ref, cum_ref):
+def send_kernel(
+    lens, here, key_in, value_in, logd_ref, out_ref, flag_ref, key_ref, value_ref, cum_ref, sems
+):
+    moves = [
+        pltpu.make_async_copy(key_in, key_ref, sems.at[0]),
+        pltpu.make_async_copy(value_in, value_ref, sems.at[1]),
+    ]
+    for move in moves:
+        move.start()
     first = here[0] * BLOCK
     ends = bounds(lens)
     front = entry_seg(first, ends)
@@ -124,6 +133,8 @@
             for g in range(NQ):
                 out_ref[owner(h, g), row : row + QUART, :] = total[g * QUART : (g + 1) * QUART, :]
 
+    for move in moves:
+        move.wait()
     emit(keep, 0)
     for h in range(HEADS):
         scal = jnp.concatenate(
@@ -164,8 +175,7 @@
 
 
 def intra_kernel(
-    lens, here, query_ref, key_ref, value_ref, logd_ref, sq_ref, sk_ref, sv_ref, sd_ref,
-    intra_ref, carried_ref, local_ref, scarried_ref,
+    lens, here, query_ref, key_ref, value_ref, logd_ref, intra_ref, carried_ref
 ):
     first = here[0] * BLOCK
     ends = bounds(lens)
@@ -186,7 +196,9 @@
         weights = (scores * factor).astype(BF)
         intra_ref[:, cols] = jnp.dot(weights, value_ref[:, cols], preferred_element_type=F32)
 
-    n = STEPS * ROWS_DEV
+
+def local_kernel(sq_ref, sk_ref, sv_ref, sd_ref, local_ref, scarried_ref):
+    n = NROW
     a = lax.broadcasted_iota(jnp.int32, (n, n), 0)
     b = lax.broadcasted_iota(jnp.int32, (n, n), 1)
     same = (b <= a) & ((a - b) % ROWS_DEV == 0)
@@ -215,7 +227,9 @@
         )
 
 
-def scan_kernel(lens, give_ref, extra_ref, entry_ref, slice_ref):
+def scan_kernel(lens, give_ref, *refs):
+    extra_ref = refs[0] if len(refs) == 3 else None
+    entry_ref, slice_ref = refs[-2:]
     ends = bounds(lens)
     state = jnp.zeros((QUART, HDIM), F32)
     for k in range(NDEV):
@@ -232,7 +246,9 @@
         earlier.append(b)
         whole = e % BLOCK == BLOCK - 1
         lead = give_ref[b, S0 + 1 + p : S0 + 2 + p, :]
-        tail = jnp.where(slot == 0, give_ref[b, T0:S0, :], extra_ref[p])
+        tail = give_ref[b, T0:S0, :]
+        if extra_ref is not None:
+            tail = jnp.where(slot == 0, tail, extra_ref[p])
         tail = jnp.where(whole, give_ref[b, 0:T0, :], tail)
         slice_ref[p] = lead * entry_ref[b] + tail
 
@@ -386,9 +402,14 @@
     give, crowded = pl.pallas_call(
         send_kernel,
         out_shape=(shape(NDEV, GIVE, HDIM), shape(1, dtype=jnp.int32)),
-        in_specs=[SMEM] * 2 + [VMEM] * 3,
+        in_specs=[SMEM] * 2 + [PLACE] * 2 + [VMEM],
         out_specs=(VMEM, SMEM),
-        scratch_shapes=[pltpu.VMEM((BLOCK, HEADS), F32)],
+        scratch_shapes=[
+            pltpu.VMEM((BLOCK, width), BF),
+            pltpu.VMEM((BLOCK, width), BF),
+            pltpu.VMEM((BLOCK, HEADS), F32),
+            pltpu.SemaphoreType.DMA((2,)),
+        ],
         compiler_params=params(),
         cost_estimate=cost(3),
         name="send",
@@ -407,41 +428,49 @@
     queries = [queries[0]] + [shift(queries[d], "seq_0", NX, d) for d in range(1, NX)]
     far_queries = over_pair(queries)
 
-    intra, carried, local_dec, scarried = pl.pallas_call(
+    intra, carried = pl.pallas_call(
         intra_kernel,
-        out_shape=(shape(BLOCK, width), shape(BLOCK, HEADS), shape(n, width), shape(n, HEADS)),
-        in_specs=[SMEM] * 2 + [VMEM] * 8,
-        out_specs=(VMEM,) * 4,
-        compiler_params=params(),
-        cost_estimate=cost(6),
+        out_shape=(shape(BLOCK, width), shape(BLOCK, HEADS)),
+        in_specs=[SMEM] * 2 + [VMEM] * 4,
+        out_specs=(VMEM,) * 2,
+        compiler_params=params(),
+        cost_estimate=cost(3),
         name="intra",
-    )(
-        prompt_lengths, here, query_in, key_in, value_in, logd,
-        step_query, step_key, step_value, step_decay.transpose(0, 2, 1),
-    )
-
-    given, intra, carried, local_dec, scarried, crowded, queries, far_queries = (
-        lax.optimization_barrier(
-            (given, intra, carried, local_dec, scarried, crowded, queries, far_queries)
-        )
-    )
-    extra = lax.cond(
+    )(prompt_lengths, here, query_in, key_in, value_in, logd)
+
+    given, intra, carried, crowded, queries, far_queries = lax.optimization_barrier(
+        (given, intra, carried, crowded, queries, far_queries)
+    )
+
+    def scan(*extra):
+        return pl.pallas_call(
+            scan_kernel,
+            out_shape=(shape(NDEV, QUART, HDIM), shape(PROMPTS, QUART, HDIM)),
+            in_specs=[SMEM] + [VMEM] * (1 + len(extra)),
+            out_specs=(VMEM,) * 2,
+            compiler_params=params(),
+            cost_estimate=cost(2),
+            name="scan",
+        )(prompt_lengths, given, *extra)
+
+    entry, own = lax.cond(
         crowded[0] > 0,
-        lambda: more_tails(key_in, value_in, log_decay, prompt_lengths, me * BLOCK),
-        lambda: jnp.zeros((LAST, QUART, HDIM), F32),
-    )
-    entry, own = pl.pallas_call(
-        scan_kernel,
-        out_shape=(shape(NDEV, QUART, HDIM), shape(PROMPTS, QUART, HDIM)),
-        in_specs=[SMEM] + [VMEM] * 2,
+        lambda: scan(more_tails(key_in, value_in, log_decay, prompt_lengths, me * BLOCK)),
+        scan,
+    )
+    slabs = [own] + [shift(own, "seq_1", NZ, 2 * d) for d in range(1, NQ)]
+    entry, slabs, step_key = lax.optimization_barrier((entry, slabs, step_key))
+    back = exchange(entry, SEQ)
+
+    local_dec, scarried = pl.pallas_call(
+        local_kernel,
+        out_shape=(shape(n, width), shape(n, HEADS)),
+        in_specs=[VMEM] * 4,
         out_specs=(VMEM,) * 2,
         compiler_params=params(),
-        cost_estimate=cost(2),
-        name="scan",
-    )(prompt_lengths, given, extra)
-    slabs = [own] + [shift(own, "seq_1", NZ, 2 * d) for d in range(1, NQ)]
-    entry, slabs = lax.optimization_barrier((entry, slabs))
-    back = exchange(entry, SEQ)
+        cost_estimate=cost(1),
+        name="local",
+    )(step_query, step_key, step_value, step_decay.transpose(0, 2, 1))
 
     products = pl.pallas_call(
         project_kernel,

time: 98.2 us -> 98.9 us (level)
  Pallas kernels: 9.85 us -> 11.8 us
  local copies, waits for them, and re-layouts: 1.76 us -> 0.09 us
    unnamed x26 -> x22, local copies, waits for them, and re-layouts: 1.73 us -> 0.07 us
    pallas_call x1 -> x2, Pallas kernels: 1.4 us -> 2.84 us  [the longest x1 2.14 us: scan(): pl.pallas_call(scan_kernel, out_shape=(shape(NDEV, QUART, HDIM), shape(PR...]
  transfers between devices with their start and end apart: 13 -> 13, of which waited for: 9 -> 9; matrix products, arithmetic and copies ran while one was open for 0% -> 0% of each run, Pallas kernels for 3% -> 4%
where the time goes in v9:
time: 98.9 us; the launch traced here: 98.5 us
  starting transfers between devices  41.3 us (42%)
  waiting for transfers between devices  31.1 us (31%)
  blocking collectives  12.7 us (13%)
  Pallas kernels  11.8 us (12%)
  between operations  1.48 us (1%)
    all_to_all x2, starting transfers between devices, exchange(): return lax.all_to_all(x, axis, split_axis=0, concat_axis=0, tiled=True)  20.2 us
    ppermute x2, waiting for transfers between devices, over_pair(): return lax.ppermute(both, 'seq_1', [(i, i ^ 1) for i in range(NZ)])  18.2 us
    ppermute x9, starting transfers between devices, shift(): return lax.ppermute(x, axis, [(i, (i + d) % size) for i in range(size)])  17.2 us
    ppermute x9, waiting for transfers between devices, shift(): return lax.ppermute(x, axis, [(i, (i + d) % size) for i in range(size)])  12.8 us
    all_to_all x1, blocking collectives, exchange(): return lax.all_to_all(x, axis, split_axis=0, concat_axis=0, tiled=True)  12.7 us
    pallas_call x1, Pallas kernels, local(): pl.pallas_call(send_kernel, out_shape=(shape(NDEV, GIVE, HDIM), shape(1,...  4.37 us
    ppermute x2, starting transfers between devices, over_pair(): return lax.ppermute(both, 'seq_1', [(i, i ^ 1) for i in range(NZ)])  3.81 us
    pallas_call x1, Pallas kernels, scan(): pl.pallas_call(scan_kernel, out_shape=(shape(NDEV, QUART, HDIM), shape(PR...  2.14 us
  transfers between devices with their start and end apart: 13, of which 9 were waited for; matrix products, arithmetic and copies ran while one was open for 0% of the time, Pallas kernels for 4%

profile of v9, /device:TPU:1, one launch (start us, length us, event | category | flops | bytes accessed | tf_op | source)
XLA Modules:
  0.0 98.5 jit_solution(5057052875783872310)
XLA Ops:
  0.6 4.4 %send.1 = (f32[32,72,128]{2,1,0:T(8,128)}, s32[1]{0:T(128)}) custom-call(s32[4]{0:T(128)} %lens.3, s32[1]{0:T(128)} %bitcast.20.here, bf16[256,1024]{1,0:T(8,128)(2,1)} %key_ref.1, bf16[256,1024]{1,0:T(8,128)(2,1)} %value_ref.1, f32[8,256]{1,0:T(8,128)} %bitcast.55), custom_call_target="tpu_custom_call" | custom-call | flops 3000000000 | bytes 9000000 | tf_op jit(solution)/shard_map/send/pallas_call | solution.py:402
  5.0 0.0 copy-start.1
  5.0 0.0 copy-start.6
  5.0 12.1 %all-to-all-start.1 = ((f32[32,72,128]{2,1,0:T(8,128)}), f32[32,72,128]{2,1,0:T(8,128)}, u32[]{:S(2)}, u32[]{:S(2)}) async-start(f32[32,72,128]{2,1,0:T(8,128)} %get-tuple-element.60), calls=%async_computation.1 | async-start | bytes 2359296 | tf_op jit(solution)/shard_map/all_to_all | solution.py:356
  17.2 0.0 copy-done.1
  17.2 0.0 copy-done.6
  17.2 0.0 copy-start
  17.2 0.0 copy-start.7
  17.2 0.0 copy-start.8
  17.2 0.0 copy-start.9
  17.2 0.0 copy-start.10
  17.3 0.6 query.1
  17.9 1.2 %collective-permute-start = (f32[2,72,128]{2,1,0:T(8,128)S(1)}, f32[2,72,128]{2,1,0:T(8,128)S(1)}, u32[]{:S(2)}, u32[]{:S(2)}) collective-permute-start(f32[2,72,128]{2,1,0:T(8,128)S(1)} %get-tuple-element.65), channel_id=1, source_target_pairs={{0,64},{64,128},{128,192},{192,0},{1,65},{65,129},{129,193},{193,1... | collective-permute-start | bytes 221192 | tf_op jit(solution)/shard_map/ppermute | solution.py:347
  19.1 2.4 %collective-permute-start.1 = (f32[2,72,128]{2,1,0:T(8,128)S(1)}, f32[2,72,128]{2,1,0:T(8,128)S(1)}, u32[]{:S(2)}, u32[]{:S(2)}) collective-permute-start(f32[2,72,128]{2,1,0:T(8,128)S(1)} %get-tuple-element.66), channel_id=1, source_target_pairs={{0,128},{64,192},{128,0},{192,64},{1,129},{65,193},{129,1},{193,65... | collective-permute-start | bytes 221192 | tf_op jit(solution)/shard_map/ppermute | solution.py:347
  21.5 1.1 %collective-permute-start.2 = (f32[2,72,128]{2,1,0:T(8,128)S(1)}, f32[2,72,128]{2,1,0:T(8,128)S(1)}, u32[]{:S(2)}, u32[]{:S(2)}) collective-permute-start(f32[2,72,128]{2,1,0:T(8,128)S(1)} %get-tuple-element.67), channel_id=1, source_target_pairs={{0,192},{64,0},{128,64},{192,128},{1,193},{65,1},{129,65},{193,129... | collective-permute-start | bytes 221192 | tf_op jit(solution)/shard_map/ppermute | solution.py:347
  22.7 0.7 collective-permute-done.refs_1_
  23.3 4.3 %collective-permute-done.1.refs_2_ = f32[2,72,128]{2,1,0:T(8,128)S(1)} collective-permute-done((f32[2,72,128]{2,1,0:T(8,128)S(1)}, f32[2,72,128]{2,1,0:T(8,128)S(1)}, u32[]{:S(2)}, u32[]{:S(2)}) %collective-permute-start.1) | collective-permute-done | bytes 73760 | tf_op jit(solution)/shard_map/ppermute | solution.py:347
  27.6 0.0 collective-permute-done.2.refs_3_
  27.7 2.4 %collective-permute-start.3 = (f32[4,72,128]{2,1,0:T(8,128)S(1)}, f32[4,72,128]{2,1,0:T(8,128)S(1)}, u32[]{:S(2)}, u32[]{:S(2)}) collective-permute-start(f32[4,72,128]{2,1,0:T(8,128)S(1)} %pad_maximum_fusion.2), channel_id=1, source_target_pairs={{0,8},{8,0},{16,24},{24,16},{32,40},{40,32},{48,56},{56,48},{1,9},... | collective-permute-start | bytes 442376 | tf_op jit(solution)/shard_map/ppermute | solution.py:352
  30.0 0.0 copy-done
  30.0 0.0 copy-done.7
  30.0 0.0 copy-done.8
  30.0 0.0 copy-done.9
  30.0 0.0 copy-done.10
  30.1 1.9 %intra.1 = (f32[256,1024]{1,0:T(8,128)S(1)}, f32[256,8]{1,0:T(8,128)S(1)}) custom-call(s32[4]{0:T(128)S(1)} %copy-done.10, s32[1]{0:T(128)} %bitcast.20.here, bf16[256,1024]{1,0:T(8,128)(2,1)S(1)} %copy-done, bf16[256,1024]{1,0:T(8,128)(2,1)S(1)} %copy-done.8, bf16[256,1024]{1,0:T(8,128)(2,1)S(1)} %copy-done.7, f32[8,256]{1,0:T(8,128)S(1)} %bitcast.56), custom_call_target="tpu_custom_call" | custom-call | flops 3000000000 | bytes 9000000 | tf_op jit(solution)/shard_map/intra/pallas_call | solution.py:431
  31.9 15.2 %collective-permute-done.3.refs_4_ = f32[4,72,128]{2,1,0:T(8,128)S(1)} collective-permute-done((f32[4,72,128]{2,1,0:T(8,128)S(1)}, f32[4,72,128]{2,1,0:T(8,128)S(1)}, u32[]{:S(2)}, u32[]{:S(2)}) %collective-permute-start.3) | collective-permute-done | bytes 147488 | tf_op jit(solution)/shard_map/ppermute | solution.py:352
  47.1 0.0 all-to-all-done.1
  47.7 2.2 %conditional.1 = ((f32[32,32,128]{2,1,0:T(8,128)}, f32[4,32,128]{2,1,0:T(8,128)S(1)})) conditional(s32[]{:T(128)} %bitcast.22, (s32[4]{0:T(128)S(1)}, f32[32,72,128]{2,1,0:T(8,128)}) %tuple.35, (bf16[256,1024]{1,0:T(8,128)(2,1)}, s32[4]{0:T(128)S(1)}, s32[]{:T(128)}, f32[256,8]{0,1:T(8,128)S(1)}, bf16[256,1024]{1,0:T(8,128)(2,1)S(1)}, ...), branch_computations={%region_0.0_spmd, %region_1.7_spmd} | conditional | flops 2136610816 | bytes 18843024 | solution.py:456
  47.8 2.1 %scan.2 = (f32[32,32,128]{2,1,0:T(8,128)}, f32[4,32,128]{2,1,0:T(8,128)S(1)}) custom-call(s32[4]{0:T(128)S(1)} %get-tuple-element.16.lens, f32[32,72,128]{2,1,0:T(8,128)} %get-tuple-element.17.give_ref), custom_call_target="tpu_custom_call" | custom-call | flops 2000000000 | bytes 6000000 | tf_op jit(solution)/shard_map/cond/branch_0_fun/scan/pallas_call | solution.py:446
  49.9 1.8 %collective-permute-start.4 = (f32[4,32,128]{2,1,0:T(8,128)S(1)}, f32[4,32,128]{2,1,0:T(8,128)S(1)}, u32[]{:S(2)}, u32[]{:S(2)}) collective-permute-start(f32[4,32,128]{2,1,0:T(8,128)S(1)} %get-tuple-element.83.refs_5_), channel_id=1, source_target_pairs={{0,16},{8,24},{16,32},{24,40},{32,48},{40,56},{48,0},{56,8},{1,17}... | collective-permute-start | bytes 196616 | tf_op jit(solution)/shard_map/ppermute | solution.py:347
  51.6 3.5 %collective-permute-start.5 = (f32[4,32,128]{2,1,0:T(8,128)S(1)}, f32[4,32,128]{2,1,0:T(8,128)S(1)}, u32[]{:S(2)}, u32[]{:S(2)}) collective-permute-start(f32[4,32,128]{2,1,0:T(8,128)S(1)} %get-tuple-element.83.refs_5_), channel_id=1, source_target_pairs={{0,32},{8,40},{16,48},{24,56},{32,0},{40,8},{48,16},{56,24},{1,33}... | collective-permute-start | bytes 196616 | tf_op jit(solution)/shard_map/ppermute | solution.py:347
  55.2 3.2 %collective-permute-start.6 = (f32[4,32,128]{2,1,0:T(8,128)S(1)}, f32[4,32,128]{2,1,0:T(8,128)S(1)}, u32[]{:S(2)}, u32[]{:S(2)}) collective-permute-start(f32[4,32,128]{2,1,0:T(8,128)S(1)} %get-tuple-element.83.refs_5_), channel_id=1, source_target_pairs={{0,48},{8,56},{16,0},{24,8},{32,16},{40,24},{48,32},{56,40},{1,49}... | collective-permute-start | bytes 196616 | tf_op jit(solution)/shard_map/ppermute | solution.py:347
  58.4 0.0 collective-permute-done.4.refs_6_
  58.4 1.2 %collective-permute-done.5.refs_7_ = f32[4,32,128]{2,1,0:T(8,128)S(1)} collective-permute-done((f32[4,32,128]{2,1,0:T(8,128)S(1)}, f32[4,32,128]{2,1,0:T(8,128)S(1)}, u32[]{:S(2)}, u32[]{:S(2)}) %collective-permute-start.5) | collective-permute-done | bytes 65568 | tf_op jit(solution)/shard_map/ppermute | solution.py:347
  59.6 1.1 %collective-permute-done.6.refs_8_ = f32[4,32,128]{2,1,0:T(8,128)S(1)} collective-permute-done((f32[4,32,128]{2,1,0:T(8,128)S(1)}, f32[4,32,128]{2,1,0:T(8,128)S(1)}, u32[]{:S(2)}, u32[]{:S(2)}) %collective-permute-start.6) | collective-permute-done | bytes 65568 | tf_op jit(solution)/shard_map/ppermute | solution.py:347
  60.7 8.1 %all-to-all-start.2 = ((f32[32,32,128]{2,1,0:T(8,128)}), f32[32,32,128]{2,1,0:T(8,128)S(1)}, u32[]{:S(2)}, u32[]{:S(2)}) async-start(f32[32,32,128]{2,1,0:T(8,128)} %get-tuple-element.72), calls=%async_computation.2 | async-start | bytes 1048576 | tf_op jit(solution)/shard_map/all_to_all | solution.py:356
  68.9 0.0 copy-start.2
  68.9 0.0 copy-start.3
  68.9 0.0 copy-start.4
  68.9 0.5 project.1
  69.4 2.7 %collective-permute-start.7 = (f32[2,64,128]{2,1,0:T(8,128)S(1)}, f32[2,64,128]{2,1,0:T(8,128)S(1)}, u32[]{:S(2)}, u32[]{:S(2)}) collective-permute-start(f32[2,64,128]{2,1,0:T(8,128)S(1)} %get-tuple-element.88), channel_id=1, source_target_pairs={{0,192},{64,0},{128,64},{192,128},{1,193},{65,1},{129,65},{193,129... | collective-permute-start | bytes 196616 | tf_op jit(solution)/shard_map/ppermute | solution.py:347
  72.1 0.5 collective-permute-start.8
  72.7 0.6 collective-permute-start.9
  73.3 2.2 %collective-permute-done.7.refs_1_ = f32[2,64,128]{2,1,0:T(8,128)S(1)} collective-permute-done((f32[2,64,128]{2,1,0:T(8,128)S(1)}, f32[2,64,128]{2,1,0:T(8,128)S(1)}, u32[]{:S(2)}, u32[]{:S(2)}) %collective-permute-start.7) | collective-permute-done | bytes 65568 | tf_op jit(solution)/shard_map/ppermute | solution.py:347
  75.5 2.1 %collective-permute-done.8.refs_2_ = f32[2,64,128]{2,1,0:T(8,128)S(1)} collective-permute-done((f32[2,64,128]{2,1,0:T(8,128)S(1)}, f32[2,64,128]{2,1,0:T(8,128)S(1)}, u32[]{:S(2)}, u32[]{:S(2)}) %collective-permute-start.8) | collective-permute-done | bytes 65568 | tf_op jit(solution)/shard_map/ppermute | solution.py:347
  77.6 1.3 %collective-permute-done.9.refs_3_ = f32[2,64,128]{2,1,0:T(8,128)S(1)} collective-permute-done((f32[2,64,128]{2,1,0:T(8,128)S(1)}, f32[2,64,128]{2,1,0:T(8,128)S(1)}, u32[]{:S(2)}, u32[]{:S(2)}) %collective-permute-start.9) | collective-permute-done | bytes 65568 | tf_op jit(solution)/shard_map/ppermute | solution.py:347
  78.9 1.4 %collective-permute-start.10 = (f32[4,64,128]{2,1,0:T(8,128)S(1)}, f32[4,64,128]{2,1,0:T(8,128)S(1)}, u32[]{:S(2)}, u32[]{:S(2)}) collective-permute-start(f32[4,64,128]{2,1,0:T(8,128)S(1)} %pad_maximum_fusion.3), channel_id=1, source_target_pairs={{0,8},{8,0},{16,24},{24,16},{32,40},{40,32},{48,56},{56,48},{1,9},... | collective-permute-start | bytes 393224 | tf_op jit(solution)/shard_map/ppermute | solution.py:352
  80.3 0.0 copy-done.2
  80.3 0.0 copy-done.3
  80.3 0.0 copy-done.4
  80.3 0.7 local.1
  81.0 3.1 %collective-permute-done.10.refs_4_ = f32[4,64,128]{2,1,0:T(8,128)S(1)} collective-permute-done((f32[4,64,128]{2,1,0:T(8,128)S(1)}, f32[4,64,128]{2,1,0:T(8,128)S(1)}, u32[]{:S(2)}, u32[]{:S(2)}) %collective-permute-start.10) | collective-permute-done | bytes 131104 | tf_op jit(solution)/shard_map/ppermute | solution.py:352
  84.1 0.0 all-to-all-done.2.back_ref
  84.1 0.0 copy-start.5
  84.1 0.6 mixed.1
  84.7 12.7 %all_to_all.19.sums_ref = f32[8,4,128]{2,1,0:T(4,128)S(1)} all-to-all(f32[8,4,128]{2,1,0:T(4,128)S(1)} %get-tuple-element.91), channel_id=1, replica_groups=mesh['seq_0'=4,'seq_1'=8,'head'=8] {'head'}, dimensions={0} | all-to-all | bytes 32768 | tf_op jit(solution)/shard_map/all_to_all | solution.py:356
  97.4 0.0 copy-done.5
  97.4 1.1 %final.1 = (bf16[256,1024]{1,0:T(8,128)(2,1)}, bf16[4,16,1024]{2,1,0:T(8,128)(2,1)}) custom-call(f32[8,4,128]{2,1,0:T(4,128)S(1)} %all_to_all.19.sums_ref, f32[256,1024]{1,0:T(8,128)S(1)} %get-tuple-element.92.mixed_ref, f32[64,1024]{1,0:T(8,128)S(1)} %get-tuple-element.93.dec_ref, f32[1,1024]{1,0:T(1,128)S(1)} %bitcast.47), custom_call_target="tpu_custom_call" | custom-call | flops 2000000000 | bytes 6000000 | tf_op jit(solution)/shard_map/final/pallas_call | solution.py:500
  (10 shorter events, 0.1 us)
Async XLA Ops:
  5.0 12.2 %copy-start.1 = (bf16[4,16,1024]{2,1,0:T(8,128)(2,1)S(1)}, bf16[4,16,1024]{2,1,0:T(8,128)(2,1)}, u32[]{:S(2)}) copy-start(bf16[4,16,1024]{2,1,0:T(8,128)(2,1)} %sq_ref.1) | copy-start | bytes 393220
  5.0 12.2 %copy-start.6 = (s32[16]{0:T(128)S(1)}, s32[16]{0:T(128)}, u32[]{:S(2)}) copy-start(s32[16]{0:T(128)} %rows.1) | copy-start | bytes 196
  5.0 42.0 %all-to-all-start.1 = ((f32[32,72,128]{2,1,0:T(8,128)}), f32[32,72,128]{2,1,0:T(8,128)}, u32[]{:S(2)}, u32[]{:S(2)}) async-start(f32[32,72,128]{2,1,0:T(8,128)} %get-tuple-element.60), calls=%async_computation.1 | async-start | bytes 2359296 | tf_op jit(solution)/shard_map/all_to_all | solution.py:356
  17.2 12.8 %copy-start = (bf16[256,1024]{1,0:T(8,128)(2,1)S(1)}, bf16[256,1024]{1,0:T(8,128)(2,1)}, u32[]{:S(2)}) copy-start(bf16[256,1024]{1,0:T(8,128)(2,1)} %query_ref.5) | copy-start | bytes 1572868
  17.2 12.8 %copy-start.7 = (bf16[256,1024]{1,0:T(8,128)(2,1)S(1)}, bf16[256,1024]{1,0:T(8,128)(2,1)}, u32[]{:S(2)}) copy-start(bf16[256,1024]{1,0:T(8,128)(2,1)} %value_ref.1) | copy-start | bytes 1572868
  17.2 12.8 %copy-start.8 = (bf16[256,1024]{1,0:T(8,128)(2,1)S(1)}, bf16[256,1024]{1,0:T(8,128)(2,1)}, u32[]{:S(2)}) copy-start(bf16[256,1024]{1,0:T(8,128)(2,1)} %key_ref.1) | copy-start | bytes 1572868
  17.2 12.8 %copy-start.9 = (f32[256,8]{0,1:T(8,128)S(1)}, f32[256,8]{0,1:T(8,128)}, u32[]{:S(2)}) copy-start(f32[256,8]{0,1:T(8,128)} %param.16) | copy-start | bytes 24580
  17.2 12.8 %copy-start.10 = (s32[4]{0:T(128)S(1)}, s32[4]{0:T(128)}, u32[]{:S(2)}) copy-start(s32[4]{0:T(128)} %lens.3) | copy-start | bytes 52
  17.9 5.5 %collective-permute-start = (f32[2,72,128]{2,1,0:T(8,128)S(1)}, f32[2,72,128]{2,1,0:T(8,128)S(1)}, u32[]{:S(2)}, u32[]{:S(2)}) collective-permute-start(f32[2,72,128]{2,1,0:T(8,128)S(1)} %get-tuple-element.65), channel_id=1, source_target_pairs={{0,64},{64,128},{128,192},{192,0},{1,65},{65,129},{129,193},{193,1... | collective-permute-start | bytes 221192 | tf_op jit(solution)/shard_map/ppermute | solution.py:347
  19.1 8.5 %collective-permute-start.1 = (f32[2,72,128]{2,1,0:T(8,128)S(1)}, f32[2,72,128]{2,1,0:T(8,128)S(1)}, u32[]{:S(2)}, u32[]{:S(2)}) collective-permute-start(f32[2,72,128]{2,1,0:T(8,128)S(1)} %get-tuple-element.66), channel_id=1, source_target_pairs={{0,128},{64,192},{128,0},{192,64},{1,129},{65,193},{129,1},{193,65... | collective-permute-start | bytes 221192 | tf_op jit(solution)/shard_map/ppermute | solution.py:347
  21.5 6.1 %collective-permute-start.2 = (f32[2,72,128]{2,1,0:T(8,128)S(1)}, f32[2,72,128]{2,1,0:T(8,128)S(1)}, u32[]{:S(2)}, u32[]{:S(2)}) collective-permute-start(f32[2,72,128]{2,1,0:T(8,128)S(1)} %get-tuple-element.67), channel_id=1, source_target_pairs={{0,192},{64,0},{128,64},{192,128},{1,193},{65,1},{129,65},{193,129... | collective-permute-start | bytes 221192 | tf_op jit(solution)/shard_map/ppermute | solution.py:347
  27.7 19.4 %collective-permute-start.3 = (f32[4,72,128]{2,1,0:T(8,128)S(1)}, f32[4,72,128]{2,1,0:T(8,128)S(1)}, u32[]{:S(2)}, u32[]{:S(2)}) collective-permute-start(f32[4,72,128]{2,1,0:T(8,128)S(1)} %pad_maximum_fusion.2), channel_id=1, source_target_pairs={{0,8},{8,0},{16,24},{24,16},{32,40},{40,32},{48,56},{56,48},{1,9},... | collective-permute-start | bytes 442376 | tf_op jit(solution)/shard_map/ppermute | solution.py:352
  49.9 8.5 %collective-permute-start.4 = (f32[4,32,128]{2,1,0:T(8,128)S(1)}, f32[4,32,128]{2,1,0:T(8,128)S(1)}, u32[]{:S(2)}, u32[]{:S(2)}) collective-permute-start(f32[4,32,128]{2,1,0:T(8,128)S(1)} %get-tuple-element.83.refs_5_), channel_id=1, source_target_pairs={{0,16},{8,24},{16,32},{24,40},{32,48},{40,56},{48,0},{56,8},{1,17}... | collective-permute-start | bytes 196616 | tf_op jit(solution)/shard_map/ppermute | solution.py:347
  51.6 8.0 %collective-permute-start.5 = (f32[4,32,128]{2,1,0:T(8,128)S(1)}, f32[4,32,128]{2,1,0:T(8,128)S(1)}, u32[]{:S(2)}, u32[]{:S(2)}) collective-permute-start(f32[4,32,128]{2,1,0:T(8,128)S(1)} %get-tuple-element.83.refs_5_), channel_id=1, source_target_pairs={{0,32},{8,40},{16,48},{24,56},{32,0},{40,8},{48,16},{56,24},{1,33}... | collective-permute-start | bytes 196616 | tf_op jit(solution)/shard_map/ppermute | solution.py:347
  55.2 5.5 %collective-permute-start.6 = (f32[4,32,128]{2,1,0:T(8,128)S(1)}, f32[4,32,128]{2,1,0:T(8,128)S(1)}, u32[]{:S(2)}, u32[]{:S(2)}) collective-permute-start(f32[4,32,128]{2,1,0:T(8,128)S(1)} %get-tuple-element.83.refs_5_), channel_id=1, source_target_pairs={{0,48},{8,56},{16,0},{24,8},{32,16},{40,24},{48,32},{56,40},{1,49}... | collective-permute-start | bytes 196616 | tf_op jit(solution)/shard_map/ppermute | solution.py:347
  60.7 23.4 %all-to-all-start.2 = ((f32[32,32,128]{2,1,0:T(8,128)}), f32[32,32,128]{2,1,0:T(8,128)S(1)}, u32[]{:S(2)}, u32[]{:S(2)}) async-start(f32[32,32,128]{2,1,0:T(8,128)} %get-tuple-element.72), calls=%async_computation.2 | async-start | bytes 1048576 | tf_op jit(solution)/shard_map/all_to_all | solution.py:356
  68.9 11.5 %copy-start.2 = (bf16[4,16,1024]{2,1,0:T(8,128)(2,1)S(1)}, bf16[4,16,1024]{2,1,0:T(8,128)(2,1)}, u32[]{:S(2)}) copy-start(bf16[4,16,1024]{2,1,0:T(8,128)(2,1)} %sk_ref) | copy-start | bytes 393220
  68.9 11.5 %copy-start.3 = (bf16[4,16,1024]{2,1,0:T(8,128)(2,1)S(1)}, bf16[4,16,1024]{2,1,0:T(8,128)(2,1)}, u32[]{:S(2)}) copy-start(bf16[4,16,1024]{2,1,0:T(8,128)(2,1)} %sv_ref.1) | copy-start | bytes 393220
  68.9 11.4 %copy-start.4 = (f32[4,16,8]{1,2,0:T(8,128)S(1)}, f32[4,16,8]{1,2,0:T(8,128)}, u32[]{:S(2)}) copy-start(f32[4,16,8]{1,2,0:T(8,128)} %param.22) | copy-start | bytes 6148
  69.4 6.1 %collective-permute-start.7 = (f32[2,64,128]{2,1,0:T(8,128)S(1)}, f32[2,64,128]{2,1,0:T(8,128)S(1)}, u32[]{:S(2)}, u32[]{:S(2)}) collective-permute-start(f32[2,64,128]{2,1,0:T(8,128)S(1)} %get-tuple-element.88), channel_id=1, source_target_pairs={{0,192},{64,0},{128,64},{192,128},{1,193},{65,1},{129,65},{193,129... | collective-permute-start | bytes 196616 | tf_op jit(solution)/shard_map/ppermute | solution.py:347
  72.1 5.4 %collective-permute-start.8 = (f32[2,64,128]{2,1,0:T(8,128)S(1)}, f32[2,64,128]{2,1,0:T(8,128)S(1)}, u32[]{:S(2)}, u32[]{:S(2)}) collective-permute-start(f32[2,64,128]{2,1,0:T(8,128)S(1)} %get-tuple-element.89), channel_id=1, source_target_pairs={{0,128},{64,192},{128,0},{192,64},{1,129},{65,193},{129,1},{193,65... | collective-permute-start | bytes 196616 | tf_op jit(solution)/shard_map/ppermute | solution.py:347
  72.7 6.2 %collective-permute-start.9 = (f32[2,64,128]{2,1,0:T(8,128)S(1)}, f32[2,64,128]{2,1,0:T(8,128)S(1)}, u32[]{:S(2)}, u32[]{:S(2)}) collective-permute-start(f32[2,64,128]{2,1,0:T(8,128)S(1)} %get-tuple-element.90), channel_id=1, source_target_pairs={{0,64},{64,128},{128,192},{192,0},{1,65},{65,129},{129,193},{193,1... | collective-permute-start | bytes 196616 | tf_op jit(solution)/shard_map/ppermute | solution.py:347
  78.9 5.2 %collective-permute-start.10 = (f32[4,64,128]{2,1,0:T(8,128)S(1)}, f32[4,64,128]{2,1,0:T(8,128)S(1)}, u32[]{:S(2)}, u32[]{:S(2)}) collective-permute-start(f32[4,64,128]{2,1,0:T(8,128)S(1)} %pad_maximum_fusion.3), channel_id=1, source_target_pairs={{0,8},{8,0},{16,24},{24,16},{32,40},{40,32},{48,56},{56,48},{1,9},... | collective-permute-start | bytes 393224 | tf_op jit(solution)/shard_map/ppermute | solution.py:352
  84.1 13.3 %copy-start.5 = (f32[1024]{0:T(1024)S(1)}, f32[1024]{0:T(1024)}, u32[]{:S(2)}) copy-start(f32[1024]{0:T(1024)} %param.17) | copy-start | bytes 12292

commit v10 on v7

--- a/solution.py
+++ b/solution.py
@@ -88,16 +88,32 @@
     return (head // 2) * NZ + 2 * quarter + head % 2
 
 
-def send_kernel(lens, here, key_ref, value_ref, logd_ref, out_ref, flag_ref, cum_ref):
+def cum_rows_of(logd):
+    s = lax.broadcasted_iota(jnp.int32, (BLOCK, BLOCK), 0)
+    t = lax.broadcasted_iota(jnp.int32, (BLOCK, BLOCK), 1)
+    tri = (s <= t).astype(BF)
+    total = jnp.zeros((HEADS, BLOCK), F32)
+    rest = logd
+    for _ in range(3):
+        term = rest.astype(BF)
+        total = total + jnp.dot(term, tri, preferred_element_type=F32)
+        rest = rest - term.astype(F32)
+    return total
+
+
+def send_kernel(lens, here, key_ref, value_ref, logd_ref, out_ref, flag_ref):
     first = here[0] * BLOCK
     ends = bounds(lens)
     front = entry_seg(first, ends)
     seg_last = seg_of(first + (BLOCK - 1), ends)
-    cum = cum_columns(logd_ref[...])
-    cum_ref[...] = cum
-    tok = lax.broadcasted_iota(jnp.int32, (BLOCK, HEADS), 0)
+    cum = cum_rows_of(logd_ref[...])
+    tok = lax.broadcasted_iota(jnp.int32, (HEADS, BLOCK), 1)
     seg = seg_of(tok + first, ends)
-    last = cum[BLOCK - 1 : BLOCK, :]
+
+    def at_token(spot):
+        return jnp.sum(jnp.where(tok == spot, cum, 0.0), axis=1, keepdims=True)
+
+    last = cum[:, BLOCK - 1 : BLOCK]
     keep = jnp.where(seg == seg_last, jnp.exp(last - cum), 0.0)
     factors = [jnp.exp(last) * (seg_last == front).astype(F32)]
     found = jnp.int32(-1)
@@ -106,8 +122,7 @@
     for p in range(LAST):
         at = ends[p] - 1 - first
         inside = (at >= 0) & (at < BLOCK)
-        reached = cum_ref[pl.ds(jnp.clip(at, 0, BLOCK - 1), 1), :]
-        factors.append(jnp.exp(reached) * (inside & (front == p)).astype(F32))
+        factors.append(jnp.exp(at_token(at)) * (inside & (front == p)).astype(F32))
         take = (at >= 0) & (at < BLOCK - 1) & (found < 0)
         found = jnp.where(take, p, found)
         spot = jnp.where(take, at, spot)
@@ -115,34 +130,26 @@
             same = (ends[p] - 1) // BLOCK == (ends[p - 1] - 1) // BLOCK
             crowded = crowded | (same & (ends[p] % BLOCK != 0)).astype(jnp.int32)
     flag_ref[0] = crowded
-
-    def emit(factor, row):
-        for h in range(HEADS):
-            cols = slice(h * HDIM, (h + 1) * HDIM)
-            keyed = (key_ref[:, cols].astype(F32) * factor[:, h : h + 1]).astype(BF)
-            total = contract_rows(keyed, value_ref[:, cols])
-            for g in range(NQ):
-                out_ref[owner(h, g), row : row + QUART, :] = total[g * QUART : (g + 1) * QUART, :]
-
-    emit(keep, 0)
+    taken = (tok <= spot) & (seg == found)
+    tail = jnp.where(taken, jnp.exp(jnp.where(taken, at_token(spot) - cum, 0.0)), 0.0)
+
     for h in range(HEADS):
+        cols = slice(h * HDIM, (h + 1) * HDIM)
+        keys = key_ref[:, cols].T.astype(F32)
+        scaled = jnp.concatenate(
+            [(keys * keep[h : h + 1, :]).astype(BF), (keys * tail[h : h + 1, :]).astype(BF)], axis=0
+        )
+        total = jnp.dot(scaled, value_ref[:, cols], preferred_element_type=F32)
         scal = jnp.concatenate(
-            [jnp.broadcast_to(f[:, h : h + 1], (1, HDIM)) for f in factors]
+            [jnp.broadcast_to(f[h : h + 1, :], (1, HDIM)) for f in factors]
             + [jnp.zeros((8 - len(factors), HDIM), F32)],
             axis=0,
         )
         for g in range(NQ):
+            rows = slice(g * QUART, (g + 1) * QUART)
+            out_ref[owner(h, g), 0:T0, :] = total[rows, :]
+            out_ref[owner(h, g), T0:S0, :] = total[HDIM + g * QUART : HDIM + (g + 1) * QUART, :]
             out_ref[owner(h, g), S0:GIVE, :] = scal
-
-    @pl.when(found < 0)
-    def _():
-        out_ref[:, T0:S0, :] = jnp.zeros((NDEV, QUART, HDIM), F32)
-
-    @pl.when(found >= 0)
-    def _():
-        reached = cum_ref[pl.ds(spot, 1), :]
-        taken = (tok <= spot) & (seg == found)
-        emit(jnp.where(taken, jnp.exp(jnp.where(taken, reached - cum, 0.0)), 0.0), T0)
 
 
 def mate_head(here, dx, db):
@@ -164,8 +171,7 @@
 
 
 def intra_kernel(
-    lens, here, query_ref, key_ref, value_ref, logd_ref, sq_ref, sk_ref, sv_ref, sd_ref,
-    intra_ref, carried_ref, local_ref, scarried_ref,
+    lens, here, query_ref, key_ref, value_ref, logd_ref, intra_ref, carried_ref
 ):
     first = here[0] * BLOCK
     ends = bounds(lens)
@@ -186,7 +192,9 @@
         weights = (scores * factor).astype(BF)
         intra_ref[:, cols] = jnp.dot(weights, value_ref[:, cols], preferred_element_type=F32)
 
-    n = STEPS * ROWS_DEV
+
+def local_kernel(sq_ref, sk_ref, sv_ref, sd_ref, local_ref, scarried_ref):
+    n = NROW
     a = lax.broadcasted_iota(jnp.int32, (n, n), 0)
     b = lax.broadcasted_iota(jnp.int32, (n, n), 1)
     same = (b <= a) & ((a - b) % ROWS_DEV == 0)
@@ -388,7 +396,6 @@
         out_shape=(shape(NDEV, GIVE, HDIM), shape(1, dtype=jnp.int32)),
         in_specs=[SMEM] * 2 + [VMEM] * 3,
         out_specs=(VMEM, SMEM),
-        scratch_shapes=[pltpu.VMEM((BLOCK, HEADS), F32)],
         compiler_params=params(),
         cost_estimate=cost(3),
         name="send",
@@ -407,23 +414,18 @@
     queries = [queries[0]] + [shift(queries[d], "seq_0", NX, d) for d in range(1, NX)]
     far_queries = over_pair(queries)
 
-    intra, carried, local_dec, scarried = pl.pallas_call(
+    intra, carried = pl.pallas_call(
         intra_kernel,
-        out_shape=(shape(BLOCK, width), shape(BLOCK, HEADS), shape(n, width), shape(n, HEADS)),
-        in_specs=[SMEM] * 2 + [VMEM] * 8,
-        out_specs=(VMEM,) * 4,
-        compiler_params=params(),
-        cost_estimate=cost(6),
+        out_shape=(shape(BLOCK, width), shape(BLOCK, HEADS)),
+        in_specs=[SMEM] * 2 + [VMEM] * 4,
+        out_specs=(VMEM,) * 2,
+        compiler_params=params(),
+        cost_estimate=cost(3),
         name="intra",
-    )(
-        prompt_lengths, here, query_in, key_in, value_in, logd,
-        step_query, step_key, step_value, step_decay.transpose(0, 2, 1),
-    )
-
-    given, intra, carried, local_dec, scarried, crowded, queries, far_queries = (
-        lax.optimization_barrier(
-            (given, intra, carried, local_dec, scarried, crowded, queries, far_queries)
-        )
+    )(prompt_lengths, here, query_in, key_in, value_in, logd)
+
+    given, intra, carried, crowded, queries, far_queries = lax.optimization_barrier(
+        (given, intra, carried, crowded, queries, far_queries)
     )
     extra = lax.cond(
         crowded[0] > 0,
@@ -440,8 +442,18 @@
         name="scan",
     )(prompt_lengths, given, extra)
     slabs = [own] + [shift(own, "seq_1", NZ, 2 * d) for d in range(1, NQ)]
-    entry, slabs = lax.optimization_barrier((entry, slabs))
+    entry, slabs, step_key = lax.optimization_barrier((entry, slabs, step_key))
     back = exchange(entry, SEQ)
+
+    local_dec, scarried = pl.pallas_call(
+        local_kernel,
+        out_shape=(shape(n, width), shape(n, HEADS)),
+        in_specs=[VMEM] * 4,
+        out_specs=(VMEM,) * 2,
+        compiler_params=params(),
+        cost_estimate=cost(1),
+        name="local",
+    )(step_query, step_key, step_value, step_decay.transpose(0, 2, 1))
 
     products = pl.pallas_call(
         project_kernel,

time: 98.2 us -> 97.7 us (level)
  waiting for transfers between devices: 30.5 us -> 31.6 us
  local copies, waits for them, and re-layouts: 1.76 us -> 0.72 us
    unnamed x26 -> x22, local copies, waits for them, and re-layouts: 1.73 us -> 0.07 us
    ppermute x2, waiting for transfers between devices: 18 us -> 19 us  [over_pair(): return lax.ppermute(both, 'seq_1', [(i, i ^ 1) for i in range(NZ)])]
  transfers between devices with their start and end apart: 13 -> 13, of which waited for: 9 -> 9; matrix products, arithmetic and copies ran while one was open for 0% -> 0% of each run, Pallas kernels for 3% -> 4%
where the time goes in v10:
time: 97.7 us; the launch traced here: 97.3 us
  starting transfers between devices  40.7 us (42%)
  waiting for transfers between devices  31.6 us (32%)
  blocking collectives  12.6 us (13%)
  Pallas kernels  10 us (10%)
  between operations  1.48 us (2%)
    all_to_all x2, starting transfers between devices, exchange(): return lax.all_to_all(x, axis, split_axis=0, concat_axis=0, tiled=True)  20.4 us
    ppermute x2, waiting for transfers between devices, over_pair(): return lax.ppermute(both, 'seq_1', [(i, i ^ 1) for i in range(NZ)])  19 us
    ppermute x9, starting transfers between devices, shift(): return lax.ppermute(x, axis, [(i, (i + d) % size) for i in range(size)])  17.2 us
    ppermute x9, waiting for transfers between devices, shift(): return lax.ppermute(x, axis, [(i, (i + d) % size) for i in range(size)])  12.7 us
    all_to_all x1, blocking collectives, exchange(): return lax.all_to_all(x, axis, split_axis=0, concat_axis=0, tiled=True)  12.6 us
    ppermute x2, starting transfers between devices, over_pair(): return lax.ppermute(both, 'seq_1', [(i, i ^ 1) for i in range(NZ)])  3.18 us
    pallas_call x1, Pallas kernels, local(): pl.pallas_call(send_kernel, out_shape=(shape(NDEV, GIVE, HDIM), shape(1,...  3.07 us
  transfers between devices with their start and end apart: 13, of which 9 were waited for; matrix products, arithmetic and copies ran while one was open for 0% of the time, Pallas kernels for 4%

profile of v10, /device:TPU:1, one launch (start us, length us, event | category | flops | bytes accessed | tf_op | source)
XLA Modules:
  0.0 97.3 jit_solution(11119224033485567702)
XLA Ops:
  0.6 3.1 %send.1 = (f32[32,72,128]{2,1,0:T(8,128)}, s32[1]{0:T(128)}) custom-call(s32[4]{0:T(128)} %lens.5, s32[1]{0:T(128)} %bitcast.20.here, bf16[256,1024]{1,0:T(8,128)(2,1)} %key_ref.3, bf16[256,1024]{1,0:T(8,128)(2,1)} %value_ref.3, f32[8,256]{1,0:T(8,128)} %bitcast.55), custom_call_target="tpu_custom_call" | custom-call | flops 3000000000 | bytes 9000000 | tf_op jit(solution)/shard_map/send/pallas_call | solution.py:394
  3.7 0.0 copy-start.1
  3.7 0.0 copy-start.6
  3.7 12.0 %all-to-all-start.1 = ((f32[32,72,128]{2,1,0:T(8,128)}), f32[32,72,128]{2,1,0:T(8,128)S(1)}, u32[]{:S(2)}, u32[]{:S(2)}) async-start(f32[32,72,128]{2,1,0:T(8,128)} %get-tuple-element.54), calls=%async_computation.1 | async-start | bytes 2359296 | tf_op jit(solution)/shard_map/all_to_all | solution.py:348
  15.8 0.0 copy-done.1
  15.8 0.0 copy-done.6
  15.8 0.0 copy-start
  15.8 0.0 copy-start.8
  15.8 0.0 copy-start.10
  15.8 0.0 copy-start.11
  15.8 0.0 copy-start.12
  15.8 0.6 query.1
  16.4 1.3 %collective-permute-start = (f32[2,72,128]{2,1,0:T(8,128)S(1)}, f32[2,72,128]{2,1,0:T(8,128)S(1)}, u32[]{:S(2)}, u32[]{:S(2)}) collective-permute-start(f32[2,72,128]{2,1,0:T(8,128)S(1)} %get-tuple-element.59), channel_id=1, source_target_pairs={{0,64},{64,128},{128,192},{192,0},{1,65},{65,129},{129,193},{193,1... | collective-permute-start | bytes 221192 | tf_op jit(solution)/shard_map/ppermute | solution.py:339
  17.7 2.4 %collective-permute-start.1 = (f32[2,72,128]{2,1,0:T(8,128)S(1)}, f32[2,72,128]{2,1,0:T(8,128)S(1)}, u32[]{:S(2)}, u32[]{:S(2)}) collective-permute-start(f32[2,72,128]{2,1,0:T(8,128)S(1)} %get-tuple-element.60), channel_id=1, source_target_pairs={{0,128},{64,192},{128,0},{192,64},{1,129},{65,193},{129,1},{193,65... | collective-permute-start | bytes 221192 | tf_op jit(solution)/shard_map/ppermute | solution.py:339
  20.2 1.1 %collective-permute-start.2 = (f32[2,72,128]{2,1,0:T(8,128)S(1)}, f32[2,72,128]{2,1,0:T(8,128)S(1)}, u32[]{:S(2)}, u32[]{:S(2)}) collective-permute-start(f32[2,72,128]{2,1,0:T(8,128)S(1)} %get-tuple-element.61), channel_id=1, source_target_pairs={{0,192},{64,0},{128,64},{192,128},{1,193},{65,1},{129,65},{193,129... | collective-permute-start | bytes 221192 | tf_op jit(solution)/shard_map/ppermute | solution.py:339
  21.3 0.6 collective-permute-done.refs_1_
  21.9 4.3 %collective-permute-done.1.refs_2_ = f32[2,72,128]{2,1,0:T(8,128)S(1)} collective-permute-done((f32[2,72,128]{2,1,0:T(8,128)S(1)}, f32[2,72,128]{2,1,0:T(8,128)S(1)}, u32[]{:S(2)}, u32[]{:S(2)}) %collective-permute-start.1) | collective-permute-done | bytes 73760 | tf_op jit(solution)/shard_map/ppermute | solution.py:339
  26.2 0.0 collective-permute-done.2.refs_3_
  26.2 2.3 %collective-permute-start.3 = (f32[4,72,128]{2,1,0:T(8,128)S(1)}, f32[4,72,128]{2,1,0:T(8,128)S(1)}, u32[]{:S(2)}, u32[]{:S(2)}) collective-permute-start(f32[4,72,128]{2,1,0:T(8,128)S(1)} %pad_maximum_fusion.2), channel_id=1, source_target_pairs={{0,8},{8,0},{16,24},{24,16},{32,40},{40,32},{48,56},{56,48},{1,9},... | collective-permute-start | bytes 442376 | tf_op jit(solution)/shard_map/ppermute | solution.py:344
  28.5 0.0 copy-done
  28.5 0.0 copy-done.8
  28.5 0.0 copy-done.10
  28.5 0.0 copy-done.11
  28.5 0.0 copy-done.12
  28.5 1.9 %intra.1 = (f32[256,1024]{1,0:T(8,128)S(1)}, f32[256,8]{1,0:T(8,128)S(1)}) custom-call(s32[4]{0:T(128)S(1)} %copy-done.12, s32[1]{0:T(128)} %bitcast.20.here, bf16[256,1024]{1,0:T(8,128)(2,1)S(1)} %copy-done, bf16[256,1024]{1,0:T(8,128)(2,1)S(1)} %copy-done.10, bf16[256,1024]{1,0:T(8,128)(2,1)S(1)} %copy-done.8, f32[8,256]{1,0:T(8,128)S(1)} %bitcast.56), custom_call_target="tpu_custom_call" | custom-call | flops 3000000000 | bytes 9000000 | tf_op jit(solution)/shard_map/intra/pallas_call | solution.py:417
  30.4 15.3 %collective-permute-done.3.refs_4_ = f32[4,72,128]{2,1,0:T(8,128)S(1)} collective-permute-done((f32[4,72,128]{2,1,0:T(8,128)S(1)}, f32[4,72,128]{2,1,0:T(8,128)S(1)}, u32[]{:S(2)}, u32[]{:S(2)}) %collective-permute-start.3) | collective-permute-done | bytes 147488 | tf_op jit(solution)/shard_map/ppermute | solution.py:344
  45.7 0.0 all-to-all-done.1.give_ref
  46.3 0.6 conditional.1
  46.4 0.6 broadcast.53
  47.0 1.7 %scan.1 = (f32[32,32,128]{2,1,0:T(8,128)}, f32[4,32,128]{2,1,0:T(8,128)S(1)}) custom-call(s32[4]{0:T(128)S(1)} %copy-done.12, f32[32,72,128]{2,1,0:T(8,128)S(1)} %all-to-all-done.1.give_ref, f32[3,32,128]{2,1,0:T(8,128)} %get-tuple-element.119.extra_ref), custom_call_target="tpu_custom_call" | custom-call | flops 2000000000 | bytes 6000000 | tf_op jit(solution)/shard_map/scan/pallas_call | solution.py:435
  48.6 1.8 %collective-permute-start.4 = (f32[4,32,128]{2,1,0:T(8,128)S(1)}, f32[4,32,128]{2,1,0:T(8,128)S(1)}, u32[]{:S(2)}, u32[]{:S(2)}) collective-permute-start(f32[4,32,128]{2,1,0:T(8,128)S(1)} %get-tuple-element.77.refs_5_), channel_id=1, source_target_pairs={{0,16},{8,24},{16,32},{24,40},{32,48},{40,56},{48,0},{56,8},{1,17}... | collective-permute-start | bytes 196616 | tf_op jit(solution)/shard_map/ppermute | solution.py:339
  50.4 3.5 %collective-permute-start.5 = (f32[4,32,128]{2,1,0:T(8,128)S(1)}, f32[4,32,128]{2,1,0:T(8,128)S(1)}, u32[]{:S(2)}, u32[]{:S(2)}) collective-permute-start(f32[4,32,128]{2,1,0:T(8,128)S(1)} %get-tuple-element.77.refs_5_), channel_id=1, source_target_pairs={{0,32},{8,40},{16,48},{24,56},{32,0},{40,8},{48,16},{56,24},{1,33}... | collective-permute-start | bytes 196616 | tf_op jit(solution)/shard_map/ppermute | solution.py:339
  53.9 3.3 %collective-permute-start.6 = (f32[4,32,128]{2,1,0:T(8,128)S(1)}, f32[4,32,128]{2,1,0:T(8,128)S(1)}, u32[]{:S(2)}, u32[]{:S(2)}) collective-permute-start(f32[4,32,128]{2,1,0:T(8,128)S(1)} %get-tuple-element.77.refs_5_), channel_id=1, source_target_pairs={{0,48},{8,56},{16,0},{24,8},{32,16},{40,24},{48,32},{56,40},{1,49}... | collective-permute-start | bytes 196616 | tf_op jit(solution)/shard_map/ppermute | solution.py:339
  57.3 0.0 collective-permute-done.4.refs_6_
  57.3 1.1 %collective-permute-done.5.refs_7_ = f32[4,32,128]{2,1,0:T(8,128)S(1)} collective-permute-done((f32[4,32,128]{2,1,0:T(8,128)S(1)}, f32[4,32,128]{2,1,0:T(8,128)S(1)}, u32[]{:S(2)}, u32[]{:S(2)}) %collective-permute-start.5) | collective-permute-done | bytes 65568 | tf_op jit(solution)/shard_map/ppermute | solution.py:339
  58.4 1.0 %collective-permute-done.6.refs_8_ = f32[4,32,128]{2,1,0:T(8,128)S(1)} collective-permute-done((f32[4,32,128]{2,1,0:T(8,128)S(1)}, f32[4,32,128]{2,1,0:T(8,128)S(1)}, u32[]{:S(2)}, u32[]{:S(2)}) %collective-permute-start.6) | collective-permute-done | bytes 65568 | tf_op jit(solution)/shard_map/ppermute | solution.py:339
  59.4 8.4 %all-to-all-start.2 = ((f32[32,32,128]{2,1,0:T(8,128)}), f32[32,32,128]{2,1,0:T(8,128)S(1)}, u32[]{:S(2)}, u32[]{:S(2)}) async-start(f32[32,32,128]{2,1,0:T(8,128)} %get-tuple-element.66), calls=%async_computation.2 | async-start | bytes 1048576 | tf_op jit(solution)/shard_map/all_to_all | solution.py:348
  67.7 0.0 copy-start.2
  67.7 0.0 copy-start.3
  67.8 0.0 copy-start.4
  67.8 0.5 project.1
  68.3 2.6 %collective-permute-start.7 = (f32[2,64,128]{2,1,0:T(8,128)S(1)}, f32[2,64,128]{2,1,0:T(8,128)S(1)}, u32[]{:S(2)}, u32[]{:S(2)}) collective-permute-start(f32[2,64,128]{2,1,0:T(8,128)S(1)} %get-tuple-element.82), channel_id=1, source_target_pairs={{0,192},{64,0},{128,64},{192,128},{1,193},{65,1},{129,65},{193,129... | collective-permute-start | bytes 196616 | tf_op jit(solution)/shard_map/ppermute | solution.py:339
  70.8 0.5 collective-permute-start.8
  71.4 0.6 collective-permute-start.9
  72.0 0.6 collective-permute-done.7.refs_1_
  72.6 3.9 %collective-permute-done.8.refs_2_ = f32[2,64,128]{2,1,0:T(8,128)S(1)} collective-permute-done((f32[2,64,128]{2,1,0:T(8,128)S(1)}, f32[2,64,128]{2,1,0:T(8,128)S(1)}, u32[]{:S(2)}, u32[]{:S(2)}) %collective-permute-start.8) | collective-permute-done | bytes 65568 | tf_op jit(solution)/shard_map/ppermute | solution.py:339
  76.5 1.3 %collective-permute-done.9.refs_3_ = f32[2,64,128]{2,1,0:T(8,128)S(1)} collective-permute-done((f32[2,64,128]{2,1,0:T(8,128)S(1)}, f32[2,64,128]{2,1,0:T(8,128)S(1)}, u32[]{:S(2)}, u32[]{:S(2)}) %collective-permute-start.9) | collective-permute-done | bytes 65568 | tf_op jit(solution)/shard_map/ppermute | solution.py:339
  77.7 0.9 collective-permute-start.10
  78.6 0.0 copy-done.2
  78.6 0.0 copy-done.3
  78.6 0.0 copy-done.4
  78.6 0.7 local.1
  79.3 3.7 %collective-permute-done.10.refs_4_ = f32[4,64,128]{2,1,0:T(8,128)S(1)} collective-permute-done((f32[4,64,128]{2,1,0:T(8,128)S(1)}, f32[4,64,128]{2,1,0:T(8,128)S(1)}, u32[]{:S(2)}, u32[]{:S(2)}) %collective-permute-start.10) | collective-permute-done | bytes 131104 | tf_op jit(solution)/shard_map/ppermute | solution.py:344
  83.0 0.0 all-to-all-done.2.back_ref
  83.0 0.0 copy-start.5
  83.0 0.6 mixed.1
  83.6 12.6 %all_to_all.19.sums_ref = f32[8,4,128]{2,1,0:T(4,128)S(1)} all-to-all(f32[8,4,128]{2,1,0:T(4,128)S(1)} %get-tuple-element.85), channel_id=1, replica_groups=mesh['seq_0'=4,'seq_1'=8,'head'=8] {'head'}, dimensions={0} | all-to-all | bytes 32768 | tf_op jit(solution)/shard_map/all_to_all | solution.py:348
  96.2 0.0 copy-done.5
  96.2 1.1 %final.1 = (bf16[256,1024]{1,0:T(8,128)(2,1)}, bf16[4,16,1024]{2,1,0:T(8,128)(2,1)}) custom-call(f32[8,4,128]{2,1,0:T(4,128)S(1)} %all_to_all.19.sums_ref, f32[256,1024]{1,0:T(8,128)S(1)} %get-tuple-element.86.mixed_ref, f32[64,1024]{1,0:T(8,128)S(1)} %get-tuple-element.87.dec_ref, f32[1,1024]{1,0:T(1,128)S(1)} %bitcast.47), custom_call_target="tpu_custom_call" | custom-call | flops 2000000000 | bytes 6000000 | tf_op jit(solution)/shard_map/final/pallas_call | solution.py:483
  (10 shorter events, 0.1 us)
Async XLA Ops:
  3.7 12.0 %copy-start.1 = (bf16[4,16,1024]{2,1,0:T(8,128)(2,1)S(1)}, bf16[4,16,1024]{2,1,0:T(8,128)(2,1)}, u32[]{:S(2)}) copy-start(bf16[4,16,1024]{2,1,0:T(8,128)(2,1)} %sq_ref.1) | copy-start | bytes 393220
  3.7 12.0 %copy-start.6 = (s32[16]{0:T(128)S(1)}, s32[16]{0:T(128)}, u32[]{:S(2)}) copy-start(s32[16]{0:T(128)} %rows.1) | copy-start | bytes 196
  3.7 42.0 %all-to-all-start.1 = ((f32[32,72,128]{2,1,0:T(8,128)}), f32[32,72,128]{2,1,0:T(8,128)S(1)}, u32[]{:S(2)}, u32[]{:S(2)}) async-start(f32[32,72,128]{2,1,0:T(8,128)} %get-tuple-element.54), calls=%async_computation.1 | async-start | bytes 2359296 | tf_op jit(solution)/shard_map/all_to_all | solution.py:348
  15.8 12.7 %copy-start = (bf16[256,1024]{1,0:T(8,128)(2,1)S(1)}, bf16[256,1024]{1,0:T(8,128)(2,1)}, u32[]{:S(2)}) copy-start(bf16[256,1024]{1,0:T(8,128)(2,1)} %query_ref.5) | copy-start | bytes 1572868
  15.8 12.7 %copy-start.8 = (bf16[256,1024]{1,0:T(8,128)(2,1)S(1)}, bf16[256,1024]{1,0:T(8,128)(2,1)}, u32[]{:S(2)}) copy-start(bf16[256,1024]{1,0:T(8,128)(2,1)} %value_ref.3) | copy-start | bytes 1572868
  15.8 12.7 %copy-start.10 = (bf16[256,1024]{1,0:T(8,128)(2,1)S(1)}, bf16[256,1024]{1,0:T(8,128)(2,1)}, u32[]{:S(2)}) copy-start(bf16[256,1024]{1,0:T(8,128)(2,1)} %key_ref.3) | copy-start | bytes 1572868
  15.8 12.7 %copy-start.11 = (f32[256,8]{0,1:T(8,128)S(1)}, f32[256,8]{0,1:T(8,128)}, u32[]{:S(2)}) copy-start(f32[256,8]{0,1:T(8,128)} %param.16) | copy-start | bytes 24580
  15.8 12.7 %copy-start.12 = (s32[4]{0:T(128)S(1)}, s32[4]{0:T(128)}, u32[]{:S(2)}) copy-start(s32[4]{0:T(128)} %lens.5) | copy-start | bytes 52
  16.4 5.5 %collective-permute-start = (f32[2,72,128]{2,1,0:T(8,128)S(1)}, f32[2,72,128]{2,1,0:T(8,128)S(1)}, u32[]{:S(2)}, u32[]{:S(2)}) collective-permute-start(f32[2,72,128]{2,1,0:T(8,128)S(1)} %get-tuple-element.59), channel_id=1, source_target_pairs={{0,64},{64,128},{128,192},{192,0},{1,65},{65,129},{129,193},{193,1... | collective-permute-start | bytes 221192 | tf_op jit(solution)/shard_map/ppermute | solution.py:339
  17.7 8.4 %collective-permute-start.1 = (f32[2,72,128]{2,1,0:T(8,128)S(1)}, f32[2,72,128]{2,1,0:T(8,128)S(1)}, u32[]{:S(2)}, u32[]{:S(2)}) collective-permute-start(f32[2,72,128]{2,1,0:T(8,128)S(1)} %get-tuple-element.60), channel_id=1, source_target_pairs={{0,128},{64,192},{128,0},{192,64},{1,129},{65,193},{129,1},{193,65... | collective-permute-start | bytes 221192 | tf_op jit(solution)/shard_map/ppermute | solution.py:339
  20.2 6.0 %collective-permute-start.2 = (f32[2,72,128]{2,1,0:T(8,128)S(1)}, f32[2,72,128]{2,1,0:T(8,128)S(1)}, u32[]{:S(2)}, u32[]{:S(2)}) collective-permute-start(f32[2,72,128]{2,1,0:T(8,128)S(1)} %get-tuple-element.61), channel_id=1, source_target_pairs={{0,192},{64,0},{128,64},{192,128},{1,193},{65,1},{129,65},{193,129... | collective-permute-start | bytes 221192 | tf_op jit(solution)/shard_map/ppermute | solution.py:339
  26.2 19.5 %collective-permute-start.3 = (f32[4,72,128]{2,1,0:T(8,128)S(1)}, f32[4,72,128]{2,1,0:T(8,128)S(1)}, u32[]{:S(2)}, u32[]{:S(2)}) collective-permute-start(f32[4,72,128]{2,1,0:T(8,128)S(1)} %pad_maximum_fusion.2), channel_id=1, source_target_pairs={{0,8},{8,0},{16,24},{24,16},{32,40},{40,32},{48,56},{56,48},{1,9},... | collective-permute-start | bytes 442376 | tf_op jit(solution)/shard_map/ppermute | solution.py:344
  48.6 8.6 %collective-permute-start.4 = (f32[4,32,128]{2,1,0:T(8,128)S(1)}, f32[4,32,128]{2,1,0:T(8,128)S(1)}, u32[]{:S(2)}, u32[]{:S(2)}) collective-permute-start(f32[4,32,128]{2,1,0:T(8,128)S(1)} %get-tuple-element.77.refs_5_), channel_id=1, source_target_pairs={{0,16},{8,24},{16,32},{24,40},{32,48},{40,56},{48,0},{56,8},{1,17}... | collective-permute-start | bytes 196616 | tf_op jit(solution)/shard_map/ppermute | solution.py:339
  50.4 8.0 %collective-permute-start.5 = (f32[4,32,128]{2,1,0:T(8,128)S(1)}, f32[4,32,128]{2,1,0:T(8,128)S(1)}, u32[]{:S(2)}, u32[]{:S(2)}) collective-permute-start(f32[4,32,128]{2,1,0:T(8,128)S(1)} %get-tuple-element.77.refs_5_), channel_id=1, source_target_pairs={{0,32},{8,40},{16,48},{24,56},{32,0},{40,8},{48,16},{56,24},{1,33}... | collective-permute-start | bytes 196616 | tf_op jit(solution)/shard_map/ppermute | solution.py:339
  53.9 5.4 %collective-permute-start.6 = (f32[4,32,128]{2,1,0:T(8,128)S(1)}, f32[4,32,128]{2,1,0:T(8,128)S(1)}, u32[]{:S(2)}, u32[]{:S(2)}) collective-permute-start(f32[4,32,128]{2,1,0:T(8,128)S(1)} %get-tuple-element.77.refs_5_), channel_id=1, source_target_pairs={{0,48},{8,56},{16,0},{24,8},{32,16},{40,24},{48,32},{56,40},{1,49}... | collective-permute-start | bytes 196616 | tf_op jit(solution)/shard_map/ppermute | solution.py:339
  59.4 23.6 %all-to-all-start.2 = ((f32[32,32,128]{2,1,0:T(8,128)}), f32[32,32,128]{2,1,0:T(8,128)S(1)}, u32[]{:S(2)}, u32[]{:S(2)}) async-start(f32[32,32,128]{2,1,0:T(8,128)} %get-tuple-element.66), calls=%async_computation.2 | async-start | bytes 1048576 | tf_op jit(solution)/shard_map/all_to_all | solution.py:348
  67.7 10.9 %copy-start.2 = (bf16[4,16,1024]{2,1,0:T(8,128)(2,1)S(1)}, bf16[4,16,1024]{2,1,0:T(8,128)(2,1)}, u32[]{:S(2)}) copy-start(bf16[4,16,1024]{2,1,0:T(8,128)(2,1)} %sk_ref) | copy-start | bytes 393220
  67.7 10.9 %copy-start.3 = (bf16[4,16,1024]{2,1,0:T(8,128)(2,1)S(1)}, bf16[4,16,1024]{2,1,0:T(8,128)(2,1)}, u32[]{:S(2)}) copy-start(bf16[4,16,1024]{2,1,0:T(8,128)(2,1)} %sv_ref.1) | copy-start | bytes 393220
  67.8 10.8 %copy-start.4 = (f32[4,16,8]{1,2,0:T(8,128)S(1)}, f32[4,16,8]{1,2,0:T(8,128)}, u32[]{:S(2)}) copy-start(f32[4,16,8]{1,2,0:T(8,128)} %param.22) | copy-start | bytes 6148
  68.3 4.3 %collective-permute-start.7 = (f32[2,64,128]{2,1,0:T(8,128)S(1)}, f32[2,64,128]{2,1,0:T(8,128)S(1)}, u32[]{:S(2)}, u32[]{:S(2)}) collective-permute-start(f32[2,64,128]{2,1,0:T(8,128)S(1)} %get-tuple-element.82), channel_id=1, source_target_pairs={{0,192},{64,0},{128,64},{192,128},{1,193},{65,1},{129,65},{193,129... | collective-permute-start | bytes 196616 | tf_op jit(solution)/shard_map/ppermute | solution.py:339
  70.8 5.6 %collective-permute-start.8 = (f32[2,64,128]{2,1,0:T(8,128)S(1)}, f32[2,64,128]{2,1,0:T(8,128)S(1)}, u32[]{:S(2)}, u32[]{:S(2)}) collective-permute-start(f32[2,64,128]{2,1,0:T(8,128)S(1)} %get-tuple-element.83), channel_id=1, source_target_pairs={{0,128},{64,192},{128,0},{192,64},{1,129},{65,193},{129,1},{193,65... | collective-permute-start | bytes 196616 | tf_op jit(solution)/shard_map/ppermute | solution.py:339
  71.4 6.3 %collective-permute-start.9 = (f32[2,64,128]{2,1,0:T(8,128)S(1)}, f32[2,64,128]{2,1,0:T(8,128)S(1)}, u32[]{:S(2)}, u32[]{:S(2)}) collective-permute-start(f32[2,64,128]{2,1,0:T(8,128)S(1)} %get-tuple-element.84), channel_id=1, source_target_pairs={{0,64},{64,128},{128,192},{192,0},{1,65},{65,129},{129,193},{193,1... | collective-permute-start | bytes 196616 | tf_op jit(solution)/shard_map/ppermute | solution.py:339
  77.7 5.3 %collective-permute-start.10 = (f32[4,64,128]{2,1,0:T(8,128)S(1)}, f32[4,64,128]{2,1,0:T(8,128)S(1)}, u32[]{:S(2)}, u32[]{:S(2)}) collective-permute-start(f32[4,64,128]{2,1,0:T(8,128)S(1)} %pad_maximum_fusion.3), channel_id=1, source_target_pairs={{0,8},{8,0},{16,24},{24,16},{32,40},{40,32},{48,56},{56,48},{1,9},... | collective-permute-start | bytes 393224 | tf_op jit(solution)/shard_map/ppermute | solution.py:344
  83.0 13.2 %copy-start.5 = (f32[1024]{0:T(1024)S(1)}, f32[1024]{0:T(1024)}, u32[]{:S(2)}) copy-start(f32[1024]{0:T(1024)} %param.17) | copy-start | bytes 12292

commit v11 on v10

--- a/solution.py
+++ b/solution.py
@@ -223,7 +223,7 @@
         )
 
 
-def scan_kernel(lens, give_ref, extra_ref, entry_ref, slice_ref):
+def slice_kernel(lens, give_ref, extra_ref, slice_ref, entry_ref):
     ends = bounds(lens)
     state = jnp.zeros((QUART, HDIM), F32)
     for k in range(NDEV):
@@ -243,6 +243,13 @@
         tail = jnp.where(slot == 0, give_ref[b, T0:S0, :], extra_ref[p])
         tail = jnp.where(whole, give_ref[b, 0:T0, :], tail)
         slice_ref[p] = lead * entry_ref[b] + tail
+
+
+def entry_kernel(give_ref, entry_ref):
+    state = jnp.zeros((QUART, HDIM), F32)
+    for k in range(NDEV):
+        entry_ref[k] = state
+        state = give_ref[k, S0 : S0 + 1, :] * state + give_ref[k, 0:T0, :]
 
 
 def project_kernel(here, *refs):
@@ -278,9 +285,24 @@
             ref[db] = res[at : at + NROW, :]
 
 
-def mixed_kernel(here, query_ref, back_ref, intra_ref, carried_ref, local_ref, scarried_ref, *refs):
+def mixed_kernel(query_ref, back_ref, intra_ref, carried_ref, mixed_ref, sums_ref):
+    acc = jnp.zeros((BLOCK, HDIM), F32)
+    for h in range(HEADS):
+        cols = slice(h * HDIM, (h + 1) * HDIM)
+        state = jnp.concatenate([back_ref[owner(h, g)] for g in range(NQ)], axis=0).astype(BF)
+        outer = jnp.dot(query_ref[:, cols], state, preferred_element_type=F32)
+        mixed = intra_ref[:, cols] + outer * carried_ref[:, h : h + 1]
+        mixed_ref[:, cols] = mixed
+        acc = acc + mixed * mixed
+    flat = jnp.sum(acc.T, axis=0, keepdims=True)
+    sums_ref[...] = jnp.concatenate(
+        [flat[:, :HDIM], flat[:, HDIM:], jnp.zeros((6, HDIM), F32)], axis=0
+    )
+
+
+def decode_kernel(here, local_ref, scarried_ref, sums_ref, *refs):
     near, far = refs[:NX], refs[NX]
-    mixed_ref, dec_ref, send_ref, carry_ref = refs[NX + 1 :]
+    dec_ref, send_ref, carry_ref = refs[NX + 1 :]
     for dx in range(NX):
         carry_ref[mate_head(here, dx, 0)] = near[dx][0]
         carry_ref[mate_head(here, dx, 1)] = far[dx]
@@ -292,17 +314,7 @@
         acc = acc + dec * dec
     full = jnp.concatenate([acc, jnp.zeros((HDIM - NROW, HDIM), F32)], axis=0)
     dflat = jnp.sum(full.T, axis=0, keepdims=True)
-
-    acc = jnp.zeros((BLOCK, HDIM), F32)
-    for h in range(HEADS):
-        cols = slice(h * HDIM, (h + 1) * HDIM)
-        state = jnp.concatenate([back_ref[owner(h, g)] for g in range(NQ)], axis=0).astype(BF)
-        outer = jnp.dot(query_ref[:, cols], state, preferred_element_type=F32)
-        mixed = intra_ref[:, cols] + outer * carried_ref[:, h : h + 1]
-        mixed_ref[:, cols] = mixed
-        acc = acc + mixed * mixed
-    flat = jnp.sum(acc.T, axis=0, keepdims=True)
-    both = jnp.concatenate([flat[:, :HDIM], flat[:, HDIM:], dflat, dflat], axis=0)
+    both = jnp.concatenate([sums_ref[0:2, :], dflat, dflat], axis=0)
     for k in range(HEADS):
         send_ref[k] = both
 
@@ -432,15 +444,26 @@
         lambda: more_tails(key_in, value_in, log_decay, prompt_lengths, me * BLOCK),
         lambda: jnp.zeros((LAST, QUART, HDIM), F32),
     )
-    entry, own = pl.pallas_call(
-        scan_kernel,
-        out_shape=(shape(NDEV, QUART, HDIM), shape(PROMPTS, QUART, HDIM)),
+    own = pl.pallas_call(
+        slice_kernel,
+        out_shape=shape(PROMPTS, QUART, HDIM),
         in_specs=[SMEM] + [VMEM] * 2,
-        out_specs=(VMEM,) * 2,
+        out_specs=VMEM,
+        scratch_shapes=[pltpu.VMEM((NDEV, QUART, HDIM), F32)],
+        compiler_params=params(),
+        cost_estimate=cost(1),
+        name="slice",
+    )(prompt_lengths, given, extra)
+    given, own = lax.optimization_barrier((given, own))
+    entry = pl.pallas_call(
+        entry_kernel,
+        out_shape=shape(NDEV, QUART, HDIM),
+        in_specs=[VMEM],
+        out_specs=VMEM,
         compiler_params=params(),
         cost_estimate=cost(2),
-        name="scan",
-    )(prompt_lengths, given, extra)
+        name="entry",
+    )(given)
     slabs = [own] + [shift(own, "seq_1", NZ, 2 * d) for d in range(1, NQ)]
     entry, slabs, step_key = lax.optimization_barrier((entry, slabs, step_key))
     back = exchange(entry, SEQ)
@@ -468,16 +491,25 @@
     products = [products[0]] + [shift(products[d], "seq_0", NX, -d) for d in range(1, NX)]
     far_products = over_pair(products)
 
-    mixed, dec, sums_send = pl.pallas_call(
+    mixed, sums = pl.pallas_call(
         mixed_kernel,
-        out_shape=(shape(BLOCK, width), shape(n, width), shape(HEADS, 4, HDIM)),
-        in_specs=[SMEM] + [VMEM] * (7 + NX),
-        out_specs=(VMEM,) * 3,
+        out_shape=(shape(BLOCK, width), shape(8, HDIM)),
+        in_specs=[VMEM] * 4,
+        out_specs=(VMEM,) * 2,
+        compiler_params=params(),
+        cost_estimate=cost(1),
+        name="mixed",
+    )(query_in, back, intra, carried)
+    dec, sums_send = pl.pallas_call(
+        decode_kernel,
+        out_shape=(shape(n, width), shape(HEADS, 4, HDIM)),
+        in_specs=[SMEM] + [VMEM] * (4 + NX),
+        out_specs=(VMEM,) * 2,
         scratch_shapes=[pltpu.VMEM((HEADS, NROW, HDIM), F32)],
         compiler_params=params(),
-        cost_estimate=cost(2),
-        name="mixed",
-    )(here, query_in, back, intra, carried, local_dec, scarried, *products, far_products)
+        cost_estimate=cost(1),
+        name="decode",
+    )(here, local_dec, scarried, sums, *products, far_products)
     sums_all = exchange(sums_send, "head")
 
     return pl.pallas_call(

time: 97.7 us -> 95.7 us (0.980)
  waiting for transfers between devices: 31.6 us -> 28.8 us
    ppermute x2, waiting for transfers between devices: 19 us -> 16.6 us  [over_pair(): return lax.ppermute(both, 'seq_1', [(i, i ^ 1) for i in range(NZ)])]
    ppermute x9, waiting for transfers between devices: 12.7 us -> 11.4 us  [shift(): return lax.ppermute(x, axis, [(i, (i + d) % size) for i in range(size)])]
    pallas_call x2 -> x4, Pallas kernels: 2.25 us -> 2.23 us  [the longest x1 0.86 us: local(): pl.pallas_call(entry_kernel, out_shape=shape(NDEV, QUART, HDIM), in_specs...]
  transfers between devices with their start and end apart: 13 -> 13, of which waited for: 9 -> 10; matrix products, arithmetic and copies ran while one was open for 0% -> 0% of each run, Pallas kernels for 4% -> 5%
where the time goes in v11:
time: 95.7 us; the launch traced here: 95.3 us
  starting transfers between devices  41.3 us (43%)
  waiting for transfers between devices  28.8 us (30%)
  blocking collectives  12.6 us (13%)
  Pallas kernels  10 us (10%)
  between operations  1.51 us (2%)
  local copies, waits for them, and re-layouts  1.05 us (1%)
    all_to_all x2, starting transfers between devices, exchange(): return lax.all_to_all(x, axis, split_axis=0, concat_axis=0, tiled=True)  20.7 us
    ppermute x9, starting transfers between devices, shift(): return lax.ppermute(x, axis, [(i, (i + d) % size) for i in range(size)])  17.3 us
    ppermute x2, waiting for transfers between devices, over_pair(): return lax.ppermute(both, 'seq_1', [(i, i ^ 1) for i in range(NZ)])  16.6 us
    all_to_all x1, blocking collectives, exchange(): return lax.all_to_all(x, axis, split_axis=0, concat_axis=0, tiled=True)  12.6 us
    ppermute x9, waiting for transfers between devices, shift(): return lax.ppermute(x, axis, [(i, (i + d) % size) for i in range(size)])  11.4 us
    ppermute x2, starting transfers between devices, over_pair(): return lax.ppermute(both, 'seq_1', [(i, i ^ 1) for i in range(NZ)])  3.3 us
    pallas_call x1, Pallas kernels, local(): pl.pallas_call(send_kernel, out_shape=(shape(NDEV, GIVE, HDIM), shape(1,...  3.07 us
  transfers between devices with their start and end apart: 13, of which 10 were waited for; matrix products, arithmetic and copies ran while one was open for 0% of the time, Pallas kernels for 5%

profile of v11, /device:TPU:1, one launch (start us, length us, event | category | flops | bytes accessed | tf_op | source)
XLA Modules:
  0.0 95.3 jit_solution(17229323154027648380)
XLA Ops:
  0.6 3.1 %send.1 = (f32[32,72,128]{2,1,0:T(8,128)}, s32[1]{0:T(128)}) custom-call(s32[4]{0:T(128)} %lens.5, s32[1]{0:T(128)} %bitcast.20.here, bf16[256,1024]{1,0:T(8,128)(2,1)} %key_ref.3, bf16[256,1024]{1,0:T(8,128)(2,1)} %value_ref.3, f32[8,256]{1,0:T(8,128)} %bitcast.55), custom_call_target="tpu_custom_call" | custom-call | flops 3000000000 | bytes 9000000 | tf_op jit(solution)/shard_map/send/pallas_call | solution.py:406
  3.7 0.0 copy-start.1
  3.7 0.0 copy-start.6
  3.7 12.0 %all-to-all-start.1 = ((f32[32,72,128]{2,1,0:T(8,128)}), f32[32,72,128]{2,1,0:T(8,128)S(1)}, u32[]{:S(2)}, u32[]{:S(2)}) async-start(f32[32,72,128]{2,1,0:T(8,128)} %get-tuple-element.55), calls=%async_computation.1 | async-start | bytes 2359296 | tf_op jit(solution)/shard_map/all_to_all | solution.py:360
  15.8 0.0 copy-done.1
  15.8 0.0 copy-done.6
  15.8 0.0 copy-start
  15.8 0.0 copy-start.9
  15.8 0.0 copy-start.10
  15.8 0.0 copy-start.11
  15.8 0.0 copy-start.12
  15.8 0.6 query.1
  16.4 1.3 %collective-permute-start = (f32[2,72,128]{2,1,0:T(8,128)S(1)}, f32[2,72,128]{2,1,0:T(8,128)S(1)}, u32[]{:S(2)}, u32[]{:S(2)}) collective-permute-start(f32[2,72,128]{2,1,0:T(8,128)S(1)} %get-tuple-element.60), channel_id=1, source_target_pairs={{0,64},{64,128},{128,192},{192,0},{1,65},{65,129},{129,193},{193,1... | collective-permute-start | bytes 221192 | tf_op jit(solution)/shard_map/ppermute | solution.py:351
  17.7 2.4 %collective-permute-start.1 = (f32[2,72,128]{2,1,0:T(8,128)S(1)}, f32[2,72,128]{2,1,0:T(8,128)S(1)}, u32[]{:S(2)}, u32[]{:S(2)}) collective-permute-start(f32[2,72,128]{2,1,0:T(8,128)S(1)} %get-tuple-element.61), channel_id=1, source_target_pairs={{0,128},{64,192},{128,0},{192,64},{1,129},{65,193},{129,1},{193,65... | collective-permute-start | bytes 221192 | tf_op jit(solution)/shard_map/ppermute | solution.py:351
  20.2 1.1 %collective-permute-start.2 = (f32[2,72,128]{2,1,0:T(8,128)S(1)}, f32[2,72,128]{2,1,0:T(8,128)S(1)}, u32[]{:S(2)}, u32[]{:S(2)}) collective-permute-start(f32[2,72,128]{2,1,0:T(8,128)S(1)} %get-tuple-element.62), channel_id=1, source_target_pairs={{0,192},{64,0},{128,64},{192,128},{1,193},{65,1},{129,65},{193,129... | collective-permute-start | bytes 221192 | tf_op jit(solution)/shard_map/ppermute | solution.py:351
  21.3 0.6 collective-permute-done.refs_1_
  21.9 4.3 %collective-permute-done.1.refs_2_ = f32[2,72,128]{2,1,0:T(8,128)S(1)} collective-permute-done((f32[2,72,128]{2,1,0:T(8,128)S(1)}, f32[2,72,128]{2,1,0:T(8,128)S(1)}, u32[]{:S(2)}, u32[]{:S(2)}) %collective-permute-start.1) | collective-permute-done | bytes 73760 | tf_op jit(solution)/shard_map/ppermute | solution.py:351
  26.2 0.0 collective-permute-done.2.refs_3_
  26.2 2.3 %collective-permute-start.3 = (f32[4,72,128]{2,1,0:T(8,128)S(1)}, f32[4,72,128]{2,1,0:T(8,128)S(1)}, u32[]{:S(2)}, u32[]{:S(2)}) collective-permute-start(f32[4,72,128]{2,1,0:T(8,128)S(1)} %pad_maximum_fusion.2), channel_id=1, source_target_pairs={{0,8},{8,0},{16,24},{24,16},{32,40},{40,32},{48,56},{56,48},{1,9},... | collective-permute-start | bytes 442376 | tf_op jit(solution)/shard_map/ppermute | solution.py:356
  28.5 0.0 copy-done
  28.5 0.0 copy-done.9
  28.5 0.0 copy-done.10
  28.5 0.0 copy-done.11
  28.5 0.0 copy-done.12
  28.5 1.9 %intra.1 = (f32[256,1024]{1,0:T(8,128)S(1)}, f32[256,8]{1,0:T(8,128)S(1)}) custom-call(s32[4]{0:T(128)S(1)} %copy-done.12, s32[1]{0:T(128)} %bitcast.20.here, bf16[256,1024]{1,0:T(8,128)(2,1)S(1)} %copy-done, bf16[256,1024]{1,0:T(8,128)(2,1)S(1)} %copy-done.10, bf16[256,1024]{1,0:T(8,128)(2,1)S(1)} %copy-done.9, f32[8,256]{1,0:T(8,128)S(1)} %bitcast.56), custom_call_target="tpu_custom_call" | custom-call | flops 3000000000 | bytes 9000000 | tf_op jit(solution)/shard_map/intra/pallas_call | solution.py:429
  30.4 0.0 copy-start.7
  30.4 0.9 copy-done.7
  31.4 14.3 %collective-permute-done.3.refs_4_ = f32[4,72,128]{2,1,0:T(8,128)S(1)} collective-permute-done((f32[4,72,128]{2,1,0:T(8,128)S(1)}, f32[4,72,128]{2,1,0:T(8,128)S(1)}, u32[]{:S(2)}, u32[]{:S(2)}) %collective-permute-start.3) | collective-permute-done | bytes 147488 | tf_op jit(solution)/shard_map/ppermute | solution.py:356
  45.7 0.0 all-to-all-done.1.give_ref
  46.4 0.6 slice.73.refs_5_
  47.0 1.8 %collective-permute-start.4 = (f32[4,32,128]{2,1,0:T(8,128)S(1)}, f32[4,32,128]{2,1,0:T(8,128)S(1)}, u32[]{:S(2)}, u32[]{:S(2)}) collective-permute-start(f32[4,32,128]{2,1,0:T(8,128)S(1)} %slice.73.refs_5_), channel_id=1, source_target_pairs={{0,16},{8,24},{16,32},{24,40},{32,48},{40,56},{48,0},{56,8},{1,17}... | collective-permute-start | bytes 196616 | tf_op jit(solution)/shard_map/ppermute | solution.py:351
  48.8 3.5 %collective-permute-start.5 = (f32[4,32,128]{2,1,0:T(8,128)S(1)}, f32[4,32,128]{2,1,0:T(8,128)S(1)}, u32[]{:S(2)}, u32[]{:S(2)}) collective-permute-start(f32[4,32,128]{2,1,0:T(8,128)S(1)} %slice.73.refs_5_), channel_id=1, source_target_pairs={{0,32},{8,40},{16,48},{24,56},{32,0},{40,8},{48,16},{56,24},{1,33}... | collective-permute-start | bytes 196616 | tf_op jit(solution)/shard_map/ppermute | solution.py:351
  52.4 3.3 %collective-permute-start.6 = (f32[4,32,128]{2,1,0:T(8,128)S(1)}, f32[4,32,128]{2,1,0:T(8,128)S(1)}, u32[]{:S(2)}, u32[]{:S(2)}) collective-permute-start(f32[4,32,128]{2,1,0:T(8,128)S(1)} %slice.73.refs_5_), channel_id=1, source_target_pairs={{0,48},{8,56},{16,0},{24,8},{32,16},{40,24},{48,32},{56,40},{1,49}... | collective-permute-start | bytes 196616 | tf_op jit(solution)/shard_map/ppermute | solution.py:351
  55.7 0.9 entry.1
  56.5 0.0 collective-permute-done.4.refs_6_
  56.5 0.2 collective-permute-done.5.refs_7_
  56.8 0.6 collective-permute-done.6.refs_8_
  57.4 8.7 %all-to-all-start.2 = ((f32[32,32,128]{2,1,0:T(8,128)}), f32[32,32,128]{2,1,0:T(8,128)S(1)}, u32[]{:S(2)}, u32[]{:S(2)}) async-start(f32[32,32,128]{2,1,0:T(8,128)} %entry.1), calls=%async_computation.2 | async-start | bytes 1048576 | tf_op jit(solution)/shard_map/all_to_all | solution.py:360
  66.1 0.0 copy-start.2
  66.1 0.0 copy-start.3
  66.1 0.0 copy-start.4
  66.1 0.5 project.1
  66.6 2.6 %collective-permute-start.7 = (f32[2,64,128]{2,1,0:T(8,128)S(1)}, f32[2,64,128]{2,1,0:T(8,128)S(1)}, u32[]{:S(2)}, u32[]{:S(2)}) collective-permute-start(f32[2,64,128]{2,1,0:T(8,128)S(1)} %get-tuple-element.84), channel_id=1, source_target_pairs={{0,192},{64,0},{128,64},{192,128},{1,193},{65,1},{129,65},{193,129... | collective-permute-start | bytes 196616 | tf_op jit(solution)/shard_map/ppermute | solution.py:351
  69.2 0.5 collective-permute-start.8
  69.7 0.6 collective-permute-start.9
  70.3 1.2 %collective-permute-done.7.refs_1_ = f32[2,64,128]{2,1,0:T(8,128)S(1)} collective-permute-done((f32[2,64,128]{2,1,0:T(8,128)S(1)}, f32[2,64,128]{2,1,0:T(8,128)S(1)}, u32[]{:S(2)}, u32[]{:S(2)}) %collective-permute-start.7) | collective-permute-done | bytes 65568 | tf_op jit(solution)/shard_map/ppermute | solution.py:351
  71.5 3.3 %collective-permute-done.8.refs_2_ = f32[2,64,128]{2,1,0:T(8,128)S(1)} collective-permute-done((f32[2,64,128]{2,1,0:T(8,128)S(1)}, f32[2,64,128]{2,1,0:T(8,128)S(1)}, u32[]{:S(2)}, u32[]{:S(2)}) %collective-permute-start.8) | collective-permute-done | bytes 65568 | tf_op jit(solution)/shard_map/ppermute | solution.py:351
  74.8 1.3 %collective-permute-done.9.refs_3_ = f32[2,64,128]{2,1,0:T(8,128)S(1)} collective-permute-done((f32[2,64,128]{2,1,0:T(8,128)S(1)}, f32[2,64,128]{2,1,0:T(8,128)S(1)}, u32[]{:S(2)}, u32[]{:S(2)}) %collective-permute-start.9) | collective-permute-done | bytes 65568 | tf_op jit(solution)/shard_map/ppermute | solution.py:351
  76.1 1.0 %collective-permute-start.10 = (f32[4,64,128]{2,1,0:T(8,128)S(1)}, f32[4,64,128]{2,1,0:T(8,128)S(1)}, u32[]{:S(2)}, u32[]{:S(2)}) collective-permute-start(f32[4,64,128]{2,1,0:T(8,128)S(1)} %pad_maximum_fusion.3), channel_id=1, source_target_pairs={{0,8},{8,0},{16,24},{24,16},{32,40},{40,32},{48,56},{56,48},{1,9},... | collective-permute-start | bytes 393224 | tf_op jit(solution)/shard_map/ppermute | solution.py:356
  77.1 0.0 copy-done.2
  77.1 0.0 copy-done.3
  77.1 0.0 copy-done.4
  77.1 0.0 copy-start.8
  77.1 0.7 local.1
  77.8 0.8 all-to-all-done.2.back_ref
  78.6 0.0 copy-done.8
  78.6 0.5 mixed.1
  79.1 2.3 %collective-permute-done.10.refs_4_ = f32[4,64,128]{2,1,0:T(8,128)S(1)} collective-permute-done((f32[4,64,128]{2,1,0:T(8,128)S(1)}, f32[4,64,128]{2,1,0:T(8,128)S(1)}, u32[]{:S(2)}, u32[]{:S(2)}) %collective-permute-start.10) | collective-permute-done | bytes 131104 | tf_op jit(solution)/shard_map/ppermute | solution.py:356
  81.4 0.0 copy-start.5
  81.4 0.3 decode.1
  81.6 12.6 %all_to_all.19.sums_ref = f32[8,4,128]{2,1,0:T(4,128)S(1)} all-to-all(f32[8,4,128]{2,1,0:T(4,128)S(1)} %get-tuple-element.87), channel_id=1, replica_groups=mesh['seq_0'=4,'seq_1'=8,'head'=8] {'head'}, dimensions={0} | all-to-all | bytes 32768 | tf_op jit(solution)/shard_map/all_to_all | solution.py:360
  94.2 0.0 copy-done.5
  94.2 1.1 %final.1 = (bf16[256,1024]{1,0:T(8,128)(2,1)}, bf16[4,16,1024]{2,1,0:T(8,128)(2,1)}) custom-call(f32[8,4,128]{2,1,0:T(4,128)S(1)} %all_to_all.19.sums_ref, f32[256,1024]{1,0:T(8,128)S(1)} %get-tuple-element.88.mixed_ref, f32[64,1024]{1,0:T(8,128)S(1)} %get-tuple-element.89.dec_ref, f32[1,1024]{1,0:T(1,128)S(1)} %bitcast.47), custom_call_target="tpu_custom_call" | custom-call | flops 2000000000 | bytes 6000000 | tf_op jit(solution)/shard_map/final/pallas_call | solution.py:515
  (12 shorter events, 0.1 us)
Async XLA Ops:
  3.7 12.0 %copy-start.1 = (bf16[4,16,1024]{2,1,0:T(8,128)(2,1)S(1)}, bf16[4,16,1024]{2,1,0:T(8,128)(2,1)}, u32[]{:S(2)}) copy-start(bf16[4,16,1024]{2,1,0:T(8,128)(2,1)} %sq_ref.1) | copy-start | bytes 393220
  3.7 12.0 %copy-start.6 = (s32[16]{0:T(128)S(1)}, s32[16]{0:T(128)}, u32[]{:S(2)}) copy-start(s32[16]{0:T(128)} %rows.1) | copy-start | bytes 196
  3.7 42.0 %all-to-all-start.1 = ((f32[32,72,128]{2,1,0:T(8,128)}), f32[32,72,128]{2,1,0:T(8,128)S(1)}, u32[]{:S(2)}, u32[]{:S(2)}) async-start(f32[32,72,128]{2,1,0:T(8,128)} %get-tuple-element.55), calls=%async_computation.1 | async-start | bytes 2359296 | tf_op jit(solution)/shard_map/all_to_all | solution.py:360
  15.8 12.7 %copy-start = (bf16[256,1024]{1,0:T(8,128)(2,1)S(1)}, bf16[256,1024]{1,0:T(8,128)(2,1)}, u32[]{:S(2)}) copy-start(bf16[256,1024]{1,0:T(8,128)(2,1)} %query_ref.5) | copy-start | bytes 1572868
  15.8 12.7 %copy-start.9 = (bf16[256,1024]{1,0:T(8,128)(2,1)S(1)}, bf16[256,1024]{1,0:T(8,128)(2,1)}, u32[]{:S(2)}) copy-start(bf16[256,1024]{1,0:T(8,128)(2,1)} %value_ref.3) | copy-start | bytes 1572868
  15.8 12.7 %copy-start.10 = (bf16[256,1024]{1,0:T(8,128)(2,1)S(1)}, bf16[256,1024]{1,0:T(8,128)(2,1)}, u32[]{:S(2)}) copy-start(bf16[256,1024]{1,0:T(8,128)(2,1)} %key_ref.3) | copy-start | bytes 1572868
  15.8 12.7 %copy-start.11 = (f32[256,8]{0,1:T(8,128)S(1)}, f32[256,8]{0,1:T(8,128)}, u32[]{:S(2)}) copy-start(f32[256,8]{0,1:T(8,128)} %param.16) | copy-start | bytes 24580
  15.8 12.7 %copy-start.12 = (s32[4]{0:T(128)S(1)}, s32[4]{0:T(128)}, u32[]{:S(2)}) copy-start(s32[4]{0:T(128)} %lens.5) | copy-start | bytes 52
  16.4 5.5 %collective-permute-start = (f32[2,72,128]{2,1,0:T(8,128)S(1)}, f32[2,72,128]{2,1,0:T(8,128)S(1)}, u32[]{:S(2)}, u32[]{:S(2)}) collective-permute-start(f32[2,72,128]{2,1,0:T(8,128)S(1)} %get-tuple-element.60), channel_id=1, source_target_pairs={{0,64},{64,128},{128,192},{192,0},{1,65},{65,129},{129,193},{193,1... | collective-permute-start | bytes 221192 | tf_op jit(solution)/shard_map/ppermute | solution.py:351
  17.7 8.4 %collective-permute-start.1 = (f32[2,72,128]{2,1,0:T(8,128)S(1)}, f32[2,72,128]{2,1,0:T(8,128)S(1)}, u32[]{:S(2)}, u32[]{:S(2)}) collective-permute-start(f32[2,72,128]{2,1,0:T(8,128)S(1)} %get-tuple-element.61), channel_id=1, source_target_pairs={{0,128},{64,192},{128,0},{192,64},{1,129},{65,193},{129,1},{193,65... | collective-permute-start | bytes 221192 | tf_op jit(solution)/shard_map/ppermute | solution.py:351
  20.2 6.0 %collective-permute-start.2 = (f32[2,72,128]{2,1,0:T(8,128)S(1)}, f32[2,72,128]{2,1,0:T(8,128)S(1)}, u32[]{:S(2)}, u32[]{:S(2)}) collective-permute-start(f32[2,72,128]{2,1,0:T(8,128)S(1)} %get-tuple-element.62), channel_id=1, source_target_pairs={{0,192},{64,0},{128,64},{192,128},{1,193},{65,1},{129,65},{193,129... | collective-permute-start | bytes 221192 | tf_op jit(solution)/shard_map/ppermute | solution.py:351
  26.2 19.5 %collective-permute-start.3 = (f32[4,72,128]{2,1,0:T(8,128)S(1)}, f32[4,72,128]{2,1,0:T(8,128)S(1)}, u32[]{:S(2)}, u32[]{:S(2)}) collective-permute-start(f32[4,72,128]{2,1,0:T(8,128)S(1)} %pad_maximum_fusion.2), channel_id=1, source_target_pairs={{0,8},{8,0},{16,24},{24,16},{32,40},{40,32},{48,56},{56,48},{1,9},... | collective-permute-start | bytes 442376 | tf_op jit(solution)/shard_map/ppermute | solution.py:356
  30.4 1.0 %copy-start.7 = (f32[256,1024]{1,0:T(8,128)}, f32[256,1024]{1,0:T(8,128)S(1)}, u32[]{:S(2)}) copy-start(f32[256,1024]{1,0:T(8,128)S(1)} %get-tuple-element.71.intra_ref) | copy-start | bytes 3145732
  47.0 9.6 %collective-permute-start.4 = (f32[4,32,128]{2,1,0:T(8,128)S(1)}, f32[4,32,128]{2,1,0:T(8,128)S(1)}, u32[]{:S(2)}, u32[]{:S(2)}) collective-permute-start(f32[4,32,128]{2,1,0:T(8,128)S(1)} %slice.73.refs_5_), channel_id=1, source_target_pairs={{0,16},{8,24},{16,32},{24,40},{32,48},{40,56},{48,0},{56,8},{1,17}... | collective-permute-start | bytes 196616 | tf_op jit(solution)/shard_map/ppermute | solution.py:351
  48.8 8.0 %collective-permute-start.5 = (f32[4,32,128]{2,1,0:T(8,128)S(1)}, f32[4,32,128]{2,1,0:T(8,128)S(1)}, u32[]{:S(2)}, u32[]{:S(2)}) collective-permute-start(f32[4,32,128]{2,1,0:T(8,128)S(1)} %slice.73.refs_5_), channel_id=1, source_target_pairs={{0,32},{8,40},{16,48},{24,56},{32,0},{40,8},{48,16},{56,24},{1,33}... | collective-permute-start | bytes 196616 | tf_op jit(solution)/shard_map/ppermute | solution.py:351
  52.4 5.0 %collective-permute-start.6 = (f32[4,32,128]{2,1,0:T(8,128)S(1)}, f32[4,32,128]{2,1,0:T(8,128)S(1)}, u32[]{:S(2)}, u32[]{:S(2)}) collective-permute-start(f32[4,32,128]{2,1,0:T(8,128)S(1)} %slice.73.refs_5_), channel_id=1, source_target_pairs={{0,48},{8,56},{16,0},{24,8},{32,16},{40,24},{48,32},{56,40},{1,49}... | collective-permute-start | bytes 196616 | tf_op jit(solution)/shard_map/ppermute | solution.py:351
  57.4 21.2 %all-to-all-start.2 = ((f32[32,32,128]{2,1,0:T(8,128)}), f32[32,32,128]{2,1,0:T(8,128)S(1)}, u32[]{:S(2)}, u32[]{:S(2)}) async-start(f32[32,32,128]{2,1,0:T(8,128)} %entry.1), calls=%async_computation.2 | async-start | bytes 1048576 | tf_op jit(solution)/shard_map/all_to_all | solution.py:360
  66.1 11.0 %copy-start.2 = (bf16[4,16,1024]{2,1,0:T(8,128)(2,1)S(1)}, bf16[4,16,1024]{2,1,0:T(8,128)(2,1)}, u32[]{:S(2)}) copy-start(bf16[4,16,1024]{2,1,0:T(8,128)(2,1)} %sk_ref) | copy-start | bytes 393220
  66.1 11.0 %copy-start.3 = (bf16[4,16,1024]{2,1,0:T(8,128)(2,1)S(1)}, bf16[4,16,1024]{2,1,0:T(8,128)(2,1)}, u32[]{:S(2)}) copy-start(bf16[4,16,1024]{2,1,0:T(8,128)(2,1)} %sv_ref.1) | copy-start | bytes 393220
  66.1 11.0 %copy-start.4 = (f32[4,16,8]{1,2,0:T(8,128)S(1)}, f32[4,16,8]{1,2,0:T(8,128)}, u32[]{:S(2)}) copy-start(f32[4,16,8]{1,2,0:T(8,128)} %param.22) | copy-start | bytes 6148
  66.6 4.8 %collective-permute-start.7 = (f32[2,64,128]{2,1,0:T(8,128)S(1)}, f32[2,64,128]{2,1,0:T(8,128)S(1)}, u32[]{:S(2)}, u32[]{:S(2)}) collective-permute-start(f32[2,64,128]{2,1,0:T(8,128)S(1)} %get-tuple-element.84), channel_id=1, source_target_pairs={{0,192},{64,0},{128,64},{192,128},{1,193},{65,1},{129,65},{193,129... | collective-permute-start | bytes 196616 | tf_op jit(solution)/shard_map/ppermute | solution.py:351
  69.2 5.6 %collective-permute-start.8 = (f32[2,64,128]{2,1,0:T(8,128)S(1)}, f32[2,64,128]{2,1,0:T(8,128)S(1)}, u32[]{:S(2)}, u32[]{:S(2)}) collective-permute-start(f32[2,64,128]{2,1,0:T(8,128)S(1)} %get-tuple-element.85), channel_id=1, source_target_pairs={{0,128},{64,192},{128,0},{192,64},{1,129},{65,193},{129,1},{193,65... | collective-permute-start | bytes 196616 | tf_op jit(solution)/shard_map/ppermute | solution.py:351
  69.7 6.3 %collective-permute-start.9 = (f32[2,64,128]{2,1,0:T(8,128)S(1)}, f32[2,64,128]{2,1,0:T(8,128)S(1)}, u32[]{:S(2)}, u32[]{:S(2)}) collective-permute-start(f32[2,64,128]{2,1,0:T(8,128)S(1)} %get-tuple-element.86), channel_id=1, source_target_pairs={{0,64},{64,128},{128,192},{192,0},{1,65},{65,129},{129,193},{193,1... | collective-permute-start | bytes 196616 | tf_op jit(solution)/shard_map/ppermute | solution.py:351
  76.1 5.3 %collective-permute-start.10 = (f32[4,64,128]{2,1,0:T(8,128)S(1)}, f32[4,64,128]{2,1,0:T(8,128)S(1)}, u32[]{:S(2)}, u32[]{:S(2)}) collective-permute-start(f32[4,64,128]{2,1,0:T(8,128)S(1)} %pad_maximum_fusion.3), channel_id=1, source_target_pairs={{0,8},{8,0},{16,24},{24,16},{32,40},{40,32},{48,56},{56,48},{1,9},... | collective-permute-start | bytes 393224 | tf_op jit(solution)/shard_map/ppermute | solution.py:356
  77.1 1.5 %copy-start.8 = (f32[256,1024]{1,0:T(8,128)S(1)}, f32[256,1024]{1,0:T(8,128)}, u32[]{:S(2)}) copy-start(f32[256,1024]{1,0:T(8,128)} %copy-done.7) | copy-start | bytes 3145732
  81.4 12.9 %copy-start.5 = (f32[1024]{0:T(1024)S(1)}, f32[1024]{0:T(1024)}, u32[]{:S(2)}) copy-start(f32[1024]{0:T(1024)} %param.17) | copy-start | bytes 12292

commit v12 on v11

--- a/solution.py
+++ b/solution.py
@@ -25,6 +25,7 @@
 ROWS_DEV = 16
 NROW = STEPS * ROWS_DEV
 LAST = PROMPTS - 1
+ORDER = (0, 2, 1, 3)
 ASK = NROW + 8
 
 T0 = QUART
@@ -163,7 +164,7 @@
     ids = jnp.zeros((8, HDIM), F32)
     for k in range(ROWS_DEV):
         ids = jnp.where(lane == k, rows[k].astype(F32), ids)
-    for dx, out_ref in enumerate(out_refs):
+    for dx, out_ref in zip(ORDER, out_refs):
         for db in range(2):
             cols = pl.ds(pl.multiple_of(mate_head(here, dx, db) * HDIM, HDIM), HDIM)
             out_ref[db, :NROW, :] = query_ref[:, :, cols].astype(F32).reshape(NROW, HDIM)
@@ -255,7 +256,7 @@
 def project_kernel(here, *refs):
     near, far, slabs, outs, st_ref = refs[:NX], refs[NX], refs[NX + 1 : NX + 1 + NQ], refs[NX + 1 + NQ : -1], refs[-1]
     quarter = lax.rem(here[0], NZ) // 2
-    for d, ref in enumerate(slabs):
+    for d, ref in zip(ORDER, slabs):
         origin = lax.rem(quarter - d + NQ, NQ)
         for p in range(PROMPTS):
             at = pl.multiple_of(p * HDIM + origin * QUART, QUART)
@@ -303,9 +304,9 @@
 def decode_kernel(here, local_ref, scarried_ref, sums_ref, *refs):
     near, far = refs[:NX], refs[NX]
     dec_ref, send_ref, carry_ref = refs[NX + 1 :]
-    for dx in range(NX):
-        carry_ref[mate_head(here, dx, 0)] = near[dx][0]
-        carry_ref[mate_head(here, dx, 1)] = far[dx]
+    for k, dx in enumerate(ORDER):
+        carry_ref[mate_head(here, dx, 0)] = near[k][0]
+        carry_ref[mate_head(here, dx, 1)] = far[k]
     acc = jnp.zeros((NROW, HDIM), F32)
     for h in range(HEADS):
         cols = slice(h * HDIM, (h + 1) * HDIM)
@@ -354,6 +355,10 @@
 def over_pair(pieces):
     both = jnp.stack([piece[1] for piece in pieces])
     return lax.ppermute(both, "seq_1", [(i, i ^ 1) for i in range(NZ)])
+
+
+def spread(pieces, axis, size, step):
+    return [shift(x, axis, size, step * d) if d else x for x, d in zip(pieces, ORDER)]
 
 
 def exchange(x, axis):
@@ -423,7 +428,7 @@
         cost_estimate=cost(1),
         name="query",
     )(here, row_prompt, step_query)
-    queries = [queries[0]] + [shift(queries[d], "seq_0", NX, d) for d in range(1, NX)]
+    queries = spread(queries, "seq_0", NX, 1)
     far_queries = over_pair(queries)
 
     intra, carried = pl.pallas_call(
@@ -464,7 +469,7 @@
         cost_estimate=cost(2),
         name="entry",
     )(given)
-    slabs = [own] + [shift(own, "seq_1", NZ, 2 * d) for d in range(1, NQ)]
+    slabs = spread([own] * NQ, "seq_1", NZ, 2)
     entry, slabs, step_key = lax.optimization_barrier((entry, slabs, step_key))
     back = exchange(entry, SEQ)
 
@@ -488,7 +493,7 @@
         cost_estimate=cost(2),
         name="project",
     )(here, *queries, far_queries, *slabs)
-    products = [products[0]] + [shift(products[d], "seq_0", NX, -d) for d in range(1, NX)]
+    products = spread(products, "seq_0", NX, -1)
     far_products = over_pair(products)
 
     mixed, sums = pl.pallas_call(

time: 95.7 us -> 95.9 us (level)
  starting transfers between devices: 41.3 us -> 39.4 us
  waiting for transfers between devices: 28.8 us -> 30.3 us
    all_to_all x2, starting transfers between devices: 20.7 us -> 18.3 us  [exchange(): return lax.all_to_all(x, axis, split_axis=0, concat_axis=0, tiled=True)]
    ppermute x9, waiting for transfers between devices: 11.4 us -> 13.3 us  [shift(): return lax.ppermute(x, axis, [(i, (i + d) % size) for i in range(size)])]
    ppermute x9, starting transfers between devices: 17.3 us -> 18.5 us  [shift(): return lax.ppermute(x, axis, [(i, (i + d) % size) for i in range(size)])]
  transfers between devices with their start and end apart: 13 -> 13, of which waited for: 10 -> 7; matrix products, arithmetic and copies ran while one was open for 0% -> 0% of each run, Pallas kernels for 5% -> 5%
where the time goes in v12:
time: 95.9 us; the launch traced here: 95.5 us
  starting transfers between devices  39.4 us (41%)
  waiting for transfers between devices  30.3 us (32%)
  blocking collectives  12.6 us (13%)
  Pallas kernels  10 us (10%)
  local copies, waits for them, and re-layouts  1.57 us (2%)
  between operations  1.52 us (2%)
    ppermute x9, starting transfers between devices, shift(): return lax.ppermute(x, axis, [(i, (i + d) % size) for i in range(size)])  18.5 us
    all_to_all x2, starting transfers between devices, exchange(): return lax.all_to_all(x, axis, split_axis=0, concat_axis=0, tiled=True)  18.3 us
    ppermute x2, waiting for transfers between devices, over_pair(): return lax.ppermute(both, 'seq_1', [(i, i ^ 1) for i in range(NZ)])  17 us
    ppermute x9, waiting for transfers between devices, shift(): return lax.ppermute(x, axis, [(i, (i + d) % size) for i in range(size)])  13.3 us
    all_to_all x1, blocking collectives, exchange(): return lax.all_to_all(x, axis, split_axis=0, concat_axis=0, tiled=True)  12.6 us
    pallas_call x1, Pallas kernels, local(): pl.pallas_call(send_kernel, out_shape=(shape(NDEV, GIVE, HDIM), shape(1,...  3.07 us
    ppermute x2, starting transfers between devices, over_pair(): return lax.ppermute(both, 'seq_1', [(i, i ^ 1) for i in range(NZ)])  2.61 us
  transfers between devices with their start and end apart: 13, of which 7 were waited for; matrix products, arithmetic and copies ran while one was open for 0% of the time, Pallas kernels for 5%

profile of v12, /device:TPU:1, one launch (start us, length us, event | category | flops | bytes accessed | tf_op | source)
XLA Modules:
  0.0 95.5 jit_solution(5516806159408544891)
XLA Ops:
  0.6 3.1 %send.1 = (f32[32,72,128]{2,1,0:T(8,128)}, s32[1]{0:T(128)}) custom-call(s32[4]{0:T(128)} %lens.5, s32[1]{0:T(128)} %bitcast.20.here, bf16[256,1024]{1,0:T(8,128)(2,1)} %key_ref.3, bf16[256,1024]{1,0:T(8,128)(2,1)} %value_ref.3, f32[8,256]{1,0:T(8,128)} %bitcast.55), custom_call_target="tpu_custom_call" | custom-call | flops 3000000000 | bytes 9000000 | tf_op jit(solution)/shard_map/send/pallas_call | solution.py:411
  3.7 0.0 copy-start.1
  3.7 0.0 copy-start.6
  3.7 12.0 %all-to-all-start.1 = ((f32[32,72,128]{2,1,0:T(8,128)}), f32[32,72,128]{2,1,0:T(8,128)S(1)}, u32[]{:S(2)}, u32[]{:S(2)}) async-start(f32[32,72,128]{2,1,0:T(8,128)} %get-tuple-element.55), calls=%async_computation.1 | async-start | bytes 2359296 | tf_op jit(solution)/shard_map/all_to_all | solution.py:365
  15.8 0.0 copy-done.1
  15.8 0.0 copy-done.6
  15.8 0.0 copy-start
  15.8 0.0 copy-start.9
  15.8 0.0 copy-start.10
  15.8 0.0 copy-start.11
  15.8 0.0 copy-start.12
  15.8 0.6 query.1
  16.4 2.8 %collective-permute-start = (f32[2,72,128]{2,1,0:T(8,128)S(1)}, f32[2,72,128]{2,1,0:T(8,128)S(1)}, u32[]{:S(2)}, u32[]{:S(2)}) collective-permute-start(f32[2,72,128]{2,1,0:T(8,128)S(1)} %get-tuple-element.60), channel_id=1, source_target_pairs={{0,128},{64,192},{128,0},{192,64},{1,129},{65,193},{129,1},{193,65... | collective-permute-start | bytes 221192 | tf_op jit(solution)/shard_map/ppermute | solution.py:352
  19.3 0.3 collective-permute-start.1
  19.6 2.4 %collective-permute-start.2 = (f32[2,72,128]{2,1,0:T(8,128)S(1)}, f32[2,72,128]{2,1,0:T(8,128)S(1)}, u32[]{:S(2)}, u32[]{:S(2)}) collective-permute-start(f32[2,72,128]{2,1,0:T(8,128)S(1)} %get-tuple-element.62), channel_id=1, source_target_pairs={{0,192},{64,0},{128,64},{192,128},{1,193},{65,1},{129,65},{193,129... | collective-permute-start | bytes 221192 | tf_op jit(solution)/shard_map/ppermute | solution.py:352
  21.9 0.0 collective-permute-done.refs_1_
  22.0 3.7 %collective-permute-done.1.refs_2_ = f32[2,72,128]{2,1,0:T(8,128)S(1)} collective-permute-done((f32[2,72,128]{2,1,0:T(8,128)S(1)}, f32[2,72,128]{2,1,0:T(8,128)S(1)}, u32[]{:S(2)}, u32[]{:S(2)}) %collective-permute-start.1) | collective-permute-done | bytes 73760 | tf_op jit(solution)/shard_map/ppermute | solution.py:352
  25.6 0.0 collective-permute-done.2.refs_3_
  25.6 2.2 %collective-permute-start.3 = (f32[4,72,128]{2,1,0:T(8,128)S(1)}, f32[4,72,128]{2,1,0:T(8,128)S(1)}, u32[]{:S(2)}, u32[]{:S(2)}) collective-permute-start(f32[4,72,128]{2,1,0:T(8,128)S(1)} %pad_maximum_fusion.2), channel_id=1, source_target_pairs={{0,8},{8,0},{16,24},{24,16},{32,40},{40,32},{48,56},{56,48},{1,9},... | collective-permute-start | bytes 442376 | tf_op jit(solution)/shard_map/ppermute | solution.py:357
  27.9 0.0 copy-done
  27.9 0.0 copy-done.9
  27.9 0.0 copy-done.10
  27.9 0.0 copy-done.11
  27.9 0.0 copy-done.12
  27.9 1.9 %intra.1 = (f32[256,1024]{1,0:T(8,128)S(1)}, f32[256,8]{1,0:T(8,128)S(1)}) custom-call(s32[4]{0:T(128)S(1)} %copy-done.12, s32[1]{0:T(128)} %bitcast.20.here, bf16[256,1024]{1,0:T(8,128)(2,1)S(1)} %copy-done, bf16[256,1024]{1,0:T(8,128)(2,1)S(1)} %copy-done.10, bf16[256,1024]{1,0:T(8,128)(2,1)S(1)} %copy-done.9, f32[8,256]{1,0:T(8,128)S(1)} %bitcast.56), custom_call_target="tpu_custom_call" | custom-call | flops 3000000000 | bytes 9000000 | tf_op jit(solution)/shard_map/intra/pallas_call | solution.py:434
  29.8 0.0 copy-start.7
  29.8 0.9 copy-done.7
  30.7 15.0 %collective-permute-done.3.refs_4_ = f32[4,72,128]{2,1,0:T(8,128)S(1)} collective-permute-done((f32[4,72,128]{2,1,0:T(8,128)S(1)}, f32[4,72,128]{2,1,0:T(8,128)S(1)}, u32[]{:S(2)}, u32[]{:S(2)}) %collective-permute-start.3) | collective-permute-done | bytes 147488 | tf_op jit(solution)/shard_map/ppermute | solution.py:357
  45.7 0.0 all-to-all-done.1.give_ref
  46.4 0.6 slice.73.refs_5_
  47.0 5.1 %collective-permute-start.4 = (f32[4,32,128]{2,1,0:T(8,128)S(1)}, f32[4,32,128]{2,1,0:T(8,128)S(1)}, u32[]{:S(2)}, u32[]{:S(2)}) collective-permute-start(f32[4,32,128]{2,1,0:T(8,128)S(1)} %slice.73.refs_5_), channel_id=1, source_target_pairs={{0,32},{8,40},{16,48},{24,56},{32,0},{40,8},{48,16},{56,24},{1,33}... | collective-permute-start | bytes 196616 | tf_op jit(solution)/shard_map/ppermute | solution.py:352
  52.1 0.2 collective-permute-start.5
  52.4 3.3 %collective-permute-start.6 = (f32[4,32,128]{2,1,0:T(8,128)S(1)}, f32[4,32,128]{2,1,0:T(8,128)S(1)}, u32[]{:S(2)}, u32[]{:S(2)}) collective-permute-start(f32[4,32,128]{2,1,0:T(8,128)S(1)} %slice.73.refs_5_), channel_id=1, source_target_pairs={{0,48},{8,56},{16,0},{24,8},{32,16},{40,24},{48,32},{56,40},{1,49}... | collective-permute-start | bytes 196616 | tf_op jit(solution)/shard_map/ppermute | solution.py:352
  55.7 0.9 entry.1
  56.6 0.0 collective-permute-done.4.refs_6_
  56.6 3.1 %collective-permute-done.5.refs_7_ = f32[4,32,128]{2,1,0:T(8,128)S(1)} collective-permute-done((f32[4,32,128]{2,1,0:T(8,128)S(1)}, f32[4,32,128]{2,1,0:T(8,128)S(1)}, u32[]{:S(2)}, u32[]{:S(2)}) %collective-permute-start.5) | collective-permute-done | bytes 65568 | tf_op jit(solution)/shard_map/ppermute | solution.py:352
  59.7 0.0 collective-permute-done.6.refs_8_
  59.7 6.3 %all-to-all-start.2 = ((f32[32,32,128]{2,1,0:T(8,128)}), f32[32,32,128]{2,1,0:T(8,128)S(1)}, u32[]{:S(2)}, u32[]{:S(2)}) async-start(f32[32,32,128]{2,1,0:T(8,128)} %entry.1), calls=%async_computation.2 | async-start | bytes 1048576 | tf_op jit(solution)/shard_map/all_to_all | solution.py:365
  66.0 0.0 copy-start.2
  66.0 0.0 copy-start.3
  66.0 0.0 copy-start.4
  66.1 0.5 project.1
  66.5 2.8 %collective-permute-start.7 = (f32[2,64,128]{2,1,0:T(8,128)S(1)}, f32[2,64,128]{2,1,0:T(8,128)S(1)}, u32[]{:S(2)}, u32[]{:S(2)}) collective-permute-start(f32[2,64,128]{2,1,0:T(8,128)S(1)} %get-tuple-element.84), channel_id=1, source_target_pairs={{0,128},{64,192},{128,0},{192,64},{1,129},{65,193},{129,1},{193,65... | collective-permute-start | bytes 196616 | tf_op jit(solution)/shard_map/ppermute | solution.py:352
  69.4 0.9 collective-permute-start.8
  70.3 0.6 collective-permute-start.9
  70.8 0.5 collective-permute-done.7.refs_1_
  71.3 2.7 %collective-permute-done.8.refs_2_ = f32[2,64,128]{2,1,0:T(8,128)S(1)} collective-permute-done((f32[2,64,128]{2,1,0:T(8,128)S(1)}, f32[2,64,128]{2,1,0:T(8,128)S(1)}, u32[]{:S(2)}, u32[]{:S(2)}) %collective-permute-start.8) | collective-permute-done | bytes 65568 | tf_op jit(solution)/shard_map/ppermute | solution.py:352
  74.0 3.3 %collective-permute-done.9.refs_3_ = f32[2,64,128]{2,1,0:T(8,128)S(1)} collective-permute-done((f32[2,64,128]{2,1,0:T(8,128)S(1)}, f32[2,64,128]{2,1,0:T(8,128)S(1)}, u32[]{:S(2)}, u32[]{:S(2)}) %collective-permute-start.9) | collective-permute-done | bytes 65568 | tf_op jit(solution)/shard_map/ppermute | solution.py:352
  77.4 0.4 collective-permute-start.10
  77.8 0.0 copy-done.2
  77.8 0.0 copy-done.3
  77.8 0.0 copy-done.4
  77.8 0.0 copy-start.8
  77.8 0.7 local.1
  78.5 0.0 all-to-all-done.2.back_ref
  78.5 0.5 copy-done.8
  79.0 0.5 mixed.1
  79.5 2.1 %collective-permute-done.10.refs_4_ = f32[4,64,128]{2,1,0:T(8,128)S(1)} collective-permute-done((f32[4,64,128]{2,1,0:T(8,128)S(1)}, f32[4,64,128]{2,1,0:T(8,128)S(1)}, u32[]{:S(2)}, u32[]{:S(2)}) %collective-permute-start.10) | collective-permute-done | bytes 131104 | tf_op jit(solution)/shard_map/ppermute | solution.py:357
  81.6 0.0 copy-start.5
  81.6 0.3 decode.1
  81.9 12.6 %all_to_all.19.sums_ref = f32[8,4,128]{2,1,0:T(4,128)S(1)} all-to-all(f32[8,4,128]{2,1,0:T(4,128)S(1)} %get-tuple-element.87), channel_id=1, replica_groups=mesh['seq_0'=4,'seq_1'=8,'head'=8] {'head'}, dimensions={0} | all-to-all | bytes 32768 | tf_op jit(solution)/shard_map/all_to_all | solution.py:365
  94.5 0.0 copy-done.5
  94.5 1.1 %final.1 = (bf16[256,1024]{1,0:T(8,128)(2,1)}, bf16[4,16,1024]{2,1,0:T(8,128)(2,1)}) custom-call(f32[8,4,128]{2,1,0:T(4,128)S(1)} %all_to_all.19.sums_ref, f32[256,1024]{1,0:T(8,128)S(1)} %get-tuple-element.88.mixed_ref, f32[64,1024]{1,0:T(8,128)S(1)} %get-tuple-element.89.dec_ref, f32[1,1024]{1,0:T(1,128)S(1)} %bitcast.47), custom_call_target="tpu_custom_call" | custom-call | flops 2000000000 | bytes 6000000 | tf_op jit(solution)/shard_map/final/pallas_call | solution.py:520
  (12 shorter events, 0.1 us)
Async XLA Ops:
  3.7 12.0 %copy-start.1 = (bf16[4,16,1024]{2,1,0:T(8,128)(2,1)S(1)}, bf16[4,16,1024]{2,1,0:T(8,128)(2,1)}, u32[]{:S(2)}) copy-start(bf16[4,16,1024]{2,1,0:T(8,128)(2,1)} %sq_ref.1) | copy-start | bytes 393220
  3.7 12.0 %copy-start.6 = (s32[16]{0:T(128)S(1)}, s32[16]{0:T(128)}, u32[]{:S(2)}) copy-start(s32[16]{0:T(128)} %rows.1) | copy-start | bytes 196
  3.7 42.0 %all-to-all-start.1 = ((f32[32,72,128]{2,1,0:T(8,128)}), f32[32,72,128]{2,1,0:T(8,128)S(1)}, u32[]{:S(2)}, u32[]{:S(2)}) async-start(f32[32,72,128]{2,1,0:T(8,128)} %get-tuple-element.55), calls=%async_computation.1 | async-start | bytes 2359296 | tf_op jit(solution)/shard_map/all_to_all | solution.py:365
  15.8 12.1 %copy-start = (bf16[256,1024]{1,0:T(8,128)(2,1)S(1)}, bf16[256,1024]{1,0:T(8,128)(2,1)}, u32[]{:S(2)}) copy-start(bf16[256,1024]{1,0:T(8,128)(2,1)} %query_ref.5) | copy-start | bytes 1572868
  15.8 12.1 %copy-start.9 = (bf16[256,1024]{1,0:T(8,128)(2,1)S(1)}, bf16[256,1024]{1,0:T(8,128)(2,1)}, u32[]{:S(2)}) copy-start(bf16[256,1024]{1,0:T(8,128)(2,1)} %value_ref.3) | copy-start | bytes 1572868
  15.8 12.1 %copy-start.10 = (bf16[256,1024]{1,0:T(8,128)(2,1)S(1)}, bf16[256,1024]{1,0:T(8,128)(2,1)}, u32[]{:S(2)}) copy-start(bf16[256,1024]{1,0:T(8,128)(2,1)} %key_ref.3) | copy-start | bytes 1572868
  15.8 12.1 %copy-start.11 = (f32[256,8]{0,1:T(8,128)S(1)}, f32[256,8]{0,1:T(8,128)}, u32[]{:S(2)}) copy-start(f32[256,8]{0,1:T(8,128)} %param.16) | copy-start | bytes 24580
  15.8 12.1 %copy-start.12 = (s32[4]{0:T(128)S(1)}, s32[4]{0:T(128)}, u32[]{:S(2)}) copy-start(s32[4]{0:T(128)} %lens.5) | copy-start | bytes 52
  16.4 5.5 %collective-permute-start = (f32[2,72,128]{2,1,0:T(8,128)S(1)}, f32[2,72,128]{2,1,0:T(8,128)S(1)}, u32[]{:S(2)}, u32[]{:S(2)}) collective-permute-start(f32[2,72,128]{2,1,0:T(8,128)S(1)} %get-tuple-element.60), channel_id=1, source_target_pairs={{0,128},{64,192},{128,0},{192,64},{1,129},{65,193},{129,1},{193,65... | collective-permute-start | bytes 221192 | tf_op jit(solution)/shard_map/ppermute | solution.py:352
  19.3 6.3 %collective-permute-start.1 = (f32[2,72,128]{2,1,0:T(8,128)S(1)}, f32[2,72,128]{2,1,0:T(8,128)S(1)}, u32[]{:S(2)}, u32[]{:S(2)}) collective-permute-start(f32[2,72,128]{2,1,0:T(8,128)S(1)} %get-tuple-element.61), channel_id=1, source_target_pairs={{0,64},{64,128},{128,192},{192,0},{1,65},{65,129},{129,193},{193,1... | collective-permute-start | bytes 221192 | tf_op jit(solution)/shard_map/ppermute | solution.py:352
  19.6 6.0 %collective-permute-start.2 = (f32[2,72,128]{2,1,0:T(8,128)S(1)}, f32[2,72,128]{2,1,0:T(8,128)S(1)}, u32[]{:S(2)}, u32[]{:S(2)}) collective-permute-start(f32[2,72,128]{2,1,0:T(8,128)S(1)} %get-tuple-element.62), channel_id=1, source_target_pairs={{0,192},{64,0},{128,64},{192,128},{1,193},{65,1},{129,65},{193,129... | collective-permute-start | bytes 221192 | tf_op jit(solution)/shard_map/ppermute | solution.py:352
  25.6 20.0 %collective-permute-start.3 = (f32[4,72,128]{2,1,0:T(8,128)S(1)}, f32[4,72,128]{2,1,0:T(8,128)S(1)}, u32[]{:S(2)}, u32[]{:S(2)}) collective-permute-start(f32[4,72,128]{2,1,0:T(8,128)S(1)} %pad_maximum_fusion.2), channel_id=1, source_target_pairs={{0,8},{8,0},{16,24},{24,16},{32,40},{40,32},{48,56},{56,48},{1,9},... | collective-permute-start | bytes 442376 | tf_op jit(solution)/shard_map/ppermute | solution.py:357
  29.8 1.0 %copy-start.7 = (f32[256,1024]{1,0:T(8,128)}, f32[256,1024]{1,0:T(8,128)S(1)}, u32[]{:S(2)}) copy-start(f32[256,1024]{1,0:T(8,128)S(1)} %get-tuple-element.71.intra_ref) | copy-start | bytes 3145732
  47.0 9.6 %collective-permute-start.4 = (f32[4,32,128]{2,1,0:T(8,128)S(1)}, f32[4,32,128]{2,1,0:T(8,128)S(1)}, u32[]{:S(2)}, u32[]{:S(2)}) collective-permute-start(f32[4,32,128]{2,1,0:T(8,128)S(1)} %slice.73.refs_5_), channel_id=1, source_target_pairs={{0,32},{8,40},{16,48},{24,56},{32,0},{40,8},{48,16},{56,24},{1,33}... | collective-permute-start | bytes 196616 | tf_op jit(solution)/shard_map/ppermute | solution.py:352
  52.1 7.6 %collective-permute-start.5 = (f32[4,32,128]{2,1,0:T(8,128)S(1)}, f32[4,32,128]{2,1,0:T(8,128)S(1)}, u32[]{:S(2)}, u32[]{:S(2)}) collective-permute-start(f32[4,32,128]{2,1,0:T(8,128)S(1)} %slice.73.refs_5_), channel_id=1, source_target_pairs={{0,16},{8,24},{16,32},{24,40},{32,48},{40,56},{48,0},{56,8},{1,17}... | collective-permute-start | bytes 196616 | tf_op jit(solution)/shard_map/ppermute | solution.py:352
  52.4 7.3 %collective-permute-start.6 = (f32[4,32,128]{2,1,0:T(8,128)S(1)}, f32[4,32,128]{2,1,0:T(8,128)S(1)}, u32[]{:S(2)}, u32[]{:S(2)}) collective-permute-start(f32[4,32,128]{2,1,0:T(8,128)S(1)} %slice.73.refs_5_), channel_id=1, source_target_pairs={{0,48},{8,56},{16,0},{24,8},{32,16},{40,24},{48,32},{56,40},{1,49}... | collective-permute-start | bytes 196616 | tf_op jit(solution)/shard_map/ppermute | solution.py:352
  59.7 18.8 %all-to-all-start.2 = ((f32[32,32,128]{2,1,0:T(8,128)}), f32[32,32,128]{2,1,0:T(8,128)S(1)}, u32[]{:S(2)}, u32[]{:S(2)}) async-start(f32[32,32,128]{2,1,0:T(8,128)} %entry.1), calls=%async_computation.2 | async-start | bytes 1048576 | tf_op jit(solution)/shard_map/all_to_all | solution.py:365
  66.0 11.8 %copy-start.2 = (bf16[4,16,1024]{2,1,0:T(8,128)(2,1)S(1)}, bf16[4,16,1024]{2,1,0:T(8,128)(2,1)}, u32[]{:S(2)}) copy-start(bf16[4,16,1024]{2,1,0:T(8,128)(2,1)} %sk_ref) | copy-start | bytes 393220
  66.0 11.8 %copy-start.3 = (bf16[4,16,1024]{2,1,0:T(8,128)(2,1)S(1)}, bf16[4,16,1024]{2,1,0:T(8,128)(2,1)}, u32[]{:S(2)}) copy-start(bf16[4,16,1024]{2,1,0:T(8,128)(2,1)} %sv_ref.1) | copy-start | bytes 393220
  66.0 11.8 %copy-start.4 = (f32[4,16,8]{1,2,0:T(8,128)S(1)}, f32[4,16,8]{1,2,0:T(8,128)}, u32[]{:S(2)}) copy-start(f32[4,16,8]{1,2,0:T(8,128)} %param.22) | copy-start | bytes 6148
  66.5 4.8 %collective-permute-start.7 = (f32[2,64,128]{2,1,0:T(8,128)S(1)}, f32[2,64,128]{2,1,0:T(8,128)S(1)}, u32[]{:S(2)}, u32[]{:S(2)}) collective-permute-start(f32[2,64,128]{2,1,0:T(8,128)S(1)} %get-tuple-element.84), channel_id=1, source_target_pairs={{0,128},{64,192},{128,0},{192,64},{1,129},{65,193},{129,1},{193,65... | collective-permute-start | bytes 196616 | tf_op jit(solution)/shard_map/ppermute | solution.py:352
  69.4 4.7 %collective-permute-start.8 = (f32[2,64,128]{2,1,0:T(8,128)S(1)}, f32[2,64,128]{2,1,0:T(8,128)S(1)}, u32[]{:S(2)}, u32[]{:S(2)}) collective-permute-start(f32[2,64,128]{2,1,0:T(8,128)S(1)} %get-tuple-element.85), channel_id=1, source_target_pairs={{0,192},{64,0},{128,64},{192,128},{1,193},{65,1},{129,65},{193,129... | collective-permute-start | bytes 196616 | tf_op jit(solution)/shard_map/ppermute | solution.py:352
  70.3 7.1 %collective-permute-start.9 = (f32[2,64,128]{2,1,0:T(8,128)S(1)}, f32[2,64,128]{2,1,0:T(8,128)S(1)}, u32[]{:S(2)}, u32[]{:S(2)}) collective-permute-start(f32[2,64,128]{2,1,0:T(8,128)S(1)} %get-tuple-element.86), channel_id=1, source_target_pairs={{0,64},{64,128},{128,192},{192,0},{1,65},{65,129},{129,193},{193,1... | collective-permute-start | bytes 196616 | tf_op jit(solution)/shard_map/ppermute | solution.py:352
  77.4 4.2 %collective-permute-start.10 = (f32[4,64,128]{2,1,0:T(8,128)S(1)}, f32[4,64,128]{2,1,0:T(8,128)S(1)}, u32[]{:S(2)}, u32[]{:S(2)}) collective-permute-start(f32[4,64,128]{2,1,0:T(8,128)S(1)} %pad_maximum_fusion.3), channel_id=1, source_target_pairs={{0,8},{8,0},{16,24},{24,16},{32,40},{40,32},{48,56},{56,48},{1,9},... | collective-permute-start | bytes 393224 | tf_op jit(solution)/shard_map/ppermute | solution.py:357
  77.8 1.2 %copy-start.8 = (f32[256,1024]{1,0:T(8,128)S(1)}, f32[256,1024]{1,0:T(8,128)}, u32[]{:S(2)}) copy-start(f32[256,1024]{1,0:T(8,128)} %copy-done.7) | copy-start | bytes 3145732
  81.6 12.9 %copy-start.5 = (f32[1024]{0:T(1024)S(1)}, f32[1024]{0:T(1024)}, u32[]{:S(2)}) copy-start(f32[1024]{0:T(1024)} %param.17) | copy-start | bytes 12292
